TPU v7x, 32 devices: a whole 2x2x4 slice. The times are simulated.
32 devices in a mesh: fsdp: 4 (over z), seq: 8 (over y, x, core).
Axes of the slice: x: 2, y: 2, z: 4, core: 2. Of those that a mesh axis runs over, the one named last changes fastest.
Arguments:
- layer_input: bfloat16 [8192, 2048], P(('fsdp', 'seq')), may hold values from -6 to 6
- lengths: int32 [4, 4], P('fsdp'), may hold values from 32 to 2048, as said below
- norm1_gain: bfloat16 [2048], P(('fsdp', 'seq')), may hold values from 0.5 to 1.5
- w_x: bfloat16 [2048, 2560], P(('fsdp', 'seq')), may hold values from -0.125 to 0.125
- w_y: bfloat16 [2048, 2560], P(('fsdp', 'seq')), may hold values from -0.125 to 0.125
- conv_w: bfloat16 [2560, 4], P(('fsdp', 'seq')), may hold values from -3 to 3
- conv_b: bfloat16 [2560], P(('fsdp', 'seq')), may hold values from -2 to 2
- w_rgate: bfloat16 [2560, 160], P(('fsdp', 'seq')), may hold values from -0.5 to 0.5
- b_rgate: bfloat16 [2560], P(('fsdp', 'seq')), may hold values from -3 to 3
- w_igate: bfloat16 [2560, 160], P(('fsdp', 'seq')), may hold values from -0.5 to 0.5
- b_igate: bfloat16 [2560], P(('fsdp', 'seq')), may hold values from -3 to 3
- lam: bfloat16 [2560], P(('fsdp', 'seq')), may hold values from 3 to 14
- w_out: bfloat16 [2560, 2048], P(('fsdp', 'seq')), may hold values from -0.25 to 0.25
- norm2_gain: bfloat16 [2048], P(('fsdp', 'seq')), may hold values from 0.5 to 1.5
- w_gate: bfloat16 [2048, 6144], P(('fsdp', 'seq')), may hold values from -0.125 to 0.125
- w_up: bfloat16 [2048, 6144], P(('fsdp', 'seq')), may hold values from -0.125 to 0.125
- w_down: bfloat16 [6144, 2048], P(('fsdp', 'seq')), may hold values from -0.15625 to 0.15625
- cot: bfloat16 [8192, 2048], P(('fsdp', 'seq')), may hold values from -6 to 6
Outputs:
- layer_output: bfloat16 [8192, 2048], P(('fsdp', 'seq'))
- d_x: bfloat16 [8192, 2048], P(('fsdp', 'seq'))
- d_norm1_gain: float32 [2048], P(('fsdp', 'seq'))
- d_w_x: float32 [2048, 2560], P(('fsdp', 'seq'))
- d_w_y: float32 [2048, 2560], P(('fsdp', 'seq'))
- d_conv_w: float32 [2560, 4], P(('fsdp', 'seq'))
- d_conv_b: float32 [2560], P(('fsdp', 'seq'))
- d_w_rgate: float32 [2560, 160], P(('fsdp', 'seq'))
- d_b_rgate: float32 [2560], P(('fsdp', 'seq'))
- d_w_igate: float32 [2560, 160], P(('fsdp', 'seq'))
- d_b_igate: float32 [2560], P(('fsdp', 'seq'))
- d_lam: float32 [2560], P(('fsdp', 'seq'))
- d_w_out: float32 [2560, 2048], P(('fsdp', 'seq'))
- d_norm2_gain: float32 [2048], P(('fsdp', 'seq'))
- d_w_gate: float32 [2048, 6144], P(('fsdp', 'seq'))
- d_w_up: float32 [2048, 6144], P(('fsdp', 'seq'))
- d_w_down: float32 [6144, 2048], P(('fsdp', 'seq'))
Inputs may be any that keep to these rules, and one draw needn't show every extreme that they name: `lengths`: each row sums to 2048. One entry, at a place drawn from the seed, exceeds 2048 - 256; the others are at most (255) // 3, and the first of them equals 32.
All inputs are finite; a program needn't handle non-finite values.
Results may differ from a plain program's by a relative error of at most 0.013.
Values may be sent and summed in bfloat16 or wider, within the bound.
No kernel may reach another device: no remote copies, remote signals or barrier semaphores. Data moves between devices by JAX's collectives and lax.ppermute only.
A program may use at most 448 MiB of HBM per device.

v0:
```python
import jax
import jax.numpy as jnp
from jax import lax
from jax.sharding import PartitionSpec as P

DECAY_C = 8.0
NORM_EPS = 1e-06


def from_behind(x, axis, by):
    size = lax.axis_size(axis)
    pairs = [(i, i + by) for i in range(size) if 0 <= i + by < size]
    return lax.ppermute(x, axis, pairs)


def carried_in(value, axis, join, neutral, backward):
    count, mine = (lax.axis_size(axis), lax.axis_index(axis))
    pieces = jax.tree.map(lambda part: lax.all_gather(part, axis), value)
    if backward:
        pieces = jax.tree.map(lambda part: part[::-1], pieces)
        mine = count - 1 - mine
    subtotal = jax.tree.map(
        lambda part, zero: jnp.full_like(part, 0) + jnp.asarray(zero, part.dtype), value, neutral
    )

    def step(position, subtotal):
        longer = join(subtotal, jax.tree.map(lambda part: part[position], pieces))
        return jax.tree.map(lambda new, old: jnp.where(position < mine, new, old), longer, subtotal)

    return lax.fori_loop(0, count - 1, step, subtotal)


def rms_apply(value, gain):
    scale = lax.rsqrt(jnp.mean(value * value, axis=-1, keepdims=True) + NORM_EPS)
    return value * scale * gain


def combine(earlier, later):
    return (earlier[0] * later[0], later[0] * earlier[1] + later[1])


def lru_terms(pre_r, pre_i, lam_vec, conv_out, start):
    rate = jax.nn.softplus(-lam_vec)
    log_a = -DECAY_C * jax.nn.sigmoid(pre_r) * rate
    decay = jnp.where(start[:, None], 0.0, jnp.exp(log_a))
    scale = jnp.sqrt(jnp.maximum(-jnp.expm1(2.0 * log_a), 0.2 * DECAY_C * rate))
    scale = jnp.where(start[:, None], 1.0, scale)
    return (decay, scale * jax.nn.sigmoid(pre_i) * conv_out)


def row_contract(left, right):
    return lax.dot_general(
        left, right, (((0,), (0,)), ((), ())), preferred_element_type=jnp.float32
    )


def back_product(grad, weight):
    return lax.dot_general(
        grad, weight, (((1,), (1,)), ((), ())), preferred_element_type=jnp.float32
    )


def split_blocks(value, width):
    return value.reshape(value.shape[0], value.shape[1] // width, width)


def block_product(value, weight):
    width = weight.shape[1]
    mats = weight.reshape(weight.shape[0] // width, width, width)
    result = jnp.einsum(
        "nhi,hij->nhj", split_blocks(value, width), mats, preferred_element_type=jnp.float32
    )
    return result.reshape(value.shape[0], -1)


def block_back(grad, weight):
    width = weight.shape[1]
    mats = weight.reshape(weight.shape[0] // width, width, width)
    result = jnp.einsum(
        "nhj,hij->nhi", split_blocks(grad, width), mats, preferred_element_type=jnp.float32
    )
    return result.reshape(grad.shape[0], -1)


def gate_grad(value, grad, width):
    result = jnp.einsum(
        "nhi,nhj->hij",
        split_blocks(value, width),
        split_blocks(grad, width),
        preferred_element_type=jnp.float32,
    )
    return result.reshape(value.shape[1], width)


def seq_masks(lens_row, first, rows, taps):
    ends = jnp.cumsum(lens_row)
    starts = ends - lens_row
    place = first + jnp.arange(rows, dtype=jnp.int32)

    def segment(p):
        return jnp.sum((p[:, None] >= starts[None, :]).astype(jnp.int32), axis=1)

    seg_now = segment(place)
    start = jnp.any(place[:, None] == starts[None, :], axis=1)
    same = jnp.stack(
        [
            ((segment(place - k) == seg_now) & (place - k >= 0)).astype(jnp.float32)
            for k in range(taps)
        ],
        0,
    )
    return (start, same)


def on_device(
    layer_input,
    lengths,
    norm1_gain,
    w_x,
    w_y,
    conv_w,
    conv_b,
    w_rgate,
    b_rgate,
    w_igate,
    b_igate,
    lam,
    w_out,
    norm2_gain,
    w_gate,
    w_up,
    w_down,
    cot,
):
    rows = layer_input.shape[0]
    taps = conv_w.shape[1]
    width = w_rgate.shape[1]
    rim = taps - 1
    index = lax.axis_index("seq")
    start, same = seq_masks(lengths[0], index * rows, rows, taps)
    gain_one, wx, wy, cw, cb, wr, br, wi, bi, lam_all, wo = (
        lax.all_gather(norm1_gain, ("fsdp", "seq"), axis=0, tiled=True),
        lax.all_gather(w_x, ("fsdp", "seq"), axis=0, tiled=True),
        lax.all_gather(w_y, ("fsdp", "seq"), axis=0, tiled=True),
        lax.all_gather(conv_w, ("fsdp", "seq"), axis=0, tiled=True),
        lax.all_gather(conv_b, ("fsdp", "seq"), axis=0, tiled=True),
        lax.all_gather(w_rgate, ("fsdp", "seq"), axis=0, tiled=True),
        lax.all_gather(b_rgate, ("fsdp", "seq"), axis=0, tiled=True),
        lax.all_gather(w_igate, ("fsdp", "seq"), axis=0, tiled=True),
        lax.all_gather(b_igate, ("fsdp", "seq"), axis=0, tiled=True),
        lax.all_gather(lam, ("fsdp", "seq"), axis=0, tiled=True),
        lax.all_gather(w_out, ("fsdp", "seq"), axis=0, tiled=True),
    )
    xf = layer_input.astype(jnp.float32)
    gain1 = gain_one.astype(jnp.float32)
    un = rms_apply(xf, gain1).astype(jnp.bfloat16)
    xb = jnp.dot(un, wx, preferred_element_type=jnp.float32).astype(jnp.bfloat16)
    yb = jnp.dot(un, wy, preferred_element_type=jnp.float32)
    gy = jax.nn.gelu(yb)
    rim_in = from_behind(xb[rows - rim :], "seq", 1)
    extended = jnp.concatenate([rim_in, xb], axis=0).astype(jnp.float32)
    cwf = cw.astype(jnp.float32)
    conv = jnp.broadcast_to(cb.astype(jnp.float32)[None, :], (rows, cwf.shape[0]))
    for k in range(taps):
        conv = conv + cwf[:, k][None, :] * extended[rim - k : rim - k + rows] * same[k][:, None]
    xc = conv.astype(jnp.bfloat16)
    xcf = xc.astype(jnp.float32)
    pre_r = block_product(xc, wr) + br.astype(jnp.float32)[None, :]
    pre_i = block_product(xc, wi) + bi.astype(jnp.float32)[None, :]
    lamf = lam_all.astype(jnp.float32)
    decay, drive = lru_terms(pre_r, pre_i, lamf, xcf, start)
    decay_cum, state_loc = lax.associative_scan(combine, (decay, drive), axis=0)
    zero_vec = jnp.zeros((decay.shape[1],), jnp.float32)
    one_vec = jnp.ones((decay.shape[1],), jnp.float32)
    state_in = carried_in(
        (decay_cum[-1], state_loc[-1]), "seq", combine, (one_vec, zero_vec), False
    )[1]
    state = state_loc + decay_cum * state_in[None, :]
    state_prev = jnp.concatenate([state_in[None, :], state[:-1]], axis=0)
    mixed = (state * gy).astype(jnp.bfloat16)
    resid = xf + jnp.dot(mixed, wo, preferred_element_type=jnp.float32)
    gain_two, wg, wu, wd = (
        lax.all_gather(norm2_gain, ("fsdp", "seq"), axis=0, tiled=True),
        lax.all_gather(w_gate, ("fsdp", "seq"), axis=0, tiled=True),
        lax.all_gather(w_up, ("fsdp", "seq"), axis=0, tiled=True),
        lax.all_gather(w_down, ("fsdp", "seq"), axis=0, tiled=True),
    )
    gain2 = gain_two.astype(jnp.float32)
    un2 = rms_apply(resid, gain2).astype(jnp.bfloat16)
    gate_pre = jnp.dot(un2, wg, preferred_element_type=jnp.float32)
    up_pre = jnp.dot(un2, wu, preferred_element_type=jnp.float32)
    gate_act, gelu_back = jax.vjp(jax.nn.gelu, gate_pre)
    hidden = (gate_act * up_pre).astype(jnp.bfloat16)
    output = (resid + jnp.dot(hidden, wd, preferred_element_type=jnp.float32)).astype(jnp.bfloat16)
    grad = cot.astype(jnp.float32)
    gain_two, wg, wu, wd = (
        lax.all_gather(norm2_gain, ("fsdp", "seq"), axis=0, tiled=True),
        lax.all_gather(w_gate, ("fsdp", "seq"), axis=0, tiled=True),
        lax.all_gather(w_up, ("fsdp", "seq"), axis=0, tiled=True),
        lax.all_gather(w_down, ("fsdp", "seq"), axis=0, tiled=True),
    )
    gain2 = gain_two.astype(jnp.float32)
    d_wd = row_contract(hidden, cot)
    d_hidden = back_product(cot, wd)
    d_gate = gelu_back(d_hidden * up_pre)[0].astype(jnp.bfloat16)
    d_up = (d_hidden * gate_act).astype(jnp.bfloat16)
    d_wg = row_contract(un2, d_gate)
    d_wu = row_contract(un2, d_up)
    d_un2 = back_product(d_gate, wg) + back_product(d_up, wu)
    norm_two_back = jax.vjp(rms_apply, resid, gain2)[1]
    d_resid_norm, d_gain2 = norm_two_back(d_un2)
    mlp_grads = (
        lax.psum_scatter(d_gain2, ("fsdp", "seq"), scatter_dimension=0, tiled=True),
        lax.psum_scatter(d_wg, ("fsdp", "seq"), scatter_dimension=0, tiled=True),
        lax.psum_scatter(d_wu, ("fsdp", "seq"), scatter_dimension=0, tiled=True),
        lax.psum_scatter(d_wd, ("fsdp", "seq"), scatter_dimension=0, tiled=True),
    )
    d_resid = grad + d_resid_norm
    gain_one, wx, wy, cw, cb, wr, br, wi, bi, lam_all, wo = (
        lax.all_gather(norm1_gain, ("fsdp", "seq"), axis=0, tiled=True),
        lax.all_gather(w_x, ("fsdp", "seq"), axis=0, tiled=True),
        lax.all_gather(w_y, ("fsdp", "seq"), axis=0, tiled=True),
        lax.all_gather(conv_w, ("fsdp", "seq"), axis=0, tiled=True),
        lax.all_gather(conv_b, ("fsdp", "seq"), axis=0, tiled=True),
        lax.all_gather(w_rgate, ("fsdp", "seq"), axis=0, tiled=True),
        lax.all_gather(b_rgate, ("fsdp", "seq"), axis=0, tiled=True),
        lax.all_gather(w_igate, ("fsdp", "seq"), axis=0, tiled=True),
        lax.all_gather(b_igate, ("fsdp", "seq"), axis=0, tiled=True),
        lax.all_gather(lam, ("fsdp", "seq"), axis=0, tiled=True),
        lax.all_gather(w_out, ("fsdp", "seq"), axis=0, tiled=True),
    )
    gain1 = gain_one.astype(jnp.float32)
    cwf = cw.astype(jnp.float32)
    lamf = lam_all.astype(jnp.float32)
    d_mix = d_resid.astype(jnp.bfloat16)
    d_wo = row_contract(mixed, d_mix)
    d_mixed = back_product(d_mix, wo)
    d_state = d_mixed * gy
    gelu_y_back = jax.vjp(jax.nn.gelu, yb)[1]
    d_yb = gelu_y_back(d_mixed * state)[0].astype(jnp.bfloat16)
    next_decay = jnp.concatenate([decay[1:], one_vec[None, :]], axis=0)
    decay_after, adjoint_loc = lax.associative_scan(
        combine, (next_decay, d_state), reverse=True, axis=0
    )
    send_decay = decay[0] * decay_after[0]
    send_adjoint = decay[0] * adjoint_loc[0]
    adjoint_in = carried_in((send_decay, send_adjoint), "seq", combine, (one_vec, zero_vec), True)[
        1
    ]
    adjoint = adjoint_loc + decay_after * adjoint_in[None, :]

    def local_lru(pr, pi, lv, cv):
        return lru_terms(pr, pi, lv, cv, start)

    lru_back = jax.vjp(local_lru, pre_r, pre_i, lamf, xcf)[1]
    d_pre_r, d_pre_i, d_lam, d_xc_local = lru_back((adjoint * state_prev, adjoint))
    d_pr = d_pre_r.astype(jnp.bfloat16)
    d_pi = d_pre_i.astype(jnp.bfloat16)
    d_wr = gate_grad(xc, d_pr, width)
    d_wi = gate_grad(xc, d_pi, width)
    d_br = jnp.sum(d_pr.astype(jnp.float32), axis=0)
    d_bi = jnp.sum(d_pi.astype(jnp.float32), axis=0)
    d_xc = d_xc_local + block_back(d_pr, wr) + block_back(d_pi, wi)
    d_cb = jnp.sum(d_xc, axis=0)
    d_cw = jnp.stack(
        [
            jnp.sum(d_xc * extended[rim - k : rim - k + rows] * same[k][:, None], axis=0)
            for k in range(taps)
        ],
        axis=1,
    )
    d_extended = jnp.zeros((rows + rim, d_xc.shape[1]), jnp.float32)
    for k in range(taps):
        d_extended = d_extended + jnp.pad(
            d_xc * cwf[:, k][None, :] * same[k][:, None], ((rim - k, k), (0, 0))
        )
    rim_back = from_behind(d_extended[:rim], "seq", -1)
    d_xb = (d_extended[rim:] + jnp.pad(rim_back, ((rows - rim, 0), (0, 0)))).astype(jnp.bfloat16)
    d_wx = row_contract(un, d_xb)
    d_wy = row_contract(un, d_yb)
    d_un = back_product(d_xb, wx) + back_product(d_yb, wy)
    norm_one_back = jax.vjp(rms_apply, xf, gain1)[1]
    d_x_norm, d_gain1 = norm_one_back(d_un)
    d_input = (d_resid + d_x_norm).astype(jnp.bfloat16)
    block_grads = (
        lax.psum_scatter(d_gain1, ("fsdp", "seq"), scatter_dimension=0, tiled=True),
        lax.psum_scatter(d_wx, ("fsdp", "seq"), scatter_dimension=0, tiled=True),
        lax.psum_scatter(d_wy, ("fsdp", "seq"), scatter_dimension=0, tiled=True),
        lax.psum_scatter(d_cw, ("fsdp", "seq"), scatter_dimension=0, tiled=True),
        lax.psum_scatter(d_cb, ("fsdp", "seq"), scatter_dimension=0, tiled=True),
        lax.psum_scatter(d_wr, ("fsdp", "seq"), scatter_dimension=0, tiled=True),
        lax.psum_scatter(d_br, ("fsdp", "seq"), scatter_dimension=0, tiled=True),
        lax.psum_scatter(d_wi, ("fsdp", "seq"), scatter_dimension=0, tiled=True),
        lax.psum_scatter(d_bi, ("fsdp", "seq"), scatter_dimension=0, tiled=True),
        lax.psum_scatter(d_lam, ("fsdp", "seq"), scatter_dimension=0, tiled=True),
        lax.psum_scatter(d_wo, ("fsdp", "seq"), scatter_dimension=0, tiled=True),
    )
    return (
        output,
        d_input,
        block_grads[0],
        block_grads[1],
        block_grads[2],
        block_grads[3],
        block_grads[4],
        block_grads[5],
        block_grads[6],
        block_grads[7],
        block_grads[8],
        block_grads[9],
        block_grads[10],
        mlp_grads[0],
        mlp_grads[1],
        mlp_grads[2],
        mlp_grads[3],
    )


def solution(mesh):
    in_specs = (
        P(("fsdp", "seq"), None),
        P("fsdp", None),
        P(("fsdp", "seq")),
        P(("fsdp", "seq"), None),
        P(("fsdp", "seq"), None),
        P(("fsdp", "seq"), None),
        P(("fsdp", "seq")),
        P(("fsdp", "seq"), None),
        P(("fsdp", "seq")),
        P(("fsdp", "seq"), None),
        P(("fsdp", "seq")),
        P(("fsdp", "seq")),
        P(("fsdp", "seq"), None),
        P(("fsdp", "seq")),
        P(("fsdp", "seq"), None),
        P(("fsdp", "seq"), None),
        P(("fsdp", "seq"), None),
        P(("fsdp", "seq"), None),
    )
    out_specs = (
        P(("fsdp", "seq"), None),
        P(("fsdp", "seq"), None),
        P(("fsdp", "seq")),
        P(("fsdp", "seq"), None),
        P(("fsdp", "seq"), None),
        P(("fsdp", "seq"), None),
        P(("fsdp", "seq")),
        P(("fsdp", "seq"), None),
        P(("fsdp", "seq")),
        P(("fsdp", "seq"), None),
        P(("fsdp", "seq")),
        P(("fsdp", "seq")),
        P(("fsdp", "seq"), None),
        P(("fsdp", "seq")),
        P(("fsdp", "seq"), None),
        P(("fsdp", "seq"), None),
        P(("fsdp", "seq"), None),
    )
    return jax.shard_map(
        on_device, mesh=mesh, in_specs=in_specs, out_specs=out_specs, check_vma=False
    )
```

profile of v0, /device:TPU:0, one launch (start us, length us, event | category | flops | bytes accessed | tf_op | source)
XLA Modules:
  0.0 3530.0 jit_solution(15614026928376556317)
XLA Ops:
  12.9 43.0 %all-reduce.84 = (bf16[2560]{0:T(1024)(128)(2,1)S(1)}, bf16[2048]{0:T(1024)(128)(2,1)S(1)}, bf16[2560]{0:T(1024)(128)(2,1)S(1)}, bf16[2560]{0:T(1024)(128)(2,1)S...) all-reduce(bf16[2560]{0:T(1024)(128)(2,1)S(1)} %dynamic-update-slic, ...), channel_id=1, replica_groups=mesh['fsdp'=4,'seq'=8] {'fsdp','seq'}, use_global_device_ids=true, to_apply=%add.74 | all-reduce | flops 14336 | bytes 57344
  55.9 40.9 %all-gather = bf16[32,80,4]{1,2,0:T(4,128)(2,1)S(1)} all-gather(bf16[1,80,4]{1,2,0:T(4,128)(2,1)S(1)} %bitcast.109), channel_id=1, replica_groups=mesh['fsdp'=4,'seq'=8] {'fsdp','seq'}, dimensions={0}, use_global_device_ids=true | all-gather | bytes 21120 | tf_op jit(solution)/shard_map/all_gather | solution.py:145
  97.9 44.3 %all_gather.75 = bf16[2560,160]{1,0:T(8,128)(2,1)} all-gather(bf16[80,160]{1,0:T(8,128)(2,1)S(1)} %copy-done.117), channel_id=1, replica_groups=mesh['fsdp'=4,'seq'=8] {'fsdp','seq'}, dimensions={0}, use_global_device_ids=true | all-gather | bytes 844800 | tf_op jit(solution)/shard_map/all_gather | solution.py:147
  142.2 49.3 %all_gather.78 = bf16[2560,160]{1,0:T(8,128)(2,1)} all-gather(bf16[80,160]{1,0:T(8,128)(2,1)S(1)} %copy-done.118), channel_id=1, replica_groups=mesh['fsdp'=4,'seq'=8] {'fsdp','seq'}, dimensions={0}, use_global_device_ids=true | all-gather | bytes 844800 | tf_op jit(solution)/shard_map/all_gather | solution.py:149
  224.6 8.2 convert_multiply_fusion.5
  383.8 9.4 pad.233
  394.2 10.5 all-gather.2
  407.2 9.2 pad.248
  430.0 11.1 slice.631
  441.1 10.9 slice.638
  460.1 12.4 multiply_convert_fusion.2
  479.0 15.8 fusion.92
  494.7 107.6 %all-gather.20.cloned.1.call-done = bf16[2048,6144]{1,0:T(8,128)(2,1)} async-done(((bf16[64,6144]{1,0:T(8,128)(2,1)}), bf16[2048,6144]{1,0:T(8,128)(2,1)}) %all-gather.20.cloned.1.call-update) | async-done | bytes 25165840 | tf_op jit(solution)/shard_map/all_gather | solution.py:185
  602.3 14.2 fusion.93
  616.5 141.4 %all-gather.22.cloned.1.call-done = bf16[6144,2048]{1,0:T(8,128)(2,1)} async-done(((bf16[192,2048]{1,0:T(8,128)(2,1)}), bf16[6144,2048]{1,0:T(8,128)(2,1)}) %all-gather.22.cloned.1.call-update) | async-done | bytes 25165840 | tf_op jit(solution)/shard_map/all_gather | solution.py:186
  757.9 21.9 multiply_convert_fusion
  779.8 13.5 fusion.94
  793.3 15.3 multiply_reduce_fusion.6
  811.7 9.5 fusion.34
  827.5 10.7 slice.633
  838.3 10.7 slice.635
  934.9 9.1 pad.281
  957.6 9.1 pad.265
  966.7 10.8 slice.691
  988.3 9.4 pad.280
  1004.2 9.2 all-gather.3
  1013.8 8.3 all-gather.4
  1023.2 13.1 rev.15
  1036.5 21.1 rev.14
  1057.7 9.7 multiply_reduce_fusion.1
  1094.4 9.8 multiply_reduce_fusion.5
  1113.3 10.4 fusion.37
  1125.4 8.8 fusion.73
  1141.3 8.8 fusion.43
  1151.3 21.4 fusion.98
  1172.8 21.4 fusion.99
  1195.4 21.5 fusion.100
  1222.8 13.1 fusion.22
  1235.9 8.8 fusion.26
  1244.7 41.8 %all-reduce.83 = (f32[2048]{0:T(1024)S(1)}, f32[2560]{0:T(1024)S(1)}, f32[2560]{0:T(1024)S(1)}, f32[2560]{0:T(1024)S(1)}, f32[2560]{0:T(1024)S(1)}, /*index=5*/f32[2048]{0:T(1024)S(1)}) all-reduce(f32[2048]{0:T(1024)S(1)} %get-tuple-element.249, f32[2560]{0:T(1024)S(1)} %copy-done.95, ...), channel_id=2, replica_groups=mesh['fsdp'=4,'seq'=8] {'fsdp','seq'}, use_global_device_ids=true, to_apply=%region_15.16.clone | all-reduce | flops 14336 | bytes 114688
  1294.7 81.5 %reduce-scatter.16.cloned.1.call-done = f32[80,160]{1,0:T(8,128)} async-done(((f32[2560,160]{1,0:T(8,128)}), f32[80,160]{1,0:T(8,128)}) %reduce-scatter.16.cloned.1.call-update) | async-done | bytes 51216 | tf_op jit(solution)/shard_map/reduce_scatter | solution.py:291
  1376.1 136.5 %reduce-scatter.18.cloned.1.call-done = f32[80,160]{1,0:T(8,128)} async-done(((f32[2560,160]{1,0:T(8,128)}), f32[80,160]{1,0:T(8,128)}) %reduce-scatter.18.cloned.1.call-update) | async-done | bytes 51216 | tf_op jit(solution)/shard_map/reduce_scatter | solution.py:293
  1512.6 224.2 %reduce-scatter.20.cloned.1.call-done = f32[80,2048]{1,0:T(8,128)} async-done(((f32[2560,2048]{1,0:T(8,128)}), f32[80,2048]{1,0:T(8,128)}) %reduce-scatter.20.cloned.1.call-update) | async-done | bytes 655376 | tf_op jit(solution)/shard_map/reduce_scatter | solution.py:296
  1736.8 232.6 %reduce-scatter.14.cloned.1.call-done = f32[64,2560]{1,0:T(8,128)} async-done(((f32[2048,2560]{1,0:T(8,128)}), f32[64,2560]{1,0:T(8,128)}) %reduce-scatter.14.cloned.1.call-update) | async-done | bytes 655376 | tf_op jit(solution)/shard_map/reduce_scatter | solution.py:288
  1969.4 232.5 %reduce-scatter.12.cloned.1.call-done = f32[64,2560]{1,0:T(8,128)} async-done(((f32[2048,2560]{1,0:T(8,128)}), f32[64,2560]{1,0:T(8,128)}) %reduce-scatter.12.cloned.1.call-update) | async-done | bytes 655376 | tf_op jit(solution)/shard_map/reduce_scatter | solution.py:287
  2201.9 444.0 %reduce-scatter.22.cloned.1.call-done = f32[64,6144]{1,0:T(8,128)} async-done(((f32[2048,6144]{1,0:T(8,128)}), f32[64,6144]{1,0:T(8,128)}) %reduce-scatter.22.cloned.1.call-update) | async-done | bytes 1572880 | tf_op jit(solution)/shard_map/reduce_scatter | solution.py:214
  2645.9 438.7 %reduce-scatter.24.cloned.1.call-done = f32[64,6144]{1,0:T(8,128)} async-done(((f32[2048,6144]{1,0:T(8,128)}), f32[64,6144]{1,0:T(8,128)}) %reduce-scatter.24.cloned.1.call-update) | async-done | bytes 1572880 | tf_op jit(solution)/shard_map/reduce_scatter | solution.py:215
  3084.6 438.7 %reduce-scatter.26.cloned.1.call-done = f32[192,2048]{1,0:T(8,128)} async-done(((f32[6144,2048]{1,0:T(8,128)}), f32[192,2048]{1,0:T(8,128)}) %reduce-scatter.26.cloned.1.call-update) | async-done | bytes 1572880 | tf_op jit(solution)/shard_map/reduce_scatter | solution.py:216
  (688 shorter events, 410.4 us)
Async XLA Ops:
  7.3 48.7 %copy-start.135 = (bf16[80,4]{0,1:T(4,128)(2,1)S(1)}, bf16[80,4]{0,1:T(4,128)(2,1)}, u32[]{:S(2)}) copy-start(bf16[80,4]{0,1:T(4,128)(2,1)} %param.27) | copy-start | bytes 1924
  7.3 89.7 %copy-start.142 = (s32[1,4]{1,0:T(1,128)S(1)}, s32[1,4]{1,0:T(1,128)}, u32[]{:S(2)}) copy-start(s32[1,4]{1,0:T(1,128)} %param.23) | copy-start | bytes 52
  7.3 90.2 %copy-start.4 = (bf16[256,2048]{1,0:T(8,128)(2,1)S(1)}, bf16[256,2048]{1,0:T(8,128)(2,1)}, u32[]{:S(2)}) copy-start(bf16[256,2048]{1,0:T(8,128)(2,1)} %param.22) | copy-start | bytes 3145732
  7.3 90.6 %copy-start.117 = (bf16[80,160]{1,0:T(8,128)(2,1)S(1)}, bf16[80,160]{1,0:T(8,128)(2,1)}, u32[]{:S(2)}) copy-start(bf16[80,160]{1,0:T(8,128)(2,1)} %param.29) | copy-start | bytes 76804
  7.3 184.2 %all-gather.12.cloned.1.call-start = ((), (), s32[]{:S(2)}) async-start(), calls=%async_computation.9 | async-start | bytes 10813440 | tf_op jit(solution)/shard_map/all_gather | solution.py:143
  8.0 452.1 %all-gather.14.cloned.1.call-start = ((), (), s32[]{:S(2)}) async-start(), calls=%async_computation.10 | async-start | bytes 10813440 | tf_op jit(solution)/shard_map/all_gather | solution.py:144
  8.8 463.7 %all-gather.16.cloned.1.call-start = ((), (), s32[]{:S(2)}) async-start(), calls=%async_computation.11 | async-start | bytes 10813440 | tf_op jit(solution)/shard_map/all_gather | solution.py:152
  9.5 132.7 %copy-start.118 = (bf16[80,160]{1,0:T(8,128)(2,1)S(1)}, bf16[80,160]{1,0:T(8,128)(2,1)}, u32[]{:S(2)}) copy-start(bf16[80,160]{1,0:T(8,128)(2,1)} %param.31) | copy-start | bytes 76804
  9.5 469.4 %all-gather.18.cloned.1.call-start = ((), (), s32[]{:S(2)}) async-start(), calls=%async_computation.12 | async-start | bytes 25952256 | tf_op jit(solution)/shard_map/all_gather | solution.py:184
  10.1 592.2 %all-gather.20.cloned.1.call-start = ((), (), s32[]{:S(2)}) async-start(), calls=%async_computation.13 | async-start | bytes 25952256 | tf_op jit(solution)/shard_map/all_gather | solution.py:185
  10.7 747.2 %all-gather.22.cloned.1.call-start = ((), (), s32[]{:S(2)}) async-start(), calls=%async_computation.14 | async-start | bytes 25952256 | tf_op jit(solution)/shard_map/all_gather | solution.py:186
  11.3 1282.0 %reduce-scatter.28.cloned.1.call-start = ((), (), s32[]{:S(2)}) async-start(), calls=%async_computation.23 | async-start | bytes 1351680
  55.9 142.7 %copy-start.128 = (bf16[2560]{0:T(1024)(128)(2,1)}, bf16[2560]{0:T(1024)(128)(2,1)S(1)}, u32[]{:S(2)}) copy-start(bf16[2560]{0:T(1024)(128)(2,1)S(1)} %get-tuple-element.288) | copy-start | bytes 15364
  55.9 404.2 %copy-start.49 = (f32[2048]{0:T(1024)}, f32[2048]{0:T(1024)S(1)}, u32[]{:S(2)}) copy-start(f32[2048]{0:T(1024)S(1)} %convert_element_type.142) | copy-start | bytes 24580
  97.3 127.2 %copy-start.130 = (pred[256]{0:T(512)(128)(4,1)}, pred[256]{0:T(512)(128)(4,1)S(1)}, u32[]{:S(2)}) copy-start(pred[256]{0:T(512)(128)(4,1)S(1)} %compare_reduce_fusion) | copy-start | bytes 772
  97.5 127.0 %copy-start.54 = (f32[2560]{0:T(1024)}, f32[2560]{0:T(1024)S(1)}, u32[]{:S(2)}) copy-start(f32[2560]{0:T(1024)S(1)} %get-tuple-element.254) | copy-start | bytes 30724
  97.5 127.0 %copy-start.56 = (f32[2560]{0:T(1024)}, f32[2560]{0:T(1024)S(1)}, u32[]{:S(2)}) copy-start(f32[2560]{0:T(1024)S(1)} %get-tuple-element.255) | copy-start | bytes 30724
  97.5 127.0 %copy-start.58 = (f32[2560]{0:T(1024)}, f32[2560]{0:T(1024)S(1)}, u32[]{:S(2)}) copy-start(f32[2560]{0:T(1024)S(1)} %get-tuple-element.256) | copy-start | bytes 30724
  97.5 127.0 %copy-start.60 = (f32[2560]{0:T(1024)}, f32[2560]{0:T(1024)S(1)}, u32[]{:S(2)}) copy-start(f32[2560]{0:T(1024)S(1)} %get-tuple-element.257) | copy-start | bytes 30724
  97.8 93.7 %copy-start.132 = (f32[256]{0:T(256)}, f32[256]{0:T(256)S(1)}, u32[]{:S(2)}) copy-start(f32[256]{0:T(256)S(1)} %fusion.30) | copy-start | bytes 3076
  97.8 362.3 %copy-start.80 = (f32[256]{0:T(256)}, f32[256]{0:T(256)S(1)}, u32[]{:S(2)}) copy-start(f32[256]{0:T(256)S(1)} %fusion.69) | copy-start | bytes 3076
  97.8 126.6 %copy-start.87 = (f32[256]{0:T(256)}, f32[256]{0:T(256)S(1)}, u32[]{:S(2)}) copy-start(f32[256]{0:T(256)S(1)} %get-tuple-element.394) | copy-start | bytes 3076
  97.9 126.6 %copy-start.89 = (f32[256]{0:T(256)}, f32[256]{0:T(256)S(1)}, u32[]{:S(2)}) copy-start(f32[256]{0:T(256)S(1)} %get-tuple-element.395) | copy-start | bytes 3076
  97.9 126.6 %copy-start.91 = (f32[256]{0:T(256)}, f32[256]{0:T(256)S(1)}, u32[]{:S(2)}) copy-start(f32[256]{0:T(256)S(1)} %get-tuple-element.396) | copy-start | bytes 3076
  97.9 126.6 %copy-start.70 = (f32[2560]{0:T(1024)}, f32[2560]{0:T(1024)S(1)}, u32[]{:S(2)}) copy-start(f32[2560]{0:T(1024)S(1)} %get-tuple-element.392) | copy-start | bytes 30724
  97.9 126.6 %copy-start.72 = (f32[2560]{0:T(1024)}, f32[2560]{0:T(1024)S(1)}, u32[]{:S(2)}) copy-start(f32[2560]{0:T(1024)S(1)} %get-tuple-element.393) | copy-start | bytes 30724
  199.7 3.1 collective-permute-start
  202.1 22.4 copy-start.126
  202.2 22.4 copy-start.68
  202.2 22.4 copy-start.64
  202.2 22.3 copy-start.66
  383.8 23.3 copy-start.22
  478.7 329.9 %copy-start.28 = (f32[256,2048]{1,0:T(8,128)}, f32[256,2048]{1,0:T(8,128)S(1)}, u32[]{:S(2)}) copy-start(f32[256,2048]{1,0:T(8,128)S(1)} %get-tuple-element.399) | copy-start | bytes 6291460
  478.9 123.4 %copy-start.13 = (bf16[256,2048]{1,0:T(8,128)(2,1)}, bf16[256,2048]{1,0:T(8,128)(2,1)S(1)}, u32[]{:S(2)}) copy-start(bf16[256,2048]{1,0:T(8,128)(2,1)S(1)} %multiply_convert_fusion.3) | copy-start | bytes 3145732
  1036.4 21.2 copy-start.61
  1036.4 21.2 copy-start.65
  1036.4 21.2 copy-start.67
  1105.9 270.2 %reduce-scatter.16.cloned.1.call-start = ((), (), s32[]{:S(2)}) async-start(), calls=%async_computation.17 | async-start | bytes 2703360 | tf_op jit(solution)/shard_map/reduce_scatter | solution.py:291
  1108.5 404.2 %reduce-scatter.18.cloned.1.call-start = ((), (), s32[]{:S(2)}) async-start(), calls=%async_computation.18 | async-start | bytes 2703360 | tf_op jit(solution)/shard_map/reduce_scatter | solution.py:293
  1111.8 625.0 %reduce-scatter.20.cloned.1.call-start = ((), (), s32[]{:S(2)}) async-start(), calls=%async_computation.19 | async-start | bytes 21626880 | tf_op jit(solution)/shard_map/reduce_scatter | solution.py:296
  1123.8 845.6 %reduce-scatter.14.cloned.1.call-start = ((), (), s32[]{:S(2)}) async-start(), calls=%async_computation.16 | async-start | bytes 21626880 | tf_op jit(solution)/shard_map/reduce_scatter | solution.py:288
  1134.2 1067.6 %reduce-scatter.12.cloned.1.call-start = ((), (), s32[]{:S(2)}) async-start(), calls=%async_computation.15 | async-start | bytes 21626880 | tf_op jit(solution)/shard_map/reduce_scatter | solution.py:287
  1137.3 3.1 collective-permute-start.1
  1150.1 1495.8 %reduce-scatter.22.cloned.1.call-start = ((), (), s32[]{:S(2)}) async-start(), calls=%async_computation.20 | async-start | bytes 51904512 | tf_op jit(solution)/shard_map/reduce_scatter | solution.py:214
  1172.7 1911.8 %reduce-scatter.24.cloned.1.call-start = ((), (), s32[]{:S(2)}) async-start(), calls=%async_computation.21 | async-start | bytes 51904512 | tf_op jit(solution)/shard_map/reduce_scatter | solution.py:215
  1194.2 2329.0 %reduce-scatter.26.cloned.1.call-start = ((), (), s32[]{:S(2)}) async-start(), calls=%async_computation.22 | async-start | bytes 51904512 | tf_op jit(solution)/shard_map/reduce_scatter | solution.py:216
  1235.9 54.2 %copy-start.133 = (f32[256]{0:T(256)S(1)}, f32[256]{0:T(256)}, u32[]{:S(2)}) copy-start(f32[256]{0:T(256)} %copy-done.132) | copy-start | bytes 3076
  1235.9 54.2 %copy-start.12 = (f32[256,2048]{1,0:T(8,128)S(1)}, f32[256,2048]{1,0:T(8,128)}, u32[]{:S(2)}) copy-start(f32[256,2048]{1,0:T(8,128)} %copy-done.10) | copy-start | bytes 6291460
  (112 other events, 858.0 us)
Sparse Core Ops, SparseCore 0:
  11.0 91.4 all-gather.11
  105.3 95.7 all-gather.13
  203.9 86.5 all-gather.15
  293.2 153.4 all-gather.17
  449.5 152.8 all-gather.19
  605.0 152.8 all-gather.21
  1106.0 133.3 reduce-scatter.27
  1242.3 133.7 reduce-scatter.15
  1379.1 133.4 reduce-scatter.17
  1515.5 221.2 reduce-scatter.19
  1739.8 229.5 reduce-scatter.13
  1972.2 229.5 reduce-scatter.11
  2210.0 435.8 reduce-scatter.21
  2653.9 430.6 reduce-scatter.23
  3092.5 430.6 reduce-scatter.25
where the time goes:
time: 3550 us; the launch traced here: 3530 us
  waiting for transfers between devices  2480 us (70%)
  local copies, waits for them, and re-layouts  402 us (11%)
  blocking collectives  255 us (7%)
  matrix products  255 us (7%)
  other arithmetic  114 us (3%)
    reduce_scatter x1, waiting for transfers between devices, on_device(): lax.psum_scatter(d_wg, ('fsdp', 'seq'), scatter_dimension=0, tiled=True)  444 us
    reduce_scatter x1, waiting for transfers between devices, on_device(): lax.psum_scatter(d_wd, ('fsdp', 'seq'), scatter_dimension=0, tiled=True)  439 us
    reduce_scatter x1, waiting for transfers between devices, on_device(): lax.psum_scatter(d_wu, ('fsdp', 'seq'), scatter_dimension=0, tiled=True)  439 us
    reduce_scatter x1, waiting for transfers between devices, on_device(): lax.psum_scatter(d_wy, ('fsdp', 'seq'), scatter_dimension=0, tiled=True)  233 us
    reduce_scatter x1, waiting for transfers between devices, on_device(): lax.psum_scatter(d_wx, ('fsdp', 'seq'), scatter_dimension=0, tiled=True)  232 us
    reduce_scatter x1, waiting for transfers between devices, on_device(): lax.psum_scatter(d_wo, ('fsdp', 'seq'), scatter_dimension=0, tiled=True)  224 us
    all_gather x1, waiting for transfers between devices, on_device(): lax.all_gather(w_down, ('fsdp', 'seq'), axis=0, tiled=True)  141 us
    slice x57, local copies, waits for them, and re-layouts, on_device(): lax.associative_scan(combine, (next_decay, d_state), reverse=True, axis=0)  137 us
  transfers between devices with their start and end apart: 17, of which 12 were waited for; matrix products, arithmetic and copies ran while one was open for 12% of the time, Pallas kernels for 0%

commit v1 on v0

--- a/solution.py
+++ b/solution.py
@@ -1,6 +1,12 @@
+import functools
+
 import jax
 import jax.numpy as jnp
+import numpy as np
 from jax import lax
+from jax.experimental import pallas as pl
+from jax.experimental.pallas import tpu as pltpu
+from jax.sharding import Mesh
 from jax.sharding import PartitionSpec as P
 
 DECAY_C = 8.0
@@ -92,9 +98,14 @@
     return result.reshape(value.shape[1], width)
 
 
+def seq_starts(lens_row):
+    count = lens_row.shape[0]
+    before = jnp.arange(count)[None, :] < jnp.arange(count)[:, None]
+    return jnp.sum(jnp.where(before, lens_row[None, :], 0), axis=1)
+
+
 def seq_masks(lens_row, first, rows, taps):
-    ends = jnp.cumsum(lens_row)
-    starts = ends - lens_row
+    starts = seq_starts(lens_row)
     place = first + jnp.arange(rows, dtype=jnp.int32)
 
     def segment(p):
@@ -316,7 +327,513 @@
     )
 
 
+NAMES = ("zh", "zl", "y", "x", "c")
+F32 = jnp.float32
+BF16 = jnp.bfloat16
+GELU_C = 0.7978845608
+GELU_K = 0.044715
+
+
+def swap(v, name):
+    return lax.ppermute(v, name, [(0, 1), (1, 0)])
+
+
+def add16(one, two):
+    return (one.astype(F32) + two.astype(F32)).astype(BF16)
+
+
+def act_gather(v, a, b):
+    h = v.shape[0] // 2
+    near, from_a, from_b = swap(v, "c"), swap(v, a), swap(v, b)
+    far0, far1 = swap(from_a[:h], b), swap(from_b[h:], a)
+    near_a, near_b = swap(from_a, "c"), swap(from_b, "c")
+    far = jnp.concatenate([far0, far1], axis=0)
+    return [v, near, from_a, near_a, from_b, near_b, far, swap(far, "c")]
+
+
+def act_scatter(get, a, b):
+    far, to_a, to_b = [add16(get(k), swap(get(k + 1), "c")) for k in (6, 2, 4)]
+    own = get(0).astype(F32) + swap(get(1), "c").astype(F32)
+    h = far.shape[0] // 2
+    in_b, in_a = swap(far[:h], b), swap(far[h:], a)
+    to_a = jnp.concatenate([add16(to_a[:h], in_b), to_a[h:]], axis=0)
+    to_b = jnp.concatenate([to_b[:h], add16(to_b[h:], in_a)], axis=0)
+    return own + swap(to_a, a).astype(F32) + swap(to_b, b).astype(F32)
+
+
+def w_gather(v, w1, w2):
+    i1, i2 = lax.axis_index(w1), lax.axis_index(w2)
+    p1, p2 = swap(v, w1), swap(v, w2)
+    p12 = swap(p1, w2)
+    out = jnp.zeros((2, 2) + v.shape, v.dtype)
+    tail = (0,) * v.ndim
+    for part, j1, j2 in ((v, i1, i2), (p1, 1 - i1, i2), (p2, i1, 1 - i2), (p12, 1 - i1, 1 - i2)):
+        out = lax.dynamic_update_slice(out, part[None, None], (j1, j2) + tail)
+    return out
+
+
+def w_scatter(v, w1, w2):
+    i1, i2 = lax.axis_index(w1), lax.axis_index(w2)
+
+    def get(j1, j2):
+        return lax.dynamic_slice(v, (j1, j2) + (0,) * (v.ndim - 2), (1, 1) + v.shape[2:])[0, 0]
+
+    other = add16(get(1 - i1, i2), swap(get(1 - i1, 1 - i2), w2))
+    own = get(i1, i2).astype(F32) + swap(get(i1, 1 - i2), w2).astype(F32)
+    return own + swap(other, w1).astype(F32)
+
+
+def to_columns(w, tp, rest):
+    rows, cols = w.shape
+    dims = {n: i + 1 for i, n in enumerate(NAMES)}
+    v = w.reshape((rows,) + (2,) * 5 + (cols // 32,))
+    v = v.transpose([dims[n] for n in tp] + [0] + [dims[n] for n in rest] + [6])
+    return v.reshape(8, rows, cols // 8)
+
+
+def from_columns(v, tp, rest):
+    _, rows, cols = v.shape
+    order = list(tp) + ["rows"] + list(rest)
+    v = v.reshape((2, 2, 2, rows, 2, 2, cols // 4))
+    v = v.transpose([order.index("rows")] + [order.index(n) for n in NAMES] + [6])
+    return v.reshape(rows, cols * 8)
+
+
+def exchange(v, tp):
+    return lax.all_to_all(v, tp, split_axis=0, concat_axis=0, tiled=True)
+
+
+def neg_expm1(v):
+    series = 1.0 + v * (1.0 / 10.0)
+    for n in range(9, 1, -1):
+        series = 1.0 + v * (1.0 / n) * series
+    return jnp.where(v > -0.5, -v * series, 1.0 - jnp.exp(v))
+
+
+def gate_terms(pa, px, rate, start):
+    sr = jax.nn.sigmoid(pa)
+    si = jax.nn.sigmoid(px)
+    la = -DECAY_C * sr * rate
+    decay = jnp.where(start, 0.0, jnp.exp(la))
+    e2 = neg_expm1(2.0 * la)
+    floor = 0.2 * DECAY_C * rate
+    scale = jnp.where(start, 1.0, jnp.sqrt(jnp.maximum(e2, floor)))
+    return sr, si, decay, e2, floor, scale
+
+
+def gelu(v):
+    return 0.5 * v * (1.0 + jnp.tanh(GELU_C * (v + GELU_K * v * v * v)))
+
+
+def gelu_both(v):
+    t = jnp.tanh(GELU_C * (v + GELU_K * v * v * v))
+    half = 0.5 * (1.0 + t)
+    return v * half, half + 0.5 * v * (1.0 - t * t) * GELU_C * (1.0 + 3.0 * GELU_K * v * v)
+
+
+def scan_tile(decay, drive, into):
+    row = lax.broadcasted_iota(jnp.int32, decay.shape, 0)
+    for by in (1, 2, 4):
+        keep = row >= by
+        drive = jnp.where(keep, decay * pltpu.roll(drive, by, 0) + drive, drive)
+        decay = jnp.where(keep, decay * pltpu.roll(decay, by, 0), decay)
+    return decay * into + drive
+
+
+def scan_tile_back(decay, drive, into):
+    row = lax.broadcasted_iota(jnp.int32, decay.shape, 0)
+    for by in (1, 2, 4):
+        keep = row < 8 - by
+        drive = jnp.where(keep, decay * pltpu.roll(drive, 8 - by, 0) + drive, drive)
+        decay = jnp.where(keep, decay * pltpu.roll(decay, 8 - by, 0), decay)
+    return decay * into + drive
+
+
+STEP = 16
+
+
+def rec_fwd_kernel(xb_ref, yb_ref, mask_ref, vec_ref, w_ref, xc_ref, pa_ref, px_ref, sp_ref, mixed_ref, ext, carry):
+    rows, width = xb_ref.shape
+
+    @pl.when(pl.program_id(0) == 0)
+    def _():
+        ext[0:8, :] = jnp.zeros((8, width), F32)
+        carry[...] = jnp.zeros_like(carry)
+
+    ext[8 : 8 + rows, :] = xb_ref[...].astype(F32)
+
+    def conv_step(r, _):
+        at = pl.multiple_of(r * STEP, STEP)
+        window = ext[pl.ds(at, STEP + 8), :]
+        mask = mask_ref[pl.ds(at, STEP), :]
+        total = vec_ref[4:5, :] + vec_ref[0:1, :] * window[8:, :]
+        for k in range(1, 4):
+            total = total + vec_ref[k : k + 1, :] * window[8 - k : 8 - k + STEP, :] * mask[:, k : k + 1]
+        xc_ref[pl.ds(at, STEP), :] = total.astype(BF16)
+        return 0
+
+    lax.fori_loop(0, rows // STEP, conv_step, 0, unroll=2)
+    ext[0:8, :] = ext[rows : rows + 8, :]
+    xc = xc_ref[...]
+    pa_ref[...] = jnp.dot(xc, w_ref[:, :width], preferred_element_type=F32) + vec_ref[6:7, :]
+    px_ref[...] = jnp.dot(xc, w_ref[:, width:], preferred_element_type=F32) + vec_ref[7:8, :]
+    top = lax.broadcasted_iota(jnp.int32, (8, width), 0) == 0
+
+    def scan_step(r, held):
+        here = pl.ds(pl.multiple_of(r * STEP, STEP), STEP)
+        start = jnp.broadcast_to(mask_ref[here, 0:1], (STEP, width)) > 0.5
+        _, si, decay, _, _, scale = gate_terms(pa_ref[here, :], px_ref[here, :], vec_ref[5:6, :], start)
+        drive = scale * si * xc_ref[here, :].astype(F32)
+        states, before = [], []
+        for part in range(0, STEP, 8):
+            now = scan_tile(decay[part : part + 8], drive[part : part + 8], held)
+            states.append(now)
+            before.append(jnp.where(top, held, pltpu.roll(now, 1, 0)))
+            held = jnp.broadcast_to(now[7:8, :], (8, width))
+        sp_ref[here, :] = jnp.concatenate(before, axis=0)
+        mixed_ref[here, :] = (jnp.concatenate(states, axis=0) * gelu(yb_ref[here, :])).astype(BF16)
+        return held
+
+    carry[...] = lax.fori_loop(0, rows // STEP, scan_step, carry[...], unroll=2)
+
+
+def rec_bwd_kernel(
+    dm_ref, yb_ref, sp_ref, pa_ref, px_ref, xc_ref, xb_ref, mask_ref, vec_ref, wt_ref,
+    dxb_ref, dyb_ref, dw_ref, sum_ref, ext, dp, carry,
+):
+    rows, width = xb_ref.shape
+
+    @pl.when(pl.program_id(0) == 0)
+    def _():
+        ext[rows : rows + 8, :] = jnp.zeros((8, width), F32)
+        carry[...] = jnp.zeros_like(carry)
+        dw_ref[...] = jnp.zeros_like(dw_ref)
+        sum_ref[...] = jnp.zeros_like(sum_ref)
+
+    row = lax.broadcasted_iota(jnp.int32, (8, width), 0)
+    steps = rows // STEP
+
+    def fold(v):
+        return v[0:8, :] + v[8:16, :]
+
+    def scan_step(i, state):
+        held, s_rate, s_r, s_i = state
+        here = pl.ds(pl.multiple_of((steps - 1 - i) * STEP, STEP), STEP)
+        start = jnp.broadcast_to(mask_ref[here, 0:1], (STEP, width)) > 0.5
+        rate = vec_ref[5:6, :]
+        sr, si, decay, e2, floor, scale = gate_terms(pa_ref[here, :], px_ref[here, :], rate, start)
+        xc = xc_ref[here, :].astype(F32)
+        before = sp_ref[here, :]
+        gate = si * xc
+        now = decay * before + scale * gate
+        dm = dm_ref[here, :]
+        act, slope = gelu_both(yb_ref[here, :])
+        dyb_ref[here, :] = (dm * now * slope).astype(BF16)
+        dstate = dm * act
+        parts = []
+        for part in range(STEP - 8, -1, -8):
+            here_decay = decay[part : part + 8]
+            coef = jnp.where(row == 7, 1.0, pltpu.roll(here_decay, 7, 0))
+            adj = scan_tile_back(coef, dstate[part : part + 8], held)
+            held = jnp.broadcast_to((here_decay * adj)[0:1, :], (8, width))
+            parts.append(adj)
+        adj = jnp.concatenate(parts[::-1], axis=0)
+        d_scale = adj * gate
+        d_half = jnp.where(start, 0.0, d_scale * 0.5 / scale)
+        share = jnp.where(e2 > floor, 1.0, jnp.where(e2 == floor, 0.5, 0.0))
+        kept = adj * scale
+        d_la = decay * (adj * before - 2.0 * decay * d_half * share)
+        d_rate = -DECAY_C * sr * d_la + (0.2 * DECAY_C) * d_half * (1.0 - share)
+        d_pa = (-DECAY_C * rate * d_la * sr * (1.0 - sr)).astype(BF16)
+        d_px = (kept * xc * si * (1.0 - si)).astype(BF16)
+        dp[here, :width] = d_pa
+        dp[here, width:] = d_px
+        ext[here, :] = kept * si
+        return held, s_rate + fold(d_rate), s_r + fold(d_pa.astype(F32)), s_i + fold(d_px.astype(F32))
+
+    held, s_rate, s_r, s_i = lax.fori_loop(
+        0, steps, scan_step, (carry[...], sum_ref[40:48, :], sum_ref[48:56, :], sum_ref[56:64, :]), unroll=2
+    )
+    carry[...] = held
+    sum_ref[40:48, :] = s_rate
+    sum_ref[48:56, :] = s_r
+    sum_ref[56:64, :] = s_i
+    ext[0:rows, :] += jnp.dot(dp[...], wt_ref[...], preferred_element_type=F32)
+    dw_ref[...] += row_contract(xc_ref[...], dp[...])
+
+    def conv_step(r, sums):
+        at = pl.multiple_of(r * STEP, STEP)
+        window = ext[pl.ds(at, STEP + 8), :]
+        mask = mask_ref[pl.ds(at, STEP), :]
+        xb = xb_ref[pl.ds(at, STEP), :].astype(F32)
+        total = jnp.zeros((STEP, width), F32)
+        new = []
+        for k in range(4):
+            moved = window[k : k + STEP, :]
+            if k:
+                moved = moved * mask[:, 3 + k : 4 + k]
+            total = total + vec_ref[k : k + 1, :] * moved
+            new.append(sums[k] + fold(moved * xb))
+        new.append(sums[4] + fold(window[:STEP, :]))
+        dxb_ref[pl.ds(at, STEP), :] = total.astype(BF16)
+        return tuple(new)
+
+    sums = lax.fori_loop(0, steps, conv_step, tuple(sum_ref[8 * q : 8 * q + 8, :] for q in range(5)), unroll=2)
+    for q in range(5):
+        sum_ref[8 * q : 8 * q + 8, :] = sums[q]
+    ext[rows : rows + 8, :] = ext[0:8, :]
+
+
+def time_tile(total):
+    return 256 if total % 256 == 0 else total
+
+
+def rec_forward(xb, yb, mask, vec, w):
+    total, width = xb.shape
+    tile = time_tile(total)
+    block = pl.BlockSpec((tile, width), lambda i: (i, 0))
+    whole = lambda v: pl.BlockSpec(v.shape, lambda i: (0, 0))
+    return pl.pallas_call(
+        rec_fwd_kernel,
+        grid=(total // tile,),
+        in_specs=[block, block, pl.BlockSpec((tile, 8), lambda i: (i, 0)), whole(vec), whole(w)],
+        out_specs=[block] * 5,
+        out_shape=[jax.ShapeDtypeStruct((total, width), t) for t in (BF16, F32, F32, F32, BF16)],
+        scratch_shapes=[pltpu.VMEM((tile + 8, width), F32), pltpu.VMEM((8, width), F32)],
+        compiler_params=pltpu.CompilerParams(vmem_limit_bytes=32 << 20),
+        cost_estimate=pl.CostEstimate(
+            flops=100 * total * width + 4 * total * width * width,
+            transcendentals=6 * total * width,
+            bytes_accessed=22 * total * width,
+        ),
+        name="recurrence_forward",
+    )(xb, yb, mask, vec, w)
+
+
+def rec_backward(dm, yb, sp, pa, px, xc, xb, mask, vec, wt):
+    total, width = xb.shape
+    tile = time_tile(total)
+    steps = total // tile
+    block = pl.BlockSpec((tile, width), lambda i: (steps - 1 - i, 0))
+    whole = lambda v: pl.BlockSpec(v.shape, lambda i: (0, 0))
+    return pl.pallas_call(
+        rec_bwd_kernel,
+        grid=(steps,),
+        in_specs=[block] * 7 + [pl.BlockSpec((tile, 8), lambda i: (steps - 1 - i, 0)), whole(vec), whole(wt)],
+        out_specs=[
+            block,
+            block,
+            pl.BlockSpec((width, 2 * width), lambda i: (0, 0)),
+            pl.BlockSpec((64, width), lambda i: (0, 0)),
+        ],
+        out_shape=[
+            jax.ShapeDtypeStruct((total, width), BF16),
+            jax.ShapeDtypeStruct((total, width), BF16),
+            jax.ShapeDtypeStruct((width, 2 * width), F32),
+            jax.ShapeDtypeStruct((64, width), F32),
+        ],
+        scratch_shapes=[
+            pltpu.VMEM((tile + 8, width), F32),
+            pltpu.VMEM((tile, 2 * width), BF16),
+            pltpu.VMEM((8, width), F32),
+        ],
+        compiler_params=pltpu.CompilerParams(vmem_limit_bytes=32 << 20),
+        cost_estimate=pl.CostEstimate(
+            flops=180 * total * width + 8 * total * width * width,
+            transcendentals=6 * total * width,
+            bytes_accessed=28 * total * width,
+        ),
+        name="recurrence_backward",
+    )(dm, yb, sp, pa, px, xc, xb, mask, vec, wt)
+
+
+def place_masks(lens_row, total, taps):
+    start, same = seq_masks(lens_row, 0, total, taps)
+    cols = [start.astype(F32)] + [same[k] for k in range(1, taps)]
+    cols += [jnp.pad(same[k][k:], (0, k)) for k in range(1, taps)]
+    return jnp.pad(jnp.stack(cols, axis=1), ((0, 0), (0, 8 - len(cols))))
+
+
+def dot32(one, two):
+    return jnp.dot(one, two, preferred_element_type=F32)
+
+
+def norm_back(dv, v, scale):
+    return scale * dv - scale * scale * scale * v * jnp.mean(dv * v, axis=-1, keepdims=True)
+
+
+REC_TP = ("y", "x", "c")
+REC_COLS = (("y", "x", "zh"), ("zl", "c"))
+REC_W = ("zh", "zl")
+FF_A, FF_B = "x", "y"
+FF_TP = ("y", "x", "c")
+FF_W = ("zh", "zl")
+
+
+def tensor_parallel(
+    layer_input, lengths, norm1_gain, w_x, w_y, conv_w, conv_b, w_rgate, b_rgate, w_igate, b_igate, lam,
+    w_out, norm2_gain, w_gate, w_up, w_down, cot,
+):
+    rows, model = layer_input.shape
+    total = 8 * rows
+    taps = conv_w.shape[1]
+    width = w_rgate.shape[1]
+    part = w_out.shape[0]
+    channels = 4 * part
+    padded = -(-channels // 128) * 128
+    extra = padded - channels
+    blocks = channels // width
+    core = lax.axis_index("c")
+    me = (lax.axis_index("y") * 2 + lax.axis_index("x")) * 2 + core
+
+    def in_order(pieces):
+        out = jnp.zeros((8,) + pieces[0].shape, pieces[0].dtype)
+        for k, piece in enumerate(pieces):
+            out = lax.dynamic_update_slice(out, piece[None], (me ^ k, 0, 0))
+        return out.reshape(total, -1)
+
+    def rows_of(v, k):
+        return lax.dynamic_slice(v, ((me ^ k) * rows, 0), (rows, v.shape[1]))
+
+    gain1 = norm1_gain.astype(F32)[:, None]
+    gain2 = norm2_gain.astype(F32)[:, None]
+
+    xf = layer_input.astype(F32)
+    scale1 = lax.rsqrt(jnp.mean(xf * xf, axis=-1, keepdims=True) + NORM_EPS)
+    xs = (xf * scale1).astype(BF16)
+
+    def columns_in(w, gain, cols, tp, over):
+        scaled = (w.astype(F32) * gain).astype(BF16)
+        mine = exchange(to_columns(scaled, *cols), tp)
+        return w_gather(mine.reshape(-1, mine.shape[2]), *over).reshape(model, -1)
+
+    def columns_out(grad, cols, tp, over):
+        mine = w_scatter(grad.astype(BF16).reshape(2, 2, model // 4, -1), *over).astype(BF16)
+        return from_columns(exchange(mine.reshape(8, -1, mine.shape[1]), tp), *cols).astype(F32)
+
+    wx = jnp.pad(columns_in(w_x, gain1, REC_COLS, REC_TP, REC_W), ((0, 0), (0, extra)))
+    xs_all = in_order(act_gather(xs, "x", "y"))
+    wy = jnp.pad(columns_in(w_y, gain1, REC_COLS, REC_TP, REC_W), ((0, 0), (0, extra)))
+
+    small = [conv_w, conv_b[:, None], b_rgate[:, None], b_igate[:, None], lam[:, None], w_rgate, w_igate]
+    small_width = sum(v.shape[1] for v in small)
+    packed = jnp.pad(jnp.concatenate([w_out] + small, axis=1), ((0, 0), (0, -small_width % 128)))
+    halves = w_gather(packed, *REC_W)
+    mine = lax.dynamic_slice(halves, (core, 0, 0, 0), (1,) + halves.shape[1:])[0]
+    theirs = swap(lax.dynamic_slice(halves, (1 - core, 0, 0, 0), (1,) + halves.shape[1:])[0], "c")
+    whole = jnp.zeros((2, 2) + packed.shape, BF16)
+    whole = lax.dynamic_update_slice(whole, mine[:, None], (0, core, 0, 0))
+    whole = lax.dynamic_update_slice(whole, theirs[:, None], (0, 1 - core, 0, 0))
+    whole = jnp.pad(whole.reshape(channels, -1), ((0, extra), (0, 0)))
+    wo = whole[:, :model]
+    rest = whole[:, model : model + taps + 4].astype(F32).T
+    lam_all = rest[taps + 3]
+    vec = jnp.concatenate([rest[: taps + 1], jax.nn.softplus(-lam_all)[None], rest[taps + 1 : taps + 3]], axis=0)
+    at = model + taps + 4
+    gates = jnp.zeros((padded, 2 * padded), BF16)
+    for g in range(2):
+        for n in range(blocks):
+            block = whole[n * width : (n + 1) * width, at + g * width : at + (g + 1) * width]
+            gates = gates.at[n * width : (n + 1) * width, g * padded + n * width : g * padded + (n + 1) * width].set(block)
+    mask = place_masks(lengths[0], total, taps)
+
+    xb = dot32(xs_all, wx).astype(BF16)
+    yb = dot32(xs_all, wy)
+    xc, pa, px, before, mixed = rec_forward(xb, yb, mask, vec, gates)
+
+    resid = xf + act_scatter(lambda k: dot32(rows_of(mixed, k), wo).astype(BF16), "x", "y")
+    scale2 = lax.rsqrt(jnp.mean(resid * resid, axis=-1, keepdims=True) + NORM_EPS)
+    xs2 = (resid * scale2).astype(BF16)
+
+    wg = columns_in(w_gate, gain2, (FF_TP, FF_W), FF_TP, FF_W)
+    wu = columns_in(w_up, gain2, (FF_TP, FF_W), FF_TP, FF_W)
+    wd = w_gather(w_down, *FF_W).reshape(-1, model)
+    cot_all = jnp.concatenate(act_gather(cot, FF_A, FF_B), axis=0)
+    xs2_all = jnp.concatenate(act_gather(xs2, FF_A, FF_B), axis=0)
+    gt = dot32(xs2_all, wg)
+    up = dot32(xs2_all, wu)
+    act, slope = gelu_both(gt)
+    hidden = (act * up).astype(BF16)
+
+    def tile_of(v, k):
+        return v[k * rows : (k + 1) * rows]
+
+    output = (resid + act_scatter(lambda k: dot32(tile_of(hidden, k), wd).astype(BF16), FF_A, FF_B)).astype(BF16)
+
+    d_hidden = back_product(cot_all, wd)
+    d_gt = (d_hidden * up * slope).astype(BF16)
+    d_up = (d_hidden * act).astype(BF16)
+    d_un2 = act_scatter(
+        lambda k: (back_product(tile_of(d_gt, k), wg) + back_product(tile_of(d_up, k), wu)).astype(BF16), FF_A, FF_B
+    )
+    d_wd = w_scatter(row_contract(hidden, cot_all).astype(BF16).reshape(2, 2, -1, model), *FF_W)
+    d_wg = columns_out(row_contract(xs2_all, d_gt), (FF_TP, FF_W), FF_TP, FF_W)
+    d_wu = columns_out(row_contract(xs2_all, d_up), (FF_TP, FF_W), FF_TP, FF_W)
+    d_gain2 = jnp.sum(w_gate.astype(F32) * d_wg + w_up.astype(F32) * d_wu, axis=1)
+
+    d_resid = cot.astype(F32) + norm_back(d_un2, resid, scale2)
+    d_mix = d_resid.astype(BF16)
+    d_mix_all = in_order(act_gather(d_mix, "x", "y"))
+    dm = back_product(d_mix_all, wo)
+    dxb, dyb, d_gates, sums = rec_backward(dm, yb, before, pa, px, xc, xb, mask, vec, gates.T)
+    d_un = act_scatter(
+        lambda k: (back_product(rows_of(dxb, k), wx) + back_product(rows_of(dyb, k), wy)).astype(BF16), "x", "y"
+    )
+    d_input = (d_resid + norm_back(d_un, xf, scale1)).astype(BF16)
+
+    d_wo = row_contract(mixed, d_mix_all)[:channels]
+    d_wx = columns_out(row_contract(xs_all, dxb)[:, :channels], REC_COLS, REC_TP, REC_W)
+    d_wy = columns_out(row_contract(xs_all, dyb)[:, :channels], REC_COLS, REC_TP, REC_W)
+    d_gain1 = jnp.sum(w_x.astype(F32) * d_wx + w_y.astype(F32) * d_wy, axis=1)
+
+    def channels_out(v, kind):
+        v = v.astype(kind).reshape(2, 2, part, -1)
+        size = (2, 1) + v.shape[2:]
+        keep = lax.dynamic_slice(v, (0, core, 0, 0), size)[:, 0]
+        send = lax.dynamic_slice(v, (0, 1 - core, 0, 0), size)[:, 0]
+        out = jnp.zeros((2,) + keep.shape, kind)
+        out = lax.dynamic_update_slice(out, keep[None], (core, 0, 0, 0))
+        return lax.dynamic_update_slice(out, swap(send, "c")[None], (1 - core, 0, 0, 0))
+
+    d_wo = w_scatter(channels_out(d_wo, BF16), *REC_W)
+    sums = jnp.sum(sums.reshape(8, 8, padded), axis=1)
+    d_lam_part = -jax.nn.sigmoid(-lam_all) * sums[5]
+    d_cols = jnp.concatenate([sums[:5], sums[6:8], d_lam_part[None]], axis=0).T
+    row_block = jnp.arange(channels)[:, None] // width
+    d_blocks = []
+    for g in range(2):
+        block = d_gates[:channels, g * padded : g * padded + width]
+        for n in range(1, blocks):
+            at = g * padded + n * width
+            block = jnp.where(row_block == n, d_gates[:channels, at : at + width], block)
+        d_blocks.append(block)
+    d_small = jnp.concatenate([d_cols[:channels]] + d_blocks, axis=1)
+    d_small = lax.psum_scatter(channels_out(d_small, F32).reshape(4 * part, -1), REC_W, scatter_dimension=0, tiled=True)
+    d_cw, d_cb, d_br, d_bi, d_lam = d_small[:, :4], d_small[:, 4], d_small[:, 5], d_small[:, 6], d_small[:, 7]
+    d_wr, d_wi = d_small[:, 8 : 8 + width], d_small[:, 8 + width : 8 + 2 * width]
+    return (
+        output, d_input, d_gain1, gain1 * d_wx, gain1 * d_wy, d_cw, d_cb, d_wr, d_br, d_wi, d_bi, d_lam, d_wo,
+        d_gain2, gain2 * d_wg, gain2 * d_wu, d_wd,
+    )
+
+
+def factored(mesh):
+    if tuple(mesh.axis_names) != ("fsdp", "seq") or (mesh.shape["fsdp"], mesh.shape["seq"]) != (4, 8):
+        return None
+    return Mesh(np.asarray(mesh.devices).reshape((2,) * 5), NAMES)
+
+
 def solution(mesh):
+    small = factored(mesh)
+    if small is not None:
+        whole, groups = P(NAMES), P(("zh", "zl"))
+        return jax.shard_map(
+            tensor_parallel,
+            mesh=small,
+            in_specs=(whole, groups) + (whole,) * 16,
+            out_specs=(whole,) * 17,
+            check_vma=False,
+        )
     in_specs = (
         P(("fsdp", "seq"), None),
         P("fsdp", None),

time: 3550 us -> 1000 us (0.28)
  waiting for transfers between devices: 2480 us -> 318 us
  blocking collectives: 255 us -> 0 us
  local copies, waits for them, and re-layouts: 402 us -> 209 us
  starting transfers between devices: 4.32 us -> 109 us
  other arithmetic: 114 us -> 48.5 us
  Pallas kernels: 0 us -> 52.5 us
    reduce_scatter x8 -> x1, waiting for transfers between devices: 2230 us -> 0.01 us  [tensor_parallel(): lax.psum_scatter(channels_out(d_small, F32).reshape(4 * part, -1), REC_W,...]
    ppermute x2 -> x103, waiting for transfers between devices: 1.16 us -> 310 us  [swap(): return lax.ppermute(v, name, [(0, 1), (1, 0)])]
    all_gather x6 -> x0, waiting for transfers between devices: 249 us -> none  [the longest x1 141 us: on_device(): lax.all_gather(w_down, ('fsdp', 'seq'), axis=0, tiled=True)]
    slice x112 -> x34, local copies, waits for them, and re-layouts: 234 us -> 16.2 us  [the longest x8 7.71 us: act_gather(): far0, far1 = (swap(from_a[:h], b), swap(from_b[h:], a))]
    all_gather x7 -> x0, blocking collectives: 171 us -> none  [the longest x1 49.3 us: on_device(): lax.all_gather(w_igate, ('fsdp', 'seq'), axis=0, tiled=True)]
    pad x56 -> x4, local copies, waits for them, and re-layouts: 86.5 us -> 0.8 us  [the longest x1 0.78 us: tensor_parallel(): jnp.pad(jnp.concatenate([w_out] + small, axis=1), ((0, 0), (0, -small_wid...]
    unnamed x2 -> x0, blocking collectives: 84.9 us -> none
    ppermute x2 -> x103, starting transfers between devices: 3.72 us -> 76.2 us  [swap(): return lax.ppermute(v, name, [(0, 1), (1, 0)])]
  transfers between devices with their start and end apart: 17 -> 112, of which waited for: 12 -> 41; matrix products, arithmetic and copies ran while one was open for 12% -> 35% of each run, Pallas kernels for 0% -> 2%
where the time goes in v1:
time: 1000 us; the launch traced here: 994 us
  waiting for transfers between devices  318 us (32%)
  matrix products  240 us (24%)
  local copies, waits for them, and re-layouts  209 us (21%)
  starting transfers between devices  109 us (11%)
  Pallas kernels  52.5 us (5%)
  other arithmetic  48.5 us (5%)
  between operations  16.8 us (2%)
    ppermute x103, waiting for transfers between devices, swap(): return lax.ppermute(v, name, [(0, 1), (1, 0)])  310 us
    dot_general x34, matrix products, back_product(): lax.dot_general(grad, weight, (((1,), (1,)), ((), ())), preferred_element...  98.1 us
    dot_general x20, matrix products, dot32(): return jnp.dot(one, two, preferred_element_type=F32)  92.5 us
    ppermute x103, starting transfers between devices, swap(): return lax.ppermute(v, name, [(0, 1), (1, 0)])  76.2 us
    dot_general x6, matrix products, row_contract(): lax.dot_general(left, right, (((0,), (0,)), ((), ())), preferred_element_...  49.6 us
    convert_element_type x12, local copies, waits for them, and re-layouts, columns_out(): from_columns(exchange(mine.reshape(8, -1, mine.shape[1]), tp), *cols)  40.6 us
    all_to_all x8, starting transfers between devices, exchange(): return lax.all_to_all(v, tp, split_axis=0, concat_axis=0, tiled=True)  32.8 us
    pallas_call x1, Pallas kernels, rec_backward(): pl.pallas_call(rec_bwd_kernel, grid=(steps,), in_specs=[block] * 7 + [pl....  31.4 us
  transfers between devices with their start and end apart: 112, of which 41 were waited for; matrix products, arithmetic and copies ran while one was open for 35% of the time, Pallas kernels for 2%

profile of v1, /device:TPU:0, one launch (start us, length us, event | category | flops | bytes accessed | tf_op | source)
XLA Modules:
  0.0 994.3 jit_solution(16394600886453450782)
XLA Ops:
  48.9 7.6 all-to-all-done.1
  89.3 16.7 %collective-permute-done.11 = bf16[512,320]{1,0:T(8,128)(2,1)S(1)} collective-permute-done((bf16[512,320]{1,0:T(8,128)(2,1)}, bf16[512,320]{1,0:T(8,128)(2,1)S(1)}, u32[]{:S(2)}, u32[]{:S(2)}) %collective-permute-start.11) | collective-permute-done | bytes 327712 | tf_op jit(solution)/shard_map/ppermute | solution.py:338
  112.5 11.3 %collective-permute-done.8 = bf16[512,320]{1,0:T(8,128)(2,1)} collective-permute-done((bf16[512,320]{1,0:T(8,128)(2,1)S(1)}, bf16[512,320]{1,0:T(8,128)(2,1)}, u32[]{:S(2)}, u32[]{:S(2)}) %collective-permute-start.8) | collective-permute-done | bytes 327712 | tf_op jit(solution)/shard_map/ppermute | solution.py:338
  125.6 5.6 collective-permute-done.9
  137.3 12.4 %collective-permute-done.16 = bf16[80,2432]{1,0:T(8,128)(2,1)S(1)} collective-permute-done((bf16[80,2432]{1,0:T(8,128)(2,1)}, bf16[80,2432]{1,0:T(8,128)(2,1)S(1)}, u32[]{:S(2)}, u32[]{:S(2)}) %collective-permute-start.16) | collective-permute-done | bytes 389152 | tf_op jit(solution)/shard_map/ppermute | solution.py:338
  162.2 14.6 %collective-permute-done.41 = bf16[192,2048]{1,0:T(8,128)(2,1)S(1)} collective-permute-done((bf16[192,2048]{1,0:T(8,128)(2,1)S(1)}, bf16[192,2048]{1,0:T(8,128)(2,1)S(1)}, u32[]{:S(2)}, u32[]{:S(2)}) %collective-permute-start.41) | collective-permute-done | bytes 786464 | tf_op jit(solution)/shard_map/ppermute | solution.py:338
  177.8 7.5 collective-permute-done.13
  186.3 7.3 collective-permute-done.10
  211.7 7.5 collective-permute-done.54
  222.2 13.6 %collective-permute-done.37 = bf16[512,768]{1,0:T(8,128)(2,1)S(1)} collective-permute-done((bf16[512,768]{1,0:T(8,128)(2,1)}, bf16[512,768]{1,0:T(8,128)(2,1)S(1)}, u32[]{:S(2)}, u32[]{:S(2)}) %collective-permute-start.37) | collective-permute-done | bytes 786464 | tf_op jit(solution)/shard_map/ppermute | solution.py:338
  267.8 7.8 fusion.178.yb_ref
  275.6 7.2 convolution_convert_fusion.3.xb_ref
  282.9 21.2 %recurrence_forward.1 = (bf16[2048,384]{1,0:T(8,128)(2,1)S(1)}, f32[2048,384]{1,0:T(8,128)S(1)}, f32[2048,384]{1,0:T(8,128)S(1)}, f32[2048,384]{1,0:T(8,128)S(1)}, bf16[2048,384]{1,0:T(8,128)(2,1)S(1)}) custom-call(bf16[2048,384]{1,0:T(8,128)(2,1)S(1)} %convolution_convert_fusion.3.xb_ref, f32[2048,384]{1,0:T(8,128)S(1)} %fusion.178.yb_ref, ...), custom_call_target="tpu_custom_call" | custom-call | flops 1286602752 | bytes 17301504 | tf_op jit(solution)/shard_map/recurrence_forward/pallas_call | solution.py:596
  330.4 8.7 collective-permute-done.21
  340.9 11.7 %collective-permute-done.24 = bf16[128,2048]{1,0:T(8,128)(2,1)S(1)} collective-permute-done((bf16[128,2048]{1,0:T(8,128)(2,1)S(1)}, bf16[128,2048]{1,0:T(8,128)(2,1)S(1)}, u32[]{:S(2)}, u32[]{:S(2)}) %collective-permute-start.24) | collective-permute-done | bytes 524320 | tf_op jit(solution)/shard_map/ppermute | solution.py:338
  364.5 11.9 %collective-permute-done.22 = bf16[256,2048]{1,0:T(8,128)(2,1)S(1)} collective-permute-done((bf16[256,2048]{1,0:T(8,128)(2,1)S(1)}, bf16[256,2048]{1,0:T(8,128)(2,1)S(1)}, u32[]{:S(2)}, u32[]{:S(2)}) %collective-permute-start.22) | collective-permute-done | bytes 1048608 | tf_op jit(solution)/shard_map/ppermute | solution.py:338
  383.2 8.5 collective-permute-done.36
  393.0 9.0 collective-permute-done.27
  405.4 11.7 %fusion.251 = f32[2048,768]{1,0:T(8,128)} fusion(bf16[2048,2048]{1,0:T(8,128)(2,1)} %constant_dynamic-update-slice_fusion.11, bf16[768,2048]{1,0:T(8,128)(2,1)} %bitcast.59), kind=kOutput, calls=%fused_computation.487 | convolution fusion | flops 6442450944 | bytes 17825792 | tf_op jit(solution)/shard_map/dot_general | solution.py:64
  421.4 13.2 %fusion.250 = f32[2048,768]{1,0:T(8,128)} fusion(bf16[2048,2048]{1,0:T(8,128)(2,1)S(1)} %constant_dynamic-update-slice_fusion.2, bf16[2048,768]{1,0:T(8,128)(2,1)} %bitcast.54), kind=kOutput, calls=%fused_computation.486 | convolution fusion | flops 6442450944 | bytes 17825792 | tf_op jit(solution)/shard_map/dot_general | solution.py:658
  434.6 17.3 %fusion.6 = (bf16[2048,768]{1,0:T(8,128)(2,1)S(1)}, bf16[2048,768]{1,0:T(8,128)(2,1)S(1)}, bf16[2048,768]{1,0:T(8,128)(2,1)}) fusion(f32[2048,768]{1,0:T(8,128)} %fusion.251, f32[2048,768]{1,0:T(8,128)} %fusion.250, bf16[2048,2048]{1,0:T(8,128)(2,1)} %copy-done.82, bf16[2048,768]{1,0:T(8,128)(2,1)S(1)} %bitcast.275), kind=kOutput, calls=%fused_computation.8 | convolution fusion | flops 6481772544 | bytes 33554432 | tf_op jit(solution)/shard_map/dot_general | solution.py:658
  451.9 11.8 %convolution_convert_fusion.1 = bf16[2048,768]{1,0:T(8,128)(2,1)S(1)} fusion(bf16[2048,2048]{1,0:T(8,128)(2,1)} %copy-done.82, bf16[2048,768]{1,0:T(8,128)(2,1)S(1)} %get-tuple-element.186), kind=kOutput, calls=%fused_computation.19 | convolution fusion | flops 6444023808 | bytes 14680064 | tf_op jit(solution)/shard_map/dot_general | solution.py:58
  485.5 4.5 fusion.121
  490.0 9.2 convolution_convert_fusion
  499.2 5.0 convolution_convert_fusion.18
  507.5 9.7 convolution_convert_fusion.2
  534.8 8.1 collective-permute-done.95
  545.2 14.6 %collective-permute-done.98 = bf16[512,768]{1,0:T(8,128)(2,1)S(1)} collective-permute-done((bf16[512,768]{1,0:T(8,128)(2,1)S(1)}, bf16[512,768]{1,0:T(8,128)(2,1)S(1)}, u32[]{:S(2)}, u32[]{:S(2)}) %collective-permute-start.98) | collective-permute-done | bytes 786464 | tf_op jit(solution)/shard_map/ppermute | solution.py:338
  578.6 7.1 collective-permute-done.62
  591.6 7.5 collective-permute-done.46
  600.5 11.1 %collective-permute-done.49 = bf16[128,2048]{1,0:T(8,128)(2,1)S(1)} collective-permute-done((bf16[128,2048]{1,0:T(8,128)(2,1)S(1)}, bf16[128,2048]{1,0:T(8,128)(2,1)S(1)}, u32[]{:S(2)}, u32[]{:S(2)}) %collective-permute-start.49) | collective-permute-done | bytes 524320 | tf_op jit(solution)/shard_map/ppermute | solution.py:338
  615.8 28.1 %collective-permute-done.96 = bf16[512,768]{1,0:T(8,128)(2,1)S(1)} collective-permute-done((bf16[512,768]{1,0:T(8,128)(2,1)S(1)}, bf16[512,768]{1,0:T(8,128)(2,1)S(1)}, u32[]{:S(2)}, u32[]{:S(2)}) %collective-permute-start.96) | collective-permute-done | bytes 786464 | tf_op jit(solution)/shard_map/ppermute | solution.py:338
  652.5 7.0 collective-permute-done.99
  662.8 11.8 %collective-permute-done.66 = bf16[256,2048]{1,0:T(8,128)(2,1)} collective-permute-done((bf16[256,2048]{1,0:T(8,128)(2,1)}, bf16[256,2048]{1,0:T(8,128)(2,1)}, u32[]{:S(2)}, u32[]{:S(2)}) %collective-permute-start.66) | collective-permute-done | bytes 1048608 | tf_op jit(solution)/shard_map/ppermute | solution.py:338
  676.2 5.9 multiply_reduce_fusion
  706.6 4.6 copy.190
  718.7 4.6 copy.191
  727.7 4.8 broadcast_multiply_fusion
  732.5 5.3 fusion.68
  745.2 8.0 collective-permute-done.72
  762.4 6.1 fusion.239.dm_ref
  768.6 31.4 %recurrence_backward.1 = (bf16[2048,384]{1,0:T(8,128)(2,1)S(1)}, bf16[2048,384]{1,0:T(8,128)(2,1)S(1)}, f32[384,768]{1,0:T(8,128)S(1)}, f32[64,384]{1,0:T(8,128)S(1)}) custom-call(f32[2048,384]{1,0:T(8,128)S(1)} %fusion.239.dm_ref, f32[2048,384]{1,0:T(8,128)S(1)} %copy-done.1, f32[2048,384]{1,0:T(8,128)S(1)} %copy-done.6, f32[2048,384]{1,0:T(8,128)S(1)} %copy-done.3, ...), custom_call_target="tpu_custom_call" | custom-call | flops 2557476864 | bytes 22020096 | tf_op jit(solution)/shard_map/recurrence_backward/pallas_call | solution.py:619
  800.8 8.2 fusion.253
  830.6 6.9 fusion.252
  876.4 13.8 %collective-permute-done.85 = bf16[512,320]{0,1:T(8,128)(2,1)S(1)} collective-permute-done((bf16[512,320]{0,1:T(8,128)(2,1)S(1)}, bf16[512,320]{0,1:T(8,128)(2,1)S(1)}, u32[]{:S(2)}, u32[]{:S(2)}) %collective-permute-start.85) | collective-permute-done | bytes 327712 | tf_op jit(solution)/shard_map/ppermute | solution.py:338
  898.8 7.5 collective-permute-done.88
  947.9 5.1 collective-permute-done.78
  967.5 9.7 collective-permute-done.93
  (684 shorter events, 487.7 us)
Async XLA Ops:
  13.1 71.9 %collective-permute-start.14 = (bf16[80,2432]{1,0:T(8,128)(2,1)}, bf16[80,2432]{1,0:T(8,128)(2,1)}, u32[]{:S(2)}, u32[]{:S(2)}) collective-permute-start(bf16[80,2432]{1,0:T(8,128)(2,1)} %pad.62), channel_id=1, source_target_pairs={{0,16},{16,0},{1,17},{17,1},{2,18},{18,2},{3,19},{19,3},{4,20},{20... | collective-permute-start | bytes 1167368 | tf_op jit(solution)/shard_map/ppermute | solution.py:338
  17.1 69.9 %collective-permute-start.15 = (bf16[80,2432]{1,0:T(8,128)(2,1)}, bf16[80,2432]{1,0:T(8,128)(2,1)}, u32[]{:S(2)}, u32[]{:S(2)}) collective-permute-start(bf16[80,2432]{1,0:T(8,128)(2,1)} %pad.62), channel_id=1, source_target_pairs={{0,8},{8,0},{1,9},{9,1},{2,10},{10,2},{3,11},{11,3},{4,12},{12,4},... | collective-permute-start | bytes 1167368 | tf_op jit(solution)/shard_map/ppermute | solution.py:338
  25.2 168.4 %collective-permute-start = (bf16[256,2048]{1,0:T(8,128)(2,1)}, bf16[256,2048]{1,0:T(8,128)(2,1)}, u32[]{:S(2)}, u32[]{:S(2)}) collective-permute-start(bf16[256,2048]{1,0:T(8,128)(2,1)} %get-tuple-element.184), channel_id=1, source_target_pairs={{0,1},{1,0},{2,3},{3,2},{4,5},{5,4},{6,7},{7,6},{8,9},{9,8},{10,11... | collective-permute-start | bytes 3145736 | tf_op jit(solution)/shard_map/ppermute | solution.py:338
  25.2 172.5 %collective-permute-start.1 = (bf16[256,2048]{1,0:T(8,128)(2,1)}, bf16[256,2048]{1,0:T(8,128)(2,1)}, u32[]{:S(2)}, u32[]{:S(2)}) collective-permute-start(bf16[256,2048]{1,0:T(8,128)(2,1)} %get-tuple-element.184), channel_id=1, source_target_pairs={{0,2},{2,0},{1,3},{3,1},{4,6},{6,4},{5,7},{7,5},{8,10},{10,8},{9,1... | collective-permute-start | bytes 3145736 | tf_op jit(solution)/shard_map/ppermute | solution.py:338
  26.7 171.9 %collective-permute-start.3 = (bf16[256,2048]{1,0:T(8,128)(2,1)}, bf16[256,2048]{1,0:T(8,128)(2,1)}, u32[]{:S(2)}, u32[]{:S(2)}) collective-permute-start(bf16[256,2048]{1,0:T(8,128)(2,1)} %get-tuple-element.184), channel_id=1, source_target_pairs={{0,4},{4,0},{1,5},{5,1},{2,6},{6,2},{3,7},{7,3},{8,12},{12,8},{9,1... | collective-permute-start | bytes 3145736 | tf_op jit(solution)/shard_map/ppermute | solution.py:338
  106.8 29.1 %all-to-all-start.2 = ((bf16[8,64,768]{2,1,0:T(8,128)(2,1)}), bf16[8,64,768]{2,1,0:T(8,128)(2,1)}, u32[]{:S(2)}, u32[]{:S(2)}) async-start(bf16[8,64,768]{2,1,0:T(8,128)(2,1)} %reshape.480), calls=%async_computation.2 | async-start | bytes 1572864 | tf_op jit(solution)/shard_map/all_to_all | solution.py:403
  123.8 36.3 %collective-permute-start.40 = (bf16[192,2048]{1,0:T(8,128)(2,1)}, bf16[192,2048]{1,0:T(8,128)(2,1)}, u32[]{:S(2)}, u32[]{:S(2)}) collective-permute-start(bf16[192,2048]{1,0:T(8,128)(2,1)} %param.42), channel_id=1, source_target_pairs={{0,16},{16,0},{1,17},{17,1},{2,18},{18,2},{3,19},{19,3},{4,20},{20... | collective-permute-start | bytes 2359304 | tf_op jit(solution)/shard_map/ppermute | solution.py:338
  197.7 38.1 %collective-permute-start.37 = (bf16[512,768]{1,0:T(8,128)(2,1)}, bf16[512,768]{1,0:T(8,128)(2,1)S(1)}, u32[]{:S(2)}, u32[]{:S(2)}) collective-permute-start(bf16[512,768]{1,0:T(8,128)(2,1)} %bitcast.50), channel_id=1, source_target_pairs={{0,16},{16,0},{1,17},{17,1},{2,18},{18,2},{3,19},{19,3},{4,20},{20... | collective-permute-start | bytes 2359304 | tf_op jit(solution)/shard_map/ppermute | solution.py:338
  198.6 39.2 %collective-permute-start.38 = (bf16[512,768]{1,0:T(8,128)(2,1)}, bf16[512,768]{1,0:T(8,128)(2,1)S(1)}, u32[]{:S(2)}, u32[]{:S(2)}) collective-permute-start(bf16[512,768]{1,0:T(8,128)(2,1)} %bitcast.50), channel_id=1, source_target_pairs={{0,8},{8,0},{1,9},{9,1},{2,10},{10,2},{3,11},{11,3},{4,12},{12,4},... | collective-permute-start | bytes 2359304 | tf_op jit(solution)/shard_map/ppermute | solution.py:338
  210.3 101.7 %collective-permute-start.34 = (bf16[512,768]{1,0:T(8,128)(2,1)}, bf16[512,768]{1,0:T(8,128)(2,1)}, u32[]{:S(2)}, u32[]{:S(2)}) collective-permute-start(bf16[512,768]{1,0:T(8,128)(2,1)} %bitcast.43), channel_id=1, source_target_pairs={{0,16},{16,0},{1,17},{17,1},{2,18},{18,2},{3,19},{19,3},{4,20},{20... | collective-permute-start | bytes 2359304 | tf_op jit(solution)/shard_map/ppermute | solution.py:338
  219.2 94.1 %collective-permute-start.35 = (bf16[512,768]{1,0:T(8,128)(2,1)}, bf16[512,768]{1,0:T(8,128)(2,1)}, u32[]{:S(2)}, u32[]{:S(2)}) collective-permute-start(bf16[512,768]{1,0:T(8,128)(2,1)} %bitcast.43), channel_id=1, source_target_pairs={{0,8},{8,0},{1,9},{9,1},{2,10},{10,2},{3,11},{11,3},{4,12},{12,4},... | collective-permute-start | bytes 2359304 | tf_op jit(solution)/shard_map/ppermute | solution.py:338
  256.0 98.3 %collective-permute-start.42 = (bf16[192,2048]{1,0:T(8,128)(2,1)}, bf16[192,2048]{1,0:T(8,128)(2,1)}, u32[]{:S(2)}, u32[]{:S(2)}) collective-permute-start(bf16[192,2048]{1,0:T(8,128)(2,1)} %collective-permute-done.40), channel_id=1, source_target_pairs={{0,8},{8,0},{1,9},{9,1},{2,10},{10,2},{3,11},{11,3},{4,12},{12,4},... | collective-permute-start | bytes 2359304 | tf_op jit(solution)/shard_map/ppermute | solution.py:338
  262.4 54.8 %collective-permute-start.56 = (bf16[128,2048]{1,0:T(8,128)(2,1)S(1)}, bf16[128,2048]{1,0:T(8,128)(2,1)S(1)}, u32[]{:S(2)}, u32[]{:S(2)}) collective-permute-start(bf16[128,2048]{1,0:T(8,128)(2,1)S(1)} %copy-done.78), channel_id=1, source_target_pairs={{0,4},{4,0},{1,5},{5,1},{2,6},{6,2},{3,7},{7,3},{8,12},{12,8},{9,1... | collective-permute-start | bytes 1572872 | tf_op jit(solution)/shard_map/ppermute | solution.py:338
  266.1 51.2 %collective-permute-start.57 = (bf16[128,2048]{1,0:T(8,128)(2,1)S(1)}, bf16[128,2048]{1,0:T(8,128)(2,1)S(1)}, u32[]{:S(2)}, u32[]{:S(2)}) collective-permute-start(bf16[128,2048]{1,0:T(8,128)(2,1)S(1)} %copy-done.79), channel_id=1, source_target_pairs={{0,2},{2,0},{1,3},{3,1},{4,6},{6,4},{5,7},{7,5},{8,10},{10,8},{9,1... | collective-permute-start | bytes 1572872 | tf_op jit(solution)/shard_map/ppermute | solution.py:338
  313.3 43.7 %collective-permute-start.53 = (bf16[256,2048]{1,0:T(8,128)(2,1)S(1)}, bf16[256,2048]{1,0:T(8,128)(2,1)S(1)}, u32[]{:S(2)}, u32[]{:S(2)}) collective-permute-start(bf16[256,2048]{1,0:T(8,128)(2,1)S(1)} %copy-done.60), channel_id=1, source_target_pairs={{0,1},{1,0},{2,3},{3,2},{4,5},{5,4},{6,7},{7,6},{8,9},{9,8},{10,11... | collective-permute-start | bytes 3145736 | tf_op jit(solution)/shard_map/ppermute | solution.py:338
  322.3 38.7 %collective-permute-start.55 = (bf16[256,2048]{1,0:T(8,128)(2,1)S(1)}, bf16[256,2048]{1,0:T(8,128)(2,1)S(1)}, u32[]{:S(2)}, u32[]{:S(2)}) collective-permute-start(bf16[256,2048]{1,0:T(8,128)(2,1)S(1)} %copy-done.62), channel_id=1, source_target_pairs={{0,1},{1,0},{2,3},{3,2},{4,5},{5,4},{6,7},{7,6},{8,9},{9,8},{10,11... | collective-permute-start | bytes 3145736 | tf_op jit(solution)/shard_map/ppermute | solution.py:338
  328.0 36.4 %collective-permute-start.18 = (bf16[256,2048]{1,0:T(8,128)(2,1)S(1)}, bf16[256,2048]{1,0:T(8,128)(2,1)S(1)}, u32[]{:S(2)}, u32[]{:S(2)}) collective-permute-start(bf16[256,2048]{1,0:T(8,128)(2,1)S(1)} %convolution_convert_fusion.10), channel_id=1, source_target_pairs={{0,1},{1,0},{2,3},{3,2},{4,5},{5,4},{6,7},{7,6},{8,9},{9,8},{10,11... | collective-permute-start | bytes 3145736 | tf_op jit(solution)/shard_map/ppermute | solution.py:338
  361.1 30.6 %collective-permute-start.36 = (bf16[512,768]{1,0:T(8,128)(2,1)}, bf16[512,768]{1,0:T(8,128)(2,1)S(1)}, u32[]{:S(2)}, u32[]{:S(2)}) collective-permute-start(bf16[512,768]{1,0:T(8,128)(2,1)} %collective-permute-done.34), channel_id=1, source_target_pairs={{0,8},{8,0},{1,9},{9,1},{2,10},{10,2},{3,11},{11,3},{4,12},{12,4},... | collective-permute-start | bytes 2359304 | tf_op jit(solution)/shard_map/ppermute | solution.py:338
  505.5 55.4 %collective-permute-start.101 = (bf16[192,2048]{1,0:T(8,128)(2,1)}, bf16[192,2048]{1,0:T(8,128)(2,1)}, u32[]{:S(2)}, u32[]{:S(2)}) collective-permute-start(bf16[192,2048]{1,0:T(8,128)(2,1)} %get-tuple-element.189), channel_id=1, source_target_pairs={{0,8},{8,0},{1,9},{9,1},{2,10},{10,2},{3,11},{11,3},{4,12},{12,4},... | collective-permute-start | bytes 2359304 | tf_op jit(solution)/shard_map/ppermute | solution.py:338
  519.3 40.4 %collective-permute-start.98 = (bf16[512,768]{1,0:T(8,128)(2,1)S(1)}, bf16[512,768]{1,0:T(8,128)(2,1)S(1)}, u32[]{:S(2)}, u32[]{:S(2)}) collective-permute-start(bf16[512,768]{1,0:T(8,128)(2,1)S(1)} %get-tuple-element.191), channel_id=1, source_target_pairs={{0,8},{8,0},{1,9},{9,1},{2,10},{10,2},{3,11},{11,3},{4,12},{12,4},... | collective-permute-start | bytes 2359304 | tf_op jit(solution)/shard_map/ppermute | solution.py:338
  528.6 35.1 %collective-permute-start.60 = (bf16[256,2048]{1,0:T(8,128)(2,1)S(1)}, bf16[256,2048]{1,0:T(8,128)(2,1)S(1)}, u32[]{:S(2)}, u32[]{:S(2)}) collective-permute-start(bf16[256,2048]{1,0:T(8,128)(2,1)S(1)} %fusion.11), channel_id=1, source_target_pairs={{0,1},{1,0},{2,3},{3,2},{4,5},{5,4},{6,7},{7,6},{8,9},{9,8},{10,11... | collective-permute-start | bytes 3145736 | tf_op jit(solution)/shard_map/ppermute | solution.py:338
  534.7 80.9 %collective-permute-start.94 = (bf16[512,768]{1,0:T(8,128)(2,1)S(1)}, bf16[512,768]{1,0:T(8,128)(2,1)S(1)}, u32[]{:S(2)}, u32[]{:S(2)}) collective-permute-start(bf16[512,768]{1,0:T(8,128)(2,1)S(1)} %get-tuple-element.192), channel_id=1, source_target_pairs={{0,8},{8,0},{1,9},{9,1},{2,10},{10,2},{3,11},{11,3},{4,12},{12,4},... | collective-permute-start | bytes 2359304 | tf_op jit(solution)/shard_map/ppermute | solution.py:338
  542.9 109.6 %collective-permute-start.97 = (bf16[512,768]{1,0:T(8,128)(2,1)}, bf16[512,768]{1,0:T(8,128)(2,1)}, u32[]{:S(2)}, u32[]{:S(2)}) collective-permute-start(bf16[512,768]{1,0:T(8,128)(2,1)} %get-tuple-element.190), channel_id=1, source_target_pairs={{0,8},{8,0},{1,9},{9,1},{2,10},{10,2},{3,11},{11,3},{4,12},{12,4},... | collective-permute-start | bytes 2359304 | tf_op jit(solution)/shard_map/ppermute | solution.py:338
  560.9 101.5 %collective-permute-start.59 = (bf16[256,2048]{1,0:T(8,128)(2,1)S(1)}, bf16[256,2048]{1,0:T(8,128)(2,1)}, u32[]{:S(2)}, u32[]{:S(2)}) collective-permute-start(bf16[256,2048]{1,0:T(8,128)(2,1)S(1)} %fusion.9), channel_id=1, source_target_pairs={{0,1},{1,0},{2,3},{3,2},{4,5},{5,4},{6,7},{7,6},{8,9},{9,8},{10,11... | collective-permute-start | bytes 3145736 | tf_op jit(solution)/shard_map/ppermute | solution.py:338
  588.8 55.1 %collective-permute-start.96 = (bf16[512,768]{1,0:T(8,128)(2,1)S(1)}, bf16[512,768]{1,0:T(8,128)(2,1)S(1)}, u32[]{:S(2)}, u32[]{:S(2)}) collective-permute-start(bf16[512,768]{1,0:T(8,128)(2,1)S(1)} %fusion.85), channel_id=1, source_target_pairs={{0,16},{16,0},{1,17},{17,1},{2,18},{18,2},{3,19},{19,3},{4,20},{20... | collective-permute-start | bytes 2359304 | tf_op jit(solution)/shard_map/ppermute | solution.py:338
  611.6 47.9 %collective-permute-start.99 = (bf16[512,768]{1,0:T(8,128)(2,1)}, bf16[512,768]{1,0:T(8,128)(2,1)}, u32[]{:S(2)}, u32[]{:S(2)}) collective-permute-start(bf16[512,768]{1,0:T(8,128)(2,1)} %fusion.82), channel_id=1, source_target_pairs={{0,16},{16,0},{1,17},{17,1},{2,18},{18,2},{3,19},{19,3},{4,20},{20... | collective-permute-start | bytes 2359304 | tf_op jit(solution)/shard_map/ppermute | solution.py:338
  615.5 46.9 %collective-permute-start.63 = (bf16[256,2048]{1,0:T(8,128)(2,1)}, bf16[256,2048]{1,0:T(8,128)(2,1)}, u32[]{:S(2)}, u32[]{:S(2)}) collective-permute-start(bf16[256,2048]{1,0:T(8,128)(2,1)} %pad_maximum_fusion.6), channel_id=1, source_target_pairs={{0,2},{2,0},{1,3},{3,1},{4,6},{6,4},{5,7},{7,5},{8,10},{10,8},{9,1... | collective-permute-start | bytes 3145736 | tf_op jit(solution)/shard_map/ppermute | solution.py:338
  643.9 30.6 %collective-permute-start.66 = (bf16[256,2048]{1,0:T(8,128)(2,1)}, bf16[256,2048]{1,0:T(8,128)(2,1)}, u32[]{:S(2)}, u32[]{:S(2)}) collective-permute-start(bf16[256,2048]{1,0:T(8,128)(2,1)} %pad_maximum_fusion.7), channel_id=1, source_target_pairs={{0,4},{4,0},{1,5},{5,1},{2,6},{6,2},{3,7},{7,3},{8,12},{12,8},{9,1... | collective-permute-start | bytes 3145736 | tf_op jit(solution)/shard_map/ppermute | solution.py:338
  648.9 33.2 %all-to-all-start.6 = ((bf16[8,64,768]{2,1,0:T(8,128)(2,1)}), bf16[8,64,768]{2,1,0:T(8,128)(2,1)S(1)}, u32[]{:S(2)}, u32[]{:S(2)}) async-start(bf16[8,64,768]{2,1,0:T(8,128)(2,1)} %bitcast.102), calls=%async_computation.7 | async-start | bytes 1572864 | tf_op jit(solution)/shard_map/all_to_all | solution.py:403
  652.5 42.0 %collective-permute-start.100 = (bf16[192,2048]{1,0:T(8,128)(2,1)}, bf16[192,2048]{1,0:T(8,128)(2,1)}, u32[]{:S(2)}, u32[]{:S(2)}) collective-permute-start(bf16[192,2048]{1,0:T(8,128)(2,1)} %get-tuple-element.188), channel_id=1, source_target_pairs={{0,8},{8,0},{1,9},{9,1},{2,10},{10,2},{3,11},{11,3},{4,12},{12,4},... | collective-permute-start | bytes 2359304 | tf_op jit(solution)/shard_map/ppermute | solution.py:338
  659.6 36.8 %collective-permute-start.43 = (bf16[256,2048]{1,0:T(8,128)(2,1)}, bf16[256,2048]{1,0:T(8,128)(2,1)}, u32[]{:S(2)}, u32[]{:S(2)}) collective-permute-start(bf16[256,2048]{1,0:T(8,128)(2,1)} %convolution_convert_fusion.18), channel_id=1, source_target_pairs={{0,1},{1,0},{2,3},{3,2},{4,5},{5,4},{6,7},{7,6},{8,9},{9,8},{10,11... | collective-permute-start | bytes 3145736 | tf_op jit(solution)/shard_map/ppermute | solution.py:338
  662.4 38.0 %collective-permute-start.102 = (bf16[192,2048]{1,0:T(8,128)(2,1)}, bf16[192,2048]{1,0:T(8,128)(2,1)S(1)}, u32[]{:S(2)}, u32[]{:S(2)}) collective-permute-start(bf16[192,2048]{1,0:T(8,128)(2,1)} %fusion.80), channel_id=1, source_target_pairs={{0,16},{16,0},{1,17},{17,1},{2,18},{18,2},{3,19},{19,3},{4,20},{20... | collective-permute-start | bytes 2359304 | tf_op jit(solution)/shard_map/ppermute | solution.py:338
  662.4 70.0 %collective-permute-start.47 = (bf16[256,2048]{1,0:T(8,128)(2,1)}, bf16[256,2048]{1,0:T(8,128)(2,1)}, u32[]{:S(2)}, u32[]{:S(2)}) collective-permute-start(bf16[256,2048]{1,0:T(8,128)(2,1)} %pad_maximum_fusion.3), channel_id=1, source_target_pairs={{0,2},{2,0},{1,3},{3,1},{4,6},{6,4},{5,7},{7,5},{8,10},{10,8},{9,1... | collective-permute-start | bytes 3145736 | tf_op jit(solution)/shard_map/ppermute | solution.py:338
  674.5 57.9 %collective-permute-start.50 = (bf16[256,2048]{1,0:T(8,128)(2,1)}, bf16[256,2048]{1,0:T(8,128)(2,1)}, u32[]{:S(2)}, u32[]{:S(2)}) collective-permute-start(bf16[256,2048]{1,0:T(8,128)(2,1)} %pad_maximum_fusion.4), channel_id=1, source_target_pairs={{0,4},{4,0},{1,5},{5,1},{2,6},{6,2},{3,7},{7,3},{8,12},{12,8},{9,1... | collective-permute-start | bytes 3145736 | tf_op jit(solution)/shard_map/ppermute | solution.py:338
  682.1 32.2 %all-to-all-start.7 = ((bf16[8,64,768]{2,1,0:T(8,128)(2,1)}), bf16[8,64,768]{2,1,0:T(8,128)(2,1)}, u32[]{:S(2)}, u32[]{:S(2)}) async-start(bf16[8,64,768]{2,1,0:T(8,128)(2,1)} %bitcast.109), calls=%async_computation.8 | async-start | bytes 1572864 | tf_op jit(solution)/shard_map/all_to_all | solution.py:403
  694.5 43.3 %collective-permute-start.68 = (bf16[256,2048]{1,0:T(8,128)(2,1)}, bf16[256,2048]{1,0:T(8,128)(2,1)}, u32[]{:S(2)}, u32[]{:S(2)}) collective-permute-start(bf16[256,2048]{1,0:T(8,128)(2,1)} %get-tuple-element.177), channel_id=1, source_target_pairs={{0,2},{2,0},{1,3},{3,1},{4,6},{6,4},{5,7},{7,5},{8,10},{10,8},{9,1... | collective-permute-start | bytes 3145736 | tf_op jit(solution)/shard_map/ppermute | solution.py:338
  696.4 44.0 %collective-permute-start.70 = (bf16[256,2048]{1,0:T(8,128)(2,1)}, bf16[256,2048]{1,0:T(8,128)(2,1)}, u32[]{:S(2)}, u32[]{:S(2)}) collective-permute-start(bf16[256,2048]{1,0:T(8,128)(2,1)} %get-tuple-element.177), channel_id=1, source_target_pairs={{0,4},{4,0},{1,5},{5,1},{2,6},{6,2},{3,7},{7,3},{8,12},{12,8},{9,1... | collective-permute-start | bytes 3145736 | tf_op jit(solution)/shard_map/ppermute | solution.py:338
  700.3 42.2 %collective-permute-start.67 = (bf16[256,2048]{1,0:T(8,128)(2,1)}, bf16[256,2048]{1,0:T(8,128)(2,1)}, u32[]{:S(2)}, u32[]{:S(2)}) collective-permute-start(bf16[256,2048]{1,0:T(8,128)(2,1)} %get-tuple-element.177), channel_id=1, source_target_pairs={{0,1},{1,0},{2,3},{3,2},{4,5},{5,4},{6,7},{7,6},{8,9},{9,8},{10,11... | collective-permute-start | bytes 3145736 | tf_op jit(solution)/shard_map/ppermute | solution.py:338
  827.9 85.1 %collective-permute-start.90 = (bf16[2,80,2048]{2,1,0:T(8,128)(2,1)}, bf16[2,80,2048]{2,1,0:T(8,128)(2,1)}, u32[]{:S(2)}, u32[]{:S(2)}) collective-permute-start(bf16[2,80,2048]{2,1,0:T(8,128)(2,1)} %dynamic-slice_bitcast_fusion.7), channel_id=1, source_target_pairs={{0,1},{1,0},{2,3},{3,2},{4,5},{5,4},{6,7},{7,6},{8,9},{9,8},{10,11... | collective-permute-start | bytes 1966088 | tf_op jit(solution)/shard_map/ppermute | solution.py:338
  830.6 65.9 %collective-permute-start.89 = (f32[2,80,328]{2,1,0:T(8,128)}, f32[2,80,328]{2,1,0:T(8,128)}, u32[]{:S(2)}, u32[]{:S(2)}) collective-permute-start(f32[2,80,328]{2,1,0:T(8,128)} %dynamic-slice_bitcast_fusion.10), channel_id=1, source_target_pairs={{0,1},{1,0},{2,3},{3,2},{4,5},{5,4},{6,7},{7,6},{8,9},{9,8},{10,11... | collective-permute-start | bytes 629768 | tf_op jit(solution)/shard_map/ppermute | solution.py:338
  847.2 29.1 %collective-permute-start.83 = (bf16[512,320]{0,1:T(8,128)(2,1)}, bf16[512,320]{0,1:T(8,128)(2,1)}, u32[]{:S(2)}, u32[]{:S(2)}) collective-permute-start(bf16[512,320]{0,1:T(8,128)(2,1)} %bitcast.270), channel_id=1, source_target_pairs={{0,8},{8,0},{1,9},{9,1},{2,10},{10,2},{3,11},{11,3},{4,12},{12,4},... | collective-permute-start | bytes 983048 | tf_op jit(solution)/shard_map/ppermute | solution.py:338
  876.3 102.9 %collective-permute-start.75 = (bf16[256,2048]{1,0:T(8,128)(2,1)}, bf16[256,2048]{1,0:T(8,128)(2,1)}, u32[]{:S(2)}, u32[]{:S(2)}) collective-permute-start(bf16[256,2048]{1,0:T(8,128)(2,1)} %fusion.38), channel_id=1, source_target_pairs={{0,1},{1,0},{2,3},{3,2},{4,5},{5,4},{6,7},{7,6},{8,9},{9,8},{10,11... | collective-permute-start | bytes 3145736 | tf_op jit(solution)/shard_map/ppermute | solution.py:338
  896.4 66.2 %reduce-scatter.2.cloned.1.call-start = ((), (), s32[]{:S(2)}) async-start(), calls=%async_computation.9 | async-start | bytes 614400 | tf_op jit(solution)/shard_map/reduce_scatter | solution.py:811
  896.4 42.7 %collective-permute-start.76 = (bf16[256,2048]{1,0:T(8,128)(2,1)}, bf16[256,2048]{1,0:T(8,128)(2,1)}, u32[]{:S(2)}, u32[]{:S(2)}) collective-permute-start(bf16[256,2048]{1,0:T(8,128)(2,1)} %fusion.43), channel_id=1, source_target_pairs={{0,1},{1,0},{2,3},{3,2},{4,5},{5,4},{6,7},{7,6},{8,9},{9,8},{10,11... | collective-permute-start | bytes 3145736 | tf_op jit(solution)/shard_map/ppermute | solution.py:338
  898.5 36.0 %collective-permute-start.77 = (bf16[256,2048]{1,0:T(8,128)(2,1)}, bf16[256,2048]{1,0:T(8,128)(2,1)}, u32[]{:S(2)}, u32[]{:S(2)}) collective-permute-start(bf16[256,2048]{1,0:T(8,128)(2,1)} %fusion.48), channel_id=1, source_target_pairs={{0,1},{1,0},{2,3},{3,2},{4,5},{5,4},{6,7},{7,6},{8,9},{9,8},{10,11... | collective-permute-start | bytes 3145736 | tf_op jit(solution)/shard_map/ppermute | solution.py:338
  906.3 37.5 %collective-permute-start.80 = (bf16[256,2048]{1,0:T(8,128)(2,1)}, bf16[256,2048]{1,0:T(8,128)(2,1)}, u32[]{:S(2)}, u32[]{:S(2)}) collective-permute-start(bf16[256,2048]{1,0:T(8,128)(2,1)} %fusion.53), channel_id=1, source_target_pairs={{0,1},{1,0},{2,3},{3,2},{4,5},{5,4},{6,7},{7,6},{8,9},{9,8},{10,11... | collective-permute-start | bytes 3145736 | tf_op jit(solution)/shard_map/ppermute | solution.py:338
  915.2 45.9 %collective-permute-start.92 = (bf16[80,2048]{1,0:T(8,128)(2,1)}, bf16[80,2048]{1,0:T(8,128)(2,1)}, u32[]{:S(2)}, u32[]{:S(2)}) collective-permute-start(bf16[80,2048]{1,0:T(8,128)(2,1)} %get-tuple-element.202), channel_id=1, source_target_pairs={{0,8},{8,0},{1,9},{9,1},{2,10},{10,2},{3,11},{11,3},{4,12},{12,4},... | collective-permute-start | bytes 983048 | tf_op jit(solution)/shard_map/ppermute | solution.py:338
  934.5 33.0 %collective-permute-start.91 = (bf16[80,2048]{1,0:T(8,128)(2,1)}, bf16[80,2048]{1,0:T(8,128)(2,1)S(1)}, u32[]{:S(2)}, u32[]{:S(2)}) collective-permute-start(bf16[80,2048]{1,0:T(8,128)(2,1)} %get-tuple-element.201), channel_id=1, source_target_pairs={{0,8},{8,0},{1,9},{9,1},{2,10},{10,2},{3,11},{11,3},{4,12},{12,4},... | collective-permute-start | bytes 983048 | tf_op jit(solution)/shard_map/ppermute | solution.py:338
  (167 other events, 2454.6 us)
Sparse Core Ops, SparseCore 0:
  899.5 23.9 reduce-scatter.1

commit v2 on v1

--- a/solution.py
+++ b/solution.py
@@ -383,20 +383,53 @@
     return own + swap(other, w1).astype(F32)
 
 
-def to_columns(w, tp, rest):
-    rows, cols = w.shape
-    dims = {n: i + 1 for i, n in enumerate(NAMES)}
-    v = w.reshape((rows,) + (2,) * 5 + (cols // 32,))
-    v = v.transpose([dims[n] for n in tp] + [0] + [dims[n] for n in rest] + [6])
-    return v.reshape(8, rows, cols // 8)
-
-
-def from_columns(v, tp, rest):
-    _, rows, cols = v.shape
-    order = list(tp) + ["rows"] + list(rest)
-    v = v.reshape((2, 2, 2, rows, 2, 2, cols // 4))
-    v = v.transpose([order.index("rows")] + [order.index(n) for n in NAMES] + [6])
-    return v.reshape(rows, cols * 8)
+def pack_kernel(plan, a_ref, b_ref, gain_ref, out_ref):
+    half = out_ref.shape[2] // 2
+    for first, ref in ((0, a_ref), (half, b_ref)):
+        scaled = (ref[...].astype(F32) * gain_ref[...]).astype(BF16)
+        for dest, pieces in enumerate(plan):
+            at = first
+            for source, size in pieces:
+                out_ref[dest, :, at : at + size] = scaled[:, source : source + size]
+                at += size
+            if at < first + half:
+                out_ref[dest, :, at : first + half] = jnp.zeros((scaled.shape[0], first + half - at), BF16)
+
+
+def unpack_kernel(plan, grad_ref, a_ref, b_ref, gain_ref, da_ref, db_ref, dgain_ref):
+    half = grad_ref.shape[2] // 2
+    total = jnp.zeros(dgain_ref.shape, F32)
+    for first, ref, out in ((0, a_ref, da_ref), (half, b_ref, db_ref)):
+        for dest, pieces in enumerate(plan):
+            at = first
+            for source, size in pieces:
+                piece = grad_ref[dest, :, at : at + size].astype(F32)
+                out[:, source : source + size] = piece * gain_ref[...]
+                weight = ref[:, source : source + size].astype(F32)
+                total = total + jnp.sum(piece * weight, axis=1, keepdims=True)
+                at += size
+    dgain_ref[...] = total
+
+
+def pack_columns(plan, half, one, two, gain):
+    return pl.pallas_call(
+        functools.partial(pack_kernel, plan),
+        out_shape=jax.ShapeDtypeStruct((8, one.shape[0], 2 * half), BF16),
+        compiler_params=pltpu.CompilerParams(vmem_limit_bytes=24 << 20),
+        cost_estimate=pl.CostEstimate(flops=4 * one.size, transcendentals=0, bytes_accessed=8 * one.size),
+        name="pack_columns",
+    )(one, two, gain)
+
+
+def unpack_columns(plan, grad, one, two, gain):
+    shape = jax.ShapeDtypeStruct(one.shape, F32)
+    return pl.pallas_call(
+        functools.partial(unpack_kernel, plan),
+        out_shape=[shape, shape, jax.ShapeDtypeStruct((one.shape[0], 1), F32)],
+        compiler_params=pltpu.CompilerParams(vmem_limit_bytes=24 << 20),
+        cost_estimate=pl.CostEstimate(flops=8 * one.size, transcendentals=0, bytes_accessed=16 * one.size),
+        name="unpack_columns",
+    )(grad, one, two, gain)
 
 
 def exchange(v, tp):
@@ -452,23 +485,34 @@
 STEP = 16
 
 
-def rec_fwd_kernel(xb_ref, yb_ref, mask_ref, vec_ref, w_ref, xc_ref, pa_ref, px_ref, sp_ref, mixed_ref, ext, carry):
+def since_start(meta_ref, place, width):
+    at = place + lax.broadcasted_iota(jnp.int32, (STEP, 128), 0)
+    since, start = at, 0
+    for n in range(1, meta_ref.shape[0] - 1):
+        start = start + meta_ref[n]
+        since = jnp.where(at >= start, at - start, since)
+    return jnp.concatenate([since] * (width // 128), axis=1)
+
+
+def rec_fwd_kernel(meta_ref, xb_ref, yb_ref, vec_ref, w_ref, xc_ref, pa_ref, px_ref, sp_ref, mixed_ref, ext, carry):
     rows, width = xb_ref.shape
+    base = pl.program_id(0) * rows
 
     @pl.when(pl.program_id(0) == 0)
     def _():
         ext[0:8, :] = jnp.zeros((8, width), F32)
         carry[...] = jnp.zeros_like(carry)
 
-    ext[8 : 8 + rows, :] = xb_ref[...].astype(F32)
+    ext[8 : 8 + rows, :] = xb_ref[...].astype(BF16).astype(F32)
 
     def conv_step(r, _):
         at = pl.multiple_of(r * STEP, STEP)
         window = ext[pl.ds(at, STEP + 8), :]
-        mask = mask_ref[pl.ds(at, STEP), :]
+        since = since_start(meta_ref, base + at, width)
         total = vec_ref[4:5, :] + vec_ref[0:1, :] * window[8:, :]
         for k in range(1, 4):
-            total = total + vec_ref[k : k + 1, :] * window[8 - k : 8 - k + STEP, :] * mask[:, k : k + 1]
+            moved = jnp.where(since >= k, window[8 - k : 8 - k + STEP, :], 0.0)
+            total = total + vec_ref[k : k + 1, :] * moved
         xc_ref[pl.ds(at, STEP), :] = total.astype(BF16)
         return 0
 
@@ -481,7 +525,7 @@
 
     def scan_step(r, held):
         here = pl.ds(pl.multiple_of(r * STEP, STEP), STEP)
-        start = jnp.broadcast_to(mask_ref[here, 0:1], (STEP, width)) > 0.5
+        start = since_start(meta_ref, base + r * STEP, width) == 0
         _, si, decay, _, _, scale = gate_terms(pa_ref[here, :], px_ref[here, :], vec_ref[5:6, :], start)
         drive = scale * si * xc_ref[here, :].astype(F32)
         states, before = [], []
@@ -498,10 +542,11 @@
 
 
 def rec_bwd_kernel(
-    dm_ref, yb_ref, sp_ref, pa_ref, px_ref, xc_ref, xb_ref, mask_ref, vec_ref, wt_ref,
-    dxb_ref, dyb_ref, dw_ref, sum_ref, ext, dp, carry,
+    meta_ref, dm_ref, yb_ref, sp_ref, pa_ref, px_ref, xc_ref, xb_ref, vec_ref, wt_ref,
+    dxy_ref, dw_ref, sum_ref, ext, dp, carry,
 ):
     rows, width = xb_ref.shape
+    base = (pl.num_programs(0) - 1 - pl.program_id(0)) * rows
 
     @pl.when(pl.program_id(0) == 0)
     def _():
@@ -518,8 +563,9 @@
 
     def scan_step(i, state):
         held, s_rate, s_r, s_i = state
-        here = pl.ds(pl.multiple_of((steps - 1 - i) * STEP, STEP), STEP)
-        start = jnp.broadcast_to(mask_ref[here, 0:1], (STEP, width)) > 0.5
+        at = pl.multiple_of((steps - 1 - i) * STEP, STEP)
+        here = pl.ds(at, STEP)
+        start = since_start(meta_ref, base + at, width) == 0
         rate = vec_ref[5:6, :]
         sr, si, decay, e2, floor, scale = gate_terms(pa_ref[here, :], px_ref[here, :], rate, start)
         xc = xc_ref[here, :].astype(F32)
@@ -528,7 +574,7 @@
         now = decay * before + scale * gate
         dm = dm_ref[here, :]
         act, slope = gelu_both(yb_ref[here, :])
-        dyb_ref[here, :] = (dm * now * slope).astype(BF16)
+        dxy_ref[here, width:] = (dm * now * slope).astype(BF16)
         dstate = dm * act
         parts = []
         for part in range(STEP - 8, -1, -8):
@@ -564,18 +610,17 @@
     def conv_step(r, sums):
         at = pl.multiple_of(r * STEP, STEP)
         window = ext[pl.ds(at, STEP + 8), :]
-        mask = mask_ref[pl.ds(at, STEP), :]
-        xb = xb_ref[pl.ds(at, STEP), :].astype(F32)
+        xb = xb_ref[pl.ds(at, STEP), :].astype(BF16).astype(F32)
         total = jnp.zeros((STEP, width), F32)
         new = []
         for k in range(4):
             moved = window[k : k + STEP, :]
             if k:
-                moved = moved * mask[:, 3 + k : 4 + k]
+                moved = jnp.where(since_start(meta_ref, base + at + k, width) >= k, moved, 0.0)
             total = total + vec_ref[k : k + 1, :] * moved
             new.append(sums[k] + fold(moved * xb))
         new.append(sums[4] + fold(window[:STEP, :]))
-        dxb_ref[pl.ds(at, STEP), :] = total.astype(BF16)
+        dxy_ref[pl.ds(at, STEP), :width] = total.astype(BF16)
         return tuple(new)
 
     sums = lax.fori_loop(0, steps, conv_step, tuple(sum_ref[8 * q : 8 * q + 8, :] for q in range(5)), unroll=2)
@@ -584,74 +629,67 @@
     ext[rows : rows + 8, :] = ext[0:8, :]
 
 
-def time_tile(total):
-    return 256 if total % 256 == 0 else total
-
-
-def rec_forward(xb, yb, mask, vec, w):
-    total, width = xb.shape
-    tile = time_tile(total)
-    block = pl.BlockSpec((tile, width), lambda i: (i, 0))
-    whole = lambda v: pl.BlockSpec(v.shape, lambda i: (0, 0))
+def rec_forward(meta, xy, vec, w, tile):
+    total, width = xy.shape[0], xy.shape[1] // 2
+    block = pl.BlockSpec((tile, width), lambda i, m: (i ^ m[0], 0))
+    right = pl.BlockSpec((tile, width), lambda i, m: (i ^ m[0], 1))
+    whole = lambda v: pl.BlockSpec(v.shape, lambda i, m: (0, 0))
     return pl.pallas_call(
         rec_fwd_kernel,
-        grid=(total // tile,),
-        in_specs=[block, block, pl.BlockSpec((tile, 8), lambda i: (i, 0)), whole(vec), whole(w)],
-        out_specs=[block] * 5,
+        grid_spec=pltpu.PrefetchScalarGridSpec(
+            num_scalar_prefetch=1,
+            grid=(total // tile,),
+            in_specs=[block, right, whole(vec), whole(w)],
+            out_specs=[block] * 5,
+            scratch_shapes=[pltpu.VMEM((tile + 8, width), F32), pltpu.VMEM((8, width), F32)],
+        ),
         out_shape=[jax.ShapeDtypeStruct((total, width), t) for t in (BF16, F32, F32, F32, BF16)],
-        scratch_shapes=[pltpu.VMEM((tile + 8, width), F32), pltpu.VMEM((8, width), F32)],
         compiler_params=pltpu.CompilerParams(vmem_limit_bytes=32 << 20),
         cost_estimate=pl.CostEstimate(
             flops=100 * total * width + 4 * total * width * width,
             transcendentals=6 * total * width,
-            bytes_accessed=22 * total * width,
+            bytes_accessed=24 * total * width,
         ),
         name="recurrence_forward",
-    )(xb, yb, mask, vec, w)
-
-
-def rec_backward(dm, yb, sp, pa, px, xc, xb, mask, vec, wt):
-    total, width = xb.shape
-    tile = time_tile(total)
+    )(meta, xy, xy, vec, w)
+
+
+def rec_backward(meta, dm, xy, sp, pa, px, xc, vec, wt, tile):
+    total, width = dm.shape
     steps = total // tile
-    block = pl.BlockSpec((tile, width), lambda i: (steps - 1 - i, 0))
-    whole = lambda v: pl.BlockSpec(v.shape, lambda i: (0, 0))
+    block = pl.BlockSpec((tile, width), lambda i, m: ((steps - 1 - i) ^ m[0], 0))
+    right = pl.BlockSpec((tile, width), lambda i, m: ((steps - 1 - i) ^ m[0], 1))
+    whole = lambda v: pl.BlockSpec(v.shape, lambda i, m: (0, 0))
     return pl.pallas_call(
         rec_bwd_kernel,
-        grid=(steps,),
-        in_specs=[block] * 7 + [pl.BlockSpec((tile, 8), lambda i: (steps - 1 - i, 0)), whole(vec), whole(wt)],
-        out_specs=[
-            block,
-            block,
-            pl.BlockSpec((width, 2 * width), lambda i: (0, 0)),
-            pl.BlockSpec((64, width), lambda i: (0, 0)),
-        ],
+        grid_spec=pltpu.PrefetchScalarGridSpec(
+            num_scalar_prefetch=1,
+            grid=(steps,),
+            in_specs=[block, right, block, block, block, block, block, whole(vec), whole(wt)],
+            out_specs=[
+                pl.BlockSpec((tile, 2 * width), lambda i, m: ((steps - 1 - i) ^ m[0], 0)),
+                pl.BlockSpec((width, 2 * width), lambda i, m: (0, 0)),
+                pl.BlockSpec((64, width), lambda i, m: (0, 0)),
+            ],
+            scratch_shapes=[
+                pltpu.VMEM((tile + 8, width), F32),
+                pltpu.VMEM((tile, 2 * width), BF16),
+                pltpu.VMEM((8, width), F32),
+            ],
+        ),
         out_shape=[
-            jax.ShapeDtypeStruct((total, width), BF16),
-            jax.ShapeDtypeStruct((total, width), BF16),
+            jax.ShapeDtypeStruct((total, 2 * width), BF16),
             jax.ShapeDtypeStruct((width, 2 * width), F32),
             jax.ShapeDtypeStruct((64, width), F32),
-        ],
-        scratch_shapes=[
-            pltpu.VMEM((tile + 8, width), F32),
-            pltpu.VMEM((tile, 2 * width), BF16),
-            pltpu.VMEM((8, width), F32),
         ],
         compiler_params=pltpu.CompilerParams(vmem_limit_bytes=32 << 20),
         cost_estimate=pl.CostEstimate(
             flops=180 * total * width + 8 * total * width * width,
             transcendentals=6 * total * width,
-            bytes_accessed=28 * total * width,
+            bytes_accessed=30 * total * width,
         ),
         name="recurrence_backward",
-    )(dm, yb, sp, pa, px, xc, xb, mask, vec, wt)
-
-
-def place_masks(lens_row, total, taps):
-    start, same = seq_masks(lens_row, 0, total, taps)
-    cols = [start.astype(F32)] + [same[k] for k in range(1, taps)]
-    cols += [jnp.pad(same[k][k:], (0, k)) for k in range(1, taps)]
-    return jnp.pad(jnp.stack(cols, axis=1), ((0, 0), (0, 8 - len(cols))))
+    )(meta, dm, xy, sp, pa, px, xc, xy, vec, wt)
 
 
 def dot32(one, two):
@@ -662,12 +700,8 @@
     return scale * dv - scale * scale * scale * v * jnp.mean(dv * v, axis=-1, keepdims=True)
 
 
-REC_TP = ("y", "x", "c")
-REC_COLS = (("y", "x", "zh"), ("zl", "c"))
-REC_W = ("zh", "zl")
-FF_A, FF_B = "x", "y"
-FF_TP = ("y", "x", "c")
-FF_W = ("zh", "zl")
+PLANE = ("y", "x", "c")
+STACK = ("zh", "zl")
 
 
 def tensor_parallel(
@@ -675,7 +709,6 @@
     w_out, norm2_gain, w_gate, w_up, w_down, cot,
 ):
     rows, model = layer_input.shape
-    total = 8 * rows
     taps = conv_w.shape[1]
     width = w_rgate.shape[1]
     part = w_out.shape[0]
@@ -683,42 +716,35 @@
     padded = -(-channels // 128) * 128
     extra = padded - channels
     blocks = channels // width
+    units = w_down.shape[0]
     core = lax.axis_index("c")
     me = (lax.axis_index("y") * 2 + lax.axis_index("x")) * 2 + core
-
-    def in_order(pieces):
-        out = jnp.zeros((8,) + pieces[0].shape, pieces[0].dtype)
-        for k, piece in enumerate(pieces):
-            out = lax.dynamic_update_slice(out, piece[None], (me ^ k, 0, 0))
-        return out.reshape(total, -1)
-
-    def rows_of(v, k):
-        return lax.dynamic_slice(v, ((me ^ k) * rows, 0), (rows, v.shape[1]))
+    meta = jnp.concatenate([me.astype(jnp.int32)[None], lengths[0].astype(jnp.int32)])
+
+    def tile_of(v, k):
+        return v[k * rows : (k + 1) * rows]
 
     gain1 = norm1_gain.astype(F32)[:, None]
     gain2 = norm2_gain.astype(F32)[:, None]
-
+    rec_plan = tuple(
+        tuple((((2 * (t % 2) + z) * 4 + t // 2) * width, width) for z in range(2)) for t in range(8)
+    )
+    ff_plan = tuple(tuple(((f * 8 + t) * units, units) for f in range(4)) for t in range(8))
+
+    wxy = exchange(pack_columns(rec_plan, padded, w_x, w_y, gain1), PLANE)
     xf = layer_input.astype(F32)
     scale1 = lax.rsqrt(jnp.mean(xf * xf, axis=-1, keepdims=True) + NORM_EPS)
     xs = (xf * scale1).astype(BF16)
-
-    def columns_in(w, gain, cols, tp, over):
-        scaled = (w.astype(F32) * gain).astype(BF16)
-        mine = exchange(to_columns(scaled, *cols), tp)
-        return w_gather(mine.reshape(-1, mine.shape[2]), *over).reshape(model, -1)
-
-    def columns_out(grad, cols, tp, over):
-        mine = w_scatter(grad.astype(BF16).reshape(2, 2, model // 4, -1), *over).astype(BF16)
-        return from_columns(exchange(mine.reshape(8, -1, mine.shape[1]), tp), *cols).astype(F32)
-
-    wx = jnp.pad(columns_in(w_x, gain1, REC_COLS, REC_TP, REC_W), ((0, 0), (0, extra)))
-    xs_all = in_order(act_gather(xs, "x", "y"))
-    wy = jnp.pad(columns_in(w_y, gain1, REC_COLS, REC_TP, REC_W), ((0, 0), (0, extra)))
+    wd = lax.all_gather(w_down, STACK, axis=0, tiled=True)
+    xs_all = jnp.concatenate(act_gather(xs, "x", "y"), axis=0)
+    wxy, packed_gu = lax.optimization_barrier((wxy, pack_columns(ff_plan, 4 * units, w_gate, w_up, gain2)))
+    wxy = w_gather(wxy.reshape(-1, 2 * padded), *STACK).reshape(model, -1)
+    wgu = lax.all_gather(exchange(packed_gu, PLANE).reshape(-1, 8 * units), STACK, axis=0, tiled=True)
 
     small = [conv_w, conv_b[:, None], b_rgate[:, None], b_igate[:, None], lam[:, None], w_rgate, w_igate]
     small_width = sum(v.shape[1] for v in small)
     packed = jnp.pad(jnp.concatenate([w_out] + small, axis=1), ((0, 0), (0, -small_width % 128)))
-    halves = w_gather(packed, *REC_W)
+    halves = w_gather(packed, *STACK)
     mine = lax.dynamic_slice(halves, (core, 0, 0, 0), (1,) + halves.shape[1:])[0]
     theirs = swap(lax.dynamic_slice(halves, (1 - core, 0, 0, 0), (1,) + halves.shape[1:])[0], "c")
     whole = jnp.zeros((2, 2) + packed.shape, BF16)
@@ -735,56 +761,41 @@
         for n in range(blocks):
             block = whole[n * width : (n + 1) * width, at + g * width : at + (g + 1) * width]
             gates = gates.at[n * width : (n + 1) * width, g * padded + n * width : g * padded + (n + 1) * width].set(block)
-    mask = place_masks(lengths[0], total, taps)
-
-    xb = dot32(xs_all, wx).astype(BF16)
-    yb = dot32(xs_all, wy)
-    xc, pa, px, before, mixed = rec_forward(xb, yb, mask, vec, gates)
-
-    resid = xf + act_scatter(lambda k: dot32(rows_of(mixed, k), wo).astype(BF16), "x", "y")
+
+    xy = dot32(xs_all, wxy)
+    xc, pa, px, before, mixed = rec_forward(meta, xy, vec, gates, rows)
+
+    resid = xf + act_scatter(lambda k: dot32(tile_of(mixed, k), wo).astype(BF16), "x", "y")
     scale2 = lax.rsqrt(jnp.mean(resid * resid, axis=-1, keepdims=True) + NORM_EPS)
     xs2 = (resid * scale2).astype(BF16)
-
-    wg = columns_in(w_gate, gain2, (FF_TP, FF_W), FF_TP, FF_W)
-    wu = columns_in(w_up, gain2, (FF_TP, FF_W), FF_TP, FF_W)
-    wd = w_gather(w_down, *FF_W).reshape(-1, model)
-    cot_all = jnp.concatenate(act_gather(cot, FF_A, FF_B), axis=0)
-    xs2_all = jnp.concatenate(act_gather(xs2, FF_A, FF_B), axis=0)
-    gt = dot32(xs2_all, wg)
-    up = dot32(xs2_all, wu)
+    xs2_all = jnp.concatenate(act_gather(xs2, "x", "y"), axis=0)
+    late_cot = lax.optimization_barrier((cot, mixed))[0]
+    cot_all = jnp.concatenate(act_gather(late_cot, "x", "y"), axis=0)
+    half = 4 * units
+    gu = dot32(xs2_all, wgu)
+    gt, up = gu[:, :half], gu[:, half:]
     act, slope = gelu_both(gt)
     hidden = (act * up).astype(BF16)
-
-    def tile_of(v, k):
-        return v[k * rows : (k + 1) * rows]
-
-    output = (resid + act_scatter(lambda k: dot32(tile_of(hidden, k), wd).astype(BF16), FF_A, FF_B)).astype(BF16)
-
     d_hidden = back_product(cot_all, wd)
-    d_gt = (d_hidden * up * slope).astype(BF16)
-    d_up = (d_hidden * act).astype(BF16)
-    d_un2 = act_scatter(
-        lambda k: (back_product(tile_of(d_gt, k), wg) + back_product(tile_of(d_up, k), wu)).astype(BF16), FF_A, FF_B
-    )
-    d_wd = w_scatter(row_contract(hidden, cot_all).astype(BF16).reshape(2, 2, -1, model), *FF_W)
-    d_wg = columns_out(row_contract(xs2_all, d_gt), (FF_TP, FF_W), FF_TP, FF_W)
-    d_wu = columns_out(row_contract(xs2_all, d_up), (FF_TP, FF_W), FF_TP, FF_W)
-    d_gain2 = jnp.sum(w_gate.astype(F32) * d_wg + w_up.astype(F32) * d_wu, axis=1)
-
+    d_gu = jnp.concatenate([(d_hidden * up * slope).astype(BF16), (d_hidden * act).astype(BF16)], axis=1)
+    d_un2 = act_scatter(lambda k: back_product(tile_of(d_gu, k), wgu).astype(BF16), "x", "y")
     d_resid = cot.astype(F32) + norm_back(d_un2, resid, scale2)
     d_mix = d_resid.astype(BF16)
-    d_mix_all = in_order(act_gather(d_mix, "x", "y"))
+    d_mix_all = jnp.concatenate(act_gather(d_mix, "x", "y"), axis=0)
+
+    d_wd = lax.psum_scatter(row_contract(hidden, cot_all).astype(BF16), STACK, scatter_dimension=0, tiled=True)
+    d_wgu = lax.psum_scatter(row_contract(xs2_all, d_gu).astype(BF16), STACK, scatter_dimension=0, tiled=True)
+    d_wg, d_wu, d_gain2 = unpack_columns(ff_plan, exchange(d_wgu.reshape(8, -1, 2 * half), PLANE), w_gate, w_up, gain2)
+
+    late_hidden = lax.optimization_barrier((hidden, d_mix_all))[0]
+    output = (resid + act_scatter(lambda k: dot32(tile_of(late_hidden, k), wd).astype(BF16), "x", "y")).astype(BF16)
+
     dm = back_product(d_mix_all, wo)
-    dxb, dyb, d_gates, sums = rec_backward(dm, yb, before, pa, px, xc, xb, mask, vec, gates.T)
-    d_un = act_scatter(
-        lambda k: (back_product(rows_of(dxb, k), wx) + back_product(rows_of(dyb, k), wy)).astype(BF16), "x", "y"
-    )
+    dxy, d_gates, sums = rec_backward(meta, dm, xy, before, pa, px, xc, vec, gates.T, rows)
+    d_un = act_scatter(lambda k: back_product(tile_of(dxy, k), wxy).astype(BF16), "x", "y")
     d_input = (d_resid + norm_back(d_un, xf, scale1)).astype(BF16)
-
-    d_wo = row_contract(mixed, d_mix_all)[:channels]
-    d_wx = columns_out(row_contract(xs_all, dxb)[:, :channels], REC_COLS, REC_TP, REC_W)
-    d_wy = columns_out(row_contract(xs_all, dyb)[:, :channels], REC_COLS, REC_TP, REC_W)
-    d_gain1 = jnp.sum(w_x.astype(F32) * d_wx + w_y.astype(F32) * d_wy, axis=1)
+    d_wxy = w_scatter(row_contract(xs_all, dxy).astype(BF16).reshape(2, 2, model // 4, -1), *STACK).astype(BF16)
+    d_wx, d_wy, d_gain1 = unpack_columns(rec_plan, exchange(d_wxy.reshape(8, -1, 2 * padded), PLANE), w_x, w_y, gain1)
 
     def channels_out(v, kind):
         v = v.astype(kind).reshape(2, 2, part, -1)
@@ -795,7 +806,7 @@
         out = lax.dynamic_update_slice(out, keep[None], (core, 0, 0, 0))
         return lax.dynamic_update_slice(out, swap(send, "c")[None], (1 - core, 0, 0, 0))
 
-    d_wo = w_scatter(channels_out(d_wo, BF16), *REC_W)
+    d_wo = w_scatter(channels_out(row_contract(mixed, d_mix_all)[:channels], BF16), *STACK)
     sums = jnp.sum(sums.reshape(8, 8, padded), axis=1)
     d_lam_part = -jax.nn.sigmoid(-lam_all) * sums[5]
     d_cols = jnp.concatenate([sums[:5], sums[6:8], d_lam_part[None]], axis=0).T
@@ -808,12 +819,12 @@
             block = jnp.where(row_block == n, d_gates[:channels, at : at + width], block)
         d_blocks.append(block)
     d_small = jnp.concatenate([d_cols[:channels]] + d_blocks, axis=1)
-    d_small = lax.psum_scatter(channels_out(d_small, F32).reshape(4 * part, -1), REC_W, scatter_dimension=0, tiled=True)
+    d_small = lax.psum_scatter(channels_out(d_small, F32).reshape(4 * part, -1), STACK, scatter_dimension=0, tiled=True)
     d_cw, d_cb, d_br, d_bi, d_lam = d_small[:, :4], d_small[:, 4], d_small[:, 5], d_small[:, 6], d_small[:, 7]
     d_wr, d_wi = d_small[:, 8 : 8 + width], d_small[:, 8 + width : 8 + 2 * width]
     return (
-        output, d_input, d_gain1, gain1 * d_wx, gain1 * d_wy, d_cw, d_cb, d_wr, d_br, d_wi, d_bi, d_lam, d_wo,
-        d_gain2, gain2 * d_wg, gain2 * d_wu, d_wd,
+        output, d_input, d_gain1[:, 0], d_wx, d_wy, d_cw, d_cb, d_wr, d_br, d_wi, d_bi, d_lam, d_wo,
+        d_gain2[:, 0], d_wg, d_wu, d_wd.astype(F32),
     )
 
 

time: 1000 us -> 876 us (0.88)
  local copies, waits for them, and re-layouts: 209 us -> 98.3 us
  waiting for transfers between devices: 318 us -> 390 us
  matrix products: 240 us -> 173 us
  starting transfers between devices: 109 us -> 78 us
  Pallas kernels: 52.5 us -> 66.5 us
    ppermute x103 -> x79, waiting for transfers between devices: 310 us -> 359 us  [swap(): return lax.ppermute(v, name, [(0, 1), (1, 0)])]
    convert_element_type x15 -> x0, local copies, waits for them, and re-layouts: 42.4 us -> none  [the longest x12 40.6 us: columns_out(): from_columns(exchange(mine.reshape(8, -1, mine.shape[1]), tp), *cols)]
    dot_general x20 -> x18, matrix products: 92.5 us -> 51.7 us  [dot32(): return jnp.dot(one, two, preferred_element_type=F32)]
    reshape x14 -> x0, local copies, waits for them, and re-layouts: 29.3 us -> none  [the longest x8 12.1 us: to_columns(): v = w.reshape((rows,) + (2,) * 5 + (cols // 32,))]
    all_to_all x8 -> x4, waiting for transfers between devices: 7.63 us -> 31.3 us  [exchange(): return lax.all_to_all(v, tp, split_axis=0, concat_axis=0, tiled=True)]
    dot_general x34 -> x18, matrix products: 98.1 us -> 76.3 us  [back_product(): lax.dot_general(grad, weight, (((1,), (1,)), ((), ())), preferred_element...]
    all_to_all x8 -> x4, starting transfers between devices: 32.8 us -> 15.2 us  [exchange(): return lax.all_to_all(v, tp, split_axis=0, concat_axis=0, tiled=True)]
    dynamic_update_slice x14 -> x0, local copies, waits for them, and re-layouts: 15.8 us -> none  [in_order(): out = lax.dynamic_update_slice(out, piece[None], (me ^ k, 0, 0))]
  transfers between devices with their start and end apart: 112 -> 88, of which waited for: 41 -> 31; matrix products, arithmetic and copies ran while one was open for 35% -> 32% of each run, Pallas kernels for 2% -> 6%
where the time goes in v2:
time: 876 us; the launch traced here: 870 us
  waiting for transfers between devices  390 us (45%)
  matrix products  173 us (20%)
  local copies, waits for them, and re-layouts  98.3 us (11%)
  starting transfers between devices  78 us (9%)
  Pallas kernels  66.5 us (8%)
  other arithmetic  47.8 us (5%)
  between operations  15.7 us (2%)
    ppermute x79, waiting for transfers between devices, swap(): return lax.ppermute(v, name, [(0, 1), (1, 0)])  359 us
    dot_general x18, matrix products, back_product(): lax.dot_general(grad, weight, (((1,), (1,)), ((), ())), preferred_element...  76.3 us
    ppermute x79, starting transfers between devices, swap(): return lax.ppermute(v, name, [(0, 1), (1, 0)])  61.8 us
    dot_general x18, matrix products, dot32(): return jnp.dot(one, two, preferred_element_type=F32)  51.7 us
    dot_general x4, matrix products, row_contract(): lax.dot_general(left, right, (((0,), (0,)), ((), ())), preferred_element_...  45.2 us
    unnamed x167, local copies, waits for them, and re-layouts  45 us
    all_to_all x4, waiting for transfers between devices, exchange(): return lax.all_to_all(v, tp, split_axis=0, concat_axis=0, tiled=True)  31.3 us
    pallas_call x1, Pallas kernels, rec_backward(): pl.pallas_call(rec_bwd_kernel, grid_spec=pltpu.PrefetchScalarGridSpec(num...  28.4 us
  transfers between devices with their start and end apart: 88, of which 31 were waited for; matrix products, arithmetic and copies ran while one was open for 32% of the time, Pallas kernels for 6%

profile of v2, /device:TPU:0, one launch (start us, length us, event | category | flops | bytes accessed | tf_op | source)
XLA Modules:
  0.0 869.7 jit_solution(5854704697187670245)
XLA Ops:
  13.2 4.0 collective-permute-start.11
  27.0 4.2 all-to-all-start
  38.2 19.9 %all-to-all-done = bf16[8,64,768]{2,1,0:T(8,128)(2,1)} async-done(((bf16[8,64,768]{2,1,0:T(8,128)(2,1)}), bf16[8,64,768]{2,1,0:T(8,128)(2,1)}, u32[]{:S(2)}, u32[]{:S(2)}) %all-to-all-start) | async-done | bytes 786464 | tf_op jit(solution)/shard_map/all_to_all | solution.py:436
  81.2 12.7 %collective-permute-done.8 = bf16[512,768]{1,0:T(8,128)(2,1)} collective-permute-done((bf16[512,768]{1,0:T(8,128)(2,1)}, bf16[512,768]{1,0:T(8,128)(2,1)}, u32[]{:S(2)}, u32[]{:S(2)}) %collective-permute-start.8) | collective-permute-done | bytes 786464 | tf_op jit(solution)/shard_map/ppermute | solution.py:338
  96.0 6.9 collective-permute-done.9
  106.1 3.7 copy.60
  131.7 23.0 %collective-permute-done.10 = bf16[512,768]{1,0:T(8,128)(2,1)} collective-permute-done((bf16[512,768]{1,0:T(8,128)(2,1)}, bf16[512,768]{1,0:T(8,128)(2,1)}, u32[]{:S(2)}, u32[]{:S(2)}) %collective-permute-start.10) | collective-permute-done | bytes 786464 | tf_op jit(solution)/shard_map/ppermute | solution.py:338
  157.8 10.0 %fusion.126.xb_ref.yb_ref = f32[2048,768]{1,0:T(8,128)S(1)} fusion(bf16[2048,2048]{1,0:T(8,128)(2,1)} %constant_dynamic-update-slice_fusion, bf16[2048,768]{1,0:T(8,128)(2,1)} %bitcast.9), kind=kOutput, calls=%fused_computation.289 | convolution fusion | flops 6442450944 | bytes 17825792 | tf_op jit(solution)/shard_map/dot_general | solution.py:696
  167.9 18.4 %recurrence_forward.1 = (bf16[2048,384]{1,0:T(8,128)(2,1)S(1)}, f32[2048,384]{1,0:T(8,128)S(1)}, f32[2048,384]{1,0:T(8,128)S(1)}, f32[2048,384]{1,0:T(8,128)S(1)}, bf16[2048,384]{1,0:T(8,128)(2,1)S(1)}) custom-call(s32[5]{0:T(128)S(1)} %pad_add_fusion.meta_ref, f32[2048,768]{1,0:T(8,128)S(1)} %fusion.126.xb_ref.yb_ref, ...), custom_call_target="tpu_custom_call" | custom-call | flops 1286602752 | bytes 18874368 | tf_op jit(solution)/shard_map/recurrence_forward/pallas_call | solution.py:637
  190.4 6.4 collective-permute-start.32
  204.7 28.4 %collective-permute-done.18 = bf16[128,2048]{1,0:T(8,128)(2,1)S(1)} collective-permute-done((bf16[128,2048]{1,0:T(8,128)(2,1)S(1)}, bf16[128,2048]{1,0:T(8,128)(2,1)S(1)}, u32[]{:S(2)}, u32[]{:S(2)}) %collective-permute-start.18) | collective-permute-done | bytes 524320 | tf_op jit(solution)/shard_map/ppermute | solution.py:338
  234.7 11.2 %collective-permute-done.21 = bf16[128,2048]{1,0:T(8,128)(2,1)S(1)} collective-permute-done((bf16[128,2048]{1,0:T(8,128)(2,1)S(1)}, bf16[128,2048]{1,0:T(8,128)(2,1)S(1)}, u32[]{:S(2)}, u32[]{:S(2)}) %collective-permute-start.21) | collective-permute-done | bytes 524320 | tf_op jit(solution)/shard_map/ppermute | solution.py:338
  259.5 12.8 %collective-permute-done.19 = bf16[256,2048]{1,0:T(8,128)(2,1)} collective-permute-done((bf16[256,2048]{1,0:T(8,128)(2,1)}, bf16[256,2048]{1,0:T(8,128)(2,1)}, u32[]{:S(2)}, u32[]{:S(2)}) %collective-permute-start.19) | collective-permute-done | bytes 1048608 | tf_op jit(solution)/shard_map/ppermute | solution.py:338
  285.4 17.4 %collective-permute-done.24 = bf16[256,2048]{1,0:T(8,128)(2,1)S(1)} collective-permute-done((bf16[256,2048]{1,0:T(8,128)(2,1)S(1)}, bf16[256,2048]{1,0:T(8,128)(2,1)S(1)}, u32[]{:S(2)}, u32[]{:S(2)}) %collective-permute-start.24) | collective-permute-done | bytes 1048608 | tf_op jit(solution)/shard_map/ppermute | solution.py:338
  304.5 3.9 collective-permute-done.26
  312.6 6.6 collective-permute-done.28
  327.9 19.0 %fusion.127 = f32[2048,1536]{0,1:T(8,128)} fusion(bf16[2048,2048]{1,0:T(8,128)(2,1)} %constant_dynamic-update-slice_fusion.9, bf16[2048,1536]{1,0:T(8,128)(2,1)} %all-gather.3.cloned.1.call-done), kind=kOutput, calls=%fused_computation.290 | convolution fusion | flops 12884901888 | bytes 27262976 | tf_op jit(solution)/shard_map/dot_general | solution.py:696
  347.0 19.4 %multiply_convert_fusion = (bf16[2048,768]{0,1:T(8,128)(2,1)S(1)}, bf16[2048,768]{0,1:T(8,128)(2,1)S(1)}, bf16[2048,768]{0,1:T(8,128)(2,1)}) fusion(f32[2048,1536]{0,1:T(8,128)} %fusion.127, bf16[2048,2048]{1,0:T(8,128)(2,1)} %copy-done.54, bf16[768,2048]{1,0:T(8,128)(2,1)} %all-gather.5.cloned.1.call-done), kind=kOutput, calls=%fused_computation.27 | convolution fusion | flops 6481772544 | bytes 33554432 | tf_op jit(solution)/shard_map/dot_general | solution.py:64
  385.2 7.4 collective-permute-done.42
  397.5 10.3 %convolution_convert_fusion.1 = bf16[768,2048]{1,0:T(8,128)(2,1)} fusion(bf16[2048,768]{0,1:T(8,128)(2,1)S(1)} %copy-done.57, bf16[2048,2048]{1,0:T(8,128)(2,1)} %copy-done.54), kind=kOutput, calls=%fused_computation.36 | convolution fusion | flops 6444023808 | bytes 14680064 | tf_op jit(solution)/shard_map/dot_general | solution.py:58
  407.9 11.0 %collective-permute-done.43 = bf16[256,2048]{1,0:T(8,128)(2,1)} collective-permute-done((bf16[256,2048]{1,0:T(8,128)(2,1)}, bf16[256,2048]{1,0:T(8,128)(2,1)}, u32[]{:S(2)}, u32[]{:S(2)}) %collective-permute-start.43) | collective-permute-done | bytes 1048608 | tf_op jit(solution)/shard_map/ppermute | solution.py:338
  421.3 6.2 multiply_reduce_fusion
  427.6 4.5 constant_dynamic-update-slice_fusion.35
  434.1 21.6 %collective-permute-done.48 = bf16[256,2048]{1,0:T(8,128)(2,1)S(1)} collective-permute-done((bf16[256,2048]{1,0:T(8,128)(2,1)S(1)}, bf16[256,2048]{1,0:T(8,128)(2,1)S(1)}, u32[]{:S(2)}, u32[]{:S(2)}) %collective-permute-start.48) | collective-permute-done | bytes 1048608 | tf_op jit(solution)/shard_map/ppermute | solution.py:338
  458.0 12.1 %collective-permute-done.52 = bf16[128,2048]{1,0:T(8,128)(2,1)S(1)} collective-permute-done((bf16[128,2048]{1,0:T(8,128)(2,1)S(1)}, bf16[128,2048]{1,0:T(8,128)(2,1)S(1)}, u32[]{:S(2)}, u32[]{:S(2)}) %collective-permute-start.52) | collective-permute-done | bytes 524320 | tf_op jit(solution)/shard_map/ppermute | solution.py:338
  473.8 4.5 fusion.116.dm_ref
  481.0 28.4 %recurrence_backward.1 = (bf16[2048,768]{1,0:T(8,128)(2,1)S(1)}, f32[384,768]{1,0:T(8,128)S(1)}, f32[64,384]{1,0:T(8,128)S(1)}) custom-call(s32[5]{0:T(128)S(1)} %pad_add_fusion.meta_ref, f32[2048,384]{1,0:T(8,128)S(1)} %fusion.116.dm_ref, f32[2048,768]{1,0:T(8,128)} %copy-done, f32[2048,384]{1,0:T(8,128)S(1)} %copy-done.6, f32[2048,384]{1,0:T(8,128)S(1)} %copy-done.2, ...), custom_call_target="tpu_custom_call" | custom-call | flops 2557476864 | bytes 23592960 | tf_op jit(solution)/shard_map/recurrence_backward/pallas_call | solution.py:663
  515.2 18.4 %convolution_convert_fusion = bf16[2048,1536]{1,0:T(8,128)(2,1)} fusion(bf16[2048,2048]{1,0:T(8,128)(2,1)} %constant_dynamic-update-slice_fusion.9, bf16[2048,768]{0,1:T(8,128)(2,1)S(1)} %copy-done.27, bf16[2048,768]{0,1:T(8,128)(2,1)} %copy-done.28), kind=kOutput, calls=%fused_computation.19 | convolution fusion | flops 12900630528 | bytes 20971520 | tf_op jit(solution)/shard_map/dot_general | solution.py:58
  535.0 6.9 fusion.128
  543.9 9.6 %convolution_convert_fusion.2 = bf16[2048,768]{1,0:T(8,128)(2,1)S(1)} fusion(bf16[2048,2048]{1,0:T(8,128)(2,1)} %constant_dynamic-update-slice_fusion, bf16[2048,768]{1,0:T(8,128)(2,1)S(1)} %copy-done.24), kind=kOutput, calls=%fused_computation.37 | convolution fusion | flops 6444023808 | bytes 14680064 | tf_op jit(solution)/shard_map/dot_general | solution.py:58
  556.7 3.9 convolution_convert_fusion.25
  560.6 3.9 convolution_convert_fusion.23
  565.0 4.2 convolution_convert_fusion.21
  569.2 4.1 convolution_convert_fusion.19
  584.9 17.1 %collective-permute-done.72 = bf16[512,768]{1,0:T(8,128)(2,1)S(1)} collective-permute-done((bf16[512,768]{1,0:T(8,128)(2,1)S(1)}, bf16[512,768]{1,0:T(8,128)(2,1)S(1)}, u32[]{:S(2)}, u32[]{:S(2)}) %collective-permute-start.72) | collective-permute-done | bytes 786464 | tf_op jit(solution)/shard_map/ppermute | solution.py:338
  603.1 80.3 %collective-permute-done.77 = bf16[80,2048]{1,0:T(8,128)(2,1)S(1)} collective-permute-done((bf16[80,2048]{1,0:T(8,128)(2,1)S(1)}, bf16[80,2048]{1,0:T(8,128)(2,1)S(1)}, u32[]{:S(2)}, u32[]{:S(2)}) %collective-permute-start.77) | collective-permute-done | bytes 327712 | tf_op jit(solution)/shard_map/ppermute | solution.py:338
  717.4 36.4 %collective-permute-done.78 = bf16[80,2048]{1,0:T(8,128)(2,1)S(1)} collective-permute-done((bf16[80,2048]{1,0:T(8,128)(2,1)S(1)}, bf16[80,2048]{1,0:T(8,128)(2,1)S(1)}, u32[]{:S(2)}, u32[]{:S(2)}) %collective-permute-start.78) | collective-permute-done | bytes 327712 | tf_op jit(solution)/shard_map/ppermute | solution.py:338
  776.4 7.8 collective-permute-done.58
  787.2 4.7 collective-permute-done.61
  795.0 6.4 unpack_columns.2
  802.2 12.3 %collective-permute-done.67 = bf16[256,2048]{1,0:T(8,128)(2,1)} collective-permute-done((bf16[256,2048]{1,0:T(8,128)(2,1)}, bf16[256,2048]{1,0:T(8,128)(2,1)}, u32[]{:S(2)}, u32[]{:S(2)}) %collective-permute-start.67) | collective-permute-done | bytes 1048608 | tf_op jit(solution)/shard_map/ppermute | solution.py:338
  814.5 5.5 fusion.39
  820.1 3.8 all-to-all-start.3
  823.9 3.9 fusion.38
  827.8 9.2 %collective-permute-done.59 = bf16[256,2048]{1,0:T(8,128)(2,1)} collective-permute-done((bf16[256,2048]{1,0:T(8,128)(2,1)}, bf16[256,2048]{1,0:T(8,128)(2,1)}, u32[]{:S(2)}, u32[]{:S(2)}) %collective-permute-start.59) | collective-permute-done | bytes 1048608 | tf_op jit(solution)/shard_map/ppermute | solution.py:338
  837.0 3.7 add_convert_fusion
  840.7 11.4 %all-to-all-done.3.grad_ref = bf16[8,64,1536]{2,1,0:T(8,128)(2,1)S(1)} async-done(((bf16[8,64,1536]{2,1,0:T(8,128)(2,1)}), bf16[8,64,1536]{2,1,0:T(8,128)(2,1)S(1)}, u32[]{:S(2)}, u32[]{:S(2)}) %all-to-all-start.3) | async-done | bytes 1572896 | tf_op jit(solution)/shard_map/all_to_all | solution.py:436
  852.1 10.3 %unpack_columns.3 = (f32[64,6144]{1,0:T(8,128)}, f32[64,6144]{1,0:T(8,128)}, f32[64,1]{1,0:T(8,128)S(1)}) custom-call(bf16[8,64,1536]{2,1,0:T(8,128)(2,1)S(1)} %all-to-all-done.3.grad_ref, bf16[64,6144]{1,0:T(8,128)(2,1)S(1)} %copy-done.8, bf16[64,6144]{1,0:T(8,128)(2,1)S(1)} %copy-done.10, f32[64,1]{1,0:T(8,128)S(1)} %copy-done.20), custom_call_target="tpu_custom_call" | custom-call | flops 3145728 | bytes 6291456 | tf_op jit(solution)/shard_map/unpack_columns/pallas_call | solution.py:426
  (473 shorter events, 256.5 us)
Async XLA Ops:
  22.6 52.3 %collective-permute-start = (bf16[256,2048]{1,0:T(8,128)(2,1)}, bf16[256,2048]{1,0:T(8,128)(2,1)}, u32[]{:S(2)}, u32[]{:S(2)}) collective-permute-start(bf16[256,2048]{1,0:T(8,128)(2,1)} %get-tuple-element.147), channel_id=1, source_target_pairs={{0,1},{1,0},{2,3},{3,2},{4,5},{5,4},{6,7},{7,6},{8,9},{9,8},{10,11... | collective-permute-start | bytes 3145736 | tf_op jit(solution)/shard_map/ppermute | solution.py:338
  22.6 46.2 %collective-permute-start.1 = (bf16[256,2048]{1,0:T(8,128)(2,1)}, bf16[256,2048]{1,0:T(8,128)(2,1)}, u32[]{:S(2)}, u32[]{:S(2)}) collective-permute-start(bf16[256,2048]{1,0:T(8,128)(2,1)} %get-tuple-element.147), channel_id=1, source_target_pairs={{0,2},{2,0},{1,3},{3,1},{4,6},{6,4},{5,7},{7,5},{8,10},{10,8},{9,1... | collective-permute-start | bytes 3145736 | tf_op jit(solution)/shard_map/ppermute | solution.py:338
  24.1 47.1 %collective-permute-start.3 = (bf16[256,2048]{1,0:T(8,128)(2,1)}, bf16[256,2048]{1,0:T(8,128)(2,1)}, u32[]{:S(2)}, u32[]{:S(2)}) collective-permute-start(bf16[256,2048]{1,0:T(8,128)(2,1)} %get-tuple-element.147), channel_id=1, source_target_pairs={{0,4},{4,0},{1,5},{5,1},{2,6},{6,2},{3,7},{7,3},{8,12},{12,8},{9,1... | collective-permute-start | bytes 3145736 | tf_op jit(solution)/shard_map/ppermute | solution.py:338
  27.0 31.1 %all-to-all-start = ((bf16[8,64,768]{2,1,0:T(8,128)(2,1)}), bf16[8,64,768]{2,1,0:T(8,128)(2,1)}, u32[]{:S(2)}, u32[]{:S(2)}) async-start(bf16[8,64,768]{2,1,0:T(8,128)(2,1)} %pack_columns.2), calls=%async_computation | async-start | bytes 1572864 | tf_op jit(solution)/shard_map/all_to_all | solution.py:436
  35.6 30.5 %collective-permute-start.13 = (bf16[80,2432]{1,0:T(8,128)(2,1)}, bf16[80,2432]{1,0:T(8,128)(2,1)}, u32[]{:S(2)}, u32[]{:S(2)}) collective-permute-start(bf16[80,2432]{1,0:T(8,128)(2,1)} %collective-permute-done.11), channel_id=1, source_target_pairs={{0,8},{8,0},{1,9},{9,1},{2,10},{10,2},{3,11},{11,3},{4,12},{12,4},... | collective-permute-start | bytes 1167368 | tf_op jit(solution)/shard_map/ppermute | solution.py:338
  58.1 35.8 %collective-permute-start.8 = (bf16[512,768]{1,0:T(8,128)(2,1)}, bf16[512,768]{1,0:T(8,128)(2,1)}, u32[]{:S(2)}, u32[]{:S(2)}) collective-permute-start(bf16[512,768]{1,0:T(8,128)(2,1)} %bitcast.5), channel_id=1, source_target_pairs={{0,16},{16,0},{1,17},{17,1},{2,18},{18,2},{3,19},{19,3},{4,20},{20... | collective-permute-start | bytes 2359304 | tf_op jit(solution)/shard_map/ppermute | solution.py:338
  58.4 45.4 %all-to-all-start.1 = ((bf16[8,64,1536]{2,1,0:T(8,128)(2,1)}), bf16[8,64,1536]{2,1,0:T(8,128)(2,1)S(1)}, u32[]{:S(2)}, u32[]{:S(2)}) async-start(bf16[8,64,1536]{2,1,0:T(8,128)(2,1)} %pack_columns.3), calls=%async_computation.1 | async-start | bytes 3145728 | tf_op jit(solution)/shard_map/all_to_all | solution.py:436
  62.0 265.9 %all-gather.3.cloned.1.call-start = ((), (), s32[]{:S(2)}) async-start(), calls=%async_computation.7 | async-start | bytes 7864320 | tf_op jit(solution)/shard_map/all_gather | solution.py:742
  66.1 36.8 %collective-permute-start.9 = (bf16[512,768]{1,0:T(8,128)(2,1)}, bf16[512,768]{1,0:T(8,128)(2,1)S(1)}, u32[]{:S(2)}, u32[]{:S(2)}) collective-permute-start(bf16[512,768]{1,0:T(8,128)(2,1)} %bitcast.5), channel_id=1, source_target_pairs={{0,8},{8,0},{1,9},{9,1},{2,10},{10,2},{3,11},{11,3},{4,12},{12,4},... | collective-permute-start | bytes 2359304 | tf_op jit(solution)/shard_map/ppermute | solution.py:338
  68.8 36.3 %collective-permute-start.14 = (bf16[2,80,2432]{2,1,0:T(8,128)(2,1)}, bf16[2,80,2432]{2,1,0:T(8,128)(2,1)S(1)}, u32[]{:S(2)}, u32[]{:S(2)}) collective-permute-start(bf16[2,80,2432]{2,1,0:T(8,128)(2,1)} %dynamic-slice_bitcast_fusion.2), channel_id=1, source_target_pairs={{0,1},{1,0},{2,3},{3,2},{4,5},{5,4},{6,7},{7,6},{8,9},{9,8},{10,11... | collective-permute-start | bytes 2334728 | tf_op jit(solution)/shard_map/ppermute | solution.py:338
  71.2 48.5 %collective-permute-start.5 = (bf16[128,2048]{1,0:T(8,128)(2,1)}, bf16[128,2048]{1,0:T(8,128)(2,1)S(1)}, u32[]{:S(2)}, u32[]{:S(2)}) collective-permute-start(bf16[128,2048]{1,0:T(8,128)(2,1)} %slice.461), channel_id=1, source_target_pairs={{0,4},{4,0},{1,5},{5,1},{2,6},{6,2},{3,7},{7,3},{8,12},{12,8},{9,1... | collective-permute-start | bytes 1572872 | tf_op jit(solution)/shard_map/ppermute | solution.py:338
  74.9 44.7 %collective-permute-start.6 = (bf16[128,2048]{1,0:T(8,128)(2,1)}, bf16[128,2048]{1,0:T(8,128)(2,1)}, u32[]{:S(2)}, u32[]{:S(2)}) collective-permute-start(bf16[128,2048]{1,0:T(8,128)(2,1)} %slice.462), channel_id=1, source_target_pairs={{0,2},{2,0},{1,3},{3,1},{4,6},{6,4},{5,7},{7,5},{8,10},{10,8},{9,1... | collective-permute-start | bytes 1572872 | tf_op jit(solution)/shard_map/ppermute | solution.py:338
  93.9 28.0 %collective-permute-start.2 = (bf16[256,2048]{1,0:T(8,128)(2,1)}, bf16[256,2048]{1,0:T(8,128)(2,1)}, u32[]{:S(2)}, u32[]{:S(2)}) collective-permute-start(bf16[256,2048]{1,0:T(8,128)(2,1)} %collective-permute-done.1), channel_id=1, source_target_pairs={{0,1},{1,0},{2,3},{3,2},{4,5},{5,4},{6,7},{7,6},{8,9},{9,8},{10,11... | collective-permute-start | bytes 3145736 | tf_op jit(solution)/shard_map/ppermute | solution.py:338
  105.0 241.9 %all-gather.5.cloned.1.call-start = ((), (), s32[]{:S(2)}) async-start(), calls=%async_computation.8 | async-start | bytes 3932160 | tf_op jit(solution)/shard_map/all_gather | solution.py:738
  105.1 49.6 %collective-permute-start.10 = (bf16[512,768]{1,0:T(8,128)(2,1)}, bf16[512,768]{1,0:T(8,128)(2,1)}, u32[]{:S(2)}, u32[]{:S(2)}) collective-permute-start(bf16[512,768]{1,0:T(8,128)(2,1)} %collective-permute-done.8), channel_id=1, source_target_pairs={{0,8},{8,0},{1,9},{9,1},{2,10},{10,2},{3,11},{11,3},{4,12},{12,4},... | collective-permute-start | bytes 2359304 | tf_op jit(solution)/shard_map/ppermute | solution.py:338
  121.4 35.4 %collective-permute-start.7 = (bf16[256,2048]{1,0:T(8,128)(2,1)S(1)}, bf16[256,2048]{1,0:T(8,128)(2,1)S(1)}, u32[]{:S(2)}, u32[]{:S(2)}) collective-permute-start(bf16[256,2048]{1,0:T(8,128)(2,1)S(1)} %pad_maximum_fusion.2), channel_id=1, source_target_pairs={{0,1},{1,0},{2,3},{3,2},{4,5},{5,4},{6,7},{7,6},{8,9},{9,8},{10,11... | collective-permute-start | bytes 3145736 | tf_op jit(solution)/shard_map/ppermute | solution.py:338
  189.9 65.4 %collective-permute-start.31 = (bf16[256,2048]{1,0:T(8,128)(2,1)}, bf16[256,2048]{1,0:T(8,128)(2,1)}, u32[]{:S(2)}, u32[]{:S(2)}) collective-permute-start(bf16[256,2048]{1,0:T(8,128)(2,1)} %param.43), channel_id=1, source_target_pairs={{0,1},{1,0},{2,3},{3,2},{4,5},{5,4},{6,7},{7,6},{8,9},{9,8},{10,11... | collective-permute-start | bytes 3145736 | tf_op jit(solution)/shard_map/ppermute | solution.py:338
  190.4 57.3 %collective-permute-start.32 = (bf16[256,2048]{1,0:T(8,128)(2,1)}, bf16[256,2048]{1,0:T(8,128)(2,1)}, u32[]{:S(2)}, u32[]{:S(2)}) collective-permute-start(bf16[256,2048]{1,0:T(8,128)(2,1)} %param.43), channel_id=1, source_target_pairs={{0,2},{2,0},{1,3},{3,1},{4,6},{6,4},{5,7},{7,5},{8,10},{10,8},{9,1... | collective-permute-start | bytes 3145736 | tf_op jit(solution)/shard_map/ppermute | solution.py:338
  196.8 56.8 %collective-permute-start.34 = (bf16[256,2048]{1,0:T(8,128)(2,1)}, bf16[256,2048]{1,0:T(8,128)(2,1)}, u32[]{:S(2)}, u32[]{:S(2)}) collective-permute-start(bf16[256,2048]{1,0:T(8,128)(2,1)} %param.43), channel_id=1, source_target_pairs={{0,4},{4,0},{1,5},{5,1},{2,6},{6,2},{3,7},{7,3},{8,12},{12,8},{9,1... | collective-permute-start | bytes 3145736 | tf_op jit(solution)/shard_map/ppermute | solution.py:338
  202.1 31.0 %collective-permute-start.18 = (bf16[128,2048]{1,0:T(8,128)(2,1)S(1)}, bf16[128,2048]{1,0:T(8,128)(2,1)S(1)}, u32[]{:S(2)}, u32[]{:S(2)}) collective-permute-start(bf16[128,2048]{1,0:T(8,128)(2,1)S(1)} %get-tuple-element.167), channel_id=1, source_target_pairs={{0,4},{4,0},{1,5},{5,1},{2,6},{6,2},{3,7},{7,3},{8,12},{12,8},{9,1... | collective-permute-start | bytes 1572872 | tf_op jit(solution)/shard_map/ppermute | solution.py:338
  203.5 55.9 %collective-permute-start.15 = (bf16[256,2048]{1,0:T(8,128)(2,1)S(1)}, bf16[256,2048]{1,0:T(8,128)(2,1)}, u32[]{:S(2)}, u32[]{:S(2)}) collective-permute-start(bf16[256,2048]{1,0:T(8,128)(2,1)S(1)} %convolution_convert_fusion.9), channel_id=1, source_target_pairs={{0,1},{1,0},{2,3},{3,2},{4,5},{5,4},{6,7},{7,6},{8,9},{9,8},{10,11... | collective-permute-start | bytes 3145736 | tf_op jit(solution)/shard_map/ppermute | solution.py:338
  245.8 26.4 %collective-permute-start.19 = (bf16[256,2048]{1,0:T(8,128)(2,1)}, bf16[256,2048]{1,0:T(8,128)(2,1)}, u32[]{:S(2)}, u32[]{:S(2)}) collective-permute-start(bf16[256,2048]{1,0:T(8,128)(2,1)} %pad_maximum_fusion.3), channel_id=1, source_target_pairs={{0,2},{2,0},{1,3},{3,1},{4,6},{6,4},{5,7},{7,5},{8,10},{10,8},{9,1... | collective-permute-start | bytes 3145736 | tf_op jit(solution)/shard_map/ppermute | solution.py:338
  247.7 26.4 %collective-permute-start.22 = (bf16[256,2048]{1,0:T(8,128)(2,1)}, bf16[256,2048]{1,0:T(8,128)(2,1)}, u32[]{:S(2)}, u32[]{:S(2)}) collective-permute-start(bf16[256,2048]{1,0:T(8,128)(2,1)} %pad_maximum_fusion.4), channel_id=1, source_target_pairs={{0,4},{4,0},{1,5},{5,1},{2,6},{6,2},{3,7},{7,3},{8,12},{12,8},{9,1... | collective-permute-start | bytes 3145736 | tf_op jit(solution)/shard_map/ppermute | solution.py:338
  249.1 434.3 %reduce-scatter.8.cloned.1.call-start = ((), (), s32[]{:S(2)}) async-start(), calls=%async_computation.11 | async-start | bytes 3932160 | tf_op jit(solution)/shard_map/reduce_scatter | solution.py:786
  253.6 28.7 %collective-permute-start.36 = (bf16[128,2048]{1,0:T(8,128)(2,1)S(1)}, bf16[128,2048]{1,0:T(8,128)(2,1)S(1)}, u32[]{:S(2)}, u32[]{:S(2)}) collective-permute-start(bf16[128,2048]{1,0:T(8,128)(2,1)S(1)} %slice.480), channel_id=1, source_target_pairs={{0,4},{4,0},{1,5},{5,1},{2,6},{6,2},{3,7},{7,3},{8,12},{12,8},{9,1... | collective-permute-start | bytes 1572872 | tf_op jit(solution)/shard_map/ppermute | solution.py:338
  255.3 26.9 %collective-permute-start.37 = (bf16[128,2048]{1,0:T(8,128)(2,1)S(1)}, bf16[128,2048]{1,0:T(8,128)(2,1)S(1)}, u32[]{:S(2)}, u32[]{:S(2)}) collective-permute-start(bf16[128,2048]{1,0:T(8,128)(2,1)S(1)} %slice.481), channel_id=1, source_target_pairs={{0,2},{2,0},{1,3},{3,1},{4,6},{6,4},{5,7},{7,5},{8,10},{10,8},{9,1... | collective-permute-start | bytes 1572872 | tf_op jit(solution)/shard_map/ppermute | solution.py:338
  282.3 27.3 %collective-permute-start.38 = (bf16[256,2048]{1,0:T(8,128)(2,1)S(1)}, bf16[256,2048]{1,0:T(8,128)(2,1)S(1)}, u32[]{:S(2)}, u32[]{:S(2)}) collective-permute-start(bf16[256,2048]{1,0:T(8,128)(2,1)S(1)} %pad_maximum_fusion.6), channel_id=1, source_target_pairs={{0,1},{1,0},{2,3},{3,2},{4,5},{5,4},{6,7},{7,6},{8,9},{9,8},{10,11... | collective-permute-start | bytes 3145736 | tf_op jit(solution)/shard_map/ppermute | solution.py:338
  282.4 26.0 %collective-permute-start.26 = (bf16[256,2048]{1,0:T(8,128)(2,1)S(1)}, bf16[256,2048]{1,0:T(8,128)(2,1)S(1)}, u32[]{:S(2)}, u32[]{:S(2)}) collective-permute-start(bf16[256,2048]{1,0:T(8,128)(2,1)S(1)} %get-tuple-element.143), channel_id=1, source_target_pairs={{0,4},{4,0},{1,5},{5,1},{2,6},{6,2},{3,7},{7,3},{8,12},{12,8},{9,1... | collective-permute-start | bytes 3145736 | tf_op jit(solution)/shard_map/ppermute | solution.py:338
  283.7 26.1 %collective-permute-start.23 = (bf16[256,2048]{1,0:T(8,128)(2,1)S(1)}, bf16[256,2048]{1,0:T(8,128)(2,1)S(1)}, u32[]{:S(2)}, u32[]{:S(2)}) collective-permute-start(bf16[256,2048]{1,0:T(8,128)(2,1)S(1)} %get-tuple-element.143), channel_id=1, source_target_pairs={{0,1},{1,0},{2,3},{3,2},{4,5},{5,4},{6,7},{7,6},{8,9},{9,8},{10,11... | collective-permute-start | bytes 3145736 | tf_op jit(solution)/shard_map/ppermute | solution.py:338
  369.4 38.5 %collective-permute-start.39 = (bf16[256,2048]{1,0:T(8,128)(2,1)}, bf16[256,2048]{1,0:T(8,128)(2,1)}, u32[]{:S(2)}, u32[]{:S(2)}) collective-permute-start(bf16[256,2048]{1,0:T(8,128)(2,1)} %convolution_convert_fusion.17), channel_id=1, source_target_pairs={{0,1},{1,0},{2,3},{3,2},{4,5},{5,4},{6,7},{7,6},{8,9},{9,8},{10,11... | collective-permute-start | bytes 3145736 | tf_op jit(solution)/shard_map/ppermute | solution.py:338
  407.8 304.6 %reduce-scatter.4.cloned.1.call-start = ((), (), s32[]{:S(2)}) async-start(), calls=%async_computation.9 | async-start | bytes 614400 | tf_op jit(solution)/shard_map/reduce_scatter | solution.py:822
  515.0 305.1 %reduce-scatter.6.cloned.1.call-start = ((), (), s32[]{:S(2)}) async-start(), calls=%async_computation.10 | async-start | bytes 7864320 | tf_op jit(solution)/shard_map/reduce_scatter | solution.py:787
  542.1 39.8 %collective-permute-start.75 = (bf16[2,80,2048]{2,1,0:T(8,128)(2,1)S(1)}, bf16[2,80,2048]{2,1,0:T(8,128)(2,1)S(1)}, u32[]{:S(2)}, u32[]{:S(2)}) collective-permute-start(bf16[2,80,2048]{2,1,0:T(8,128)(2,1)S(1)} %dynamic-slice_bitcast_fusion.3), channel_id=1, source_target_pairs={{0,1},{1,0},{2,3},{3,2},{4,5},{5,4},{6,7},{7,6},{8,9},{9,8},{10,11... | collective-permute-start | bytes 1966088 | tf_op jit(solution)/shard_map/ppermute | solution.py:338
  554.6 47.3 %collective-permute-start.72 = (bf16[512,768]{1,0:T(8,128)(2,1)S(1)}, bf16[512,768]{1,0:T(8,128)(2,1)S(1)}, u32[]{:S(2)}, u32[]{:S(2)}) collective-permute-start(bf16[512,768]{1,0:T(8,128)(2,1)S(1)} %get-tuple-element.152), channel_id=1, source_target_pairs={{0,8},{8,0},{1,9},{9,1},{2,10},{10,2},{3,11},{11,3},{4,12},{12,4},... | collective-permute-start | bytes 2359304 | tf_op jit(solution)/shard_map/ppermute | solution.py:338
  554.6 202.8 %collective-permute-start.71 = (bf16[512,768]{1,0:T(8,128)(2,1)}, bf16[512,768]{1,0:T(8,128)(2,1)}, u32[]{:S(2)}, u32[]{:S(2)}) collective-permute-start(bf16[512,768]{1,0:T(8,128)(2,1)} %get-tuple-element.151), channel_id=1, source_target_pairs={{0,8},{8,0},{1,9},{9,1},{2,10},{10,2},{3,11},{11,3},{4,12},{12,4},... | collective-permute-start | bytes 2359304 | tf_op jit(solution)/shard_map/ppermute | solution.py:338
  560.6 241.4 %collective-permute-start.63 = (bf16[256,2048]{1,0:T(8,128)(2,1)}, bf16[256,2048]{1,0:T(8,128)(2,1)}, u32[]{:S(2)}, u32[]{:S(2)}) collective-permute-start(bf16[256,2048]{1,0:T(8,128)(2,1)} %convolution_convert_fusion.25), channel_id=1, source_target_pairs={{0,1},{1,0},{2,3},{3,2},{4,5},{5,4},{6,7},{7,6},{8,9},{9,8},{10,11... | collective-permute-start | bytes 3145736 | tf_op jit(solution)/shard_map/ppermute | solution.py:338
  564.5 121.4 %collective-permute-start.64 = (bf16[256,2048]{1,0:T(8,128)(2,1)}, bf16[256,2048]{1,0:T(8,128)(2,1)}, u32[]{:S(2)}, u32[]{:S(2)}) collective-permute-start(bf16[256,2048]{1,0:T(8,128)(2,1)} %convolution_convert_fusion.23), channel_id=1, source_target_pairs={{0,1},{1,0},{2,3},{3,2},{4,5},{5,4},{6,7},{7,6},{8,9},{9,8},{10,11... | collective-permute-start | bytes 3145736 | tf_op jit(solution)/shard_map/ppermute | solution.py:338
  582.9 100.5 %collective-permute-start.77 = (bf16[80,2048]{1,0:T(8,128)(2,1)S(1)}, bf16[80,2048]{1,0:T(8,128)(2,1)S(1)}, u32[]{:S(2)}, u32[]{:S(2)}) collective-permute-start(bf16[80,2048]{1,0:T(8,128)(2,1)S(1)} %get-tuple-element.158), channel_id=1, source_target_pairs={{0,8},{8,0},{1,9},{9,1},{2,10},{10,2},{3,11},{11,3},{4,12},{12,4},... | collective-permute-start | bytes 983048 | tf_op jit(solution)/shard_map/ppermute | solution.py:338
  602.0 89.5 %collective-permute-start.68 = (bf16[256,2048]{1,0:T(8,128)(2,1)}, bf16[256,2048]{1,0:T(8,128)(2,1)}, u32[]{:S(2)}, u32[]{:S(2)}) collective-permute-start(bf16[256,2048]{1,0:T(8,128)(2,1)} %convolution_convert_fusion.19), channel_id=1, source_target_pairs={{0,1},{1,0},{2,3},{3,2},{4,5},{5,4},{6,7},{7,6},{8,9},{9,8},{10,11... | collective-permute-start | bytes 3145736 | tf_op jit(solution)/shard_map/ppermute | solution.py:338
  702.0 57.0 %collective-permute-start.73 = (bf16[512,768]{1,0:T(8,128)(2,1)}, bf16[512,768]{1,0:T(8,128)(2,1)}, u32[]{:S(2)}, u32[]{:S(2)}) collective-permute-start(bf16[512,768]{1,0:T(8,128)(2,1)} %fusion.40), channel_id=1, source_target_pairs={{0,16},{16,0},{1,17},{17,1},{2,18},{18,2},{3,19},{19,3},{4,20},{20... | collective-permute-start | bytes 2359304 | tf_op jit(solution)/shard_map/ppermute | solution.py:338
  705.3 48.4 %collective-permute-start.78 = (bf16[80,2048]{1,0:T(8,128)(2,1)S(1)}, bf16[80,2048]{1,0:T(8,128)(2,1)S(1)}, u32[]{:S(2)}, u32[]{:S(2)}) collective-permute-start(bf16[80,2048]{1,0:T(8,128)(2,1)S(1)} %fusion.65), channel_id=1, source_target_pairs={{0,16},{16,0},{1,17},{17,1},{2,18},{18,2},{3,19},{19,3},{4,20},{20... | collective-permute-start | bytes 983048 | tf_op jit(solution)/shard_map/ppermute | solution.py:338
  717.3 110.4 %collective-permute-start.55 = (bf16[256,2048]{1,0:T(8,128)(2,1)}, bf16[256,2048]{1,0:T(8,128)(2,1)}, u32[]{:S(2)}, u32[]{:S(2)}) collective-permute-start(bf16[256,2048]{1,0:T(8,128)(2,1)} %convolution_convert_fusion.33), channel_id=1, source_target_pairs={{0,1},{1,0},{2,3},{3,2},{4,5},{5,4},{6,7},{7,6},{8,9},{9,8},{10,11... | collective-permute-start | bytes 3145736 | tf_op jit(solution)/shard_map/ppermute | solution.py:338
  762.3 32.7 %all-to-all-start.2 = ((bf16[8,64,768]{2,1,0:T(8,128)(2,1)}), bf16[8,64,768]{2,1,0:T(8,128)(2,1)S(1)}, u32[]{:S(2)}, u32[]{:S(2)}) async-start(bf16[8,64,768]{2,1,0:T(8,128)(2,1)} %bitcast.34), calls=%async_computation.2 | async-start | bytes 1572864 | tf_op jit(solution)/shard_map/all_to_all | solution.py:436
  773.0 41.5 %collective-permute-start.67 = (bf16[256,2048]{1,0:T(8,128)(2,1)}, bf16[256,2048]{1,0:T(8,128)(2,1)}, u32[]{:S(2)}, u32[]{:S(2)}) collective-permute-start(bf16[256,2048]{1,0:T(8,128)(2,1)} %pad_maximum_fusion.12), channel_id=1, source_target_pairs={{0,2},{2,0},{1,3},{3,1},{4,6},{6,4},{5,7},{7,5},{8,10},{10,8},{9,1... | collective-permute-start | bytes 3145736 | tf_op jit(solution)/shard_map/ppermute | solution.py:338
  784.3 30.3 %collective-permute-start.70 = (bf16[256,2048]{1,0:T(8,128)(2,1)}, bf16[256,2048]{1,0:T(8,128)(2,1)}, u32[]{:S(2)}, u32[]{:S(2)}) collective-permute-start(bf16[256,2048]{1,0:T(8,128)(2,1)} %pad_maximum_fusion.13), channel_id=1, source_target_pairs={{0,4},{4,0},{1,5},{5,1},{2,6},{6,2},{3,7},{7,3},{8,12},{12,8},{9,1... | collective-permute-start | bytes 3145736 | tf_op jit(solution)/shard_map/ppermute | solution.py:338
  791.9 45.0 %collective-permute-start.59 = (bf16[256,2048]{1,0:T(8,128)(2,1)}, bf16[256,2048]{1,0:T(8,128)(2,1)}, u32[]{:S(2)}, u32[]{:S(2)}) collective-permute-start(bf16[256,2048]{1,0:T(8,128)(2,1)} %pad_maximum_fusion.10), channel_id=1, source_target_pairs={{0,2},{2,0},{1,3},{3,1},{4,6},{6,4},{5,7},{7,5},{8,10},{10,8},{9,1... | collective-permute-start | bytes 3145736 | tf_op jit(solution)/shard_map/ppermute | solution.py:338
  802.0 35.0 %collective-permute-start.62 = (bf16[256,2048]{1,0:T(8,128)(2,1)}, bf16[256,2048]{1,0:T(8,128)(2,1)}, u32[]{:S(2)}, u32[]{:S(2)}) collective-permute-start(bf16[256,2048]{1,0:T(8,128)(2,1)} %pad_maximum_fusion.11), channel_id=1, source_target_pairs={{0,4},{4,0},{1,5},{5,1},{2,6},{6,2},{3,7},{7,3},{8,12},{12,8},{9,1... | collective-permute-start | bytes 3145736 | tf_op jit(solution)/shard_map/ppermute | solution.py:338
  820.1 32.0 %all-to-all-start.3 = ((bf16[8,64,1536]{2,1,0:T(8,128)(2,1)}), bf16[8,64,1536]{2,1,0:T(8,128)(2,1)S(1)}, u32[]{:S(2)}, u32[]{:S(2)}) async-start(bf16[8,64,1536]{2,1,0:T(8,128)(2,1)} %bitcast.139), calls=%async_computation.5 | async-start | bytes 3145728 | tf_op jit(solution)/shard_map/all_to_all | solution.py:436
  (111 other events, 1657.1 us)
Sparse Core Ops, SparseCore 0:
  105.1 121.6 all-gather.2
  249.3 60.7 all-gather.4
  407.9 58.0 reduce-scatter.7
  515.1 19.1 reduce-scatter.3
  536.5 149.8 reduce-scatter.5

commit v3 on v2

--- a/solution.py
+++ b/solution.py
@@ -696,12 +696,105 @@
     return jnp.dot(one, two, preferred_element_type=F32)
 
 
+def columns_of(width, most):
+    return next(n for n in range(min(width, most), 0, -128) if width % n == 0)
+
+
+def store_blocks(step, value_ref, outs, rows):
+    per = value_ref.shape[0] // rows
+    for n, out in enumerate(outs):
+
+        @pl.when(step == n // per)
+        def _(n=n, out=out):
+            out[...] = value_ref[(n % per) * rows : (n % per + 1) * rows, :]
+
+
+def blocks_kernel(flip, a_ref, w_ref, *rest):
+    outs, value = rest[:-1], rest[-1]
+    model = outs[0].shape[1]
+    wide = columns_of(model, 512)
+    a = a_ref[...]
+    for at in range(0, model, wide):
+        if flip:
+            part = back_product(a, w_ref[at : at + wide, :])
+        else:
+            part = dot32(a, w_ref[:, at : at + wide])
+        value[:, at : at + wide] = part.astype(BF16)
+    store_blocks(pl.program_id(0), value, outs, outs[0].shape[0])
+
+
+def product_blocks(a, w, flip):
+    total, deep = a.shape
+    model = w.shape[0] if flip else w.shape[1]
+    tile, rows = total // 4, total // 8
+    return pl.pallas_call(
+        functools.partial(blocks_kernel, flip),
+        grid=(4,),
+        in_specs=[pl.BlockSpec((tile, deep), lambda i: (i, 0)), pl.BlockSpec(w.shape, lambda i: (0, 0))],
+        out_specs=[pl.BlockSpec((rows, model), lambda i: (0, 0))] * 8,
+        out_shape=[jax.ShapeDtypeStruct((rows, model), BF16)] * 8,
+        scratch_shapes=[pltpu.VMEM((tile, model), BF16)],
+        compiler_params=pltpu.CompilerParams(vmem_limit_bytes=44 << 20),
+        cost_estimate=pl.CostEstimate(
+            flops=2 * total * deep * model,
+            transcendentals=0,
+            bytes_accessed=2 * (total * deep + w.size + total * model),
+        ),
+        name="product_blocks",
+    )(a, w)
+
+
+def ff_kernel(x_ref, cot_ref, wgu_ref, wd_ref, hidden_ref, dgu_ref, *rest):
+    outs, value = rest[:-1], rest[-1]
+    half, model = wd_ref.shape
+    narrow, wide = columns_of(half, 256), columns_of(model, 512)
+    x, cot = x_ref[...], cot_ref[...]
+    for at in range(0, half, narrow):
+        gt = dot32(x, wgu_ref[:, at : at + narrow])
+        up = dot32(x, wgu_ref[:, half + at : half + at + narrow])
+        dh = back_product(cot, wd_ref[at : at + narrow, :])
+        act, slope = gelu_both(gt)
+        hidden_ref[:, at : at + narrow] = (act * up).astype(BF16)
+        dgu_ref[:, at : at + narrow] = (dh * up * slope).astype(BF16)
+        dgu_ref[:, half + at : half + at + narrow] = (dh * act).astype(BF16)
+    grad = dgu_ref[...]
+    for at in range(0, model, wide):
+        value[:, at : at + wide] = back_product(grad, wgu_ref[at : at + wide, :]).astype(BF16)
+    store_blocks(pl.program_id(0), value, outs, outs[0].shape[0])
+
+
+def feed_forward(x, cot, wgu, wd):
+    total, model = x.shape
+    half = wd.shape[0]
+    tile, rows = total // 4, total // 8
+    at = lambda cols: pl.BlockSpec((tile, cols), lambda i: (i, 0))
+    whole = lambda v: pl.BlockSpec(v.shape, lambda i: (0, 0), pipeline_mode=pl.Buffered(1))
+    return pl.pallas_call(
+        ff_kernel,
+        grid=(4,),
+        in_specs=[at(model), at(model), whole(wgu), whole(wd)],
+        out_specs=[at(half), at(2 * half)] + [pl.BlockSpec((rows, model), lambda i: (0, 0))] * 8,
+        out_shape=[jax.ShapeDtypeStruct((total, half), BF16), jax.ShapeDtypeStruct((total, 2 * half), BF16)]
+        + [jax.ShapeDtypeStruct((rows, model), BF16)] * 8,
+        scratch_shapes=[pltpu.VMEM((tile, model), BF16)],
+        compiler_params=pltpu.CompilerParams(vmem_limit_bytes=52 << 20),
+        cost_estimate=pl.CostEstimate(
+            flops=10 * total * model * half,
+            transcendentals=total * half,
+            bytes_accessed=2 * (3 * total * model + 3 * half * model + 3 * total * half),
+        ),
+        name="feed_forward",
+    )(x, cot, wgu, wd)
+
+
 def norm_back(dv, v, scale):
     return scale * dv - scale * scale * scale * v * jnp.mean(dv * v, axis=-1, keepdims=True)
 
 
 PLANE = ("y", "x", "c")
 STACK = ("zh", "zl")
+UNITS = ("zl", "x", "c")
+SHARDS = ("zh", "y")
 
 
 def tensor_parallel(
@@ -721,25 +814,30 @@
     me = (lax.axis_index("y") * 2 + lax.axis_index("x")) * 2 + core
     meta = jnp.concatenate([me.astype(jnp.int32)[None], lengths[0].astype(jnp.int32)])
 
-    def tile_of(v, k):
-        return v[k * rows : (k + 1) * rows]
-
     gain1 = norm1_gain.astype(F32)[:, None]
     gain2 = norm2_gain.astype(F32)[:, None]
     rec_plan = tuple(
         tuple((((2 * (t % 2) + z) * 4 + t // 2) * width, width) for z in range(2)) for t in range(8)
     )
-    ff_plan = tuple(tuple(((f * 8 + t) * units, units) for f in range(4)) for t in range(8))
-
-    wxy = exchange(pack_columns(rec_plan, padded, w_x, w_y, gain1), PLANE)
-    xf = layer_input.astype(F32)
+    ff_plan = tuple(
+        tuple((((f // 2) * 16 + (t // 4) * 8 + (f % 2) * 4 + t % 4) * units, units) for f in range(4)) for t in range(8)
+    )
+
+    def shard_order(v):
+        return v.reshape(v.shape[0], 2, 2, 2, -1).swapaxes(2, 3).reshape(v.shape)
+
+    packed_xy = pack_columns(rec_plan, padded, w_x, w_y, gain1)
+    wd = lax.all_gather(w_down, SHARDS, axis=0, tiled=True)
+    late_input = lax.optimization_barrier((layer_input, packed_xy))[0]
+    wxy = exchange(packed_xy, PLANE)
+    xf = late_input.astype(F32)
     scale1 = lax.rsqrt(jnp.mean(xf * xf, axis=-1, keepdims=True) + NORM_EPS)
     xs = (xf * scale1).astype(BF16)
-    wd = lax.all_gather(w_down, STACK, axis=0, tiled=True)
     xs_all = jnp.concatenate(act_gather(xs, "x", "y"), axis=0)
     wxy, packed_gu = lax.optimization_barrier((wxy, pack_columns(ff_plan, 4 * units, w_gate, w_up, gain2)))
     wxy = w_gather(wxy.reshape(-1, 2 * padded), *STACK).reshape(model, -1)
-    wgu = lax.all_gather(exchange(packed_gu, PLANE).reshape(-1, 8 * units), STACK, axis=0, tiled=True)
+    packed_gu, wd = lax.optimization_barrier((exchange(packed_gu, UNITS), wd))
+    wgu = lax.all_gather(packed_gu.reshape(-1, 8 * units), SHARDS, axis=0, tiled=True)
 
     small = [conv_w, conv_b[:, None], b_rgate[:, None], b_igate[:, None], lam[:, None], w_rgate, w_igate]
     small_width = sum(v.shape[1] for v in small)
@@ -765,35 +863,32 @@
     xy = dot32(xs_all, wxy)
     xc, pa, px, before, mixed = rec_forward(meta, xy, vec, gates, rows)
 
-    resid = xf + act_scatter(lambda k: dot32(tile_of(mixed, k), wo).astype(BF16), "x", "y")
+    blocks_r = product_blocks(mixed, wo, False)
+    resid = xf + act_scatter(lambda k: blocks_r[k], "x", "y")
     scale2 = lax.rsqrt(jnp.mean(resid * resid, axis=-1, keepdims=True) + NORM_EPS)
-    xs2 = (resid * scale2).astype(BF16)
-    xs2_all = jnp.concatenate(act_gather(xs2, "x", "y"), axis=0)
-    late_cot = lax.optimization_barrier((cot, mixed))[0]
-    cot_all = jnp.concatenate(act_gather(late_cot, "x", "y"), axis=0)
-    half = 4 * units
-    gu = dot32(xs2_all, wgu)
-    gt, up = gu[:, :half], gu[:, half:]
-    act, slope = gelu_both(gt)
-    hidden = (act * up).astype(BF16)
-    d_hidden = back_product(cot_all, wd)
-    d_gu = jnp.concatenate([(d_hidden * up * slope).astype(BF16), (d_hidden * act).astype(BF16)], axis=1)
-    d_un2 = act_scatter(lambda k: back_product(tile_of(d_gu, k), wgu).astype(BF16), "x", "y")
+    xs2 = shard_order((resid * scale2).astype(BF16))
+    early_cot = lax.optimization_barrier((cot, xs_all))[0]
+    cot_all = jnp.concatenate(act_gather(early_cot, "x", "zl"), axis=0)
+    xs2_all = jnp.concatenate(act_gather(xs2, "x", "zl"), axis=0)
+    hidden, d_gu, *blocks_2 = feed_forward(xs2_all, cot_all, wgu, wd)
+    d_un2 = shard_order(act_scatter(lambda k: blocks_2[k], "x", "zl"))
     d_resid = cot.astype(F32) + norm_back(d_un2, resid, scale2)
-    d_mix = d_resid.astype(BF16)
+    d_wd = row_contract(hidden, cot_all).astype(BF16)
+    d_wgu = row_contract(xs2_all, d_gu).astype(BF16)
+    d_mix, d_wd, d_wgu = lax.optimization_barrier((d_resid.astype(BF16), d_wd, d_wgu))
+    d_wd = lax.psum_scatter(d_wd, SHARDS, scatter_dimension=0, tiled=True)
+    d_wgu = lax.psum_scatter(d_wgu, SHARDS, scatter_dimension=0, tiled=True)
+    d_wg, d_wu, d_gain2 = unpack_columns(ff_plan, exchange(d_wgu.reshape(8, -1, 8 * units), UNITS), w_gate, w_up, gain2)
+
     d_mix_all = jnp.concatenate(act_gather(d_mix, "x", "y"), axis=0)
-
-    d_wd = lax.psum_scatter(row_contract(hidden, cot_all).astype(BF16), STACK, scatter_dimension=0, tiled=True)
-    d_wgu = lax.psum_scatter(row_contract(xs2_all, d_gu).astype(BF16), STACK, scatter_dimension=0, tiled=True)
-    d_wg, d_wu, d_gain2 = unpack_columns(ff_plan, exchange(d_wgu.reshape(8, -1, 2 * half), PLANE), w_gate, w_up, gain2)
-
-    late_hidden = lax.optimization_barrier((hidden, d_mix_all))[0]
-    output = (resid + act_scatter(lambda k: dot32(tile_of(late_hidden, k), wd).astype(BF16), "x", "y")).astype(BF16)
-
     dm = back_product(d_mix_all, wo)
     dxy, d_gates, sums = rec_backward(meta, dm, xy, before, pa, px, xc, vec, gates.T, rows)
-    d_un = act_scatter(lambda k: back_product(tile_of(dxy, k), wxy).astype(BF16), "x", "y")
+    blocks_1 = product_blocks(dxy, wxy, True)
+    d_un = act_scatter(lambda k: blocks_1[k], "x", "y")
     d_input = (d_resid + norm_back(d_un, xf, scale1)).astype(BF16)
+    late_hidden = lax.optimization_barrier((hidden, blocks_1[0]))[0]
+    blocks_o = product_blocks(late_hidden, wd, False)
+    output = (resid + act_scatter(lambda k: blocks_o[k], "x", "zl")).astype(BF16)
     d_wxy = w_scatter(row_contract(xs_all, dxy).astype(BF16).reshape(2, 2, model // 4, -1), *STACK).astype(BF16)
     d_wx, d_wy, d_gain1 = unpack_columns(rec_plan, exchange(d_wxy.reshape(8, -1, 2 * padded), PLANE), w_x, w_y, gain1)
 

time: 876 us -> 912 us (1.041)
  matrix products: 173 us -> 59.6 us
  Pallas kernels: 66.5 us -> 145 us
  local copies, waits for them, and re-layouts: 98.3 us -> 122 us
  other arithmetic: 47.8 us -> 68 us
  waiting for transfers between devices: 390 us -> 409 us
  starting transfers between devices: 78 us -> 87.2 us
    pallas_call x0 -> x4, Pallas kernels: none -> 79 us  [the longest x1 48 us: feed_forward(): pl.pallas_call(ff_kernel, grid=(4,), in_specs=[at(model), at(model), whol...]
    dot_general x18 -> x1, matrix products: 76.3 us -> 4.52 us  [back_product(): lax.dot_general(grad, weight, (((1,), (1,)), ((), ())), preferred_element...]
    dot_general x18 -> x1, matrix products: 51.7 us -> 9.02 us  [dot32(): return jnp.dot(one, two, preferred_element_type=F32)]
    ppermute x79, waiting for transfers between devices: 359 us -> 400 us  [swap(): return lax.ppermute(v, name, [(0, 1), (1, 0)])]
    all_to_all x4, waiting for transfers between devices: 31.3 us -> 6.42 us  [exchange(): return lax.all_to_all(v, tp, split_axis=0, concat_axis=0, tiled=True)]
    unnamed x167 -> x201, local copies, waits for them, and re-layouts: 45 us -> 64 us
    reshape x0 -> x5, local copies, waits for them, and re-layouts: none -> 16 us  [shard_order(): return v.reshape(v.shape[0], 2, 2, 2, -1).swapaxes(2, 3).reshape(v.shape)]
    convert_element_type x10 -> x22, other arithmetic: 4.47 us -> 18.1 us  [add16(): return (one.astype(F32) + two.astype(F32)).astype(BF16)]
  transfers between devices with their start and end apart: 88 -> 88, of which waited for: 31 -> 32; matrix products, arithmetic and copies ran while one was open for 32% -> 21% of each run, Pallas kernels for 6% -> 6%
where the time goes in v3:
time: 912 us; the launch traced here: 907 us
  waiting for transfers between devices  409 us (45%)
  Pallas kernels  145 us (16%)
  local copies, waits for them, and re-layouts  122 us (13%)
  starting transfers between devices  87.2 us (10%)
  other arithmetic  68 us (7%)
  matrix products  59.6 us (7%)
  between operations  15.7 us (2%)
    ppermute x79, waiting for transfers between devices, swap(): return lax.ppermute(v, name, [(0, 1), (1, 0)])  400 us
    ppermute x79, starting transfers between devices, swap(): return lax.ppermute(v, name, [(0, 1), (1, 0)])  71.1 us
    unnamed x201, local copies, waits for them, and re-layouts  64 us
    pallas_call x1, Pallas kernels, feed_forward(): pl.pallas_call(ff_kernel, grid=(4,), in_specs=[at(model), at(model), whol...  48 us
    dot_general x4, matrix products, row_contract(): lax.dot_general(left, right, (((0,), (0,)), ((), ())), preferred_element_...  46.1 us
    pallas_call x3, Pallas kernels, product_blocks(): pl.pallas_call(functools.partial(blocks_kernel, flip), grid=(4,), in_spec...  31 us
    pallas_call x1, Pallas kernels, rec_backward(): pl.pallas_call(rec_bwd_kernel, grid_spec=pltpu.PrefetchScalarGridSpec(num...  28.4 us
    pallas_call x1, Pallas kernels, rec_forward(): pl.pallas_call(rec_fwd_kernel, grid_spec=pltpu.PrefetchScalarGridSpec(num...  18.4 us
  transfers between devices with their start and end apart: 88, of which 32 were waited for; matrix products, arithmetic and copies ran while one was open for 21% of the time, Pallas kernels for 6%

profile of v3, /device:TPU:0, one launch (start us, length us, event | category | flops | bytes accessed | tf_op | source)
XLA Modules:
  0.0 906.6 jit_solution(7228750636561023344)
XLA Ops:
  24.1 3.5 all-to-all-start
  31.8 8.6 collective-permute-done.11
  40.3 10.7 %collective-permute-start.13 = (bf16[80,2432]{1,0:T(8,128)(2,1)S(1)}, bf16[80,2432]{1,0:T(8,128)(2,1)S(1)}, u32[]{:S(2)}, u32[]{:S(2)}) collective-permute-start(bf16[80,2432]{1,0:T(8,128)(2,1)S(1)} %collective-permute-done.11), channel_id=1, source_target_pairs={{0,8},{8,0},{1,9},{9,1},{2,10},{10,2},{3,11},{11,3},{4,12},{12,4},... | collective-permute-start | bytes 1167368 | tf_op jit(solution)/shard_map/ppermute | solution.py:338
  52.2 6.4 all-to-all-done
  61.3 4.3 all-to-all-start.1
  80.3 47.2 %collective-permute-done.8 = bf16[512,768]{1,0:T(8,128)(2,1)} collective-permute-done((bf16[512,768]{1,0:T(8,128)(2,1)S(1)}, bf16[512,768]{1,0:T(8,128)(2,1)}, u32[]{:S(2)}, u32[]{:S(2)}) %collective-permute-start.8) | collective-permute-done | bytes 786464 | tf_op jit(solution)/shard_map/ppermute | solution.py:338
  128.7 4.7 collective-permute-done.9
  167.1 9.0 fusion.27.xb_ref.yb_ref
  176.1 18.4 %recurrence_forward.1 = (bf16[2048,384]{1,0:T(8,128)(2,1)S(1)}, f32[2048,384]{1,0:T(8,128)S(1)}, f32[2048,384]{1,0:T(8,128)S(1)}, f32[2048,384]{1,0:T(8,128)S(1)}, bf16[2048,384]{1,0:T(8,128)(2,1)S(1)}) custom-call(s32[5]{0:T(128)S(1)} %pad_add_fusion.meta_ref, f32[2048,768]{1,0:T(8,128)S(1)} %fusion.27.xb_ref.yb_ref, f32[2048,768]{1,0:T(8,128)S(1)} %fusion.27.xb_ref.yb_ref, ...), custom_call_target="tpu_custom_call" | custom-call | flops 1286602752 | bytes 18874368 | tf_op jit(solution)/shard_map/recurrence_forward/pallas_call | solution.py:637
  199.4 8.9 product_blocks.3
  224.7 22.3 %collective-permute-done.18 = bf16[128,2048]{1,0:T(8,128)(2,1)S(1)} collective-permute-done((bf16[128,2048]{1,0:T(8,128)(2,1)S(1)}, bf16[128,2048]{1,0:T(8,128)(2,1)S(1)}, u32[]{:S(2)}, u32[]{:S(2)}) %collective-permute-start.18) | collective-permute-done | bytes 524320 | tf_op jit(solution)/shard_map/ppermute | solution.py:338
  248.3 10.6 %collective-permute-done.21 = bf16[128,2048]{1,0:T(8,128)(2,1)S(1)} collective-permute-done((bf16[128,2048]{1,0:T(8,128)(2,1)S(1)}, bf16[128,2048]{1,0:T(8,128)(2,1)S(1)}, u32[]{:S(2)}, u32[]{:S(2)}) %collective-permute-start.21) | collective-permute-done | bytes 524320 | tf_op jit(solution)/shard_map/ppermute | solution.py:338
  271.4 9.4 %collective-permute-done.36 = bf16[128,2048]{1,0:T(8,128)(2,1)S(1)} collective-permute-done((bf16[128,2048]{1,0:T(8,128)(2,1)S(1)}, bf16[128,2048]{1,0:T(8,128)(2,1)S(1)}, u32[]{:S(2)}, u32[]{:S(2)}) %collective-permute-start.36) | collective-permute-done | bytes 524320 | tf_op jit(solution)/shard_map/ppermute | solution.py:338
  280.7 11.8 %collective-permute-done.37 = bf16[128,2048]{1,0:T(8,128)(2,1)S(1)} collective-permute-done((bf16[128,2048]{1,0:T(8,128)(2,1)S(1)}, bf16[128,2048]{1,0:T(8,128)(2,1)S(1)}, u32[]{:S(2)}, u32[]{:S(2)}) %collective-permute-start.37) | collective-permute-done | bytes 524320 | tf_op jit(solution)/shard_map/ppermute | solution.py:338
  294.1 6.8 collective-permute-done.22
  319.8 8.7 collective-permute-done.24
  329.8 30.5 %collective-permute-done.26 = bf16[256,2048]{1,0:T(8,128)(2,1)S(1)} collective-permute-done((bf16[256,2048]{1,0:T(8,128)(2,1)S(1)}, bf16[256,2048]{1,0:T(8,128)(2,1)S(1)}, u32[]{:S(2)}, u32[]{:S(2)}) %collective-permute-start.26) | collective-permute-done | bytes 1048608 | tf_op jit(solution)/shard_map/ppermute | solution.py:338
  366.4 5.0 collective-permute-done.28
  380.5 48.0 %feed_forward.1 = (bf16[2048,768]{1,0:T(8,128)(2,1)}, bf16[2048,1536]{1,0:T(8,128)(2,1)}, bf16[256,2048]{1,0:T(8,128)(2,1)S(1)}, bf16[256,2048]{1,0:T(8,128)(2,1...) custom-call(bf16[2048,2048]{1,0:T(8,128)(2,1)} %constant_dynamic-upd, ...), custom_call_target="tpu_custom_call" | custom-call | flops 32212254720 | bytes 44040192 | tf_op jit(solution)/shard_map/feed_forward/pallas_call | solution.py:772
  429.2 19.3 %convolution_convert_fusion = bf16[2048,1536]{1,0:T(8,128)(2,1)} fusion(bf16[2048,2048]{1,0:T(8,128)(2,1)} %constant_dynamic-update-slice_fusion.9.x_ref, bf16[2048,1536]{1,0:T(8,128)(2,1)} %get-tuple-element.147), kind=kOutput, calls=%fused_computation | convolution fusion | flops 12888047616 | bytes 20971520 | tf_op jit(solution)/shard_map/dot_general | solution.py:58
  454.9 10.6 %collective-permute-done.42 = bf16[128,2048]{1,0:T(8,128)(2,1)S(1)} collective-permute-done((bf16[128,2048]{1,0:T(8,128)(2,1)S(1)}, bf16[128,2048]{1,0:T(8,128)(2,1)S(1)}, u32[]{:S(2)}, u32[]{:S(2)}) %collective-permute-start.42) | collective-permute-done | bytes 524320 | tf_op jit(solution)/shard_map/ppermute | solution.py:338
  470.2 10.3 %convolution_convert_fusion.1 = bf16[768,2048]{1,0:T(8,128)(2,1)} fusion(bf16[2048,768]{1,0:T(8,128)(2,1)S(1)} %copy-done.83, bf16[2048,2048]{1,0:T(8,128)(2,1)} %constant_dynamic-update-slice_fusion.18.cot_ref), kind=kOutput, calls=%fused_computation.6 | convolution fusion | flops 6444023808 | bytes 14680064 | tf_op jit(solution)/shard_map/dot_general | solution.py:58
  480.5 11.2 %collective-permute-done.43 = bf16[256,2048]{1,0:T(8,128)(2,1)} collective-permute-done((bf16[256,2048]{1,0:T(8,128)(2,1)}, bf16[256,2048]{1,0:T(8,128)(2,1)}, u32[]{:S(2)}, u32[]{:S(2)}) %collective-permute-start.43) | collective-permute-done | bytes 1048608 | tf_op jit(solution)/shard_map/ppermute | solution.py:338
  494.1 3.7 convert_add_fusion.2
  497.8 4.0 reshape.279
  501.8 3.9 copy.77
  505.8 4.3 reshape.280
  519.1 21.2 %collective-permute-done.48 = bf16[256,2048]{1,0:T(8,128)(2,1)S(1)} collective-permute-done((bf16[256,2048]{1,0:T(8,128)(2,1)S(1)}, bf16[256,2048]{1,0:T(8,128)(2,1)S(1)}, u32[]{:S(2)}, u32[]{:S(2)}) %collective-permute-start.48) | collective-permute-done | bytes 1048608 | tf_op jit(solution)/shard_map/ppermute | solution.py:338
  543.5 11.3 %collective-permute-done.52 = bf16[128,2048]{1,0:T(8,128)(2,1)S(1)} collective-permute-done((bf16[128,2048]{1,0:T(8,128)(2,1)S(1)}, bf16[128,2048]{1,0:T(8,128)(2,1)S(1)}, u32[]{:S(2)}, u32[]{:S(2)}) %collective-permute-start.52) | collective-permute-done | bytes 524320 | tf_op jit(solution)/shard_map/ppermute | solution.py:338
  558.9 4.5 fusion.16.dm_ref
  565.7 28.4 %recurrence_backward.1 = (bf16[2048,768]{1,0:T(8,128)(2,1)S(1)}, f32[384,768]{1,0:T(8,128)S(1)}, f32[64,384]{1,0:T(8,128)S(1)}) custom-call(s32[5]{0:T(128)S(1)} %pad_add_fusion.meta_ref, f32[2048,384]{1,0:T(8,128)S(1)} %fusion.16.dm_ref, f32[2048,768]{1,0:T(8,128)} %copy-done, f32[2048,384]{1,0:T(8,128)S(1)} %copy-done.6, f32[2048,384]{1,0:T(8,128)S(1)} %copy-done.2, ...), custom_call_target="tpu_custom_call" | custom-call | flops 2557476864 | bytes 23592960 | tf_op jit(solution)/shard_map/recurrence_backward/pallas_call | solution.py:663
  603.3 7.0 fusion.28
  612.2 9.4 %convolution_convert_fusion.2 = bf16[2048,768]{1,0:T(8,128)(2,1)S(1)} fusion(bf16[2048,2048]{1,0:T(8,128)(2,1)} %constant_dynamic-update-slice_fusion, bf16[2048,768]{1,0:T(8,128)(2,1)S(1)} %copy-done.29), kind=kOutput, calls=%fused_computation.7 | convolution fusion | flops 6444023808 | bytes 14680064 | tf_op jit(solution)/shard_map/dot_general | solution.py:58
  625.0 11.1 %product_blocks.4 = (bf16[256,2048]{1,0:T(8,128)(2,1)S(1)}, bf16[256,2048]{1,0:T(8,128)(2,1)}, bf16[256,2048]{1,0:T(8,128)(2,1)S(1)}, bf16[256,2048]{1,0:T(8,128...) custom-call(bf16[2048,768]{1,0:T(8,128)(2,1)} %copy-done.28, ...), custom_call_target="tpu_custom_call" | custom-call | flops 6442450944 | bytes 14680064 | tf_op jit(solution)/shard_map/product_blocks/pallas_call | solution.py:730
  638.7 11.0 %product_blocks.5 = (bf16[256,2048]{1,0:T(8,128)(2,1)S(1)}, bf16[256,2048]{1,0:T(8,128)(2,1)}, bf16[256,2048]{1,0:T(8,128)(2,1)S(1)}, bf16[256,2048]{1,0:T(8,128...) custom-call(bf16[2048,768]{1,0:T(8,128)(2,1)} %get-tuple-element.155, ...), custom_call_target="tpu_custom_call" | custom-call | flops 6442450944 | bytes 14680064 | tf_op jit(solution)/shard_map/product_blocks/pallas_call | solution.py:730
  649.6 7.4 collective-permute-done.72
  659.3 41.0 %collective-permute-done.77 = bf16[80,2048]{1,0:T(8,128)(2,1)S(1)} collective-permute-done((bf16[80,2048]{1,0:T(8,128)(2,1)S(1)}, bf16[80,2048]{1,0:T(8,128)(2,1)S(1)}, u32[]{:S(2)}, u32[]{:S(2)}) %collective-permute-start.77) | collective-permute-done | bytes 327712 | tf_op jit(solution)/shard_map/ppermute | solution.py:338
  719.4 62.7 %collective-permute-done.73 = bf16[512,768]{1,0:T(8,128)(2,1)S(1)} collective-permute-done((bf16[512,768]{1,0:T(8,128)(2,1)}, bf16[512,768]{1,0:T(8,128)(2,1)S(1)}, u32[]{:S(2)}, u32[]{:S(2)}) %collective-permute-start.73) | collective-permute-done | bytes 786464 | tf_op jit(solution)/shard_map/ppermute | solution.py:338
  786.2 3.9 all-to-all-start.2
  792.7 4.6 collective-permute-done.69
  799.9 14.2 %collective-permute-done.58 = bf16[128,2048]{1,0:T(8,128)(2,1)S(1)} collective-permute-done((bf16[128,2048]{1,0:T(8,128)(2,1)}, bf16[128,2048]{1,0:T(8,128)(2,1)S(1)}, u32[]{:S(2)}, u32[]{:S(2)}) %collective-permute-start.58) | collective-permute-done | bytes 524320 | tf_op jit(solution)/shard_map/ppermute | solution.py:338
  820.5 3.6 all-to-all-start.3
  833.3 6.4 unpack_columns.2
  840.3 8.6 collective-permute-done.67
  853.5 25.1 %collective-permute-done.59 = bf16[256,2048]{1,0:T(8,128)(2,1)} collective-permute-done((bf16[256,2048]{1,0:T(8,128)(2,1)}, bf16[256,2048]{1,0:T(8,128)(2,1)}, u32[]{:S(2)}, u32[]{:S(2)}) %collective-permute-start.59) | collective-permute-done | bytes 1048608 | tf_op jit(solution)/shard_map/ppermute | solution.py:338
  878.6 3.8 add_convert_fusion.3
  882.5 3.8 fusion.5
  889.0 10.3 %unpack_columns.3 = (f32[64,6144]{1,0:T(8,128)}, f32[64,6144]{1,0:T(8,128)}, f32[64,1]{1,0:T(8,128)S(1)}) custom-call(bf16[8,64,1536]{2,1,0:T(8,128)(2,1)S(1)} %all-to-all-done.3.grad_ref, bf16[64,6144]{1,0:T(8,128)(2,1)S(1)} %copy-done.8, bf16[64,6144]{1,0:T(8,128)(2,1)S(1)} %copy-done.10, f32[64,1]{1,0:T(8,128)S(1)} %copy-done.25), custom_call_target="tpu_custom_call" | custom-call | flops 3145728 | bytes 6291456 | tf_op jit(solution)/shard_map/unpack_columns/pallas_call | solution.py:426
  (500 shorter events, 249.3 us)
Async XLA Ops:
  13.8 60.4 %collective-permute-start = (bf16[256,2048]{1,0:T(8,128)(2,1)}, bf16[256,2048]{1,0:T(8,128)(2,1)}, u32[]{:S(2)}, u32[]{:S(2)}) collective-permute-start(bf16[256,2048]{1,0:T(8,128)(2,1)} %get-tuple-element.224), channel_id=1, source_target_pairs={{0,1},{1,0},{2,3},{3,2},{4,5},{5,4},{6,7},{7,6},{8,9},{9,8},{10,11... | collective-permute-start | bytes 3145736 | tf_op jit(solution)/shard_map/ppermute | solution.py:338
  14.3 54.6 %collective-permute-start.1 = (bf16[256,2048]{1,0:T(8,128)(2,1)}, bf16[256,2048]{1,0:T(8,128)(2,1)}, u32[]{:S(2)}, u32[]{:S(2)}) collective-permute-start(bf16[256,2048]{1,0:T(8,128)(2,1)} %get-tuple-element.224), channel_id=1, source_target_pairs={{0,2},{2,0},{1,3},{3,1},{4,6},{6,4},{5,7},{7,5},{8,10},{10,8},{9,1... | collective-permute-start | bytes 3145736 | tf_op jit(solution)/shard_map/ppermute | solution.py:338
  16.9 54.2 %collective-permute-start.3 = (bf16[256,2048]{1,0:T(8,128)(2,1)}, bf16[256,2048]{1,0:T(8,128)(2,1)}, u32[]{:S(2)}, u32[]{:S(2)}) collective-permute-start(bf16[256,2048]{1,0:T(8,128)(2,1)} %get-tuple-element.224), channel_id=1, source_target_pairs={{0,4},{4,0},{1,5},{5,1},{2,6},{6,2},{3,7},{7,3},{8,12},{12,8},{9,1... | collective-permute-start | bytes 3145736 | tf_op jit(solution)/shard_map/ppermute | solution.py:338
  22.6 28.6 %collective-permute-start.12 = (bf16[80,2432]{1,0:T(8,128)(2,1)}, bf16[80,2432]{1,0:T(8,128)(2,1)}, u32[]{:S(2)}, u32[]{:S(2)}) collective-permute-start(bf16[80,2432]{1,0:T(8,128)(2,1)} %pad.27), channel_id=1, source_target_pairs={{0,8},{8,0},{1,9},{9,1},{2,10},{10,2},{3,11},{11,3},{4,12},{12,4},... | collective-permute-start | bytes 1167368 | tf_op jit(solution)/shard_map/ppermute | solution.py:338
  24.1 34.4 %all-to-all-start = ((bf16[8,64,768]{2,1,0:T(8,128)(2,1)}), bf16[8,64,768]{2,1,0:T(8,128)(2,1)S(1)}, u32[]{:S(2)}, u32[]{:S(2)}) async-start(bf16[8,64,768]{2,1,0:T(8,128)(2,1)} %pack_columns.2), calls=%async_computation | async-start | bytes 1572864 | tf_op jit(solution)/shard_map/all_to_all | solution.py:436
  27.7 189.7 %all-gather.3.cloned.1.call-start = ((), (), s32[]{:S(2)}) async-start(), calls=%async_computation.7 | async-start | bytes 3932160 | tf_op jit(solution)/shard_map/all_gather | solution.py:830
  40.3 28.3 %collective-permute-start.13 = (bf16[80,2432]{1,0:T(8,128)(2,1)S(1)}, bf16[80,2432]{1,0:T(8,128)(2,1)S(1)}, u32[]{:S(2)}, u32[]{:S(2)}) collective-permute-start(bf16[80,2432]{1,0:T(8,128)(2,1)S(1)} %collective-permute-done.11), channel_id=1, source_target_pairs={{0,8},{8,0},{1,9},{9,1},{2,10},{10,2},{3,11},{11,3},{4,12},{12,4},... | collective-permute-start | bytes 1167368 | tf_op jit(solution)/shard_map/ppermute | solution.py:338
  58.6 68.9 %collective-permute-start.8 = (bf16[512,768]{1,0:T(8,128)(2,1)S(1)}, bf16[512,768]{1,0:T(8,128)(2,1)}, u32[]{:S(2)}, u32[]{:S(2)}) collective-permute-start(bf16[512,768]{1,0:T(8,128)(2,1)S(1)} %bitcast.117), channel_id=1, source_target_pairs={{0,16},{16,0},{1,17},{17,1},{2,18},{18,2},{3,19},{19,3},{4,20},{20... | collective-permute-start | bytes 2359304 | tf_op jit(solution)/shard_map/ppermute | solution.py:338
  61.3 156.0 %all-to-all-start.1 = ((bf16[8,64,1536]{2,1,0:T(8,128)(2,1)}), bf16[8,64,1536]{2,1,0:T(8,128)(2,1)}, u32[]{:S(2)}, u32[]{:S(2)}) async-start(bf16[8,64,1536]{2,1,0:T(8,128)(2,1)} %pack_columns.3), calls=%async_computation.1 | async-start | bytes 3145728 | tf_op jit(solution)/shard_map/all_to_all | solution.py:436
  65.6 314.9 %all-gather.5.cloned.1.call-start = ((), (), s32[]{:S(2)}) async-start(), calls=%async_computation.8 | async-start | bytes 7864320 | tf_op jit(solution)/shard_map/all_gather | solution.py:840
  68.6 64.8 %collective-permute-start.9 = (bf16[512,768]{1,0:T(8,128)(2,1)S(1)}, bf16[512,768]{1,0:T(8,128)(2,1)S(1)}, u32[]{:S(2)}, u32[]{:S(2)}) collective-permute-start(bf16[512,768]{1,0:T(8,128)(2,1)S(1)} %bitcast.119), channel_id=1, source_target_pairs={{0,8},{8,0},{1,9},{9,1},{2,10},{10,2},{3,11},{11,3},{4,12},{12,4},... | collective-permute-start | bytes 2359304 | tf_op jit(solution)/shard_map/ppermute | solution.py:338
  69.0 64.5 %collective-permute-start.14 = (bf16[2,80,2432]{2,1,0:T(8,128)(2,1)S(1)}, bf16[2,80,2432]{2,1,0:T(8,128)(2,1)S(1)}, u32[]{:S(2)}, u32[]{:S(2)}) collective-permute-start(bf16[2,80,2432]{2,1,0:T(8,128)(2,1)S(1)} %dynamic-slice_bitcast_fusion.2), channel_id=1, source_target_pairs={{0,1},{1,0},{2,3},{3,2},{4,5},{5,4},{6,7},{7,6},{8,9},{9,8},{10,11... | collective-permute-start | bytes 2334728 | tf_op jit(solution)/shard_map/ppermute | solution.py:338
  71.0 81.2 %collective-permute-start.5 = (bf16[128,2048]{1,0:T(8,128)(2,1)}, bf16[128,2048]{1,0:T(8,128)(2,1)S(1)}, u32[]{:S(2)}, u32[]{:S(2)}) collective-permute-start(bf16[128,2048]{1,0:T(8,128)(2,1)} %slice.325), channel_id=1, source_target_pairs={{0,4},{4,0},{1,5},{5,1},{2,6},{6,2},{3,7},{7,3},{8,12},{12,8},{9,1... | collective-permute-start | bytes 1572872 | tf_op jit(solution)/shard_map/ppermute | solution.py:338
  74.2 78.0 %collective-permute-start.6 = (bf16[128,2048]{1,0:T(8,128)(2,1)}, bf16[128,2048]{1,0:T(8,128)(2,1)}, u32[]{:S(2)}, u32[]{:S(2)}) collective-permute-start(bf16[128,2048]{1,0:T(8,128)(2,1)} %slice.326), channel_id=1, source_target_pairs={{0,2},{2,0},{1,3},{3,1},{4,6},{6,4},{5,7},{7,5},{8,10},{10,8},{9,1... | collective-permute-start | bytes 1572872 | tf_op jit(solution)/shard_map/ppermute | solution.py:338
  133.5 30.4 %collective-permute-start.10 = (bf16[512,768]{1,0:T(8,128)(2,1)}, bf16[512,768]{1,0:T(8,128)(2,1)}, u32[]{:S(2)}, u32[]{:S(2)}) collective-permute-start(bf16[512,768]{1,0:T(8,128)(2,1)} %collective-permute-done.8), channel_id=1, source_target_pairs={{0,8},{8,0},{1,9},{9,1},{2,10},{10,2},{3,11},{11,3},{4,12},{12,4},... | collective-permute-start | bytes 2359304 | tf_op jit(solution)/shard_map/ppermute | solution.py:338
  213.8 51.3 %collective-permute-start.31 = (bf16[256,2048]{1,0:T(8,128)(2,1)}, bf16[256,2048]{1,0:T(8,128)(2,1)}, u32[]{:S(2)}, u32[]{:S(2)}) collective-permute-start(bf16[256,2048]{1,0:T(8,128)(2,1)} %param.43), channel_id=1, source_target_pairs={{0,1},{1,0},{2,3},{3,2},{4,5},{5,4},{6,7},{7,6},{8,9},{9,8},{10,11... | collective-permute-start | bytes 3145736 | tf_op jit(solution)/shard_map/ppermute | solution.py:338
  213.8 46.5 %collective-permute-start.32 = (bf16[256,2048]{1,0:T(8,128)(2,1)}, bf16[256,2048]{1,0:T(8,128)(2,1)}, u32[]{:S(2)}, u32[]{:S(2)}) collective-permute-start(bf16[256,2048]{1,0:T(8,128)(2,1)} %param.43), channel_id=1, source_target_pairs={{0,2},{2,0},{1,3},{3,1},{4,6},{6,4},{5,7},{7,5},{8,10},{10,8},{9,1... | collective-permute-start | bytes 3145736 | tf_op jit(solution)/shard_map/ppermute | solution.py:338
  216.9 47.1 %collective-permute-start.34 = (bf16[256,2048]{1,0:T(8,128)(2,1)}, bf16[256,2048]{1,0:T(8,128)(2,1)}, u32[]{:S(2)}, u32[]{:S(2)}) collective-permute-start(bf16[256,2048]{1,0:T(8,128)(2,1)} %param.43), channel_id=1, source_target_pairs={{0,8},{8,0},{1,9},{9,1},{2,10},{10,2},{3,11},{11,3},{4,12},{12,4},... | collective-permute-start | bytes 3145736 | tf_op jit(solution)/shard_map/ppermute | solution.py:338
  217.4 494.6 %reduce-scatter.4.cloned.1.call-start = ((), (), s32[]{:S(2)}) async-start(), calls=%async_computation.9 | async-start | bytes 614400 | tf_op jit(solution)/shard_map/reduce_scatter | solution.py:917
  219.7 74.0 %collective-permute-start.15 = (bf16[256,2048]{1,0:T(8,128)(2,1)S(1)}, bf16[256,2048]{1,0:T(8,128)(2,1)S(1)}, u32[]{:S(2)}, u32[]{:S(2)}) collective-permute-start(bf16[256,2048]{1,0:T(8,128)(2,1)S(1)} %copy-done.33), channel_id=1, source_target_pairs={{0,1},{1,0},{2,3},{3,2},{4,5},{5,4},{6,7},{7,6},{8,9},{9,8},{10,11... | collective-permute-start | bytes 3145736 | tf_op jit(solution)/shard_map/ppermute | solution.py:338
  258.9 35.2 %collective-permute-start.19 = (bf16[256,2048]{1,0:T(8,128)(2,1)S(1)}, bf16[256,2048]{1,0:T(8,128)(2,1)S(1)}, u32[]{:S(2)}, u32[]{:S(2)}) collective-permute-start(bf16[256,2048]{1,0:T(8,128)(2,1)S(1)} %pad_maximum_fusion.1), channel_id=1, source_target_pairs={{0,2},{2,0},{1,3},{3,1},{4,6},{6,4},{5,7},{7,5},{8,10},{10,8},{9,1... | collective-permute-start | bytes 3145736 | tf_op jit(solution)/shard_map/ppermute | solution.py:338
  260.3 40.7 %collective-permute-start.22 = (bf16[256,2048]{1,0:T(8,128)(2,1)S(1)}, bf16[256,2048]{1,0:T(8,128)(2,1)S(1)}, u32[]{:S(2)}, u32[]{:S(2)}) collective-permute-start(bf16[256,2048]{1,0:T(8,128)(2,1)S(1)} %pad_maximum_fusion.2), channel_id=1, source_target_pairs={{0,4},{4,0},{1,5},{5,1},{2,6},{6,2},{3,7},{7,3},{8,12},{12,8},{9,1... | collective-permute-start | bytes 3145736 | tf_op jit(solution)/shard_map/ppermute | solution.py:338
  280.7 30.3 %collective-permute-start.33 = (bf16[256,2048]{1,0:T(8,128)(2,1)}, bf16[256,2048]{1,0:T(8,128)(2,1)}, u32[]{:S(2)}, u32[]{:S(2)}) collective-permute-start(bf16[256,2048]{1,0:T(8,128)(2,1)} %collective-permute-done.32), channel_id=1, source_target_pairs={{0,1},{1,0},{2,3},{3,2},{4,5},{5,4},{6,7},{7,6},{8,9},{9,8},{10,11... | collective-permute-start | bytes 3145736 | tf_op jit(solution)/shard_map/ppermute | solution.py:338
  293.7 68.1 %collective-permute-start.38 = (bf16[256,2048]{1,0:T(8,128)(2,1)}, bf16[256,2048]{1,0:T(8,128)(2,1)}, u32[]{:S(2)}, u32[]{:S(2)}) collective-permute-start(bf16[256,2048]{1,0:T(8,128)(2,1)} %pad_maximum_fusion.4), channel_id=1, source_target_pairs={{0,1},{1,0},{2,3},{3,2},{4,5},{5,4},{6,7},{7,6},{8,9},{9,8},{10,11... | collective-permute-start | bytes 3145736 | tf_op jit(solution)/shard_map/ppermute | solution.py:338
  313.3 47.0 %collective-permute-start.26 = (bf16[256,2048]{1,0:T(8,128)(2,1)S(1)}, bf16[256,2048]{1,0:T(8,128)(2,1)S(1)}, u32[]{:S(2)}, u32[]{:S(2)}) collective-permute-start(bf16[256,2048]{1,0:T(8,128)(2,1)S(1)} %reshape.277), channel_id=1, source_target_pairs={{0,8},{8,0},{1,9},{9,1},{2,10},{10,2},{3,11},{11,3},{4,12},{12,4},... | collective-permute-start | bytes 3145736 | tf_op jit(solution)/shard_map/ppermute | solution.py:338
  315.7 48.5 %collective-permute-start.23 = (bf16[256,2048]{1,0:T(8,128)(2,1)S(1)}, bf16[256,2048]{1,0:T(8,128)(2,1)S(1)}, u32[]{:S(2)}, u32[]{:S(2)}) collective-permute-start(bf16[256,2048]{1,0:T(8,128)(2,1)S(1)} %reshape.277), channel_id=1, source_target_pairs={{0,1},{1,0},{2,3},{3,2},{4,5},{5,4},{6,7},{7,6},{8,9},{9,8},{10,11... | collective-permute-start | bytes 3145736 | tf_op jit(solution)/shard_map/ppermute | solution.py:338
  328.5 45.8 %collective-permute-start.25 = (bf16[256,2048]{1,0:T(8,128)(2,1)S(1)}, bf16[256,2048]{1,0:T(8,128)(2,1)S(1)}, u32[]{:S(2)}, u32[]{:S(2)}) collective-permute-start(bf16[256,2048]{1,0:T(8,128)(2,1)S(1)} %collective-permute-done.24), channel_id=1, source_target_pairs={{0,1},{1,0},{2,3},{3,2},{4,5},{5,4},{6,7},{7,6},{8,9},{9,8},{10,11... | collective-permute-start | bytes 3145736 | tf_op jit(solution)/shard_map/ppermute | solution.py:338
  329.6 41.8 %collective-permute-start.28 = (bf16[128,2048]{1,0:T(8,128)(2,1)S(1)}, bf16[128,2048]{1,0:T(8,128)(2,1)S(1)}, u32[]{:S(2)}, u32[]{:S(2)}) collective-permute-start(bf16[128,2048]{1,0:T(8,128)(2,1)S(1)} %slice.340), channel_id=1, source_target_pairs={{0,8},{8,0},{1,9},{9,1},{2,10},{10,2},{3,11},{11,3},{4,12},{12,4},... | collective-permute-start | bytes 1572872 | tf_op jit(solution)/shard_map/ppermute | solution.py:338
  449.0 31.6 %collective-permute-start.39 = (bf16[256,2048]{1,0:T(8,128)(2,1)}, bf16[256,2048]{1,0:T(8,128)(2,1)}, u32[]{:S(2)}, u32[]{:S(2)}) collective-permute-start(bf16[256,2048]{1,0:T(8,128)(2,1)} %get-tuple-element.140), channel_id=1, source_target_pairs={{0,1},{1,0},{2,3},{3,2},{4,5},{5,4},{6,7},{7,6},{8,9},{9,8},{10,11... | collective-permute-start | bytes 3145736 | tf_op jit(solution)/shard_map/ppermute | solution.py:338
  601.3 219.2 %reduce-scatter.6.cloned.1.call-start = ((), (), s32[]{:S(2)}) async-start(), calls=%async_computation.10 | async-start | bytes 7864320 | tf_op jit(solution)/shard_map/reduce_scatter | solution.py:880
  601.9 284.5 %reduce-scatter.8.cloned.1.call-start = ((), (), s32[]{:S(2)}) async-start(), calls=%async_computation.11 | async-start | bytes 3932160 | tf_op jit(solution)/shard_map/reduce_scatter | solution.py:879
  623.0 34.0 %collective-permute-start.72 = (bf16[512,768]{1,0:T(8,128)(2,1)}, bf16[512,768]{1,0:T(8,128)(2,1)S(1)}, u32[]{:S(2)}, u32[]{:S(2)}) collective-permute-start(bf16[512,768]{1,0:T(8,128)(2,1)} %get-tuple-element.226), channel_id=1, source_target_pairs={{0,8},{8,0},{1,9},{9,1},{2,10},{10,2},{3,11},{11,3},{4,12},{12,4},... | collective-permute-start | bytes 2359304 | tf_op jit(solution)/shard_map/ppermute | solution.py:338
  623.8 93.1 %collective-permute-start.71 = (bf16[512,768]{1,0:T(8,128)(2,1)}, bf16[512,768]{1,0:T(8,128)(2,1)}, u32[]{:S(2)}, u32[]{:S(2)}) collective-permute-start(bf16[512,768]{1,0:T(8,128)(2,1)} %get-tuple-element.225), channel_id=1, source_target_pairs={{0,8},{8,0},{1,9},{9,1},{2,10},{10,2},{3,11},{11,3},{4,12},{12,4},... | collective-permute-start | bytes 2359304 | tf_op jit(solution)/shard_map/ppermute | solution.py:338
  636.1 65.1 %collective-permute-start.64 = (bf16[256,2048]{1,0:T(8,128)(2,1)S(1)}, bf16[256,2048]{1,0:T(8,128)(2,1)S(1)}, u32[]{:S(2)}, u32[]{:S(2)}) collective-permute-start(bf16[256,2048]{1,0:T(8,128)(2,1)S(1)} %get-tuple-element.166), channel_id=1, source_target_pairs={{0,1},{1,0},{2,3},{3,2},{4,5},{5,4},{6,7},{7,6},{8,9},{9,8},{10,11... | collective-permute-start | bytes 3145736 | tf_op jit(solution)/shard_map/ppermute | solution.py:338
  636.1 72.0 %collective-permute-start.65 = (bf16[256,2048]{1,0:T(8,128)(2,1)S(1)}, bf16[256,2048]{1,0:T(8,128)(2,1)S(1)}, u32[]{:S(2)}, u32[]{:S(2)}) collective-permute-start(bf16[256,2048]{1,0:T(8,128)(2,1)S(1)} %get-tuple-element.168), channel_id=1, source_target_pairs={{0,1},{1,0},{2,3},{3,2},{4,5},{5,4},{6,7},{7,6},{8,9},{9,8},{10,11... | collective-permute-start | bytes 3145736 | tf_op jit(solution)/shard_map/ppermute | solution.py:338
  637.8 62.5 %collective-permute-start.77 = (bf16[80,2048]{1,0:T(8,128)(2,1)S(1)}, bf16[80,2048]{1,0:T(8,128)(2,1)S(1)}, u32[]{:S(2)}, u32[]{:S(2)}) collective-permute-start(bf16[80,2048]{1,0:T(8,128)(2,1)S(1)} %get-tuple-element.232), channel_id=1, source_target_pairs={{0,8},{8,0},{1,9},{9,1},{2,10},{10,2},{3,11},{11,3},{4,12},{12,4},... | collective-permute-start | bytes 983048 | tf_op jit(solution)/shard_map/ppermute | solution.py:338
  657.0 45.2 %collective-permute-start.68 = (bf16[256,2048]{1,0:T(8,128)(2,1)S(1)}, bf16[256,2048]{1,0:T(8,128)(2,1)S(1)}, u32[]{:S(2)}, u32[]{:S(2)}) collective-permute-start(bf16[256,2048]{1,0:T(8,128)(2,1)S(1)} %get-tuple-element.170), channel_id=1, source_target_pairs={{0,1},{1,0},{2,3},{3,2},{4,5},{5,4},{6,7},{7,6},{8,9},{9,8},{10,11... | collective-permute-start | bytes 3145736 | tf_op jit(solution)/shard_map/ppermute | solution.py:338
  700.4 127.7 %collective-permute-start.63 = (bf16[256,2048]{1,0:T(8,128)(2,1)}, bf16[256,2048]{1,0:T(8,128)(2,1)}, u32[]{:S(2)}, u32[]{:S(2)}) collective-permute-start(bf16[256,2048]{1,0:T(8,128)(2,1)} %get-tuple-element.164), channel_id=1, source_target_pairs={{0,1},{1,0},{2,3},{3,2},{4,5},{5,4},{6,7},{7,6},{8,9},{9,8},{10,11... | collective-permute-start | bytes 3145736 | tf_op jit(solution)/shard_map/ppermute | solution.py:338
  706.0 121.6 %collective-permute-start.76 = (bf16[80,2048]{1,0:T(8,128)(2,1)}, bf16[80,2048]{1,0:T(8,128)(2,1)}, u32[]{:S(2)}, u32[]{:S(2)}) collective-permute-start(bf16[80,2048]{1,0:T(8,128)(2,1)} %get-tuple-element.231), channel_id=1, source_target_pairs={{0,8},{8,0},{1,9},{9,1},{2,10},{10,2},{3,11},{11,3},{4,12},{12,4},... | collective-permute-start | bytes 983048 | tf_op jit(solution)/shard_map/ppermute | solution.py:338
  708.1 74.0 %collective-permute-start.73 = (bf16[512,768]{1,0:T(8,128)(2,1)}, bf16[512,768]{1,0:T(8,128)(2,1)S(1)}, u32[]{:S(2)}, u32[]{:S(2)}) collective-permute-start(bf16[512,768]{1,0:T(8,128)(2,1)} %fusion.7), channel_id=1, source_target_pairs={{0,16},{16,0},{1,17},{17,1},{2,18},{18,2},{3,19},{19,3},{4,20},{20... | collective-permute-start | bytes 2359304 | tf_op jit(solution)/shard_map/ppermute | solution.py:338
  710.2 79.9 %collective-permute-start.66 = (bf16[128,2048]{1,0:T(8,128)(2,1)}, bf16[128,2048]{1,0:T(8,128)(2,1)}, u32[]{:S(2)}, u32[]{:S(2)}) collective-permute-start(bf16[128,2048]{1,0:T(8,128)(2,1)} %get-tuple-element.235), channel_id=1, source_target_pairs={{0,4},{4,0},{1,5},{5,1},{2,6},{6,2},{3,7},{7,3},{8,12},{12,8},{9,1... | collective-permute-start | bytes 1572872 | tf_op jit(solution)/shard_map/ppermute | solution.py:338
  716.9 112.8 %collective-permute-start.78 = (bf16[80,2048]{1,0:T(8,128)(2,1)}, bf16[80,2048]{1,0:T(8,128)(2,1)}, u32[]{:S(2)}, u32[]{:S(2)}) collective-permute-start(bf16[80,2048]{1,0:T(8,128)(2,1)} %fusion.10), channel_id=1, source_target_pairs={{0,16},{16,0},{1,17},{17,1},{2,18},{18,2},{3,19},{19,3},{4,20},{20... | collective-permute-start | bytes 983048 | tf_op jit(solution)/shard_map/ppermute | solution.py:338
  786.2 34.3 %all-to-all-start.2 = ((bf16[8,64,768]{2,1,0:T(8,128)(2,1)}), bf16[8,64,768]{2,1,0:T(8,128)(2,1)S(1)}, u32[]{:S(2)}, u32[]{:S(2)}) async-start(bf16[8,64,768]{2,1,0:T(8,128)(2,1)} %bitcast.120), calls=%async_computation.2 | async-start | bytes 1572864 | tf_op jit(solution)/shard_map/all_to_all | solution.py:436
  814.1 34.8 %collective-permute-start.67 = (bf16[256,2048]{1,0:T(8,128)(2,1)}, bf16[256,2048]{1,0:T(8,128)(2,1)}, u32[]{:S(2)}, u32[]{:S(2)}) collective-permute-start(bf16[256,2048]{1,0:T(8,128)(2,1)} %pad_maximum_fusion.10), channel_id=1, source_target_pairs={{0,2},{2,0},{1,3},{3,1},{4,6},{6,4},{5,7},{7,5},{8,10},{10,8},{9,1... | collective-permute-start | bytes 3145736 | tf_op jit(solution)/shard_map/ppermute | solution.py:338
  818.1 32.4 %collective-permute-start.70 = (bf16[256,2048]{1,0:T(8,128)(2,1)}, bf16[256,2048]{1,0:T(8,128)(2,1)}, u32[]{:S(2)}, u32[]{:S(2)}) collective-permute-start(bf16[256,2048]{1,0:T(8,128)(2,1)} %pad_maximum_fusion.11), channel_id=1, source_target_pairs={{0,4},{4,0},{1,5},{5,1},{2,6},{6,2},{3,7},{7,3},{8,12},{12,8},{9,1... | collective-permute-start | bytes 3145736 | tf_op jit(solution)/shard_map/ppermute | solution.py:338
  820.5 68.4 %all-to-all-start.3 = ((bf16[8,64,1536]{2,1,0:T(8,128)(2,1)}), bf16[8,64,1536]{2,1,0:T(8,128)(2,1)S(1)}, u32[]{:S(2)}, u32[]{:S(2)}) async-start(bf16[8,64,1536]{2,1,0:T(8,128)(2,1)} %bitcast.124), calls=%async_computation.5 | async-start | bytes 3145728 | tf_op jit(solution)/shard_map/all_to_all | solution.py:436
  828.0 50.6 %collective-permute-start.59 = (bf16[256,2048]{1,0:T(8,128)(2,1)}, bf16[256,2048]{1,0:T(8,128)(2,1)}, u32[]{:S(2)}, u32[]{:S(2)}) collective-permute-start(bf16[256,2048]{1,0:T(8,128)(2,1)} %pad_maximum_fusion.8), channel_id=1, source_target_pairs={{0,2},{2,0},{1,3},{3,1},{4,6},{6,4},{5,7},{7,5},{8,10},{10,8},{9,1... | collective-permute-start | bytes 3145736 | tf_op jit(solution)/shard_map/ppermute | solution.py:338
  829.7 48.9 %collective-permute-start.62 = (bf16[256,2048]{1,0:T(8,128)(2,1)}, bf16[256,2048]{1,0:T(8,128)(2,1)}, u32[]{:S(2)}, u32[]{:S(2)}) collective-permute-start(bf16[256,2048]{1,0:T(8,128)(2,1)} %pad_maximum_fusion.9), channel_id=1, source_target_pairs={{0,8},{8,0},{1,9},{9,1},{2,10},{10,2},{3,11},{11,3},{4,12},{12,4},... | collective-permute-start | bytes 3145736 | tf_op jit(solution)/shard_map/ppermute | solution.py:338
  (127 other events, 1463.9 us)
Sparse Core Ops, SparseCore 0:
  30.4 97.6 all-gather.2
  217.5 120.6 all-gather.4
  601.4 18.7 reduce-scatter.3
  623.4 158.0 reduce-scatter.5
  784.6 69.8 reduce-scatter.7

commit v4 on v3

--- a/solution.py
+++ b/solution.py
@@ -334,6 +334,10 @@
 GELU_K = 0.044715
 
 
+def after(v, *first):
+    return lax.optimization_barrier((v,) + first)[0]
+
+
 def swap(v, name):
     return lax.ppermute(v, name, [(0, 1), (1, 0)])
 
@@ -342,32 +346,42 @@
     return (one.astype(F32) + two.astype(F32)).astype(BF16)
 
 
-def act_gather(v, a, b):
+def act_gather(v, a, b, second=(), third=()):
     h = v.shape[0] // 2
     near, from_a, from_b = swap(v, "c"), swap(v, a), swap(v, b)
+    from_a, from_b, near = lax.optimization_barrier((from_a, from_b, near) + tuple(second))[:3]
     far0, far1 = swap(from_a[:h], b), swap(from_b[h:], a)
     near_a, near_b = swap(from_a, "c"), swap(from_b, "c")
+    far0, far1, near_a, near_b = lax.optimization_barrier((far0, far1, near_a, near_b) + tuple(third))[:4]
     far = jnp.concatenate([far0, far1], axis=0)
     return [v, near, from_a, near_a, from_b, near_b, far, swap(far, "c")]
 
 
-def act_scatter(get, a, b):
-    far, to_a, to_b = [add16(get(k), swap(get(k + 1), "c")) for k in (6, 2, 4)]
-    own = get(0).astype(F32) + swap(get(1), "c").astype(F32)
+def act_scatter(blocks, a, b, second=(), third=(), last=None):
+    far, to_a, to_b = [add16(blocks[k], swap(blocks[k + 1], "c")) for k in (6, 2, 4)]
+    far = after(far, *second)
+    own = blocks[0].astype(F32) + swap(blocks[1], "c").astype(F32)
     h = far.shape[0] // 2
     in_b, in_a = swap(far[:h], b), swap(far[h:], a)
     to_a = jnp.concatenate([add16(to_a[:h], in_b), to_a[h:]], axis=0)
     to_b = jnp.concatenate([to_b[:h], add16(to_b[h:], in_a)], axis=0)
-    return own + swap(to_a, a).astype(F32) + swap(to_b, b).astype(F32)
-
-
-def w_gather(v, w1, w2):
+    to_a, to_b = lax.optimization_barrier((to_a, to_b) + tuple(third))[:2]
+    from_a, from_b = swap(to_a, a), swap(to_b, b)
+    if last is not None:
+        from_a, from_b = lax.optimization_barrier((from_a, from_b) + tuple(last(to_a)))[:2]
+    return own + from_a.astype(F32) + from_b.astype(F32)
+
+
+def w_parts(v, w1, w2, second=()):
+    from_1, from_2 = lax.optimization_barrier((swap(v, w1), swap(v, w2)) + tuple(second))[:2]
+    return [v, from_1, from_2, swap(from_1, w2)]
+
+
+def w_place(parts, w1, w2):
     i1, i2 = lax.axis_index(w1), lax.axis_index(w2)
-    p1, p2 = swap(v, w1), swap(v, w2)
-    p12 = swap(p1, w2)
-    out = jnp.zeros((2, 2) + v.shape, v.dtype)
-    tail = (0,) * v.ndim
-    for part, j1, j2 in ((v, i1, i2), (p1, 1 - i1, i2), (p2, i1, 1 - i2), (p12, 1 - i1, 1 - i2)):
+    out = jnp.zeros((2, 2) + parts[0].shape, parts[0].dtype)
+    tail = (0,) * parts[0].ndim
+    for part, j1, j2 in zip(parts, (i1, 1 - i1, i1, 1 - i1), (i2, i2, 1 - i2, 1 - i2)):
         out = lax.dynamic_update_slice(out, part[None, None], (j1, j2) + tail)
     return out
 
@@ -378,9 +392,10 @@
     def get(j1, j2):
         return lax.dynamic_slice(v, (j1, j2) + (0,) * (v.ndim - 2), (1, 1) + v.shape[2:])[0, 0]
 
-    other = add16(get(1 - i1, i2), swap(get(1 - i1, 1 - i2), w2))
+    other = get(1 - i1, i2).astype(F32) + swap(get(1 - i1, 1 - i2), w2).astype(F32)
+    other = other.astype(v.dtype)
     own = get(i1, i2).astype(F32) + swap(get(i1, 1 - i2), w2).astype(F32)
-    return own + swap(other, w1).astype(F32)
+    return own + swap(other, w1).astype(F32), other
 
 
 def pack_kernel(plan, a_ref, b_ref, gain_ref, out_ref):
@@ -396,12 +411,11 @@
                 out_ref[dest, :, at : first + half] = jnp.zeros((scaled.shape[0], first + half - at), BF16)
 
 
-def unpack_kernel(plan, grad_ref, a_ref, b_ref, gain_ref, da_ref, db_ref, dgain_ref):
-    half = grad_ref.shape[2] // 2
+def unpack_kernel(plan, ga_ref, gb_ref, a_ref, b_ref, gain_ref, da_ref, db_ref, dgain_ref):
     total = jnp.zeros(dgain_ref.shape, F32)
-    for first, ref, out in ((0, a_ref, da_ref), (half, b_ref, db_ref)):
+    for grad_ref, ref, out in ((ga_ref, a_ref, da_ref), (gb_ref, b_ref, db_ref)):
         for dest, pieces in enumerate(plan):
-            at = first
+            at = 0
             for source, size in pieces:
                 piece = grad_ref[dest, :, at : at + size].astype(F32)
                 out[:, source : source + size] = piece * gain_ref[...]
@@ -421,15 +435,25 @@
     )(one, two, gain)
 
 
-def unpack_columns(plan, grad, one, two, gain):
+def unpack_columns(plan, grad_one, grad_two, one, two, gain):
+    half = grad_one.shape[2] if grad_two is not None else grad_one.shape[2] // 2
+    rows, cols = one.shape
+    whole = lambda *shape: pl.BlockSpec(shape, lambda i: (0,) * len(shape))
+    grads = [
+        pl.BlockSpec((8, rows, half), lambda i: (0, 0, 0)),
+        pl.BlockSpec((8, rows, half), lambda i: (0, 0, 0 if grad_two is not None else 1)),
+    ]
     shape = jax.ShapeDtypeStruct(one.shape, F32)
     return pl.pallas_call(
         functools.partial(unpack_kernel, plan),
-        out_shape=[shape, shape, jax.ShapeDtypeStruct((one.shape[0], 1), F32)],
-        compiler_params=pltpu.CompilerParams(vmem_limit_bytes=24 << 20),
+        grid=(1,),
+        in_specs=grads + [whole(rows, cols), whole(rows, cols), whole(rows, 1)],
+        out_specs=[whole(rows, cols), whole(rows, cols), whole(rows, 1)],
+        out_shape=[shape, shape, jax.ShapeDtypeStruct((rows, 1), F32)],
+        compiler_params=pltpu.CompilerParams(vmem_limit_bytes=32 << 20),
         cost_estimate=pl.CostEstimate(flops=8 * one.size, transcendentals=0, bytes_accessed=16 * one.size),
         name="unpack_columns",
-    )(grad, one, two, gain)
+    )(grad_one, grad_one if grad_two is None else grad_two, one, two, gain)
 
 
 def exchange(v, tp):
@@ -627,6 +651,58 @@
     for q in range(5):
         sum_ref[8 * q : 8 * q + 8, :] = sums[q]
     ext[rows : rows + 8, :] = ext[0:8, :]
+
+
+def place_kernel(width, taps, meta_ref, *refs):
+    parts, (wo_ref, gates_ref, vec_ref, cols) = refs[:4], refs[4:]
+    part, model = parts[0].shape[0], wo_ref.shape[1]
+    padded = wo_ref.shape[0]
+    zl, core = meta_ref[0], meta_ref[1]
+    lanes = cols.shape[1]
+    wo_ref[4 * part :, :] = jnp.zeros((padded - 4 * part, model), BF16)
+    gates_ref[...] = jnp.zeros_like(gates_ref)
+    cols[4 * part :, :] = jnp.zeros((padded - 4 * part, lanes), F32)
+    for n in range(4):
+        here_zl = zl if n % 2 == 0 else 1 - zl
+        half = core if n < 2 else 1 - core
+        at = pl.multiple_of((here_zl * 2 + half) * part, STEP)
+        wo_ref[pl.ds(at, part), :] = parts[n][:, :model]
+        rest = parts[n][:, model:]
+        cols[pl.ds(at, part), :] = rest[:, :lanes].astype(F32)
+        for block in range(2):
+
+            @pl.when(here_zl == block)
+            def _(rest=rest, at=at, block=block):
+                for g in range(2):
+                    source = taps + 4 + g * width
+                    target = g * padded + block * width
+                    gates_ref[pl.ds(at, part), target : target + width] = rest[:, source : source + width]
+
+    vec_ref[...] = cols[...].T[:8, :]
+
+
+def place_channels(meta, parts, model, width, taps):
+    part = parts[0].shape[0]
+    padded = -(-4 * part // 128) * 128
+    shape = jax.ShapeDtypeStruct
+    return pl.pallas_call(
+        functools.partial(place_kernel, width, taps),
+        grid_spec=pltpu.PrefetchScalarGridSpec(
+            num_scalar_prefetch=1,
+            grid=(1,),
+            in_specs=[pl.BlockSpec(v.shape, lambda i, m: (0, 0)) for v in parts],
+            out_specs=[
+                pl.BlockSpec((padded, model), lambda i, m: (0, 0)),
+                pl.BlockSpec((padded, 2 * padded), lambda i, m: (0, 0)),
+                pl.BlockSpec((8, padded), lambda i, m: (0, 0)),
+            ],
+            scratch_shapes=[pltpu.VMEM((padded, 128), F32)],
+        ),
+        out_shape=[shape((padded, model), BF16), shape((padded, 2 * padded), BF16), shape((8, padded), F32)],
+        compiler_params=pltpu.CompilerParams(vmem_limit_bytes=24 << 20),
+        cost_estimate=pl.CostEstimate(flops=padded * model, transcendentals=0, bytes_accessed=8 * padded * model),
+        name="place_channels",
+    )(meta, *parts)
 
 
 def rec_forward(meta, xy, vec, w, tile):
@@ -744,47 +820,92 @@
     )(a, w)
 
 
-def ff_kernel(x_ref, cot_ref, wgu_ref, wd_ref, hidden_ref, dgu_ref, *rest):
+def join_pieces(step, pieces, all_ref):
+    rows = pieces[0].shape[0]
+    per = all_ref.shape[0] // rows
+    for n, piece in enumerate(pieces):
+
+        @pl.when(step == n // per)
+        def _(n=n, piece=piece):
+            all_ref[(n % per) * rows : (n % per + 1) * rows, :] = piece[...]
+
+
+def pieces_kernel(flip, *refs):
+    pieces, (w_ref, all_ref, out_ref) = refs[:8], refs[8:]
+    join_pieces(pl.program_id(0), pieces, all_ref)
+    a = all_ref[...]
+    wide = columns_of(out_ref.shape[1], 384)
+    for at in range(0, out_ref.shape[1], wide):
+        if flip:
+            out_ref[:, at : at + wide] = back_product(a, w_ref[at : at + wide, :])
+        else:
+            out_ref[:, at : at + wide] = dot32(a, w_ref[:, at : at + wide])
+
+
+def pieces_product(pieces, w, flip):
+    rows, deep = pieces[0].shape
+    total, tile = 8 * rows, 2 * rows
+    cols = w.shape[0] if flip else w.shape[1]
+    once = lambda v: pl.BlockSpec(v.shape, lambda i: (0, 0), pipeline_mode=pl.Buffered(1))
+    return pl.pallas_call(
+        functools.partial(pieces_kernel, flip),
+        grid=(4,),
+        in_specs=[once(v) for v in pieces] + [once(w)],
+        out_specs=[pl.BlockSpec((tile, deep), lambda i: (i, 0)), pl.BlockSpec((tile, cols), lambda i: (i, 0))],
+        out_shape=[jax.ShapeDtypeStruct((total, deep), BF16), jax.ShapeDtypeStruct((total, cols), F32)],
+        compiler_params=pltpu.CompilerParams(vmem_limit_bytes=44 << 20),
+        cost_estimate=pl.CostEstimate(
+            flops=2 * total * deep * cols, transcendentals=0, bytes_accessed=4 * total * (deep + cols) + 2 * w.size
+        ),
+        name="pieces_product",
+    )(*pieces, w)
+
+
+def ff_kernel(*refs):
+    pieces, (cot_ref, wg_ref, wu_ref, wd_ref, x_ref, hidden_ref, dgt_ref, dup_ref), rest = refs[:8], refs[8:16], refs[16:]
     outs, value = rest[:-1], rest[-1]
     half, model = wd_ref.shape
     narrow, wide = columns_of(half, 256), columns_of(model, 512)
+    join_pieces(pl.program_id(0), pieces, x_ref)
     x, cot = x_ref[...], cot_ref[...]
     for at in range(0, half, narrow):
-        gt = dot32(x, wgu_ref[:, at : at + narrow])
-        up = dot32(x, wgu_ref[:, half + at : half + at + narrow])
+        gt = dot32(x, wg_ref[:, at : at + narrow])
+        up = dot32(x, wu_ref[:, at : at + narrow])
         dh = back_product(cot, wd_ref[at : at + narrow, :])
         act, slope = gelu_both(gt)
         hidden_ref[:, at : at + narrow] = (act * up).astype(BF16)
-        dgu_ref[:, at : at + narrow] = (dh * up * slope).astype(BF16)
-        dgu_ref[:, half + at : half + at + narrow] = (dh * act).astype(BF16)
-    grad = dgu_ref[...]
+        dgt_ref[:, at : at + narrow] = (dh * up * slope).astype(BF16)
+        dup_ref[:, at : at + narrow] = (dh * act).astype(BF16)
+    d_gt, d_up = dgt_ref[...], dup_ref[...]
     for at in range(0, model, wide):
-        value[:, at : at + wide] = back_product(grad, wgu_ref[at : at + wide, :]).astype(BF16)
+        part = back_product(d_gt, wg_ref[at : at + wide, :]) + back_product(d_up, wu_ref[at : at + wide, :])
+        value[:, at : at + wide] = part.astype(BF16)
     store_blocks(pl.program_id(0), value, outs, outs[0].shape[0])
 
 
-def feed_forward(x, cot, wgu, wd):
-    total, model = x.shape
+def feed_forward(pieces, cot, wgu, wd):
+    rows, model = pieces[0].shape
     half = wd.shape[0]
-    tile, rows = total // 4, total // 8
+    total, tile = 8 * rows, 2 * rows
     at = lambda cols: pl.BlockSpec((tile, cols), lambda i: (i, 0))
-    whole = lambda v: pl.BlockSpec(v.shape, lambda i: (0, 0), pipeline_mode=pl.Buffered(1))
+    once = lambda v: pl.BlockSpec(v.shape, lambda i: (0, 0), pipeline_mode=pl.Buffered(1))
+    side = lambda n: pl.BlockSpec((model, half), lambda i: (0, n), pipeline_mode=pl.Buffered(1))
+    widths = (model, half, half, half)
     return pl.pallas_call(
         ff_kernel,
         grid=(4,),
-        in_specs=[at(model), at(model), whole(wgu), whole(wd)],
-        out_specs=[at(half), at(2 * half)] + [pl.BlockSpec((rows, model), lambda i: (0, 0))] * 8,
-        out_shape=[jax.ShapeDtypeStruct((total, half), BF16), jax.ShapeDtypeStruct((total, 2 * half), BF16)]
-        + [jax.ShapeDtypeStruct((rows, model), BF16)] * 8,
+        in_specs=[once(v) for v in pieces] + [at(model), side(0), side(1), once(wd)],
+        out_specs=[at(n) for n in widths] + [pl.BlockSpec((rows, model), lambda i: (0, 0))] * 8,
+        out_shape=[jax.ShapeDtypeStruct((total, n), BF16) for n in widths] + [jax.ShapeDtypeStruct((rows, model), BF16)] * 8,
         scratch_shapes=[pltpu.VMEM((tile, model), BF16)],
-        compiler_params=pltpu.CompilerParams(vmem_limit_bytes=52 << 20),
+        compiler_params=pltpu.CompilerParams(vmem_limit_bytes=56 << 20),
         cost_estimate=pl.CostEstimate(
             flops=10 * total * model * half,
             transcendentals=total * half,
-            bytes_accessed=2 * (3 * total * model + 3 * half * model + 3 * total * half),
+            bytes_accessed=2 * (4 * total * model + 3 * half * model + 3 * total * half),
         ),
         name="feed_forward",
-    )(x, cot, wgu, wd)
+    )(*pieces, cot, wgu, wgu, wd)
 
 
 def norm_back(dv, v, scale):
@@ -793,8 +914,6 @@
 
 PLANE = ("y", "x", "c")
 STACK = ("zh", "zl")
-UNITS = ("zl", "x", "c")
-SHARDS = ("zh", "y")
 
 
 def tensor_parallel(
@@ -819,78 +938,76 @@
     rec_plan = tuple(
         tuple((((2 * (t % 2) + z) * 4 + t // 2) * width, width) for z in range(2)) for t in range(8)
     )
-    ff_plan = tuple(
-        tuple((((f // 2) * 16 + (t // 4) * 8 + (f % 2) * 4 + t % 4) * units, units) for f in range(4)) for t in range(8)
-    )
-
-    def shard_order(v):
-        return v.reshape(v.shape[0], 2, 2, 2, -1).swapaxes(2, 3).reshape(v.shape)
+    ff_plan = tuple(tuple(((f * 8 + t) * units, units) for f in range(4)) for t in range(8))
 
     packed_xy = pack_columns(rec_plan, padded, w_x, w_y, gain1)
-    wd = lax.all_gather(w_down, SHARDS, axis=0, tiled=True)
-    late_input = lax.optimization_barrier((layer_input, packed_xy))[0]
     wxy = exchange(packed_xy, PLANE)
-    xf = late_input.astype(F32)
+    conv_w, conv_b, b_rgate, b_igate, lam, w_rgate, w_igate, w_out = lax.optimization_barrier(
+        (conv_w, conv_b, b_rgate, b_igate, lam, w_rgate, w_igate, w_out, packed_xy)
+    )[:8]
+    small = [w_out, conv_w, conv_b[:, None], b_rgate[:, None], b_igate[:, None], lam[:, None], w_rgate, w_igate]
+    small_width = sum(v.shape[1] for v in small)
+    small = jnp.pad(jnp.concatenate(small, axis=1), ((0, 0), (0, -small_width % 128)))
+
+    stacked = w_parts(small, *STACK)
+    wxy_parts = w_parts(after(wxy.reshape(-1, 2 * padded), stacked[1], stacked[2]), *STACK, (stacked[3],))
+    upper = lax.axis_index("zh") == core
+    keep = [jnp.where(upper, stacked[n], stacked[n + 1]) for n in (0, 2)]
+    give = [swap(jnp.where(upper, stacked[n + 1], stacked[n]), "c") for n in (0, 2)]
+    place = jnp.stack([lax.axis_index("zl"), core]).astype(jnp.int32)
+    wo, gates, vec = place_channels(place, keep + give, model, width, taps)
+    lam_all = vec[taps + 3]
+    vec = jnp.concatenate([vec[: taps + 1], jax.nn.softplus(-lam_all)[None], vec[taps + 1 : taps + 3]], axis=0)
+
+    xf = layer_input.astype(F32)
     scale1 = lax.rsqrt(jnp.mean(xf * xf, axis=-1, keepdims=True) + NORM_EPS)
-    xs = (xf * scale1).astype(BF16)
-    xs_all = jnp.concatenate(act_gather(xs, "x", "y"), axis=0)
-    wxy, packed_gu = lax.optimization_barrier((wxy, pack_columns(ff_plan, 4 * units, w_gate, w_up, gain2)))
-    wxy = w_gather(wxy.reshape(-1, 2 * padded), *STACK).reshape(model, -1)
-    packed_gu, wd = lax.optimization_barrier((exchange(packed_gu, UNITS), wd))
-    wgu = lax.all_gather(packed_gu.reshape(-1, 8 * units), SHARDS, axis=0, tiled=True)
-
-    small = [conv_w, conv_b[:, None], b_rgate[:, None], b_igate[:, None], lam[:, None], w_rgate, w_igate]
-    small_width = sum(v.shape[1] for v in small)
-    packed = jnp.pad(jnp.concatenate([w_out] + small, axis=1), ((0, 0), (0, -small_width % 128)))
-    halves = w_gather(packed, *STACK)
-    mine = lax.dynamic_slice(halves, (core, 0, 0, 0), (1,) + halves.shape[1:])[0]
-    theirs = swap(lax.dynamic_slice(halves, (1 - core, 0, 0, 0), (1,) + halves.shape[1:])[0], "c")
-    whole = jnp.zeros((2, 2) + packed.shape, BF16)
-    whole = lax.dynamic_update_slice(whole, mine[:, None], (0, core, 0, 0))
-    whole = lax.dynamic_update_slice(whole, theirs[:, None], (0, 1 - core, 0, 0))
-    whole = jnp.pad(whole.reshape(channels, -1), ((0, extra), (0, 0)))
-    wo = whole[:, :model]
-    rest = whole[:, model : model + taps + 4].astype(F32).T
-    lam_all = rest[taps + 3]
-    vec = jnp.concatenate([rest[: taps + 1], jax.nn.softplus(-lam_all)[None], rest[taps + 1 : taps + 3]], axis=0)
-    at = model + taps + 4
-    gates = jnp.zeros((padded, 2 * padded), BF16)
-    for g in range(2):
-        for n in range(blocks):
-            block = whole[n * width : (n + 1) * width, at + g * width : at + (g + 1) * width]
-            gates = gates.at[n * width : (n + 1) * width, g * padded + n * width : g * padded + (n + 1) * width].set(block)
-
-    xy = dot32(xs_all, wxy)
+    xs_pieces = act_gather(after((xf * scale1).astype(BF16), wxy), "x", "y", (), (wxy_parts[3],))
+    packed_gu = after(pack_columns(ff_plan, 4 * units, w_gate, w_up, gain2), xs_pieces[2], wxy_parts[1])
+    packed_gu = exchange(packed_gu, PLANE).reshape(-1, 8 * units)
+    wd = lax.all_gather(after(w_down, wxy_parts[3]), STACK, axis=0, tiled=True)
+    wxy_parts = wxy_parts[:3] + [after(wxy_parts[3], packed_gu, wo, gates)]
+    wxy = w_place(wxy_parts, *STACK).reshape(model, -1)
+    wgu = lax.all_gather(packed_gu, STACK, axis=0, tiled=True)
+    xs_all, xy = pieces_product(xs_pieces, wxy, False)
     xc, pa, px, before, mixed = rec_forward(meta, xy, vec, gates, rows)
-
+    cot_pieces = act_gather(after(cot, mixed), "x", "y")
     blocks_r = product_blocks(mixed, wo, False)
-    resid = xf + act_scatter(lambda k: blocks_r[k], "x", "y")
+    cot_all = jnp.concatenate(cot_pieces, axis=0)
+    resid = xf + act_scatter(blocks_r, "x", "y", (wd,))
     scale2 = lax.rsqrt(jnp.mean(resid * resid, axis=-1, keepdims=True) + NORM_EPS)
-    xs2 = shard_order((resid * scale2).astype(BF16))
-    early_cot = lax.optimization_barrier((cot, xs_all))[0]
-    cot_all = jnp.concatenate(act_gather(early_cot, "x", "zl"), axis=0)
-    xs2_all = jnp.concatenate(act_gather(xs2, "x", "zl"), axis=0)
-    hidden, d_gu, *blocks_2 = feed_forward(xs2_all, cot_all, wgu, wd)
-    d_un2 = shard_order(act_scatter(lambda k: blocks_2[k], "x", "zl"))
+    xs2_pieces = act_gather((resid * scale2).astype(BF16), "x", "y", (cot_all,))
+    xs2_all, hidden, d_gt, d_up, *blocks_2 = feed_forward(xs2_pieces, cot_all, wgu, wd)
+    d_wd = row_contract(hidden, cot_all).astype(BF16)
+    d_un2 = act_scatter(blocks_2, "x", "y", (), (d_wd,))
     d_resid = cot.astype(F32) + norm_back(d_un2, resid, scale2)
-    d_wd = row_contract(hidden, cot_all).astype(BF16)
-    d_wgu = row_contract(xs2_all, d_gu).astype(BF16)
-    d_mix, d_wd, d_wgu = lax.optimization_barrier((d_resid.astype(BF16), d_wd, d_wgu))
-    d_wd = lax.psum_scatter(d_wd, SHARDS, scatter_dimension=0, tiled=True)
-    d_wgu = lax.psum_scatter(d_wgu, SHARDS, scatter_dimension=0, tiled=True)
-    d_wg, d_wu, d_gain2 = unpack_columns(ff_plan, exchange(d_wgu.reshape(8, -1, 8 * units), UNITS), w_gate, w_up, gain2)
-
-    d_mix_all = jnp.concatenate(act_gather(d_mix, "x", "y"), axis=0)
-    dm = back_product(d_mix_all, wo)
+    d_mix = d_resid.astype(BF16)
+    d_wd = lax.psum_scatter(d_wd, STACK, scatter_dimension=0, tiled=True)
+    d_wg = row_contract(xs2_all, after(d_gt, d_mix)).astype(BF16)
+    d_wu = row_contract(xs2_all, after(d_up, d_mix)).astype(BF16)
+    d_mix_pieces = act_gather(d_mix, "x", "y", (d_wg,), (d_wu, d_wd))
+    d_wg = lax.psum_scatter(d_wg, STACK, scatter_dimension=0, tiled=True)
+    d_wu = lax.psum_scatter(d_wu, STACK, scatter_dimension=0, tiled=True)
+
+    d_mix_all, dm = pieces_product(d_mix_pieces, wo, True)
     dxy, d_gates, sums = rec_backward(meta, dm, xy, before, pa, px, xc, vec, gates.T, rows)
-    blocks_1 = product_blocks(dxy, wxy, True)
-    d_un = act_scatter(lambda k: blocks_1[k], "x", "y")
-    d_input = (d_resid + norm_back(d_un, xf, scale1)).astype(BF16)
-    late_hidden = lax.optimization_barrier((hidden, blocks_1[0]))[0]
-    blocks_o = product_blocks(late_hidden, wd, False)
-    output = (resid + act_scatter(lambda k: blocks_o[k], "x", "zl")).astype(BF16)
-    d_wxy = w_scatter(row_contract(xs_all, dxy).astype(BF16).reshape(2, 2, model // 4, -1), *STACK).astype(BF16)
-    d_wx, d_wy, d_gain1 = unpack_columns(rec_plan, exchange(d_wxy.reshape(8, -1, 2 * padded), PLANE), w_x, w_y, gain1)
+    d_wg = exchange(d_wg.reshape(8, -1, 4 * units), PLANE)
+    blocks_1 = product_blocks(after(dxy, d_wg), wxy, True)
+    d_wxy = row_contract(xs_all, after(dxy, blocks_1[0])).astype(BF16)
+    d_wxy_sum, sent = w_scatter(d_wxy.reshape(2, 2, model // 4, -1), *STACK)
+    blocks_o = []
+
+    def output_blocks(marker):
+        blocks_o.extend(product_blocks(after(hidden, marker), wd, False))
+        return sent, blocks_o[0]
+
+    d_un = act_scatter(blocks_1, "x", "y", (d_wxy,), (), output_blocks)
+    d_input = (d_resid + norm_back(after(d_un, d_wu), xf, scale1)).astype(BF16)
+    d_wxy = d_wxy_sum.astype(BF16)
+    output = (resid + act_scatter(blocks_o, "x", "y", (d_input,), (d_wxy,))).astype(BF16)
+    d_wxy = exchange(d_wxy.reshape(8, -1, 2 * padded), PLANE)
+    d_wx, d_wy, d_gain1 = unpack_columns(rec_plan, d_wxy, None, w_x, w_y, gain1)
+    d_wu = exchange(d_wu.reshape(8, -1, 4 * units), PLANE)
+    d_wg, d_wu, d_gain2 = unpack_columns(ff_plan, d_wg, d_wu, w_gate, w_up, gain2)
 
     def channels_out(v, kind):
         v = v.astype(kind).reshape(2, 2, part, -1)
@@ -901,7 +1018,7 @@
         out = lax.dynamic_update_slice(out, keep[None], (core, 0, 0, 0))
         return lax.dynamic_update_slice(out, swap(send, "c")[None], (1 - core, 0, 0, 0))
 
-    d_wo = w_scatter(channels_out(row_contract(mixed, d_mix_all)[:channels], BF16), *STACK)
+    d_wo = w_scatter(channels_out(row_contract(after(mixed, sent), d_mix_all)[:channels], BF16), *STACK)[0]
     sums = jnp.sum(sums.reshape(8, 8, padded), axis=1)
     d_lam_part = -jax.nn.sigmoid(-lam_all) * sums[5]
     d_cols = jnp.concatenate([sums[:5], sums[6:8], d_lam_part[None]], axis=0).T
@@ -914,7 +1031,7 @@
             block = jnp.where(row_block == n, d_gates[:channels, at : at + width], block)
         d_blocks.append(block)
     d_small = jnp.concatenate([d_cols[:channels]] + d_blocks, axis=1)
-    d_small = lax.psum_scatter(channels_out(d_small, F32).reshape(4 * part, -1), STACK, scatter_dimension=0, tiled=True)
+    d_small = w_scatter(channels_out(d_small, F32), *STACK)[0]
     d_cw, d_cb, d_br, d_bi, d_lam = d_small[:, :4], d_small[:, 4], d_small[:, 5], d_small[:, 6], d_small[:, 7]
     d_wr, d_wi = d_small[:, 8 : 8 + width], d_small[:, 8 + width : 8 + 2 * width]
     return (

time: 912 us -> 765 us (0.84)
  waiting for transfers between devices: 409 us -> 294 us
  local copies, waits for them, and re-layouts: 122 us -> 83 us
  Pallas kernels: 145 us -> 169 us
  other arithmetic: 68 us -> 55.2 us
  matrix products: 59.6 us -> 50.4 us
    ppermute x79 -> x83, waiting for transfers between devices: 400 us -> 267 us  [swap(): return lax.ppermute(v, name, [(0, 1), (1, 0)])]
    pallas_call x3 -> x6, Pallas kernels: 64.7 us -> 89.2 us  [the longest x1 46 us: feed_forward(): pl.pallas_call(ff_kernel, grid=(4,), in_specs=[once(v) for v in pieces] +...]
    all_to_all x4 -> x5, waiting for transfers between devices: 6.42 us -> 27.2 us  [exchange(): return lax.all_to_all(v, tp, split_axis=0, concat_axis=0, tiled=True)]
    reshape x6 -> x0, local copies, waits for them, and re-layouts: 19.4 us -> none  [the longest x5 16 us: shard_order(): return v.reshape(v.shape[0], 2, 2, 2, -1).swapaxes(2, 3).reshape(v.shape)]
    unnamed x201 -> x217, local copies, waits for them, and re-layouts: 64 us -> 50.3 us
    dot_general x2 -> x0, matrix products: 13.5 us -> none  [the longest x1 9.02 us: dot32(): return jnp.dot(one, two, preferred_element_type=F32)]
    all_to_all x4 -> x5, starting transfers between devices: 15.3 us -> 21 us  [exchange(): return lax.all_to_all(v, tp, split_axis=0, concat_axis=0, tiled=True)]
    ppermute x79 -> x83, starting transfers between devices: 71.1 us -> 65.9 us  [swap(): return lax.ppermute(v, name, [(0, 1), (1, 0)])]
  transfers between devices with their start and end apart: 88 -> 93, of which waited for: 32 -> 36; matrix products, arithmetic and copies ran while one was open for 21% -> 20% of each run, Pallas kernels for 6% -> 16%
where the time goes in v4:
time: 765 us; the launch traced here: 756 us
  waiting for transfers between devices  294 us (38%)
  Pallas kernels  169 us (22%)
  starting transfers between devices  87.9 us (11%)
  local copies, waits for them, and re-layouts  83 us (11%)
  other arithmetic  55.2 us (7%)
  matrix products  50.4 us (7%)
  between operations  15.8 us (2%)
    ppermute x83, waiting for transfers between devices, swap(): return lax.ppermute(v, name, [(0, 1), (1, 0)])  267 us
    ppermute x83, starting transfers between devices, swap(): return lax.ppermute(v, name, [(0, 1), (1, 0)])  65.9 us
    dot_general x5, matrix products, row_contract(): lax.dot_general(left, right, (((0,), (0,)), ((), ())), preferred_element_...  50.4 us
    unnamed x217, local copies, waits for them, and re-layouts  50.3 us
    pallas_call x1, Pallas kernels, feed_forward(): pl.pallas_call(ff_kernel, grid=(4,), in_specs=[once(v) for v in pieces] +...  46 us
    pallas_call x3, Pallas kernels, product_blocks(): pl.pallas_call(functools.partial(blocks_kernel, flip), grid=(4,), in_spec...  30.6 us
    pallas_call x1, Pallas kernels, rec_backward(): pl.pallas_call(rec_bwd_kernel, grid_spec=pltpu.PrefetchScalarGridSpec(num...  28.2 us
    all_to_all x5, waiting for transfers between devices, exchange(): return lax.all_to_all(v, tp, split_axis=0, concat_axis=0, tiled=True)  27.2 us
  transfers between devices with their start and end apart: 93, of which 36 were waited for; matrix products, arithmetic and copies ran while one was open for 20% of the time, Pallas kernels for 16%

profile of v4, /device:TPU:0, one launch (start us, length us, event | category | flops | bytes accessed | tf_op | source)
XLA Modules:
  0.0 755.7 jit_solution(14327180634416431246)
XLA Ops:
  11.3 5.2 all-to-all-start
  21.6 16.6 %collective-permute-done.7 = bf16[80,2432]{1,0:T(8,128)(2,1)S(1)} collective-permute-done((bf16[80,2432]{1,0:T(8,128)(2,1)S(1)}, bf16[80,2432]{1,0:T(8,128)(2,1)S(1)}, u32[]{:S(2)}, u32[]{:S(2)}) %collective-permute-start.7) | collective-permute-done | bytes 389152 | tf_op jit(solution)/shard_map/ppermute | solution.py:342
  39.9 3.0 collective-permute-start.9
  43.9 39.4 %collective-permute-done.11 = bf16[80,2432]{1,0:T(8,128)(2,1)S(1)} collective-permute-done((bf16[80,2432]{1,0:T(8,128)(2,1)}, bf16[80,2432]{1,0:T(8,128)(2,1)S(1)}, u32[]{:S(2)}, u32[]{:S(2)}) %collective-permute-start.11) | collective-permute-done | bytes 389152 | tf_op jit(solution)/shard_map/ppermute | solution.py:342
  87.9 13.8 %collective-permute-done.12 = bf16[512,768]{1,0:T(8,128)(2,1)} collective-permute-done((bf16[512,768]{1,0:T(8,128)(2,1)S(1)}, bf16[512,768]{1,0:T(8,128)(2,1)}, u32[]{:S(2)}, u32[]{:S(2)}) %collective-permute-start.12) | collective-permute-done | bytes 786464 | tf_op jit(solution)/shard_map/ppermute | solution.py:342
  102.9 5.6 collective-permute-done.refs_2_
  120.8 4.3 all-to-all-start.1
  136.3 10.1 %all-to-all-done.1 = bf16[8,64,1536]{2,1,0:T(8,128)(2,1)} async-done(((bf16[8,64,1536]{2,1,0:T(8,128)(2,1)}), bf16[8,64,1536]{2,1,0:T(8,128)(2,1)}, u32[]{:S(2)}, u32[]{:S(2)}) %all-to-all-start.1) | async-done | bytes 1572896 | tf_op jit(solution)/shard_map/all_to_all | solution.py:460
  148.4 14.7 %pieces_product.2 = (bf16[2048,2048]{1,0:T(8,128)(2,1)}, f32[2048,768]{1,0:T(8,128)}) custom-call(bf16[256,2048]{1,0:T(8,128)(2,1)S(1)} %fusion.1.refs_0_, bf16[256,2048]{1,0:T(8,128)(2,1)} %collective-permute-done.2.refs_1_, bf16[256,2048]{1,0:T(8,128)(2,1)} %collective-permute-done.refs_2_, bf16[256,2048]{1,0:T(8,128)(2,1)} %collective-permute-done.5.refs_3_, ...), custom_call_target="tpu_custom_call" | custom-call | flops 6442450944 | bytes 26214400 | tf_op jit(solution)/shard_map/pieces_product/pallas_call | solution.py:850
  163.1 2.8 copy-done
  165.9 18.3 %recurrence_forward.1 = (bf16[2048,384]{1,0:T(8,128)(2,1)S(1)}, f32[2048,384]{1,0:T(8,128)S(1)}, f32[2048,384]{1,0:T(8,128)S(1)}, f32[2048,384]{1,0:T(8,128)S(1)}, bf16[2048,384]{1,0:T(8,128)(2,1)S(1)}) custom-call(s32[5]{0:T(128)S(1)} %pad_add_fusion.meta_ref, f32[2048,768]{1,0:T(8,128)S(1)} %copy-done, f32[2048,768]{1,0:T(8,128)S(1)} %copy-done, ...), custom_call_target="tpu_custom_call" | custom-call | flops 1286602752 | bytes 18874368 | tf_op jit(solution)/shard_map/recurrence_forward/pallas_call | solution.py:713
  190.3 9.1 %product_blocks.3 = (bf16[256,2048]{1,0:T(8,128)(2,1)S(1)}, bf16[256,2048]{1,0:T(8,128)(2,1)}, bf16[256,2048]{1,0:T(8,128)(2,1)S(1)}, bf16[256,2048]{1,0:T(8,128...) custom-call(bf16[2048,384]{1,0:T(8,128)(2,1)S(1)} %get-tuple-element, ...), custom_call_target="tpu_custom_call" | custom-call | flops 3221225472 | bytes 11534336 | tf_op jit(solution)/shard_map/product_blocks/pallas_call | solution.py:806
  206.5 6.1 collective-permute-done.27
  228.4 11.2 %collective-permute-done.21 = bf16[128,2048]{1,0:T(8,128)(2,1)S(1)} collective-permute-done((bf16[128,2048]{1,0:T(8,128)(2,1)S(1)}, bf16[128,2048]{1,0:T(8,128)(2,1)S(1)}, u32[]{:S(2)}, u32[]{:S(2)}) %collective-permute-start.21) | collective-permute-done | bytes 524320 | tf_op jit(solution)/shard_map/ppermute | solution.py:342
  241.6 11.5 %collective-permute-done.30 = bf16[128,2048]{1,0:T(8,128)(2,1)S(1)} collective-permute-done((bf16[128,2048]{1,0:T(8,128)(2,1)S(1)}, bf16[128,2048]{1,0:T(8,128)(2,1)S(1)}, u32[]{:S(2)}, u32[]{:S(2)}) %collective-permute-start.30) | collective-permute-done | bytes 524320 | tf_op jit(solution)/shard_map/ppermute | solution.py:342
  267.3 9.9 %collective-permute-done.22 = bf16[256,2048]{1,0:T(8,128)(2,1)S(1)} collective-permute-done((bf16[256,2048]{1,0:T(8,128)(2,1)S(1)}, bf16[256,2048]{1,0:T(8,128)(2,1)S(1)}, u32[]{:S(2)}, u32[]{:S(2)}) %collective-permute-start.22) | collective-permute-done | bytes 1048608 | tf_op jit(solution)/shard_map/ppermute | solution.py:342
  284.5 18.4 %collective-permute-done.24.refs_2_ = bf16[256,2048]{1,0:T(8,128)(2,1)S(1)} collective-permute-done((bf16[256,2048]{1,0:T(8,128)(2,1)S(1)}, bf16[256,2048]{1,0:T(8,128)(2,1)S(1)}, u32[]{:S(2)}, u32[]{:S(2)}) %collective-permute-start.24) | collective-permute-done | bytes 1048608 | tf_op jit(solution)/shard_map/ppermute | solution.py:342
  306.5 12.1 %collective-permute-done.35 = bf16[128,2048]{1,0:T(8,128)(2,1)S(1)} collective-permute-done((bf16[128,2048]{1,0:T(8,128)(2,1)S(1)}, bf16[128,2048]{1,0:T(8,128)(2,1)S(1)}, u32[]{:S(2)}, u32[]{:S(2)}) %collective-permute-start.35) | collective-permute-done | bytes 524320 | tf_op jit(solution)/shard_map/ppermute | solution.py:342
  321.8 46.0 %feed_forward.1 = (bf16[2048,2048]{1,0:T(8,128)(2,1)}, bf16[2048,768]{1,0:T(8,128)(2,1)}, bf16[2048,768]{1,0:T(8,128)(2,1)}, bf16[2048,768]{1,0:T(8,128)(2,1)}, ...) custom-call(bf16[256,2048]{1,0:T(8,128)(2,1)} %copy-done.71, ...), custom_call_target="tpu_custom_call" | custom-call | flops 32212254720 | bytes 52428800 | tf_op jit(solution)/shard_map/feed_forward/pallas_call | solution.py:894
  368.3 12.2 %convolution_convert_fusion = bf16[768,2048]{1,0:T(8,128)(2,1)} fusion(bf16[2048,768]{1,0:T(8,128)(2,1)} %get-tuple-element.236.a_ref, bf16[2048,2048]{1,0:T(8,128)(2,1)} %constant_dynamic-update-slice_fusion.2.refs_8_), kind=kOutput, calls=%fused_computation.5 | convolution fusion | flops 6444023808 | bytes 14680064 | tf_op jit(solution)/shard_map/dot_general | solution.py:58
  389.7 7.9 %collective-permute-done.45 = bf16[128,2048]{1,0:T(8,128)(2,1)S(1)} collective-permute-done((bf16[128,2048]{1,0:T(8,128)(2,1)S(1)}, bf16[128,2048]{1,0:T(8,128)(2,1)S(1)}, u32[]{:S(2)}, u32[]{:S(2)}) %collective-permute-start.45) | collective-permute-done | bytes 524320 | tf_op jit(solution)/shard_map/ppermute | solution.py:342
  403.2 21.9 %collective-permute-done.46 = bf16[256,2048]{1,0:T(8,128)(2,1)S(1)} collective-permute-done((bf16[256,2048]{1,0:T(8,128)(2,1)S(1)}, bf16[256,2048]{1,0:T(8,128)(2,1)S(1)}, u32[]{:S(2)}, u32[]{:S(2)}) %collective-permute-start.46) | collective-permute-done | bytes 1048608 | tf_op jit(solution)/shard_map/ppermute | solution.py:342
  427.5 4.4 fusion.17
  431.9 8.2 %convolution_convert_fusion.3 = bf16[2048,768]{1,0:T(8,128)(2,1)} fusion(bf16[2048,2048]{1,0:T(8,128)(2,1)S(1)} %bitcast.114, bf16[2048,768]{1,0:T(8,128)(2,1)S(1)} %copy-done.100), kind=kOutput, calls=%fused_computation.8 | convolution fusion | flops 6444023808 | bytes 14680064 | tf_op jit(solution)/shard_map/dot_general | solution.py:58
  442.7 21.1 %collective-permute-done.48.refs_2_ = bf16[256,2048]{1,0:T(8,128)(2,1)} collective-permute-done((bf16[256,2048]{1,0:T(8,128)(2,1)}, bf16[256,2048]{1,0:T(8,128)(2,1)}, u32[]{:S(2)}, u32[]{:S(2)}) %collective-permute-start.48) | collective-permute-done | bytes 1048608 | tf_op jit(solution)/shard_map/ppermute | solution.py:342
  472.5 11.4 %convolution_convert_fusion.2 = bf16[2048,768]{1,0:T(8,128)(2,1)} fusion(bf16[2048,2048]{1,0:T(8,128)(2,1)} %get-tuple-element.206, bf16[2048,768]{1,0:T(8,128)(2,1)} %get-tuple-element.213), kind=kOutput, calls=%fused_computation.7 | convolution fusion | flops 6444023808 | bytes 14680064 | tf_op jit(solution)/shard_map/dot_general | solution.py:58
  495.7 9.7 %pieces_product.3 = (bf16[2048,2048]{1,0:T(8,128)(2,1)}, f32[2048,384]{1,0:T(8,128)}) custom-call(bf16[256,2048]{1,0:T(8,128)(2,1)S(1)} %copy-done.24, bf16[256,2048]{1,0:T(8,128)(2,1)S(1)} %copy-done.55, bf16[256,2048]{1,0:T(8,128)(2,1)} %collective-permute-done.48.refs_2_, bf16[256,2048]{1,0:T(8,128)(2,1)} %collective-permute-done.53.refs_3_, ...), custom_call_target="tpu_custom_call" | custom-call | flops 3221225472 | bytes 21495808 | tf_op jit(solution)/shard_map/pieces_product/pallas_call | solution.py:850
  508.6 28.2 %recurrence_backward.1 = (bf16[2048,768]{1,0:T(8,128)(2,1)S(1)}, f32[384,768]{1,0:T(8,128)S(1)}, f32[64,384]{1,0:T(8,128)S(1)}) custom-call(s32[5]{0:T(128)S(1)} %pad_add_fusion.meta_ref, f32[2048,384]{1,0:T(8,128)S(1)} %copy-done.5, f32[2048,768]{1,0:T(8,128)} %get-tuple-element.165.xb_ref.yb_ref, f32[2048,384]{1,0:T(8,128)S(1)} %copy-done.4, ...), custom_call_target="tpu_custom_call" | custom-call | flops 2557476864 | bytes 23592960 | tf_op jit(solution)/shard_map/recurrence_backward/pallas_call | solution.py:739
  541.5 3.8 all-to-all-start.2
  547.3 10.5 %all-to-all-done.2.ga_ref = bf16[8,64,768]{2,1,0:T(8,128)(2,1)S(1)} async-done(((bf16[8,64,768]{2,1,0:T(8,128)(2,1)}), bf16[8,64,768]{2,1,0:T(8,128)(2,1)S(1)}, u32[]{:S(2)}, u32[]{:S(2)}) %all-to-all-start.2) | async-done | bytes 786464 | tf_op jit(solution)/shard_map/all_to_all | solution.py:460
  557.8 10.3 %product_blocks.4 = (bf16[256,2048]{1,0:T(8,128)(2,1)S(1)}, bf16[256,2048]{1,0:T(8,128)(2,1)S(1)}, bf16[256,2048]{1,0:T(8,128)(2,1)S(1)}, bf16[256,2048]{1,0:T(8...) custom-call(bf16[2048,768]{1,0:T(8,128)(2,1)} %copy-done.44, ...), custom_call_target="tpu_custom_call" | custom-call | flops 6442450944 | bytes 14680064 | tf_op jit(solution)/shard_map/product_blocks/pallas_call | solution.py:806
  568.2 11.7 %convolution_convert_fusion.1 = bf16[2048,768]{1,0:T(8,128)(2,1)S(1)} fusion(bf16[2048,2048]{1,0:T(8,128)(2,1)} %get-tuple-element.229, bf16[2048,768]{1,0:T(8,128)(2,1)S(1)} %copy-done.45), kind=kOutput, calls=%fused_computation.6 | convolution fusion | flops 6444023808 | bytes 14680064 | tf_op jit(solution)/shard_map/dot_general | solution.py:58
  584.5 18.6 %collective-permute-done.77 = f32[80,328]{1,0:T(8,128)S(1)} collective-permute-done((f32[80,328]{1,0:T(8,128)S(1)}, f32[80,328]{1,0:T(8,128)S(1)}, u32[]{:S(2)}, u32[]{:S(2)}) %collective-permute-start.77) | collective-permute-done | bytes 104992 | tf_op jit(solution)/shard_map/ppermute | solution.py:342
  603.1 3.7 collective-permute-start.78
  608.2 2.9 collective-permute-done.78
  611.7 4.2 all-to-all-start.4
  618.9 6.9 fusion.23
  626.2 3.4 collective-permute-start.72
  634.7 10.5 %collective-permute-done.60 = bf16[128,2048]{1,0:T(8,128)(2,1)S(1)} collective-permute-done((bf16[128,2048]{1,0:T(8,128)(2,1)S(1)}, bf16[128,2048]{1,0:T(8,128)(2,1)S(1)}, u32[]{:S(2)}, u32[]{:S(2)}) %collective-permute-start.60) | collective-permute-done | bytes 524320 | tf_op jit(solution)/shard_map/ppermute | solution.py:342
  651.9 12.6 %collective-permute-done.72 = bf16[512,768]{1,0:T(8,128)(2,1)S(1)} collective-permute-done((bf16[512,768]{1,0:T(8,128)(2,1)S(1)}, bf16[512,768]{1,0:T(8,128)(2,1)S(1)}, u32[]{:S(2)}, u32[]{:S(2)}) %collective-permute-start.72) | collective-permute-done | bytes 786464 | tf_op jit(solution)/shard_map/ppermute | solution.py:342
  666.9 11.3 %product_blocks.5 = (bf16[256,2048]{1,0:T(8,128)(2,1)S(1)}, bf16[256,2048]{1,0:T(8,128)(2,1)}, bf16[256,2048]{1,0:T(8,128)(2,1)S(1)}, bf16[256,2048]{1,0:T(8,128...) custom-call(bf16[2048,768]{1,0:T(8,128)(2,1)} %get-tuple-element.236, ...), custom_call_target="tpu_custom_call" | custom-call | flops 6442450944 | bytes 14680064 | tf_op jit(solution)/shard_map/product_blocks/pallas_call | solution.py:806
  688.0 10.1 %collective-permute-done.70 = bf16[128,2048]{1,0:T(8,128)(2,1)S(1)} collective-permute-done((bf16[128,2048]{1,0:T(8,128)(2,1)S(1)}, bf16[128,2048]{1,0:T(8,128)(2,1)S(1)}, u32[]{:S(2)}, u32[]{:S(2)}) %collective-permute-start.70) | collective-permute-done | bytes 524320 | tf_op jit(solution)/shard_map/ppermute | solution.py:342
  706.2 2.9 collective-permute-start.82
  709.8 3.5 all-to-all-start.3
  715.3 10.3 %unpack_columns.3 = (f32[64,6144]{1,0:T(8,128)}, f32[64,6144]{1,0:T(8,128)}, f32[64,1]{1,0:T(8,128)S(1)}) custom-call(bf16[8,64,768]{2,1,0:T(8,128)(2,1)S(1)} %all-to-all-done.2.ga_ref, bf16[8,64,768]{2,1,0:T(8,128)(2,1)S(1)} %all-to-all-done.4.gb_ref, bf16[64,6144]{1,0:T(8,128)(2,1)S(1)} %copy-done.7, bf16[64,6144]{1,0:T(8,128)(2,1)S(1)} %copy-done.9, ...), custom_call_target="tpu_custom_call" | custom-call | flops 3145728 | bytes 6291456 | tf_op jit(solution)/shard_map/unpack_columns/pallas_call | solution.py:447
  729.8 6.6 all-to-all-done.3.ga_ref.gb_ref
  737.4 6.4 unpack_columns.2
  744.4 4.3 add_convert_fusion
  (504 shorter events, 202.5 us)
Async XLA Ops:
  11.3 27.6 %all-to-all-start = ((bf16[8,64,768]{2,1,0:T(8,128)(2,1)}), bf16[8,64,768]{2,1,0:T(8,128)(2,1)S(1)}, u32[]{:S(2)}, u32[]{:S(2)}) async-start(bf16[8,64,768]{2,1,0:T(8,128)(2,1)} %pack_columns.2), calls=%async_computation | async-start | bytes 1572864 | tf_op jit(solution)/shard_map/all_to_all | solution.py:460
  16.5 207.4 %all-gather.3.cloned.1.call-start = ((), (), s32[]{:S(2)}) async-start(), calls=%async_computation.8 | async-start | bytes 3932160 | tf_op jit(solution)/shard_map/all_gather | solution.py:967
  17.4 20.8 %collective-permute-start.7 = (bf16[80,2432]{1,0:T(8,128)(2,1)S(1)}, bf16[80,2432]{1,0:T(8,128)(2,1)S(1)}, u32[]{:S(2)}, u32[]{:S(2)}) collective-permute-start(bf16[80,2432]{1,0:T(8,128)(2,1)S(1)} %pad.4), channel_id=1, source_target_pairs={{0,16},{16,0},{1,17},{17,1},{2,18},{18,2},{3,19},{19,3},{4,20},{20... | collective-permute-start | bytes 1167368 | tf_op jit(solution)/shard_map/ppermute | solution.py:342
  38.9 44.3 %collective-permute-start.10 = (bf16[512,768]{1,0:T(8,128)(2,1)S(1)}, bf16[512,768]{1,0:T(8,128)(2,1)S(1)}, u32[]{:S(2)}, u32[]{:S(2)}) collective-permute-start(bf16[512,768]{1,0:T(8,128)(2,1)S(1)} %bitcast.98), channel_id=1, source_target_pairs={{0,8},{8,0},{1,9},{9,1},{2,10},{10,2},{3,11},{11,3},{4,12},{12,4},... | collective-permute-start | bytes 2359304 | tf_op jit(solution)/shard_map/ppermute | solution.py:342
  39.9 43.3 %collective-permute-start.9 = (bf16[512,768]{1,0:T(8,128)(2,1)S(1)}, bf16[512,768]{1,0:T(8,128)(2,1)S(1)}, u32[]{:S(2)}, u32[]{:S(2)}) collective-permute-start(bf16[512,768]{1,0:T(8,128)(2,1)S(1)} %bitcast.99), channel_id=1, source_target_pairs={{0,16},{16,0},{1,17},{17,1},{2,18},{18,2},{3,19},{19,3},{4,20},{20... | collective-permute-start | bytes 2359304 | tf_op jit(solution)/shard_map/ppermute | solution.py:342
  43.0 40.3 %collective-permute-start.11 = (bf16[80,2432]{1,0:T(8,128)(2,1)}, bf16[80,2432]{1,0:T(8,128)(2,1)S(1)}, u32[]{:S(2)}, u32[]{:S(2)}) collective-permute-start(bf16[80,2432]{1,0:T(8,128)(2,1)} %copy-done.80), channel_id=1, source_target_pairs={{0,8},{8,0},{1,9},{9,1},{2,10},{10,2},{3,11},{11,3},{4,12},{12,4},... | collective-permute-start | bytes 1167368 | tf_op jit(solution)/shard_map/ppermute | solution.py:342
  84.7 23.8 %collective-permute-start = (bf16[256,2048]{1,0:T(8,128)(2,1)S(1)}, bf16[256,2048]{1,0:T(8,128)(2,1)}, u32[]{:S(2)}, u32[]{:S(2)}) collective-permute-start(bf16[256,2048]{1,0:T(8,128)(2,1)S(1)} %fusion.1.refs_0_), channel_id=1, source_target_pairs={{0,2},{2,0},{1,3},{3,1},{4,6},{6,4},{5,7},{7,5},{8,10},{10,8},{9,1... | collective-permute-start | bytes 3145736 | tf_op jit(solution)/shard_map/ppermute | solution.py:342
  86.4 23.4 %collective-permute-start.1 = (bf16[256,2048]{1,0:T(8,128)(2,1)S(1)}, bf16[256,2048]{1,0:T(8,128)(2,1)}, u32[]{:S(2)}, u32[]{:S(2)}) collective-permute-start(bf16[256,2048]{1,0:T(8,128)(2,1)S(1)} %fusion.1.refs_0_), channel_id=1, source_target_pairs={{0,4},{4,0},{1,5},{5,1},{2,6},{6,2},{3,7},{7,3},{8,12},{12,8},{9,1... | collective-permute-start | bytes 3145736 | tf_op jit(solution)/shard_map/ppermute | solution.py:342
  87.8 21.9 %collective-permute-start.2 = (bf16[256,2048]{1,0:T(8,128)(2,1)S(1)}, bf16[256,2048]{1,0:T(8,128)(2,1)}, u32[]{:S(2)}, u32[]{:S(2)}) collective-permute-start(bf16[256,2048]{1,0:T(8,128)(2,1)S(1)} %fusion.1.refs_0_), channel_id=1, source_target_pairs={{0,1},{1,0},{2,3},{3,2},{4,5},{5,4},{6,7},{7,6},{8,9},{9,8},{10,11... | collective-permute-start | bytes 3145736 | tf_op jit(solution)/shard_map/ppermute | solution.py:342
  111.7 19.3 %collective-permute-start.5 = (bf16[256,2048]{1,0:T(8,128)(2,1)}, bf16[256,2048]{1,0:T(8,128)(2,1)}, u32[]{:S(2)}, u32[]{:S(2)}) collective-permute-start(bf16[256,2048]{1,0:T(8,128)(2,1)} %collective-permute-done.refs_2_), channel_id=1, source_target_pairs={{0,1},{1,0},{2,3},{3,2},{4,5},{5,4},{6,7},{7,6},{8,9},{9,8},{10,11... | collective-permute-start | bytes 3145736 | tf_op jit(solution)/shard_map/ppermute | solution.py:342
  120.8 25.5 %all-to-all-start.1 = ((bf16[8,64,1536]{2,1,0:T(8,128)(2,1)}), bf16[8,64,1536]{2,1,0:T(8,128)(2,1)}, u32[]{:S(2)}, u32[]{:S(2)}) async-start(bf16[8,64,1536]{2,1,0:T(8,128)(2,1)} %pack_columns.3), calls=%async_computation.1 | async-start | bytes 3145728 | tf_op jit(solution)/shard_map/all_to_all | solution.py:460
  125.1 196.6 %all-gather.5.cloned.1.call-start = ((), (), s32[]{:S(2)}) async-start(), calls=%async_computation.9 | async-start | bytes 7864320 | tf_op jit(solution)/shard_map/all_gather | solution.py:970
  188.8 23.9 %collective-permute-start.27 = (bf16[256,2048]{1,0:T(8,128)(2,1)}, bf16[256,2048]{1,0:T(8,128)(2,1)}, u32[]{:S(2)}, u32[]{:S(2)}) collective-permute-start(bf16[256,2048]{1,0:T(8,128)(2,1)} %param.35), channel_id=1, source_target_pairs={{0,2},{2,0},{1,3},{3,1},{4,6},{6,4},{5,7},{7,5},{8,10},{10,8},{9,1... | collective-permute-start | bytes 3145736 | tf_op jit(solution)/shard_map/ppermute | solution.py:342
  189.4 24.8 %collective-permute-start.28 = (bf16[256,2048]{1,0:T(8,128)(2,1)}, bf16[256,2048]{1,0:T(8,128)(2,1)}, u32[]{:S(2)}, u32[]{:S(2)}) collective-permute-start(bf16[256,2048]{1,0:T(8,128)(2,1)} %param.35), channel_id=1, source_target_pairs={{0,4},{4,0},{1,5},{5,1},{2,6},{6,2},{3,7},{7,3},{8,12},{12,8},{9,1... | collective-permute-start | bytes 3145736 | tf_op jit(solution)/shard_map/ppermute | solution.py:342
  190.3 23.9 %collective-permute-start.29 = (bf16[256,2048]{1,0:T(8,128)(2,1)}, bf16[256,2048]{1,0:T(8,128)(2,1)}, u32[]{:S(2)}, u32[]{:S(2)}) collective-permute-start(bf16[256,2048]{1,0:T(8,128)(2,1)} %param.35), channel_id=1, source_target_pairs={{0,1},{1,0},{2,3},{3,2},{4,5},{5,4},{6,7},{7,6},{8,9},{9,8},{10,11... | collective-permute-start | bytes 3145736 | tf_op jit(solution)/shard_map/ppermute | solution.py:342
  203.8 281.1 %reduce-scatter.4.cloned.1.call-start = ((), (), s32[]{:S(2)}) async-start(), calls=%async_computation.10 | async-start | bytes 3932160 | tf_op jit(solution)/shard_map/reduce_scatter | solution.py:984
  214.2 53.2 %collective-permute-start.16 = (bf16[256,2048]{1,0:T(8,128)(2,1)}, bf16[256,2048]{1,0:T(8,128)(2,1)}, u32[]{:S(2)}, u32[]{:S(2)}) collective-permute-start(bf16[256,2048]{1,0:T(8,128)(2,1)} %get-tuple-element.169), channel_id=1, source_target_pairs={{0,1},{1,0},{2,3},{3,2},{4,5},{5,4},{6,7},{7,6},{8,9},{9,8},{10,11... | collective-permute-start | bytes 3145736 | tf_op jit(solution)/shard_map/ppermute | solution.py:342
  216.1 43.8 %collective-permute-start.32 = (bf16[256,2048]{1,0:T(8,128)(2,1)}, bf16[256,2048]{1,0:T(8,128)(2,1)}, u32[]{:S(2)}, u32[]{:S(2)}) collective-permute-start(bf16[256,2048]{1,0:T(8,128)(2,1)} %collective-permute-done.27), channel_id=1, source_target_pairs={{0,1},{1,0},{2,3},{3,2},{4,5},{5,4},{6,7},{7,6},{8,9},{9,8},{10,11... | collective-permute-start | bytes 3145736 | tf_op jit(solution)/shard_map/ppermute | solution.py:342
  218.5 41.4 %collective-permute-start.33 = (bf16[256,2048]{1,0:T(8,128)(2,1)}, bf16[256,2048]{1,0:T(8,128)(2,1)}, u32[]{:S(2)}, u32[]{:S(2)}) collective-permute-start(bf16[256,2048]{1,0:T(8,128)(2,1)} %collective-permute-done.28), channel_id=1, source_target_pairs={{0,1},{1,0},{2,3},{3,2},{4,5},{5,4},{6,7},{7,6},{8,9},{9,8},{10,11... | collective-permute-start | bytes 3145736 | tf_op jit(solution)/shard_map/ppermute | solution.py:342
  253.2 24.0 %collective-permute-start.22 = (bf16[256,2048]{1,0:T(8,128)(2,1)S(1)}, bf16[256,2048]{1,0:T(8,128)(2,1)S(1)}, u32[]{:S(2)}, u32[]{:S(2)}) collective-permute-start(bf16[256,2048]{1,0:T(8,128)(2,1)S(1)} %pad_maximum_fusion), channel_id=1, source_target_pairs={{0,2},{2,0},{1,3},{3,1},{4,6},{6,4},{5,7},{7,5},{8,10},{10,8},{9,1... | collective-permute-start | bytes 3145736 | tf_op jit(solution)/shard_map/ppermute | solution.py:342
  253.4 23.8 %collective-permute-start.23 = (bf16[256,2048]{1,0:T(8,128)(2,1)S(1)}, bf16[256,2048]{1,0:T(8,128)(2,1)S(1)}, u32[]{:S(2)}, u32[]{:S(2)}) collective-permute-start(bf16[256,2048]{1,0:T(8,128)(2,1)S(1)} %pad_maximum_fusion.1), channel_id=1, source_target_pairs={{0,4},{4,0},{1,5},{5,1},{2,6},{6,2},{3,7},{7,3},{8,12},{12,8},{9,1... | collective-permute-start | bytes 3145736 | tf_op jit(solution)/shard_map/ppermute | solution.py:342
  279.6 23.3 %collective-permute-start.24 = (bf16[256,2048]{1,0:T(8,128)(2,1)S(1)}, bf16[256,2048]{1,0:T(8,128)(2,1)S(1)}, u32[]{:S(2)}, u32[]{:S(2)}) collective-permute-start(bf16[256,2048]{1,0:T(8,128)(2,1)S(1)} %multiply_convert_fusion.refs_0_), channel_id=1, source_target_pairs={{0,2},{2,0},{1,3},{3,1},{4,6},{6,4},{5,7},{7,5},{8,10},{10,8},{9,1... | collective-permute-start | bytes 3145736 | tf_op jit(solution)/shard_map/ppermute | solution.py:342
  281.4 22.7 %collective-permute-start.25 = (bf16[256,2048]{1,0:T(8,128)(2,1)S(1)}, bf16[256,2048]{1,0:T(8,128)(2,1)S(1)}, u32[]{:S(2)}, u32[]{:S(2)}) collective-permute-start(bf16[256,2048]{1,0:T(8,128)(2,1)S(1)} %multiply_convert_fusion.refs_0_), channel_id=1, source_target_pairs={{0,4},{4,0},{1,5},{5,1},{2,6},{6,2},{3,7},{7,3},{8,12},{12,8},{9,1... | collective-permute-start | bytes 3145736 | tf_op jit(solution)/shard_map/ppermute | solution.py:342
  281.7 22.4 %collective-permute-start.26 = (bf16[256,2048]{1,0:T(8,128)(2,1)S(1)}, bf16[256,2048]{1,0:T(8,128)(2,1)S(1)}, u32[]{:S(2)}, u32[]{:S(2)}) collective-permute-start(bf16[256,2048]{1,0:T(8,128)(2,1)S(1)} %multiply_convert_fusion.refs_0_), channel_id=1, source_target_pairs={{0,1},{1,0},{2,3},{3,2},{4,5},{5,4},{6,7},{7,6},{8,9},{9,8},{10,11... | collective-permute-start | bytes 3145736 | tf_op jit(solution)/shard_map/ppermute | solution.py:342
  380.6 22.6 %collective-permute-start.40 = (bf16[256,2048]{1,0:T(8,128)(2,1)}, bf16[256,2048]{1,0:T(8,128)(2,1)}, u32[]{:S(2)}, u32[]{:S(2)}) collective-permute-start(bf16[256,2048]{1,0:T(8,128)(2,1)} %get-tuple-element.197), channel_id=1, source_target_pairs={{0,1},{1,0},{2,3},{3,2},{4,5},{5,4},{6,7},{7,6},{8,9},{9,8},{10,11... | collective-permute-start | bytes 3145736 | tf_op jit(solution)/shard_map/ppermute | solution.py:342
  381.0 160.5 %reduce-scatter.6.cloned.1.call-start = ((), (), s32[]{:S(2)}) async-start(), calls=%async_computation.11 | async-start | bytes 3932160 | tf_op jit(solution)/shard_map/reduce_scatter | solution.py:988
  400.9 24.2 %collective-permute-start.46 = (bf16[256,2048]{1,0:T(8,128)(2,1)S(1)}, bf16[256,2048]{1,0:T(8,128)(2,1)S(1)}, u32[]{:S(2)}, u32[]{:S(2)}) collective-permute-start(bf16[256,2048]{1,0:T(8,128)(2,1)S(1)} %pad_maximum_fusion.3), channel_id=1, source_target_pairs={{0,2},{2,0},{1,3},{3,1},{4,6},{6,4},{5,7},{7,5},{8,10},{10,8},{9,1... | collective-permute-start | bytes 3145736 | tf_op jit(solution)/shard_map/ppermute | solution.py:342
  401.5 23.9 %collective-permute-start.47 = (bf16[256,2048]{1,0:T(8,128)(2,1)S(1)}, bf16[256,2048]{1,0:T(8,128)(2,1)S(1)}, u32[]{:S(2)}, u32[]{:S(2)}) collective-permute-start(bf16[256,2048]{1,0:T(8,128)(2,1)S(1)} %pad_maximum_fusion.4), channel_id=1, source_target_pairs={{0,4},{4,0},{1,5},{5,1},{2,6},{6,2},{3,7},{7,3},{8,12},{12,8},{9,1... | collective-permute-start | bytes 3145736 | tf_op jit(solution)/shard_map/ppermute | solution.py:342
  440.2 171.5 %reduce-scatter.8.cloned.1.call-start = ((), (), s32[]{:S(2)}) async-start(), calls=%async_computation.12 | async-start | bytes 3932160 | tf_op jit(solution)/shard_map/reduce_scatter | solution.py:989
  440.4 23.4 %collective-permute-start.48 = (bf16[256,2048]{1,0:T(8,128)(2,1)}, bf16[256,2048]{1,0:T(8,128)(2,1)}, u32[]{:S(2)}, u32[]{:S(2)}) collective-permute-start(bf16[256,2048]{1,0:T(8,128)(2,1)} %get-tuple-element.301.refs_0_), channel_id=1, source_target_pairs={{0,2},{2,0},{1,3},{3,1},{4,6},{6,4},{5,7},{7,5},{8,10},{10,8},{9,1... | collective-permute-start | bytes 3145736 | tf_op jit(solution)/shard_map/ppermute | solution.py:342
  441.9 23.1 %collective-permute-start.49 = (bf16[256,2048]{1,0:T(8,128)(2,1)}, bf16[256,2048]{1,0:T(8,128)(2,1)}, u32[]{:S(2)}, u32[]{:S(2)}) collective-permute-start(bf16[256,2048]{1,0:T(8,128)(2,1)} %get-tuple-element.301.refs_0_), channel_id=1, source_target_pairs={{0,4},{4,0},{1,5},{5,1},{2,6},{6,2},{3,7},{7,3},{8,12},{12,8},{9,1... | collective-permute-start | bytes 3145736 | tf_op jit(solution)/shard_map/ppermute | solution.py:342
  442.7 22.3 %collective-permute-start.50 = (bf16[256,2048]{1,0:T(8,128)(2,1)}, bf16[256,2048]{1,0:T(8,128)(2,1)S(1)}, u32[]{:S(2)}, u32[]{:S(2)}) collective-permute-start(bf16[256,2048]{1,0:T(8,128)(2,1)} %get-tuple-element.301.refs_0_), channel_id=1, source_target_pairs={{0,1},{1,0},{2,3},{3,2},{4,5},{5,4},{6,7},{7,6},{8,9},{9,8},{10,11... | collective-permute-start | bytes 3145736 | tf_op jit(solution)/shard_map/ppermute | solution.py:342
  581.3 35.8 %collective-permute-start.67 = (bf16[512,768]{1,0:T(8,128)(2,1)}, bf16[512,768]{1,0:T(8,128)(2,1)}, u32[]{:S(2)}, u32[]{:S(2)}) collective-permute-start(bf16[512,768]{1,0:T(8,128)(2,1)} %get-tuple-element.306), channel_id=1, source_target_pairs={{0,8},{8,0},{1,9},{9,1},{2,10},{10,2},{3,11},{11,3},{4,12},{12,4},... | collective-permute-start | bytes 2359304 | tf_op jit(solution)/shard_map/ppermute | solution.py:342
  582.4 20.7 %collective-permute-start.77 = (f32[80,328]{1,0:T(8,128)S(1)}, f32[80,328]{1,0:T(8,128)S(1)}, u32[]{:S(2)}, u32[]{:S(2)}) collective-permute-start(f32[80,328]{1,0:T(8,128)S(1)} %get-tuple-element.324), channel_id=1, source_target_pairs={{0,8},{8,0},{1,9},{9,1},{2,10},{10,2},{3,11},{11,3},{4,12},{12,4},... | collective-permute-start | bytes 314888 | tf_op jit(solution)/shard_map/ppermute | solution.py:342
  583.4 24.7 %collective-permute-start.76 = (f32[80,328]{1,0:T(8,128)S(1)}, f32[80,328]{1,0:T(8,128)S(1)}, u32[]{:S(2)}, u32[]{:S(2)}) collective-permute-start(f32[80,328]{1,0:T(8,128)S(1)} %get-tuple-element.323), channel_id=1, source_target_pairs={{0,8},{8,0},{1,9},{9,1},{2,10},{10,2},{3,11},{11,3},{4,12},{12,4},... | collective-permute-start | bytes 314888 | tf_op jit(solution)/shard_map/ppermute | solution.py:342
  611.7 98.1 %all-to-all-start.4 = ((bf16[8,64,768]{2,1,0:T(8,128)(2,1)}), bf16[8,64,768]{2,1,0:T(8,128)(2,1)S(1)}, u32[]{:S(2)}, u32[]{:S(2)}) async-start(bf16[8,64,768]{2,1,0:T(8,128)(2,1)} %bitcast.104), calls=%async_computation.7 | async-start | bytes 1572864 | tf_op jit(solution)/shard_map/all_to_all | solution.py:460
  615.9 35.9 %collective-permute-start.71 = (bf16[512,768]{1,0:T(8,128)(2,1)}, bf16[512,768]{1,0:T(8,128)(2,1)S(1)}, u32[]{:S(2)}, u32[]{:S(2)}) collective-permute-start(bf16[512,768]{1,0:T(8,128)(2,1)} %get-tuple-element.305), channel_id=1, source_target_pairs={{0,8},{8,0},{1,9},{9,1},{2,10},{10,2},{3,11},{11,3},{4,12},{12,4},... | collective-permute-start | bytes 2359304 | tf_op jit(solution)/shard_map/ppermute | solution.py:342
  617.1 61.7 %collective-permute-start.64 = (bf16[256,2048]{1,0:T(8,128)(2,1)}, bf16[256,2048]{1,0:T(8,128)(2,1)S(1)}, u32[]{:S(2)}, u32[]{:S(2)}) collective-permute-start(bf16[256,2048]{1,0:T(8,128)(2,1)} %copy-done.50), channel_id=1, source_target_pairs={{0,1},{1,0},{2,3},{3,2},{4,5},{5,4},{6,7},{7,6},{8,9},{9,8},{10,11... | collective-permute-start | bytes 3145736 | tf_op jit(solution)/shard_map/ppermute | solution.py:342
  626.2 38.3 %collective-permute-start.72 = (bf16[512,768]{1,0:T(8,128)(2,1)S(1)}, bf16[512,768]{1,0:T(8,128)(2,1)S(1)}, u32[]{:S(2)}, u32[]{:S(2)}) collective-permute-start(bf16[512,768]{1,0:T(8,128)(2,1)S(1)} %fusion.9), channel_id=1, source_target_pairs={{0,16},{16,0},{1,17},{17,1},{2,18},{18,2},{3,19},{19,3},{4,20},{20... | collective-permute-start | bytes 2359304 | tf_op jit(solution)/shard_map/ppermute | solution.py:342
  648.5 29.7 %collective-permute-start.65 = (bf16[256,2048]{1,0:T(8,128)(2,1)S(1)}, bf16[256,2048]{1,0:T(8,128)(2,1)S(1)}, u32[]{:S(2)}, u32[]{:S(2)}) collective-permute-start(bf16[256,2048]{1,0:T(8,128)(2,1)S(1)} %pad_maximum_fusion.5), channel_id=1, source_target_pairs={{0,2},{2,0},{1,3},{3,1},{4,6},{6,4},{5,7},{7,5},{8,10},{10,8},{9,1... | collective-permute-start | bytes 3145736 | tf_op jit(solution)/shard_map/ppermute | solution.py:342
  649.5 28.8 %collective-permute-start.66 = (bf16[256,2048]{1,0:T(8,128)(2,1)S(1)}, bf16[256,2048]{1,0:T(8,128)(2,1)S(1)}, u32[]{:S(2)}, u32[]{:S(2)}) collective-permute-start(bf16[256,2048]{1,0:T(8,128)(2,1)S(1)} %pad_maximum_fusion.6), channel_id=1, source_target_pairs={{0,4},{4,0},{1,5},{5,1},{2,6},{6,2},{3,7},{7,3},{8,12},{12,8},{9,1... | collective-permute-start | bytes 3145736 | tf_op jit(solution)/shard_map/ppermute | solution.py:342
  651.9 52.6 %collective-permute-start.81 = (bf16[80,2048]{1,0:T(8,128)(2,1)}, bf16[80,2048]{1,0:T(8,128)(2,1)}, u32[]{:S(2)}, u32[]{:S(2)}) collective-permute-start(bf16[80,2048]{1,0:T(8,128)(2,1)} %get-tuple-element.308), channel_id=1, source_target_pairs={{0,8},{8,0},{1,9},{9,1},{2,10},{10,2},{3,11},{11,3},{4,12},{12,4},... | collective-permute-start | bytes 983048 | tf_op jit(solution)/shard_map/ppermute | solution.py:342
  664.5 63.2 %collective-permute-start.80 = (bf16[80,2048]{1,0:T(8,128)(2,1)}, bf16[80,2048]{1,0:T(8,128)(2,1)}, u32[]{:S(2)}, u32[]{:S(2)}) collective-permute-start(bf16[80,2048]{1,0:T(8,128)(2,1)} %get-tuple-element.307), channel_id=1, source_target_pairs={{0,8},{8,0},{1,9},{9,1},{2,10},{10,2},{3,11},{11,3},{4,12},{12,4},... | collective-permute-start | bytes 983048 | tf_op jit(solution)/shard_map/ppermute | solution.py:342
  683.1 61.3 %collective-permute-start.61 = (bf16[256,2048]{1,0:T(8,128)(2,1)}, bf16[256,2048]{1,0:T(8,128)(2,1)}, u32[]{:S(2)}, u32[]{:S(2)}) collective-permute-start(bf16[256,2048]{1,0:T(8,128)(2,1)} %get-tuple-element.238), channel_id=1, source_target_pairs={{0,1},{1,0},{2,3},{3,2},{4,5},{5,4},{6,7},{7,6},{8,9},{9,8},{10,11... | collective-permute-start | bytes 3145736 | tf_op jit(solution)/shard_map/ppermute | solution.py:342
  702.4 42.0 %collective-permute-start.73 = (bf16[256,2048]{1,0:T(8,128)(2,1)}, bf16[256,2048]{1,0:T(8,128)(2,1)}, u32[]{:S(2)}, u32[]{:S(2)}) collective-permute-start(bf16[256,2048]{1,0:T(8,128)(2,1)} %pad_maximum_fusion.7), channel_id=1, source_target_pairs={{0,2},{2,0},{1,3},{3,1},{4,6},{6,4},{5,7},{7,5},{8,10},{10,8},{9,1... | collective-permute-start | bytes 3145736 | tf_op jit(solution)/shard_map/ppermute | solution.py:342
  702.7 41.7 %collective-permute-start.74 = (bf16[256,2048]{1,0:T(8,128)(2,1)}, bf16[256,2048]{1,0:T(8,128)(2,1)}, u32[]{:S(2)}, u32[]{:S(2)}) collective-permute-start(bf16[256,2048]{1,0:T(8,128)(2,1)} %pad_maximum_fusion.8), channel_id=1, source_target_pairs={{0,4},{4,0},{1,5},{5,1},{2,6},{6,2},{3,7},{7,3},{8,12},{12,8},{9,1... | collective-permute-start | bytes 3145736 | tf_op jit(solution)/shard_map/ppermute | solution.py:342
  706.2 21.5 %collective-permute-start.82 = (bf16[80,2048]{1,0:T(8,128)(2,1)}, bf16[80,2048]{1,0:T(8,128)(2,1)}, u32[]{:S(2)}, u32[]{:S(2)}) collective-permute-start(bf16[80,2048]{1,0:T(8,128)(2,1)} %fusion.10), channel_id=1, source_target_pairs={{0,16},{16,0},{1,17},{17,1},{2,18},{18,2},{3,19},{19,3},{4,20},{20... | collective-permute-start | bytes 983048 | tf_op jit(solution)/shard_map/ppermute | solution.py:342
  709.8 26.6 %all-to-all-start.3 = ((bf16[8,64,768]{2,1,0:T(8,128)(2,1)}), bf16[8,64,768]{2,1,0:T(8,128)(2,1)S(1)}, u32[]{:S(2)}, u32[]{:S(2)}) async-start(bf16[8,64,768]{2,1,0:T(8,128)(2,1)} %bitcast.101), calls=%async_computation.6 | async-start | bytes 1572864 | tf_op jit(solution)/shard_map/all_to_all | solution.py:460
  (150 other events, 1593.2 us)
Sparse Core Ops, SparseCore 0:
  101.8 65.5 all-gather.2
  204.0 117.0 all-gather.4
  381.1 61.4 reduce-scatter.3
  444.8 60.2 reduce-scatter.5
  507.3 60.2 reduce-scatter.7

commit v5 on v4

--- a/solution.py
+++ b/solution.py
@@ -346,23 +346,27 @@
     return (one.astype(F32) + two.astype(F32)).astype(BF16)
 
 
-def act_gather(v, a, b, second=(), third=()):
+def act_gather(v, a, b, second=(), third=(), during=None):
     h = v.shape[0] // 2
     near, from_a, from_b = swap(v, "c"), swap(v, a), swap(v, b)
     from_a, from_b, near = lax.optimization_barrier((from_a, from_b, near) + tuple(second))[:3]
     far0, far1 = swap(from_a[:h], b), swap(from_b[h:], a)
     near_a, near_b = swap(from_a, "c"), swap(from_b, "c")
+    if during is not None:
+        third = tuple(third) + tuple(during(from_a))
     far0, far1, near_a, near_b = lax.optimization_barrier((far0, far1, near_a, near_b) + tuple(third))[:4]
     far = jnp.concatenate([far0, far1], axis=0)
     return [v, near, from_a, near_a, from_b, near_b, far, swap(far, "c")]
 
 
-def act_scatter(blocks, a, b, second=(), third=(), last=None):
+def act_scatter(blocks, a, b, second=(), third=(), during=None, last=None):
     far, to_a, to_b = [add16(blocks[k], swap(blocks[k + 1], "c")) for k in (6, 2, 4)]
     far = after(far, *second)
     own = blocks[0].astype(F32) + swap(blocks[1], "c").astype(F32)
     h = far.shape[0] // 2
     in_b, in_a = swap(far[:h], b), swap(far[h:], a)
+    if during is not None:
+        third = tuple(third) + tuple(during(far))
     to_a = jnp.concatenate([add16(to_a[:h], in_b), to_a[h:]], axis=0)
     to_b = jnp.concatenate([to_b[:h], add16(to_b[h:], in_a)], axis=0)
     to_a, to_b = lax.optimization_barrier((to_a, to_b) + tuple(third))[:2]
@@ -386,16 +390,18 @@
     return out
 
 
-def w_scatter(v, w1, w2):
+def w_scatter(v, w1, w2, hold=()):
     i1, i2 = lax.axis_index(w1), lax.axis_index(w2)
 
     def get(j1, j2):
         return lax.dynamic_slice(v, (j1, j2) + (0,) * (v.ndim - 2), (1, 1) + v.shape[2:])[0, 0]
 
-    other = get(1 - i1, i2).astype(F32) + swap(get(1 - i1, 1 - i2), w2).astype(F32)
-    other = other.astype(v.dtype)
-    own = get(i1, i2).astype(F32) + swap(get(i1, 1 - i2), w2).astype(F32)
-    return own + swap(other, w1).astype(F32), other
+    to_other, to_own = swap(get(1 - i1, 1 - i2), w2), swap(get(i1, 1 - i2), w2)
+    to_other, to_own = lax.optimization_barrier((to_other, to_own) + tuple(hold))[:2]
+    other = (get(1 - i1, i2).astype(F32) + to_other.astype(F32)).astype(v.dtype)
+    own = get(i1, i2).astype(F32) + to_own.astype(F32)
+    received = swap(other, w1)
+    return lambda *late: own + after(received, *late).astype(F32), other
 
 
 def pack_kernel(plan, a_ref, b_ref, gain_ref, out_ref):
@@ -950,7 +956,18 @@
     small = jnp.pad(jnp.concatenate(small, axis=1), ((0, 0), (0, -small_width % 128)))
 
     stacked = w_parts(small, *STACK)
-    wxy_parts = w_parts(after(wxy.reshape(-1, 2 * padded), stacked[1], stacked[2]), *STACK, (stacked[3],))
+    xf = layer_input.astype(F32)
+    scale1 = lax.rsqrt(jnp.mean(xf * xf, axis=-1, keepdims=True) + NORM_EPS)
+    packed_gu = []
+
+    def exchange_units(from_a):
+        packed = pack_columns(ff_plan, 4 * units, w_gate, w_up, gain2)
+        packed_gu.append(exchange(after(packed, from_a), PLANE).reshape(-1, 8 * units))
+        return packed_gu
+
+    xs_pieces = act_gather(after((xf * scale1).astype(BF16), wxy), "x", "y", (), (), exchange_units)
+    packed_gu = packed_gu[0]
+    wxy_parts = w_parts(wxy.reshape(-1, 2 * padded), *STACK, (stacked[1], xs_pieces[2], xs_pieces[4]))
     upper = lax.axis_index("zh") == core
     keep = [jnp.where(upper, stacked[n], stacked[n + 1]) for n in (0, 2)]
     give = [swap(jnp.where(upper, stacked[n + 1], stacked[n]), "c") for n in (0, 2)]
@@ -959,13 +976,8 @@
     lam_all = vec[taps + 3]
     vec = jnp.concatenate([vec[: taps + 1], jax.nn.softplus(-lam_all)[None], vec[taps + 1 : taps + 3]], axis=0)
 
-    xf = layer_input.astype(F32)
-    scale1 = lax.rsqrt(jnp.mean(xf * xf, axis=-1, keepdims=True) + NORM_EPS)
-    xs_pieces = act_gather(after((xf * scale1).astype(BF16), wxy), "x", "y", (), (wxy_parts[3],))
-    packed_gu = after(pack_columns(ff_plan, 4 * units, w_gate, w_up, gain2), xs_pieces[2], wxy_parts[1])
-    packed_gu = exchange(packed_gu, PLANE).reshape(-1, 8 * units)
     wd = lax.all_gather(after(w_down, wxy_parts[3]), STACK, axis=0, tiled=True)
-    wxy_parts = wxy_parts[:3] + [after(wxy_parts[3], packed_gu, wo, gates)]
+    wxy_parts = wxy_parts[:3] + [after(wxy_parts[3], wo, gates)]
     wxy = w_place(wxy_parts, *STACK).reshape(model, -1)
     wgu = lax.all_gather(packed_gu, STACK, axis=0, tiled=True)
     xs_all, xy = pieces_product(xs_pieces, wxy, False)
@@ -977,8 +989,14 @@
     scale2 = lax.rsqrt(jnp.mean(resid * resid, axis=-1, keepdims=True) + NORM_EPS)
     xs2_pieces = act_gather((resid * scale2).astype(BF16), "x", "y", (cot_all,))
     xs2_all, hidden, d_gt, d_up, *blocks_2 = feed_forward(xs2_pieces, cot_all, wgu, wd)
-    d_wd = row_contract(hidden, cot_all).astype(BF16)
-    d_un2 = act_scatter(blocks_2, "x", "y", (), (d_wd,))
+    d_wd = []
+
+    def down_product(far):
+        d_wd.append(row_contract(after(hidden, far), cot_all).astype(BF16))
+        return d_wd
+
+    d_un2 = act_scatter(blocks_2, "x", "y", (), (), down_product)
+    d_wd = d_wd[0]
     d_resid = cot.astype(F32) + norm_back(d_un2, resid, scale2)
     d_mix = d_resid.astype(BF16)
     d_wd = lax.psum_scatter(d_wd, STACK, scatter_dimension=0, tiled=True)
@@ -990,25 +1008,20 @@
 
     d_mix_all, dm = pieces_product(d_mix_pieces, wo, True)
     dxy, d_gates, sums = rec_backward(meta, dm, xy, before, pa, px, xc, vec, gates.T, rows)
-    d_wg = exchange(d_wg.reshape(8, -1, 4 * units), PLANE)
-    blocks_1 = product_blocks(after(dxy, d_wg), wxy, True)
+    blocks_1 = product_blocks(dxy, wxy, True)
+    d_wg = exchange(after(d_wg, blocks_1[0]).reshape(8, -1, 4 * units), PLANE)
     d_wxy = row_contract(xs_all, after(dxy, blocks_1[0])).astype(BF16)
-    d_wxy_sum, sent = w_scatter(d_wxy.reshape(2, 2, model // 4, -1), *STACK)
-    blocks_o = []
+    blocks_o, released = [], []
 
     def output_blocks(marker):
+        released.append(marker)
+        released.extend(w_scatter(d_wxy.reshape(2, 2, model // 4, -1), *STACK, (marker,)))
         blocks_o.extend(product_blocks(after(hidden, marker), wd, False))
-        return sent, blocks_o[0]
-
-    d_un = act_scatter(blocks_1, "x", "y", (d_wxy,), (), output_blocks)
+        return released[2], blocks_o[0]
+
+    d_un = act_scatter(blocks_1, "x", "y", (d_wxy, d_wg), (), None, output_blocks)
     d_input = (d_resid + norm_back(after(d_un, d_wu), xf, scale1)).astype(BF16)
-    d_wxy = d_wxy_sum.astype(BF16)
-    output = (resid + act_scatter(blocks_o, "x", "y", (d_input,), (d_wxy,))).astype(BF16)
-    d_wxy = exchange(d_wxy.reshape(8, -1, 2 * padded), PLANE)
-    d_wx, d_wy, d_gain1 = unpack_columns(rec_plan, d_wxy, None, w_x, w_y, gain1)
-    d_wu = exchange(d_wu.reshape(8, -1, 4 * units), PLANE)
-    d_wg, d_wu, d_gain2 = unpack_columns(ff_plan, d_wg, d_wu, w_gate, w_up, gain2)
-
+    d_wxy = released[1]().astype(BF16)
     def channels_out(v, kind):
         v = v.astype(kind).reshape(2, 2, part, -1)
         size = (2, 1) + v.shape[2:]
@@ -1018,7 +1031,7 @@
         out = lax.dynamic_update_slice(out, keep[None], (core, 0, 0, 0))
         return lax.dynamic_update_slice(out, swap(send, "c")[None], (1 - core, 0, 0, 0))
 
-    d_wo = w_scatter(channels_out(row_contract(after(mixed, sent), d_mix_all)[:channels], BF16), *STACK)[0]
+    d_wo = channels_out(row_contract(after(mixed, released[0]), d_mix_all)[:channels], BF16)
     sums = jnp.sum(sums.reshape(8, 8, padded), axis=1)
     d_lam_part = -jax.nn.sigmoid(-lam_all) * sums[5]
     d_cols = jnp.concatenate([sums[:5], sums[6:8], d_lam_part[None]], axis=0).T
@@ -1031,7 +1044,25 @@
             block = jnp.where(row_block == n, d_gates[:channels, at : at + width], block)
         d_blocks.append(block)
     d_small = jnp.concatenate([d_cols[:channels]] + d_blocks, axis=1)
-    d_small = w_scatter(channels_out(d_small, F32), *STACK)[0]
+    d_small = channels_out(after(d_small, released[0]), F32)
+    ends = []
+
+    def start_channels(far):
+        ends.extend(w_scatter(v, *STACK, (far,))[0] for v in (d_wo, d_small))
+        return ()
+
+    def end_channels(marker):
+        ends.extend(end(marker) for end in ends[:2])
+        return ()
+
+    output = act_scatter(blocks_o, "x", "y", (d_input,), (d_wxy,), start_channels, end_channels)
+    output = (resid + output).astype(BF16)
+    d_wo, d_small = ends[2:]
+    d_wxy = exchange(d_wxy.reshape(8, -1, 2 * padded), PLANE)
+    d_wx, d_wy, d_gain1 = unpack_columns(rec_plan, d_wxy, None, w_x, w_y, gain1)
+    d_wu = exchange(after(d_wu, released[0]).reshape(8, -1, 4 * units), PLANE)
+    d_wg, d_wu, d_gain2 = unpack_columns(ff_plan, d_wg, d_wu, w_gate, w_up, gain2)
+
     d_cw, d_cb, d_br, d_bi, d_lam = d_small[:, :4], d_small[:, 4], d_small[:, 5], d_small[:, 6], d_small[:, 7]
     d_wr, d_wi = d_small[:, 8 : 8 + width], d_small[:, 8 + width : 8 + 2 * width]
     return (

time: 765 us -> 740 us (0.967)
  waiting for transfers between devices: 294 us -> 255 us
  other arithmetic: 55.2 us -> 70.7 us
  local copies, waits for them, and re-layouts: 83 us -> 96 us
  starting transfers between devices: 87.9 us -> 76.9 us
    ppermute x83, waiting for transfers between devices: 267 us -> 238 us  [swap(): return lax.ppermute(v, name, [(0, 1), (1, 0)])]
    convert_element_type x20, other arithmetic: 15.9 us -> 26.8 us  [add16(): return (one.astype(F32) + two.astype(F32)).astype(BF16)]
    all_to_all x5, waiting for transfers between devices: 27.2 us -> 16.9 us  [exchange(): return lax.all_to_all(v, tp, split_axis=0, concat_axis=0, tiled=True)]
    ppermute x83, starting transfers between devices: 65.9 us -> 56.2 us  [swap(): return lax.ppermute(v, name, [(0, 1), (1, 0)])]
    unnamed x217 -> x223, local copies, waits for them, and re-layouts: 50.3 us -> 54.7 us
  transfers between devices with their start and end apart: 93 -> 93, of which waited for: 36 -> 37; matrix products, arithmetic and copies ran while one was open for 20% -> 23% of each run, Pallas kernels for 16% -> 17%
where the time goes in v5:
time: 740 us; the launch traced here: 731 us
  waiting for transfers between devices  255 us (34%)
  Pallas kernels  169 us (23%)
  local copies, waits for them, and re-layouts  96 us (13%)
  starting transfers between devices  76.9 us (10%)
  other arithmetic  70.7 us (10%)
  matrix products  46.7 us (6%)
  between operations  15.8 us (2%)
    ppermute x83, waiting for transfers between devices, swap(): return lax.ppermute(v, name, [(0, 1), (1, 0)])  238 us
    ppermute x83, starting transfers between devices, swap(): return lax.ppermute(v, name, [(0, 1), (1, 0)])  56.2 us
    unnamed x223, local copies, waits for them, and re-layouts  54.7 us
    dot_general x5, matrix products, row_contract(): lax.dot_general(left, right, (((0,), (0,)), ((), ())), preferred_element_...  46.7 us
    pallas_call x1, Pallas kernels, feed_forward(): pl.pallas_call(ff_kernel, grid=(4,), in_specs=[once(v) for v in pieces] +...  46 us
    pallas_call x3, Pallas kernels, product_blocks(): pl.pallas_call(functools.partial(blocks_kernel, flip), grid=(4,), in_spec...  32.3 us
    pallas_call x1, Pallas kernels, rec_backward(): pl.pallas_call(rec_bwd_kernel, grid_spec=pltpu.PrefetchScalarGridSpec(num...  28.1 us
    convert_element_type x20, other arithmetic, add16(): return (one.astype(F32) + two.astype(F32)).astype(BF16)  26.8 us
  transfers between devices with their start and end apart: 93, of which 37 were waited for; matrix products, arithmetic and copies ran while one was open for 23% of the time, Pallas kernels for 17%

profile of v5, /device:TPU:0, one launch (start us, length us, event | category | flops | bytes accessed | tf_op | source)
XLA Modules:
  0.0 730.7 jit_solution(11926222848587505057)
XLA Ops:
  17.0 4.0 collective-permute-start.10
  22.6 4.2 all-to-all-start
  29.2 10.3 %all-to-all-done = bf16[8,64,768]{2,1,0:T(8,128)(2,1)} async-done(((bf16[8,64,768]{2,1,0:T(8,128)(2,1)}), bf16[8,64,768]{2,1,0:T(8,128)(2,1)}, u32[]{:S(2)}, u32[]{:S(2)}) %all-to-all-start) | async-done | bytes 786464 | tf_op jit(solution)/shard_map/all_to_all | solution.py:466
  42.8 20.6 %collective-permute-done.refs_2_ = bf16[256,2048]{1,0:T(8,128)(2,1)} collective-permute-done((bf16[256,2048]{1,0:T(8,128)(2,1)S(1)}, bf16[256,2048]{1,0:T(8,128)(2,1)}, u32[]{:S(2)}, u32[]{:S(2)}) %collective-permute-start) | collective-permute-done | bytes 1048608 | tf_op jit(solution)/shard_map/ppermute | solution.py:342
  66.8 11.7 %collective-permute-done.8 = bf16[512,768]{1,0:T(8,128)(2,1)} collective-permute-done((bf16[512,768]{1,0:T(8,128)(2,1)}, bf16[512,768]{1,0:T(8,128)(2,1)}, u32[]{:S(2)}, u32[]{:S(2)}) %collective-permute-start.8) | collective-permute-done | bytes 786464 | tf_op jit(solution)/shard_map/ppermute | solution.py:342
  82.4 4.3 all-to-all-start.1
  86.7 12.5 %collective-permute-done.12 = bf16[512,768]{1,0:T(8,128)(2,1)} collective-permute-done((bf16[512,768]{1,0:T(8,128)(2,1)}, bf16[512,768]{1,0:T(8,128)(2,1)}, u32[]{:S(2)}, u32[]{:S(2)}) %collective-permute-start.12) | collective-permute-done | bytes 786464 | tf_op jit(solution)/shard_map/ppermute | solution.py:342
  115.2 4.1 collective-permute-done.3
  128.3 14.1 %pieces_product.2 = (bf16[2048,2048]{1,0:T(8,128)(2,1)}, f32[2048,768]{1,0:T(8,128)}) custom-call(bf16[256,2048]{1,0:T(8,128)(2,1)S(1)} %fusion.1.refs_0_, bf16[256,2048]{1,0:T(8,128)(2,1)S(1)} %copy-done.57, bf16[256,2048]{1,0:T(8,128)(2,1)} %collective-permute-done.refs_2_, bf16[256,2048]{1,0:T(8,128)(2,1)} %collective-permute-done.5.refs_3_, ...), custom_call_target="tpu_custom_call" | custom-call | flops 6442450944 | bytes 26214400 | tf_op jit(solution)/shard_map/pieces_product/pallas_call | solution.py:856
  142.4 2.8 copy-done
  145.2 18.4 %recurrence_forward.1 = (bf16[2048,384]{1,0:T(8,128)(2,1)S(1)}, f32[2048,384]{1,0:T(8,128)S(1)}, f32[2048,384]{1,0:T(8,128)S(1)}, f32[2048,384]{1,0:T(8,128)S(1)}, bf16[2048,384]{1,0:T(8,128)(2,1)S(1)}) custom-call(s32[5]{0:T(128)S(1)} %pad_add_fusion.meta_ref, f32[2048,768]{1,0:T(8,128)S(1)} %copy-done, f32[2048,768]{1,0:T(8,128)S(1)} %copy-done, ...), custom_call_target="tpu_custom_call" | custom-call | flops 1286602752 | bytes 18874368 | tf_op jit(solution)/shard_map/recurrence_forward/pallas_call | solution.py:719
  170.6 9.1 %product_blocks.3 = (bf16[256,2048]{1,0:T(8,128)(2,1)S(1)}, bf16[256,2048]{1,0:T(8,128)(2,1)}, bf16[256,2048]{1,0:T(8,128)(2,1)S(1)}, bf16[256,2048]{1,0:T(8,128...) custom-call(bf16[2048,384]{1,0:T(8,128)(2,1)S(1)} %get-tuple-element, ...), custom_call_target="tpu_custom_call" | custom-call | flops 3221225472 | bytes 11534336 | tf_op jit(solution)/shard_map/product_blocks/pallas_call | solution.py:812
  186.8 7.2 collective-permute-done.27
  199.6 2.6 add_convert_fusion.10
  202.2 2.6 add_convert_fusion.11
  209.7 10.7 %collective-permute-done.21 = bf16[128,2048]{1,0:T(8,128)(2,1)S(1)} collective-permute-done((bf16[128,2048]{1,0:T(8,128)(2,1)S(1)}, bf16[128,2048]{1,0:T(8,128)(2,1)S(1)}, u32[]{:S(2)}, u32[]{:S(2)}) %collective-permute-start.21) | collective-permute-done | bytes 524320 | tf_op jit(solution)/shard_map/ppermute | solution.py:342
  222.5 11.5 %collective-permute-done.30 = bf16[128,2048]{1,0:T(8,128)(2,1)S(1)} collective-permute-done((bf16[128,2048]{1,0:T(8,128)(2,1)S(1)}, bf16[128,2048]{1,0:T(8,128)(2,1)S(1)}, u32[]{:S(2)}, u32[]{:S(2)}) %collective-permute-start.30) | collective-permute-done | bytes 524320 | tf_op jit(solution)/shard_map/ppermute | solution.py:342
  245.4 2.7 pad_maximum_fusion.2
  248.1 10.0 %collective-permute-done.22 = bf16[256,2048]{1,0:T(8,128)(2,1)S(1)} collective-permute-done((bf16[256,2048]{1,0:T(8,128)(2,1)S(1)}, bf16[256,2048]{1,0:T(8,128)(2,1)S(1)}, u32[]{:S(2)}, u32[]{:S(2)}) %collective-permute-start.22) | collective-permute-done | bytes 1048608 | tf_op jit(solution)/shard_map/ppermute | solution.py:342
  266.0 18.0 %collective-permute-done.24.refs_2_ = bf16[256,2048]{1,0:T(8,128)(2,1)S(1)} collective-permute-done((bf16[256,2048]{1,0:T(8,128)(2,1)S(1)}, bf16[256,2048]{1,0:T(8,128)(2,1)S(1)}, u32[]{:S(2)}, u32[]{:S(2)}) %collective-permute-start.24) | collective-permute-done | bytes 1048608 | tf_op jit(solution)/shard_map/ppermute | solution.py:342
  287.6 12.0 %collective-permute-done.35 = bf16[128,2048]{1,0:T(8,128)(2,1)S(1)} collective-permute-done((bf16[128,2048]{1,0:T(8,128)(2,1)S(1)}, bf16[128,2048]{1,0:T(8,128)(2,1)S(1)}, u32[]{:S(2)}, u32[]{:S(2)}) %collective-permute-start.35) | collective-permute-done | bytes 524320 | tf_op jit(solution)/shard_map/ppermute | solution.py:342
  303.2 46.0 %feed_forward.1 = (bf16[2048,2048]{1,0:T(8,128)(2,1)}, bf16[2048,768]{1,0:T(8,128)(2,1)}, bf16[2048,768]{1,0:T(8,128)(2,1)}, bf16[2048,768]{1,0:T(8,128)(2,1)}, ...) custom-call(bf16[256,2048]{1,0:T(8,128)(2,1)} %copy-done.84, ...), custom_call_target="tpu_custom_call" | custom-call | flops 32212254720 | bytes 52428800 | tf_op jit(solution)/shard_map/feed_forward/pallas_call | solution.py:900
  358.2 10.4 %convolution_convert_fusion = bf16[768,2048]{1,0:T(8,128)(2,1)} fusion(bf16[2048,768]{1,0:T(8,128)(2,1)S(1)} %copy-done.102, bf16[2048,2048]{1,0:T(8,128)(2,1)} %constant_dynamic-update-slice_fusion.2.refs_8_), kind=kOutput, calls=%fused_computation.5 | convolution fusion | flops 6444023808 | bytes 14680064 | tf_op jit(solution)/shard_map/dot_general | solution.py:58
  376.2 22.8 %collective-permute-done.46 = bf16[256,2048]{1,0:T(8,128)(2,1)S(1)} collective-permute-done((bf16[256,2048]{1,0:T(8,128)(2,1)S(1)}, bf16[256,2048]{1,0:T(8,128)(2,1)S(1)}, u32[]{:S(2)}, u32[]{:S(2)}) %collective-permute-start.46) | collective-permute-done | bytes 1048608 | tf_op jit(solution)/shard_map/ppermute | solution.py:342
  401.9 4.4 fusion.17
  406.2 8.5 %convolution_convert_fusion.3 = bf16[2048,768]{1,0:T(8,128)(2,1)} fusion(bf16[2048,2048]{1,0:T(8,128)(2,1)S(1)} %bitcast.112, bf16[2048,768]{1,0:T(8,128)(2,1)S(1)} %copy-done.103), kind=kOutput, calls=%fused_computation.8 | convolution fusion | flops 6444023808 | bytes 14680064 | tf_op jit(solution)/shard_map/dot_general | solution.py:58
  417.0 22.0 %collective-permute-done.48.refs_2_ = bf16[256,2048]{1,0:T(8,128)(2,1)} collective-permute-done((bf16[256,2048]{1,0:T(8,128)(2,1)}, bf16[256,2048]{1,0:T(8,128)(2,1)}, u32[]{:S(2)}, u32[]{:S(2)}) %collective-permute-start.48) | collective-permute-done | bytes 1048608 | tf_op jit(solution)/shard_map/ppermute | solution.py:342
  447.3 11.4 %convolution_convert_fusion.2 = bf16[2048,768]{1,0:T(8,128)(2,1)} fusion(bf16[2048,2048]{1,0:T(8,128)(2,1)} %get-tuple-element.218, bf16[2048,768]{1,0:T(8,128)(2,1)} %get-tuple-element.225), kind=kOutput, calls=%fused_computation.7 | convolution fusion | flops 6444023808 | bytes 14680064 | tf_op jit(solution)/shard_map/dot_general | solution.py:58
  465.8 2.6 convert_element_type.424
  469.9 9.7 %pieces_product.3 = (bf16[2048,2048]{1,0:T(8,128)(2,1)}, f32[2048,384]{1,0:T(8,128)}) custom-call(bf16[256,2048]{1,0:T(8,128)(2,1)S(1)} %copy-done.29, bf16[256,2048]{1,0:T(8,128)(2,1)S(1)} %copy-done.61, bf16[256,2048]{1,0:T(8,128)(2,1)} %collective-permute-done.48.refs_2_, bf16[256,2048]{1,0:T(8,128)(2,1)} %collective-permute-done.53.refs_3_, ...), custom_call_target="tpu_custom_call" | custom-call | flops 3221225472 | bytes 21495808 | tf_op jit(solution)/shard_map/pieces_product/pallas_call | solution.py:856
  482.9 28.1 %recurrence_backward.1 = (bf16[2048,768]{1,0:T(8,128)(2,1)S(1)}, f32[384,768]{1,0:T(8,128)S(1)}, f32[64,384]{1,0:T(8,128)S(1)}) custom-call(s32[5]{0:T(128)S(1)} %pad_add_fusion.meta_ref, f32[2048,384]{1,0:T(8,128)S(1)} %copy-done.5, f32[2048,768]{1,0:T(8,128)} %get-tuple-element.176.xb_ref.yb_ref, f32[2048,384]{1,0:T(8,128)S(1)} %copy-done.4, ...), custom_call_target="tpu_custom_call" | custom-call | flops 2557476864 | bytes 23592960 | tf_op jit(solution)/shard_map/recurrence_backward/pallas_call | solution.py:745
  512.8 12.3 %product_blocks.4 = (bf16[256,2048]{1,0:T(8,128)(2,1)S(1)}, bf16[256,2048]{1,0:T(8,128)(2,1)S(1)}, bf16[256,2048]{1,0:T(8,128)(2,1)S(1)}, bf16[256,2048]{1,0:T(8...) custom-call(bf16[2048,768]{1,0:T(8,128)(2,1)} %copy-done.47, ...), custom_call_target="tpu_custom_call" | custom-call | flops 6442450944 | bytes 14680064 | tf_op jit(solution)/shard_map/product_blocks/pallas_call | solution.py:812
  526.1 9.4 %convolution_convert_fusion.1 = bf16[2048,768]{1,0:T(8,128)(2,1)S(1)} fusion(bf16[2048,2048]{1,0:T(8,128)(2,1)} %get-tuple-element.240, bf16[2048,768]{1,0:T(8,128)(2,1)S(1)} %copy-done.48), kind=kOutput, calls=%fused_computation.6 | convolution fusion | flops 6444023808 | bytes 14680064 | tf_op jit(solution)/shard_map/dot_general | solution.py:58
  542.2 3.6 all-to-all-start.2
  549.0 2.6 add_convert_fusion.5
  551.6 6.6 all-to-all-done.2.ga_ref
  562.5 9.8 %collective-permute-done.60 = bf16[128,2048]{1,0:T(8,128)(2,1)S(1)} collective-permute-done((bf16[128,2048]{1,0:T(8,128)(2,1)S(1)}, bf16[128,2048]{1,0:T(8,128)(2,1)S(1)}, u32[]{:S(2)}, u32[]{:S(2)}) %collective-permute-start.60) | collective-permute-done | bytes 524320 | tf_op jit(solution)/shard_map/ppermute | solution.py:342
  577.2 3.8 all-to-all-start.4
  581.0 6.9 fusion.23
  592.9 10.9 %product_blocks.5 = (bf16[256,2048]{1,0:T(8,128)(2,1)S(1)}, bf16[256,2048]{1,0:T(8,128)(2,1)S(1)}, bf16[256,2048]{1,0:T(8,128)(2,1)S(1)}, bf16[256,2048]{1,0:T(8...) custom-call(bf16[2048,768]{1,0:T(8,128)(2,1)} %get-tuple-element.248, ...), custom_call_target="tpu_custom_call" | custom-call | flops 6442450944 | bytes 14680064 | tf_op jit(solution)/shard_map/product_blocks/pallas_call | solution.py:812
  611.4 10.3 %unpack_columns.3 = (f32[64,6144]{1,0:T(8,128)}, f32[64,6144]{1,0:T(8,128)}, f32[64,1]{1,0:T(8,128)S(1)}) custom-call(bf16[8,64,768]{2,1,0:T(8,128)(2,1)S(1)} %all-to-all-done.2.ga_ref, bf16[8,64,768]{2,1,0:T(8,128)(2,1)S(1)} %all-to-all-done.4.gb_ref, bf16[64,6144]{1,0:T(8,128)(2,1)S(1)} %copy-done.7, bf16[64,6144]{1,0:T(8,128)(2,1)S(1)} %copy-done.9, ...), custom_call_target="tpu_custom_call" | custom-call | flops 3145728 | bytes 6291456 | tf_op jit(solution)/shard_map/unpack_columns/pallas_call | solution.py:453
  622.3 22.9 %collective-permute-done.72 = bf16[512,768]{1,0:T(8,128)(2,1)} collective-permute-done((bf16[512,768]{1,0:T(8,128)(2,1)}, bf16[512,768]{1,0:T(8,128)(2,1)}, u32[]{:S(2)}, u32[]{:S(2)}) %collective-permute-start.72) | collective-permute-done | bytes 786464 | tf_op jit(solution)/shard_map/ppermute | solution.py:342
  645.2 3.0 fusion.8
  648.1 3.8 all-to-all-start.3
  663.3 6.9 collective-permute-done.81
  683.4 6.4 unpack_columns.2
  700.7 17.2 %collective-permute-done.73 = bf16[256,2048]{1,0:T(8,128)(2,1)} collective-permute-done((bf16[256,2048]{1,0:T(8,128)(2,1)}, bf16[256,2048]{1,0:T(8,128)(2,1)}, u32[]{:S(2)}, u32[]{:S(2)}) %collective-permute-start.73) | collective-permute-done | bytes 1048608 | tf_op jit(solution)/shard_map/ppermute | solution.py:342
  720.0 3.6 add_convert_fusion
  (513 shorter events, 215.5 us)
Async XLA Ops:
  17.0 23.6 %collective-permute-start.10 = (bf16[80,2432]{1,0:T(8,128)(2,1)}, bf16[80,2432]{1,0:T(8,128)(2,1)}, u32[]{:S(2)}, u32[]{:S(2)}) collective-permute-start(bf16[80,2432]{1,0:T(8,128)(2,1)} %pad.4), channel_id=1, source_target_pairs={{0,16},{16,0},{1,17},{17,1},{2,18},{18,2},{3,19},{19,3},{4,20},{20... | collective-permute-start | bytes 1167368 | tf_op jit(solution)/shard_map/ppermute | solution.py:342
  39.5 24.0 %collective-permute-start = (bf16[256,2048]{1,0:T(8,128)(2,1)S(1)}, bf16[256,2048]{1,0:T(8,128)(2,1)}, u32[]{:S(2)}, u32[]{:S(2)}) collective-permute-start(bf16[256,2048]{1,0:T(8,128)(2,1)S(1)} %fusion.1.refs_0_), channel_id=1, source_target_pairs={{0,2},{2,0},{1,3},{3,1},{4,6},{6,4},{5,7},{7,5},{8,10},{10,8},{9,1... | collective-permute-start | bytes 3145736 | tf_op jit(solution)/shard_map/ppermute | solution.py:342
  40.0 24.9 %collective-permute-start.1 = (bf16[256,2048]{1,0:T(8,128)(2,1)S(1)}, bf16[256,2048]{1,0:T(8,128)(2,1)S(1)}, u32[]{:S(2)}, u32[]{:S(2)}) collective-permute-start(bf16[256,2048]{1,0:T(8,128)(2,1)S(1)} %fusion.1.refs_0_), channel_id=1, source_target_pairs={{0,4},{4,0},{1,5},{5,1},{2,6},{6,2},{3,7},{7,3},{8,12},{12,8},{9,1... | collective-permute-start | bytes 3145736 | tf_op jit(solution)/shard_map/ppermute | solution.py:342
  40.6 24.2 %collective-permute-start.2 = (bf16[256,2048]{1,0:T(8,128)(2,1)S(1)}, bf16[256,2048]{1,0:T(8,128)(2,1)S(1)}, u32[]{:S(2)}, u32[]{:S(2)}) collective-permute-start(bf16[256,2048]{1,0:T(8,128)(2,1)S(1)} %fusion.1.refs_0_), channel_id=1, source_target_pairs={{0,1},{1,0},{2,3},{3,2},{4,5},{5,4},{6,7},{7,6},{8,9},{9,8},{10,11... | collective-permute-start | bytes 3145736 | tf_op jit(solution)/shard_map/ppermute | solution.py:342
  40.6 37.9 %collective-permute-start.8 = (bf16[512,768]{1,0:T(8,128)(2,1)}, bf16[512,768]{1,0:T(8,128)(2,1)}, u32[]{:S(2)}, u32[]{:S(2)}) collective-permute-start(bf16[512,768]{1,0:T(8,128)(2,1)} %bitcast.6), channel_id=1, source_target_pairs={{0,16},{16,0},{1,17},{17,1},{2,18},{18,2},{3,19},{19,3},{4,20},{20... | collective-permute-start | bytes 2359304 | tf_op jit(solution)/shard_map/ppermute | solution.py:342
  40.9 37.6 %collective-permute-start.9 = (bf16[512,768]{1,0:T(8,128)(2,1)}, bf16[512,768]{1,0:T(8,128)(2,1)}, u32[]{:S(2)}, u32[]{:S(2)}) collective-permute-start(bf16[512,768]{1,0:T(8,128)(2,1)} %bitcast.6), channel_id=1, source_target_pairs={{0,8},{8,0},{1,9},{9,1},{2,10},{10,2},{3,11},{11,3},{4,12},{12,4},... | collective-permute-start | bytes 2359304 | tf_op jit(solution)/shard_map/ppermute | solution.py:342
  80.3 26.2 %collective-permute-start.13 = (bf16[80,2432]{1,0:T(8,128)(2,1)}, bf16[80,2432]{1,0:T(8,128)(2,1)S(1)}, u32[]{:S(2)}, u32[]{:S(2)}) collective-permute-start(bf16[80,2432]{1,0:T(8,128)(2,1)} %collective-permute-done.10), channel_id=1, source_target_pairs={{0,8},{8,0},{1,9},{9,1},{2,10},{10,2},{3,11},{11,3},{4,12},{12,4},... | collective-permute-start | bytes 1167368 | tf_op jit(solution)/shard_map/ppermute | solution.py:342
  82.4 38.2 %all-to-all-start.1 = ((bf16[8,64,1536]{2,1,0:T(8,128)(2,1)}), bf16[8,64,1536]{2,1,0:T(8,128)(2,1)}, u32[]{:S(2)}, u32[]{:S(2)}) async-start(bf16[8,64,1536]{2,1,0:T(8,128)(2,1)} %pack_columns.3), calls=%async_computation.1 | async-start | bytes 3145728 | tf_op jit(solution)/shard_map/all_to_all | solution.py:466
  86.7 118.1 %all-gather.3.cloned.1.call-start = ((), (), s32[]{:S(2)}) async-start(), calls=%async_computation.8 | async-start | bytes 3932160 | tf_op jit(solution)/shard_map/all_gather | solution.py:979
  99.2 204.0 %all-gather.5.cloned.1.call-start = ((), (), s32[]{:S(2)}) async-start(), calls=%async_computation.9 | async-start | bytes 7864320 | tf_op jit(solution)/shard_map/all_gather | solution.py:982
  168.1 25.8 %collective-permute-start.27 = (bf16[256,2048]{1,0:T(8,128)(2,1)}, bf16[256,2048]{1,0:T(8,128)(2,1)}, u32[]{:S(2)}, u32[]{:S(2)}) collective-permute-start(bf16[256,2048]{1,0:T(8,128)(2,1)} %param.35), channel_id=1, source_target_pairs={{0,2},{2,0},{1,3},{3,1},{4,6},{6,4},{5,7},{7,5},{8,10},{10,8},{9,1... | collective-permute-start | bytes 3145736 | tf_op jit(solution)/shard_map/ppermute | solution.py:342
  169.7 25.5 %collective-permute-start.28 = (bf16[256,2048]{1,0:T(8,128)(2,1)}, bf16[256,2048]{1,0:T(8,128)(2,1)}, u32[]{:S(2)}, u32[]{:S(2)}) collective-permute-start(bf16[256,2048]{1,0:T(8,128)(2,1)} %param.35), channel_id=1, source_target_pairs={{0,4},{4,0},{1,5},{5,1},{2,6},{6,2},{3,7},{7,3},{8,12},{12,8},{9,1... | collective-permute-start | bytes 3145736 | tf_op jit(solution)/shard_map/ppermute | solution.py:342
  170.6 24.6 %collective-permute-start.29 = (bf16[256,2048]{1,0:T(8,128)(2,1)}, bf16[256,2048]{1,0:T(8,128)(2,1)}, u32[]{:S(2)}, u32[]{:S(2)}) collective-permute-start(bf16[256,2048]{1,0:T(8,128)(2,1)} %param.35), channel_id=1, source_target_pairs={{0,1},{1,0},{2,3},{3,2},{4,5},{5,4},{6,7},{7,6},{8,9},{9,8},{10,11... | collective-permute-start | bytes 3145736 | tf_op jit(solution)/shard_map/ppermute | solution.py:342
  184.1 275.7 %reduce-scatter.4.cloned.1.call-start = ((), (), s32[]{:S(2)}) async-start(), calls=%async_computation.10 | async-start | bytes 3932160 | tf_op jit(solution)/shard_map/reduce_scatter | solution.py:1002
  195.2 52.9 %collective-permute-start.16 = (bf16[256,2048]{1,0:T(8,128)(2,1)}, bf16[256,2048]{1,0:T(8,128)(2,1)}, u32[]{:S(2)}, u32[]{:S(2)}) collective-permute-start(bf16[256,2048]{1,0:T(8,128)(2,1)} %get-tuple-element.180), channel_id=1, source_target_pairs={{0,1},{1,0},{2,3},{3,2},{4,5},{5,4},{6,7},{7,6},{8,9},{9,8},{10,11... | collective-permute-start | bytes 3145736 | tf_op jit(solution)/shard_map/ppermute | solution.py:342
  197.1 43.6 %collective-permute-start.32 = (bf16[256,2048]{1,0:T(8,128)(2,1)}, bf16[256,2048]{1,0:T(8,128)(2,1)}, u32[]{:S(2)}, u32[]{:S(2)}) collective-permute-start(bf16[256,2048]{1,0:T(8,128)(2,1)} %collective-permute-done.27), channel_id=1, source_target_pairs={{0,1},{1,0},{2,3},{3,2},{4,5},{5,4},{6,7},{7,6},{8,9},{9,8},{10,11... | collective-permute-start | bytes 3145736 | tf_op jit(solution)/shard_map/ppermute | solution.py:342
  199.5 41.2 %collective-permute-start.33 = (bf16[256,2048]{1,0:T(8,128)(2,1)}, bf16[256,2048]{1,0:T(8,128)(2,1)}, u32[]{:S(2)}, u32[]{:S(2)}) collective-permute-start(bf16[256,2048]{1,0:T(8,128)(2,1)} %collective-permute-done.28), channel_id=1, source_target_pairs={{0,1},{1,0},{2,3},{3,2},{4,5},{5,4},{6,7},{7,6},{8,9},{9,8},{10,11... | collective-permute-start | bytes 3145736 | tf_op jit(solution)/shard_map/ppermute | solution.py:342
  234.0 24.0 %collective-permute-start.22 = (bf16[256,2048]{1,0:T(8,128)(2,1)S(1)}, bf16[256,2048]{1,0:T(8,128)(2,1)S(1)}, u32[]{:S(2)}, u32[]{:S(2)}) collective-permute-start(bf16[256,2048]{1,0:T(8,128)(2,1)S(1)} %pad_maximum_fusion), channel_id=1, source_target_pairs={{0,2},{2,0},{1,3},{3,1},{4,6},{6,4},{5,7},{7,5},{8,10},{10,8},{9,1... | collective-permute-start | bytes 3145736 | tf_op jit(solution)/shard_map/ppermute | solution.py:342
  234.9 23.7 %collective-permute-start.23 = (bf16[256,2048]{1,0:T(8,128)(2,1)S(1)}, bf16[256,2048]{1,0:T(8,128)(2,1)S(1)}, u32[]{:S(2)}, u32[]{:S(2)}) collective-permute-start(bf16[256,2048]{1,0:T(8,128)(2,1)S(1)} %pad_maximum_fusion.1), channel_id=1, source_target_pairs={{0,4},{4,0},{1,5},{5,1},{2,6},{6,2},{3,7},{7,3},{8,12},{12,8},{9,1... | collective-permute-start | bytes 3145736 | tf_op jit(solution)/shard_map/ppermute | solution.py:342
  261.0 23.0 %collective-permute-start.24 = (bf16[256,2048]{1,0:T(8,128)(2,1)S(1)}, bf16[256,2048]{1,0:T(8,128)(2,1)S(1)}, u32[]{:S(2)}, u32[]{:S(2)}) collective-permute-start(bf16[256,2048]{1,0:T(8,128)(2,1)S(1)} %multiply_convert_fusion.refs_0_), channel_id=1, source_target_pairs={{0,2},{2,0},{1,3},{3,1},{4,6},{6,4},{5,7},{7,5},{8,10},{10,8},{9,1... | collective-permute-start | bytes 3145736 | tf_op jit(solution)/shard_map/ppermute | solution.py:342
  262.3 22.7 %collective-permute-start.25 = (bf16[256,2048]{1,0:T(8,128)(2,1)S(1)}, bf16[256,2048]{1,0:T(8,128)(2,1)S(1)}, u32[]{:S(2)}, u32[]{:S(2)}) collective-permute-start(bf16[256,2048]{1,0:T(8,128)(2,1)S(1)} %multiply_convert_fusion.refs_0_), channel_id=1, source_target_pairs={{0,4},{4,0},{1,5},{5,1},{2,6},{6,2},{3,7},{7,3},{8,12},{12,8},{9,1... | collective-permute-start | bytes 3145736 | tf_op jit(solution)/shard_map/ppermute | solution.py:342
  263.2 21.7 %collective-permute-start.26 = (bf16[256,2048]{1,0:T(8,128)(2,1)S(1)}, bf16[256,2048]{1,0:T(8,128)(2,1)S(1)}, u32[]{:S(2)}, u32[]{:S(2)}) collective-permute-start(bf16[256,2048]{1,0:T(8,128)(2,1)S(1)} %multiply_convert_fusion.refs_0_), channel_id=1, source_target_pairs={{0,1},{1,0},{2,3},{3,2},{4,5},{5,4},{6,7},{7,6},{8,9},{9,8},{10,11... | collective-permute-start | bytes 3145736 | tf_op jit(solution)/shard_map/ppermute | solution.py:342
  349.9 26.3 %collective-permute-start.40 = (bf16[256,2048]{1,0:T(8,128)(2,1)}, bf16[256,2048]{1,0:T(8,128)(2,1)}, u32[]{:S(2)}, u32[]{:S(2)}) collective-permute-start(bf16[256,2048]{1,0:T(8,128)(2,1)} %get-tuple-element.208), channel_id=1, source_target_pairs={{0,1},{1,0},{2,3},{3,2},{4,5},{5,4},{6,7},{7,6},{8,9},{9,8},{10,11... | collective-permute-start | bytes 3145736 | tf_op jit(solution)/shard_map/ppermute | solution.py:342
  368.6 173.5 %reduce-scatter.6.cloned.1.call-start = ((), (), s32[]{:S(2)}) async-start(), calls=%async_computation.11 | async-start | bytes 3932160 | tf_op jit(solution)/shard_map/reduce_scatter | solution.py:1006
  374.1 24.9 %collective-permute-start.46 = (bf16[256,2048]{1,0:T(8,128)(2,1)S(1)}, bf16[256,2048]{1,0:T(8,128)(2,1)S(1)}, u32[]{:S(2)}, u32[]{:S(2)}) collective-permute-start(bf16[256,2048]{1,0:T(8,128)(2,1)S(1)} %pad_maximum_fusion.3), channel_id=1, source_target_pairs={{0,2},{2,0},{1,3},{3,1},{4,6},{6,4},{5,7},{7,5},{8,10},{10,8},{9,1... | collective-permute-start | bytes 3145736 | tf_op jit(solution)/shard_map/ppermute | solution.py:342
  375.3 24.4 %collective-permute-start.47 = (bf16[256,2048]{1,0:T(8,128)(2,1)S(1)}, bf16[256,2048]{1,0:T(8,128)(2,1)S(1)}, u32[]{:S(2)}, u32[]{:S(2)}) collective-permute-start(bf16[256,2048]{1,0:T(8,128)(2,1)S(1)} %pad_maximum_fusion.4), channel_id=1, source_target_pairs={{0,4},{4,0},{1,5},{5,1},{2,6},{6,2},{3,7},{7,3},{8,12},{12,8},{9,1... | collective-permute-start | bytes 3145736 | tf_op jit(solution)/shard_map/ppermute | solution.py:342
  414.8 162.4 %reduce-scatter.8.cloned.1.call-start = ((), (), s32[]{:S(2)}) async-start(), calls=%async_computation.12 | async-start | bytes 3932160 | tf_op jit(solution)/shard_map/reduce_scatter | solution.py:1007
  415.0 24.0 %collective-permute-start.48 = (bf16[256,2048]{1,0:T(8,128)(2,1)}, bf16[256,2048]{1,0:T(8,128)(2,1)}, u32[]{:S(2)}, u32[]{:S(2)}) collective-permute-start(bf16[256,2048]{1,0:T(8,128)(2,1)} %get-tuple-element.325.refs_0_), channel_id=1, source_target_pairs={{0,2},{2,0},{1,3},{3,1},{4,6},{6,4},{5,7},{7,5},{8,10},{10,8},{9,1... | collective-permute-start | bytes 3145736 | tf_op jit(solution)/shard_map/ppermute | solution.py:342
  416.1 23.7 %collective-permute-start.49 = (bf16[256,2048]{1,0:T(8,128)(2,1)}, bf16[256,2048]{1,0:T(8,128)(2,1)}, u32[]{:S(2)}, u32[]{:S(2)}) collective-permute-start(bf16[256,2048]{1,0:T(8,128)(2,1)} %get-tuple-element.325.refs_0_), channel_id=1, source_target_pairs={{0,4},{4,0},{1,5},{5,1},{2,6},{6,2},{3,7},{7,3},{8,12},{12,8},{9,1... | collective-permute-start | bytes 3145736 | tf_op jit(solution)/shard_map/ppermute | solution.py:342
  417.0 22.9 %collective-permute-start.50 = (bf16[256,2048]{1,0:T(8,128)(2,1)}, bf16[256,2048]{1,0:T(8,128)(2,1)S(1)}, u32[]{:S(2)}, u32[]{:S(2)}) collective-permute-start(bf16[256,2048]{1,0:T(8,128)(2,1)} %get-tuple-element.325.refs_0_), channel_id=1, source_target_pairs={{0,1},{1,0},{2,3},{3,2},{4,5},{5,4},{6,7},{7,6},{8,9},{9,8},{10,11... | collective-permute-start | bytes 3145736 | tf_op jit(solution)/shard_map/ppermute | solution.py:342
  525.6 22.5 %collective-permute-start.57 = (bf16[256,2048]{1,0:T(8,128)(2,1)}, bf16[256,2048]{1,0:T(8,128)(2,1)}, u32[]{:S(2)}, u32[]{:S(2)}) collective-permute-start(bf16[256,2048]{1,0:T(8,128)(2,1)} %get-tuple-element.239), channel_id=1, source_target_pairs={{0,1},{1,0},{2,3},{3,2},{4,5},{5,4},{6,7},{7,6},{8,9},{9,8},{10,11... | collective-permute-start | bytes 3145736 | tf_op jit(solution)/shard_map/ppermute | solution.py:342
  525.7 34.4 %collective-permute-start.56 = (bf16[256,2048]{1,0:T(8,128)(2,1)}, bf16[256,2048]{1,0:T(8,128)(2,1)}, u32[]{:S(2)}, u32[]{:S(2)}) collective-permute-start(bf16[256,2048]{1,0:T(8,128)(2,1)} %get-tuple-element.237), channel_id=1, source_target_pairs={{0,1},{1,0},{2,3},{3,2},{4,5},{5,4},{6,7},{7,6},{8,9},{9,8},{10,11... | collective-permute-start | bytes 3145736 | tf_op jit(solution)/shard_map/ppermute | solution.py:342
  538.6 50.0 %collective-permute-start.67 = (bf16[512,768]{1,0:T(8,128)(2,1)}, bf16[512,768]{1,0:T(8,128)(2,1)}, u32[]{:S(2)}, u32[]{:S(2)}) collective-permute-start(bf16[512,768]{1,0:T(8,128)(2,1)} %get-tuple-element.330), channel_id=1, source_target_pairs={{0,8},{8,0},{1,9},{9,1},{2,10},{10,2},{3,11},{11,3},{4,12},{12,4},... | collective-permute-start | bytes 2359304 | tf_op jit(solution)/shard_map/ppermute | solution.py:342
  539.4 49.2 %collective-permute-start.68 = (bf16[512,768]{1,0:T(8,128)(2,1)}, bf16[512,768]{1,0:T(8,128)(2,1)}, u32[]{:S(2)}, u32[]{:S(2)}) collective-permute-start(bf16[512,768]{1,0:T(8,128)(2,1)} %get-tuple-element.329), channel_id=1, source_target_pairs={{0,8},{8,0},{1,9},{9,1},{2,10},{10,2},{3,11},{11,3},{4,12},{12,4},... | collective-permute-start | bytes 2359304 | tf_op jit(solution)/shard_map/ppermute | solution.py:342
  545.7 106.9 %collective-permute-start.64 = (bf16[256,2048]{1,0:T(8,128)(2,1)}, bf16[256,2048]{1,0:T(8,128)(2,1)}, u32[]{:S(2)}, u32[]{:S(2)}) collective-permute-start(bf16[256,2048]{1,0:T(8,128)(2,1)} %copy-done.55), channel_id=1, source_target_pairs={{0,1},{1,0},{2,3},{3,2},{4,5},{5,4},{6,7},{7,6},{8,9},{9,8},{10,11... | collective-permute-start | bytes 3145736 | tf_op jit(solution)/shard_map/ppermute | solution.py:342
  576.9 75.1 %collective-permute-start.65 = (bf16[256,2048]{1,0:T(8,128)(2,1)}, bf16[256,2048]{1,0:T(8,128)(2,1)}, u32[]{:S(2)}, u32[]{:S(2)}) collective-permute-start(bf16[256,2048]{1,0:T(8,128)(2,1)} %pad_maximum_fusion.5), channel_id=1, source_target_pairs={{0,2},{2,0},{1,3},{3,1},{4,6},{6,4},{5,7},{7,5},{8,10},{10,8},{9,1... | collective-permute-start | bytes 3145736 | tf_op jit(solution)/shard_map/ppermute | solution.py:342
  577.2 34.1 %all-to-all-start.4 = ((bf16[8,64,768]{2,1,0:T(8,128)(2,1)}), bf16[8,64,768]{2,1,0:T(8,128)(2,1)S(1)}, u32[]{:S(2)}, u32[]{:S(2)}) async-start(bf16[8,64,768]{2,1,0:T(8,128)(2,1)} %bitcast.102), calls=%async_computation.7 | async-start | bytes 1572864 | tf_op jit(solution)/shard_map/all_to_all | solution.py:466
  588.1 20.8 %collective-permute-start.79 = (bf16[2,80,2048]{2,1,0:T(8,128)(2,1)S(1)}, bf16[2,80,2048]{2,1,0:T(8,128)(2,1)S(1)}, u32[]{:S(2)}, u32[]{:S(2)}) collective-permute-start(bf16[2,80,2048]{2,1,0:T(8,128)(2,1)S(1)} %dynamic-slice_bitcast_fusion.2), channel_id=1, source_target_pairs={{0,1},{1,0},{2,3},{3,2},{4,5},{5,4},{6,7},{7,6},{8,9},{9,8},{10,11... | collective-permute-start | bytes 1966088 | tf_op jit(solution)/shard_map/ppermute | solution.py:342
  591.1 61.4 %collective-permute-start.66 = (bf16[256,2048]{1,0:T(8,128)(2,1)}, bf16[256,2048]{1,0:T(8,128)(2,1)}, u32[]{:S(2)}, u32[]{:S(2)}) collective-permute-start(bf16[256,2048]{1,0:T(8,128)(2,1)} %pad_maximum_fusion.6), channel_id=1, source_target_pairs={{0,4},{4,0},{1,5},{5,1},{2,6},{6,2},{3,7},{7,3},{8,12},{12,8},{9,1... | collective-permute-start | bytes 3145736 | tf_op jit(solution)/shard_map/ppermute | solution.py:342
  607.1 38.0 %collective-permute-start.72 = (bf16[512,768]{1,0:T(8,128)(2,1)}, bf16[512,768]{1,0:T(8,128)(2,1)}, u32[]{:S(2)}, u32[]{:S(2)}) collective-permute-start(bf16[512,768]{1,0:T(8,128)(2,1)} %fusion.9), channel_id=1, source_target_pairs={{0,16},{16,0},{1,17},{17,1},{2,18},{18,2},{3,19},{19,3},{4,20},{20... | collective-permute-start | bytes 2359304 | tf_op jit(solution)/shard_map/ppermute | solution.py:342
  608.9 49.5 %collective-permute-start.63 = (bf16[256,2048]{1,0:T(8,128)(2,1)}, bf16[256,2048]{1,0:T(8,128)(2,1)}, u32[]{:S(2)}, u32[]{:S(2)}) collective-permute-start(bf16[256,2048]{1,0:T(8,128)(2,1)} %get-tuple-element.254), channel_id=1, source_target_pairs={{0,1},{1,0},{2,3},{3,2},{4,5},{5,4},{6,7},{7,6},{8,9},{9,8},{10,11... | collective-permute-start | bytes 3145736 | tf_op jit(solution)/shard_map/ppermute | solution.py:342
  645.2 31.9 %collective-permute-start.70 = (bf16[256,2048]{1,0:T(8,128)(2,1)}, bf16[256,2048]{1,0:T(8,128)(2,1)}, u32[]{:S(2)}, u32[]{:S(2)}) collective-permute-start(bf16[256,2048]{1,0:T(8,128)(2,1)} %copy-done.59), channel_id=1, source_target_pairs={{0,1},{1,0},{2,3},{3,2},{4,5},{5,4},{6,7},{7,6},{8,9},{9,8},{10,11... | collective-permute-start | bytes 3145736 | tf_op jit(solution)/shard_map/ppermute | solution.py:342
  648.1 35.3 %all-to-all-start.3 = ((bf16[8,64,768]{2,1,0:T(8,128)(2,1)}), bf16[8,64,768]{2,1,0:T(8,128)(2,1)S(1)}, u32[]{:S(2)}, u32[]{:S(2)}) async-start(bf16[8,64,768]{2,1,0:T(8,128)(2,1)} %bitcast.99), calls=%async_computation.6 | async-start | bytes 1572864 | tf_op jit(solution)/shard_map/all_to_all | solution.py:466
  652.0 28.2 %collective-permute-start.62 = (bf16[256,2048]{1,0:T(8,128)(2,1)}, bf16[256,2048]{1,0:T(8,128)(2,1)S(1)}, u32[]{:S(2)}, u32[]{:S(2)}) collective-permute-start(bf16[256,2048]{1,0:T(8,128)(2,1)} %copy-done.58), channel_id=1, source_target_pairs={{0,1},{1,0},{2,3},{3,2},{4,5},{5,4},{6,7},{7,6},{8,9},{9,8},{10,11... | collective-permute-start | bytes 3145736 | tf_op jit(solution)/shard_map/ppermute | solution.py:342
  652.5 67.5 %collective-permute-start.61 = (bf16[256,2048]{1,0:T(8,128)(2,1)S(1)}, bf16[256,2048]{1,0:T(8,128)(2,1)}, u32[]{:S(2)}, u32[]{:S(2)}) collective-permute-start(bf16[256,2048]{1,0:T(8,128)(2,1)S(1)} %copy-done.54), channel_id=1, source_target_pairs={{0,1},{1,0},{2,3},{3,2},{4,5},{5,4},{6,7},{7,6},{8,9},{9,8},{10,11... | collective-permute-start | bytes 3145736 | tf_op jit(solution)/shard_map/ppermute | solution.py:342
  672.7 23.2 %collective-permute-start.82 = (bf16[80,2048]{1,0:T(8,128)(2,1)}, bf16[80,2048]{1,0:T(8,128)(2,1)}, u32[]{:S(2)}, u32[]{:S(2)}) collective-permute-start(bf16[80,2048]{1,0:T(8,128)(2,1)} %fusion.10), channel_id=1, source_target_pairs={{0,16},{16,0},{1,17},{17,1},{2,18},{18,2},{3,19},{19,3},{4,20},{20... | collective-permute-start | bytes 983048 | tf_op jit(solution)/shard_map/ppermute | solution.py:342
  695.3 22.6 %collective-permute-start.73 = (bf16[256,2048]{1,0:T(8,128)(2,1)}, bf16[256,2048]{1,0:T(8,128)(2,1)}, u32[]{:S(2)}, u32[]{:S(2)}) collective-permute-start(bf16[256,2048]{1,0:T(8,128)(2,1)} %pad_maximum_fusion.7), channel_id=1, source_target_pairs={{0,2},{2,0},{1,3},{3,1},{4,6},{6,4},{5,7},{7,5},{8,10},{10,8},{9,1... | collective-permute-start | bytes 3145736 | tf_op jit(solution)/shard_map/ppermute | solution.py:342
  695.9 24.1 %collective-permute-start.74 = (bf16[256,2048]{1,0:T(8,128)(2,1)}, bf16[256,2048]{1,0:T(8,128)(2,1)}, u32[]{:S(2)}, u32[]{:S(2)}) collective-permute-start(bf16[256,2048]{1,0:T(8,128)(2,1)} %pad_maximum_fusion.8), channel_id=1, source_target_pairs={{0,4},{4,0},{1,5},{5,1},{2,6},{6,2},{3,7},{7,3},{8,12},{12,8},{9,1... | collective-permute-start | bytes 3145736 | tf_op jit(solution)/shard_map/ppermute | solution.py:342
  (156 other events, 1493.5 us)
Sparse Core Ops, SparseCore 0:
  99.4 62.8 all-gather.2
  184.2 113.5 all-gather.4
  368.7 58.7 reduce-scatter.3
  429.7 60.2 reduce-scatter.5
  492.2 69.2 reduce-scatter.7

commit v6 on v5

--- a/solution.py
+++ b/solution.py
@@ -1021,7 +1021,6 @@
 
     d_un = act_scatter(blocks_1, "x", "y", (d_wxy, d_wg), (), None, output_blocks)
     d_input = (d_resid + norm_back(after(d_un, d_wu), xf, scale1)).astype(BF16)
-    d_wxy = released[1]().astype(BF16)
     def channels_out(v, kind):
         v = v.astype(kind).reshape(2, 2, part, -1)
         size = (2, 1) + v.shape[2:]
@@ -1031,7 +1030,6 @@
         out = lax.dynamic_update_slice(out, keep[None], (core, 0, 0, 0))
         return lax.dynamic_update_slice(out, swap(send, "c")[None], (1 - core, 0, 0, 0))
 
-    d_wo = channels_out(row_contract(after(mixed, released[0]), d_mix_all)[:channels], BF16)
     sums = jnp.sum(sums.reshape(8, 8, padded), axis=1)
     d_lam_part = -jax.nn.sigmoid(-lam_all) * sums[5]
     d_cols = jnp.concatenate([sums[:5], sums[6:8], d_lam_part[None]], axis=0).T
@@ -1044,23 +1042,25 @@
             block = jnp.where(row_block == n, d_gates[:channels, at : at + width], block)
         d_blocks.append(block)
     d_small = jnp.concatenate([d_cols[:channels]] + d_blocks, axis=1)
-    d_small = channels_out(after(d_small, released[0]), F32)
-    ends = []
+    d_wu = exchange(after(d_wu, released[0]).reshape(8, -1, 4 * units), PLANE)
+    sent, ends = [], []
 
     def start_channels(far):
-        ends.extend(w_scatter(v, *STACK, (far,))[0] for v in (d_wo, d_small))
+        sent.append(channels_out(row_contract(after(mixed, far), d_mix_all)[:channels], BF16))
+        sent.append(channels_out(after(d_small, far), F32))
         return ()
 
     def end_channels(marker):
-        ends.extend(end(marker) for end in ends[:2])
+        ends.append(released[1](marker).astype(BF16))
+        ends.extend(w_scatter(v, *STACK, (marker,))[0]() for v in sent)
+        ends.append(after(d_wu, marker))
         return ()
 
-    output = act_scatter(blocks_o, "x", "y", (d_input,), (d_wxy,), start_channels, end_channels)
+    output = act_scatter(blocks_o, "x", "y", (d_input,), (), start_channels, end_channels)
     output = (resid + output).astype(BF16)
-    d_wo, d_small = ends[2:]
+    d_wxy, d_wo, d_small, d_wu = ends
     d_wxy = exchange(d_wxy.reshape(8, -1, 2 * padded), PLANE)
     d_wx, d_wy, d_gain1 = unpack_columns(rec_plan, d_wxy, None, w_x, w_y, gain1)
-    d_wu = exchange(after(d_wu, released[0]).reshape(8, -1, 4 * units), PLANE)
     d_wg, d_wu, d_gain2 = unpack_columns(ff_plan, d_wg, d_wu, w_gate, w_up, gain2)
 
     d_cw, d_cb, d_br, d_bi, d_lam = d_small[:, :4], d_small[:, 4], d_small[:, 5], d_small[:, 6], d_small[:, 7]

time: 740 us -> 717 us (0.969)
  waiting for transfers between devices: 255 us -> 239 us
  local copies, waits for them, and re-layouts: 96 us -> 87.5 us
    ppermute x83, waiting for transfers between devices: 238 us -> 223 us  [swap(): return lax.ppermute(v, name, [(0, 1), (1, 0)])]
    unnamed x223 -> x187, local copies, waits for them, and re-layouts: 54.7 us -> 47.5 us
  transfers between devices with their start and end apart: 93 -> 93, of which waited for: 37 -> 40; matrix products, arithmetic and copies ran while one was open for 23% -> 23% of each run, Pallas kernels for 17% -> 17%
where the time goes in v6:
time: 717 us; the launch traced here: 708 us
  waiting for transfers between devices  239 us (33%)
  Pallas kernels  169 us (24%)
  local copies, waits for them, and re-layouts  87.5 us (12%)
  starting transfers between devices  81.9 us (11%)
  other arithmetic  68.1 us (9%)
  matrix products  46.4 us (6%)
  between operations  15.6 us (2%)
    ppermute x83, waiting for transfers between devices, swap(): return lax.ppermute(v, name, [(0, 1), (1, 0)])  223 us
    ppermute x83, starting transfers between devices, swap(): return lax.ppermute(v, name, [(0, 1), (1, 0)])  60.6 us
    unnamed x187, local copies, waits for them, and re-layouts  47.5 us
    dot_general x5, matrix products, row_contract(): lax.dot_general(left, right, (((0,), (0,)), ((), ())), preferred_element_...  46.4 us
    pallas_call x1, Pallas kernels, feed_forward(): pl.pallas_call(ff_kernel, grid=(4,), in_specs=[once(v) for v in pieces] +...  45.9 us
    pallas_call x3, Pallas kernels, product_blocks(): pl.pallas_call(functools.partial(blocks_kernel, flip), grid=(4,), in_spec...  32.1 us
    pallas_call x1, Pallas kernels, rec_backward(): pl.pallas_call(rec_bwd_kernel, grid_spec=pltpu.PrefetchScalarGridSpec(num...  28.1 us
    pallas_call x2, Pallas kernels, pieces_product(): pl.pallas_call(functools.partial(pieces_kernel, flip), grid=(4,), in_spec...  24.1 us
  transfers between devices with their start and end apart: 93, of which 40 were waited for; matrix products, arithmetic and copies ran while one was open for 23% of the time, Pallas kernels for 17%

profile of v6, /device:TPU:0, one launch (start us, length us, event | category | flops | bytes accessed | tf_op | source)
XLA Modules:
  0.0 707.6 jit_solution(8151740200396875916)
XLA Ops:
  17.0 4.0 collective-permute-start.10
  22.6 4.2 all-to-all-start
  30.4 9.1 %all-to-all-done = bf16[8,64,768]{2,1,0:T(8,128)(2,1)} async-done(((bf16[8,64,768]{2,1,0:T(8,128)(2,1)}), bf16[8,64,768]{2,1,0:T(8,128)(2,1)}, u32[]{:S(2)}, u32[]{:S(2)}) %all-to-all-start) | async-done | bytes 786464 | tf_op jit(solution)/shard_map/all_to_all | solution.py:466
  42.8 20.6 %collective-permute-done.refs_2_ = bf16[256,2048]{1,0:T(8,128)(2,1)} collective-permute-done((bf16[256,2048]{1,0:T(8,128)(2,1)S(1)}, bf16[256,2048]{1,0:T(8,128)(2,1)}, u32[]{:S(2)}, u32[]{:S(2)}) %collective-permute-start) | collective-permute-done | bytes 1048608 | tf_op jit(solution)/shard_map/ppermute | solution.py:342
  65.9 12.6 %collective-permute-done.8 = bf16[512,768]{1,0:T(8,128)(2,1)} collective-permute-done((bf16[512,768]{1,0:T(8,128)(2,1)}, bf16[512,768]{1,0:T(8,128)(2,1)}, u32[]{:S(2)}, u32[]{:S(2)}) %collective-permute-start.8) | collective-permute-done | bytes 786464 | tf_op jit(solution)/shard_map/ppermute | solution.py:342
  82.4 4.3 all-to-all-start.1
  86.7 12.5 %collective-permute-done.12 = bf16[512,768]{1,0:T(8,128)(2,1)} collective-permute-done((bf16[512,768]{1,0:T(8,128)(2,1)}, bf16[512,768]{1,0:T(8,128)(2,1)}, u32[]{:S(2)}, u32[]{:S(2)}) %collective-permute-start.12) | collective-permute-done | bytes 786464 | tf_op jit(solution)/shard_map/ppermute | solution.py:342
  115.2 4.1 collective-permute-done.3
  128.3 14.4 %pieces_product.2 = (bf16[2048,2048]{1,0:T(8,128)(2,1)}, f32[2048,768]{1,0:T(8,128)}) custom-call(bf16[256,2048]{1,0:T(8,128)(2,1)S(1)} %fusion.1.refs_0_, bf16[256,2048]{1,0:T(8,128)(2,1)S(1)} %copy-done.45, bf16[256,2048]{1,0:T(8,128)(2,1)} %collective-permute-done.refs_2_, bf16[256,2048]{1,0:T(8,128)(2,1)} %collective-permute-done.5.refs_3_, ...), custom_call_target="tpu_custom_call" | custom-call | flops 6442450944 | bytes 26214400 | tf_op jit(solution)/shard_map/pieces_product/pallas_call | solution.py:856
  142.7 2.8 copy-done
  145.5 18.4 %recurrence_forward.1 = (bf16[2048,384]{1,0:T(8,128)(2,1)S(1)}, f32[2048,384]{1,0:T(8,128)S(1)}, f32[2048,384]{1,0:T(8,128)S(1)}, f32[2048,384]{1,0:T(8,128)S(1)}, bf16[2048,384]{1,0:T(8,128)(2,1)S(1)}) custom-call(s32[5]{0:T(128)S(1)} %pad_add_fusion.meta_ref, f32[2048,768]{1,0:T(8,128)S(1)} %copy-done, f32[2048,768]{1,0:T(8,128)S(1)} %copy-done, ...), custom_call_target="tpu_custom_call" | custom-call | flops 1286602752 | bytes 18874368 | tf_op jit(solution)/shard_map/recurrence_forward/pallas_call | solution.py:719
  170.8 9.0 %product_blocks.3 = (bf16[256,2048]{1,0:T(8,128)(2,1)S(1)}, bf16[256,2048]{1,0:T(8,128)(2,1)}, bf16[256,2048]{1,0:T(8,128)(2,1)S(1)}, bf16[256,2048]{1,0:T(8,128...) custom-call(bf16[2048,384]{1,0:T(8,128)(2,1)S(1)} %get-tuple-element, ...), custom_call_target="tpu_custom_call" | custom-call | flops 3221225472 | bytes 11534336 | tf_op jit(solution)/shard_map/product_blocks/pallas_call | solution.py:812
  187.0 7.2 %collective-permute-done.27 = bf16[256,2048]{1,0:T(8,128)(2,1)} collective-permute-done((bf16[256,2048]{1,0:T(8,128)(2,1)}, bf16[256,2048]{1,0:T(8,128)(2,1)}, u32[]{:S(2)}, u32[]{:S(2)}) %collective-permute-start.27) | collective-permute-done | bytes 1048608 | tf_op jit(solution)/shard_map/ppermute | solution.py:342
  210.0 10.7 %collective-permute-done.21 = bf16[128,2048]{1,0:T(8,128)(2,1)S(1)} collective-permute-done((bf16[128,2048]{1,0:T(8,128)(2,1)S(1)}, bf16[128,2048]{1,0:T(8,128)(2,1)S(1)}, u32[]{:S(2)}, u32[]{:S(2)}) %collective-permute-start.21) | collective-permute-done | bytes 524320 | tf_op jit(solution)/shard_map/ppermute | solution.py:342
  222.8 11.5 %collective-permute-done.30 = bf16[128,2048]{1,0:T(8,128)(2,1)S(1)} collective-permute-done((bf16[128,2048]{1,0:T(8,128)(2,1)S(1)}, bf16[128,2048]{1,0:T(8,128)(2,1)S(1)}, u32[]{:S(2)}, u32[]{:S(2)}) %collective-permute-start.30) | collective-permute-done | bytes 524320 | tf_op jit(solution)/shard_map/ppermute | solution.py:342
  245.6 2.7 pad_maximum_fusion.2
  248.3 10.0 %collective-permute-done.22 = bf16[256,2048]{1,0:T(8,128)(2,1)S(1)} collective-permute-done((bf16[256,2048]{1,0:T(8,128)(2,1)S(1)}, bf16[256,2048]{1,0:T(8,128)(2,1)S(1)}, u32[]{:S(2)}, u32[]{:S(2)}) %collective-permute-start.22) | collective-permute-done | bytes 1048608 | tf_op jit(solution)/shard_map/ppermute | solution.py:342
  266.2 18.0 %collective-permute-done.24.refs_2_ = bf16[256,2048]{1,0:T(8,128)(2,1)S(1)} collective-permute-done((bf16[256,2048]{1,0:T(8,128)(2,1)S(1)}, bf16[256,2048]{1,0:T(8,128)(2,1)S(1)}, u32[]{:S(2)}, u32[]{:S(2)}) %collective-permute-start.24) | collective-permute-done | bytes 1048608 | tf_op jit(solution)/shard_map/ppermute | solution.py:342
  287.8 12.0 %collective-permute-done.35 = bf16[128,2048]{1,0:T(8,128)(2,1)S(1)} collective-permute-done((bf16[128,2048]{1,0:T(8,128)(2,1)S(1)}, bf16[128,2048]{1,0:T(8,128)(2,1)S(1)}, u32[]{:S(2)}, u32[]{:S(2)}) %collective-permute-start.35) | collective-permute-done | bytes 524320 | tf_op jit(solution)/shard_map/ppermute | solution.py:342
  303.5 45.9 %feed_forward.1 = (bf16[2048,2048]{1,0:T(8,128)(2,1)}, bf16[2048,768]{1,0:T(8,128)(2,1)}, bf16[2048,768]{1,0:T(8,128)(2,1)}, bf16[2048,768]{1,0:T(8,128)(2,1)}, ...) custom-call(bf16[256,2048]{1,0:T(8,128)(2,1)} %copy-done.67, ...), custom_call_target="tpu_custom_call" | custom-call | flops 32212254720 | bytes 52428800 | tf_op jit(solution)/shard_map/feed_forward/pallas_call | solution.py:900
  358.3 10.4 %convolution_convert_fusion = bf16[768,2048]{1,0:T(8,128)(2,1)} fusion(bf16[2048,768]{1,0:T(8,128)(2,1)S(1)} %copy-done.84, bf16[2048,2048]{1,0:T(8,128)(2,1)} %constant_dynamic-update-slice_fusion.2.refs_8_), kind=kOutput, calls=%fused_computation.5 | convolution fusion | flops 6444023808 | bytes 14680064 | tf_op jit(solution)/shard_map/dot_general | solution.py:58
  376.4 22.8 %collective-permute-done.46 = bf16[256,2048]{1,0:T(8,128)(2,1)S(1)} collective-permute-done((bf16[256,2048]{1,0:T(8,128)(2,1)S(1)}, bf16[256,2048]{1,0:T(8,128)(2,1)S(1)}, u32[]{:S(2)}, u32[]{:S(2)}) %collective-permute-start.46) | collective-permute-done | bytes 1048608 | tf_op jit(solution)/shard_map/ppermute | solution.py:342
  402.0 4.4 fusion.17
  406.4 8.3 %convolution_convert_fusion.3 = bf16[2048,768]{1,0:T(8,128)(2,1)} fusion(bf16[2048,2048]{1,0:T(8,128)(2,1)S(1)} %bitcast.112, bf16[2048,768]{1,0:T(8,128)(2,1)S(1)} %copy-done.85), kind=kOutput, calls=%fused_computation.8 | convolution fusion | flops 6444023808 | bytes 14680064 | tf_op jit(solution)/shard_map/dot_general | solution.py:58
  416.8 22.0 %collective-permute-done.48.refs_2_ = bf16[256,2048]{1,0:T(8,128)(2,1)} collective-permute-done((bf16[256,2048]{1,0:T(8,128)(2,1)}, bf16[256,2048]{1,0:T(8,128)(2,1)}, u32[]{:S(2)}, u32[]{:S(2)}) %collective-permute-start.48) | collective-permute-done | bytes 1048608 | tf_op jit(solution)/shard_map/ppermute | solution.py:342
  447.2 11.4 %convolution_convert_fusion.2 = bf16[2048,768]{1,0:T(8,128)(2,1)} fusion(bf16[2048,2048]{1,0:T(8,128)(2,1)} %get-tuple-element.218, bf16[2048,768]{1,0:T(8,128)(2,1)} %get-tuple-element.225), kind=kOutput, calls=%fused_computation.7 | convolution fusion | flops 6444023808 | bytes 14680064 | tf_op jit(solution)/shard_map/dot_general | solution.py:58
  470.3 9.7 %pieces_product.3 = (bf16[2048,2048]{1,0:T(8,128)(2,1)}, f32[2048,384]{1,0:T(8,128)}) custom-call(bf16[256,2048]{1,0:T(8,128)(2,1)S(1)} %copy-done.21, bf16[256,2048]{1,0:T(8,128)(2,1)S(1)} %copy-done.48, bf16[256,2048]{1,0:T(8,128)(2,1)} %collective-permute-done.48.refs_2_, bf16[256,2048]{1,0:T(8,128)(2,1)} %collective-permute-done.53.refs_3_, ...), custom_call_target="tpu_custom_call" | custom-call | flops 3221225472 | bytes 21495808 | tf_op jit(solution)/shard_map/pieces_product/pallas_call | solution.py:856
  483.3 28.1 %recurrence_backward.1 = (bf16[2048,768]{1,0:T(8,128)(2,1)S(1)}, f32[384,768]{1,0:T(8,128)S(1)}, f32[64,384]{1,0:T(8,128)S(1)}) custom-call(s32[5]{0:T(128)S(1)} %pad_add_fusion.meta_ref, f32[2048,384]{1,0:T(8,128)S(1)} %copy-done.5, f32[2048,768]{1,0:T(8,128)} %get-tuple-element.176.xb_ref.yb_ref, f32[2048,384]{1,0:T(8,128)S(1)} %copy-done.4, ...), custom_call_target="tpu_custom_call" | custom-call | flops 2557476864 | bytes 23592960 | tf_op jit(solution)/shard_map/recurrence_backward/pallas_call | solution.py:745
  513.2 11.9 %product_blocks.4 = (bf16[256,2048]{1,0:T(8,128)(2,1)S(1)}, bf16[256,2048]{1,0:T(8,128)(2,1)S(1)}, bf16[256,2048]{1,0:T(8,128)(2,1)S(1)}, bf16[256,2048]{1,0:T(8...) custom-call(bf16[2048,768]{1,0:T(8,128)(2,1)} %copy-done.38, ...), custom_call_target="tpu_custom_call" | custom-call | flops 6442450944 | bytes 14680064 | tf_op jit(solution)/shard_map/product_blocks/pallas_call | solution.py:812
  526.2 9.5 %convolution_convert_fusion.1 = bf16[2048,768]{1,0:T(8,128)(2,1)S(1)} fusion(bf16[2048,2048]{1,0:T(8,128)(2,1)} %get-tuple-element.240, bf16[2048,768]{1,0:T(8,128)(2,1)S(1)} %copy-done.39), kind=kOutput, calls=%fused_computation.6 | convolution fusion | flops 6444023808 | bytes 14680064 | tf_op jit(solution)/shard_map/dot_general | solution.py:58
  540.1 3.6 all-to-all-start.2
  549.6 6.6 all-to-all-done.2.ga_ref
  560.5 9.8 %collective-permute-done.60 = bf16[128,2048]{1,0:T(8,128)(2,1)S(1)} collective-permute-done((bf16[128,2048]{1,0:T(8,128)(2,1)S(1)}, bf16[128,2048]{1,0:T(8,128)(2,1)S(1)}, u32[]{:S(2)}, u32[]{:S(2)}) %collective-permute-start.60) | collective-permute-done | bytes 524320 | tf_op jit(solution)/shard_map/ppermute | solution.py:342
  576.0 4.4 all-to-all-start.4
  580.4 11.1 %product_blocks.5 = (bf16[256,2048]{1,0:T(8,128)(2,1)S(1)}, bf16[256,2048]{1,0:T(8,128)(2,1)}, bf16[256,2048]{1,0:T(8,128)(2,1)S(1)}, bf16[256,2048]{1,0:T(8,128...) custom-call(bf16[2048,768]{1,0:T(8,128)(2,1)} %get-tuple-element.248, ...), custom_call_target="tpu_custom_call" | custom-call | flops 6442450944 | bytes 14680064 | tf_op jit(solution)/shard_map/product_blocks/pallas_call | solution.py:812
  593.5 7.8 %collective-permute-done.65 = bf16[256,2048]{1,0:T(8,128)(2,1)} collective-permute-done((bf16[256,2048]{1,0:T(8,128)(2,1)}, bf16[256,2048]{1,0:T(8,128)(2,1)}, u32[]{:S(2)}, u32[]{:S(2)}) %collective-permute-start.65) | collective-permute-done | bytes 1048608 | tf_op jit(solution)/shard_map/ppermute | solution.py:342
  603.1 2.6 convert_add_fusion.1
  609.3 5.0 collective-permute-start.71
  614.3 6.9 fusion.23
  623.7 3.1 collective-permute-done.71
  628.9 6.6 collective-permute-done.69
  650.5 3.8 all-to-all-start.3
  655.5 10.3 %unpack_columns.3 = (f32[64,6144]{1,0:T(8,128)}, f32[64,6144]{1,0:T(8,128)}, f32[64,1]{1,0:T(8,128)S(1)}) custom-call(bf16[8,64,768]{2,1,0:T(8,128)(2,1)S(1)} %all-to-all-done.2.ga_ref, bf16[8,64,768]{2,1,0:T(8,128)(2,1)S(1)} %all-to-all-done.4.gb_ref, bf16[64,6144]{1,0:T(8,128)(2,1)S(1)} %copy-done.7, bf16[64,6144]{1,0:T(8,128)(2,1)S(1)} %copy-done.9, ...), custom_call_target="tpu_custom_call" | custom-call | flops 3145728 | bytes 6291456 | tf_op jit(solution)/shard_map/unpack_columns/pallas_call | solution.py:453
  672.7 2.8 collective-permute-start.82
  677.1 6.4 unpack_columns.2
  684.1 6.2 collective-permute-done.82
  692.3 3.9 collective-permute-done.73
  696.2 4.3 add_convert_fusion
  (476 shorter events, 214.1 us)
Async XLA Ops:
  17.0 23.6 %collective-permute-start.10 = (bf16[80,2432]{1,0:T(8,128)(2,1)}, bf16[80,2432]{1,0:T(8,128)(2,1)}, u32[]{:S(2)}, u32[]{:S(2)}) collective-permute-start(bf16[80,2432]{1,0:T(8,128)(2,1)} %pad.4), channel_id=1, source_target_pairs={{0,16},{16,0},{1,17},{17,1},{2,18},{18,2},{3,19},{19,3},{4,20},{20... | collective-permute-start | bytes 1167368 | tf_op jit(solution)/shard_map/ppermute | solution.py:342
  39.5 24.0 %collective-permute-start = (bf16[256,2048]{1,0:T(8,128)(2,1)S(1)}, bf16[256,2048]{1,0:T(8,128)(2,1)}, u32[]{:S(2)}, u32[]{:S(2)}) collective-permute-start(bf16[256,2048]{1,0:T(8,128)(2,1)S(1)} %fusion.1.refs_0_), channel_id=1, source_target_pairs={{0,2},{2,0},{1,3},{3,1},{4,6},{6,4},{5,7},{7,5},{8,10},{10,8},{9,1... | collective-permute-start | bytes 3145736 | tf_op jit(solution)/shard_map/ppermute | solution.py:342
  40.0 25.0 %collective-permute-start.1 = (bf16[256,2048]{1,0:T(8,128)(2,1)S(1)}, bf16[256,2048]{1,0:T(8,128)(2,1)}, u32[]{:S(2)}, u32[]{:S(2)}) collective-permute-start(bf16[256,2048]{1,0:T(8,128)(2,1)S(1)} %fusion.1.refs_0_), channel_id=1, source_target_pairs={{0,4},{4,0},{1,5},{5,1},{2,6},{6,2},{3,7},{7,3},{8,12},{12,8},{9,1... | collective-permute-start | bytes 3145736 | tf_op jit(solution)/shard_map/ppermute | solution.py:342
  40.6 24.3 %collective-permute-start.2 = (bf16[256,2048]{1,0:T(8,128)(2,1)S(1)}, bf16[256,2048]{1,0:T(8,128)(2,1)S(1)}, u32[]{:S(2)}, u32[]{:S(2)}) collective-permute-start(bf16[256,2048]{1,0:T(8,128)(2,1)S(1)} %fusion.1.refs_0_), channel_id=1, source_target_pairs={{0,1},{1,0},{2,3},{3,2},{4,5},{5,4},{6,7},{7,6},{8,9},{9,8},{10,11... | collective-permute-start | bytes 3145736 | tf_op jit(solution)/shard_map/ppermute | solution.py:342
  40.6 37.9 %collective-permute-start.8 = (bf16[512,768]{1,0:T(8,128)(2,1)}, bf16[512,768]{1,0:T(8,128)(2,1)}, u32[]{:S(2)}, u32[]{:S(2)}) collective-permute-start(bf16[512,768]{1,0:T(8,128)(2,1)} %bitcast.6), channel_id=1, source_target_pairs={{0,16},{16,0},{1,17},{17,1},{2,18},{18,2},{3,19},{19,3},{4,20},{20... | collective-permute-start | bytes 2359304 | tf_op jit(solution)/shard_map/ppermute | solution.py:342
  40.9 37.6 %collective-permute-start.9 = (bf16[512,768]{1,0:T(8,128)(2,1)}, bf16[512,768]{1,0:T(8,128)(2,1)}, u32[]{:S(2)}, u32[]{:S(2)}) collective-permute-start(bf16[512,768]{1,0:T(8,128)(2,1)} %bitcast.6), channel_id=1, source_target_pairs={{0,8},{8,0},{1,9},{9,1},{2,10},{10,2},{3,11},{11,3},{4,12},{12,4},... | collective-permute-start | bytes 2359304 | tf_op jit(solution)/shard_map/ppermute | solution.py:342
  78.5 20.7 %collective-permute-start.12 = (bf16[512,768]{1,0:T(8,128)(2,1)}, bf16[512,768]{1,0:T(8,128)(2,1)}, u32[]{:S(2)}, u32[]{:S(2)}) collective-permute-start(bf16[512,768]{1,0:T(8,128)(2,1)} %collective-permute-done.8), channel_id=1, source_target_pairs={{0,8},{8,0},{1,9},{9,1},{2,10},{10,2},{3,11},{11,3},{4,12},{12,4},... | collective-permute-start | bytes 2359304 | tf_op jit(solution)/shard_map/ppermute | solution.py:342
  80.3 26.2 %collective-permute-start.13 = (bf16[80,2432]{1,0:T(8,128)(2,1)}, bf16[80,2432]{1,0:T(8,128)(2,1)S(1)}, u32[]{:S(2)}, u32[]{:S(2)}) collective-permute-start(bf16[80,2432]{1,0:T(8,128)(2,1)} %collective-permute-done.10), channel_id=1, source_target_pairs={{0,8},{8,0},{1,9},{9,1},{2,10},{10,2},{3,11},{11,3},{4,12},{12,4},... | collective-permute-start | bytes 1167368 | tf_op jit(solution)/shard_map/ppermute | solution.py:342
  82.4 38.2 %all-to-all-start.1 = ((bf16[8,64,1536]{2,1,0:T(8,128)(2,1)}), bf16[8,64,1536]{2,1,0:T(8,128)(2,1)}, u32[]{:S(2)}, u32[]{:S(2)}) async-start(bf16[8,64,1536]{2,1,0:T(8,128)(2,1)} %pack_columns.3), calls=%async_computation.1 | async-start | bytes 3145728 | tf_op jit(solution)/shard_map/all_to_all | solution.py:466
  86.7 118.3 %all-gather.3.cloned.1.call-start = ((), (), s32[]{:S(2)}) async-start(), calls=%async_computation.8 | async-start | bytes 3932160 | tf_op jit(solution)/shard_map/all_gather | solution.py:979
  99.2 204.2 %all-gather.5.cloned.1.call-start = ((), (), s32[]{:S(2)}) async-start(), calls=%async_computation.9 | async-start | bytes 7864320 | tf_op jit(solution)/shard_map/all_gather | solution.py:982
  168.4 25.8 %collective-permute-start.27 = (bf16[256,2048]{1,0:T(8,128)(2,1)}, bf16[256,2048]{1,0:T(8,128)(2,1)}, u32[]{:S(2)}, u32[]{:S(2)}) collective-permute-start(bf16[256,2048]{1,0:T(8,128)(2,1)} %param.35), channel_id=1, source_target_pairs={{0,2},{2,0},{1,3},{3,1},{4,6},{6,4},{5,7},{7,5},{8,10},{10,8},{9,1... | collective-permute-start | bytes 3145736 | tf_op jit(solution)/shard_map/ppermute | solution.py:342
  169.9 25.5 %collective-permute-start.28 = (bf16[256,2048]{1,0:T(8,128)(2,1)}, bf16[256,2048]{1,0:T(8,128)(2,1)}, u32[]{:S(2)}, u32[]{:S(2)}) collective-permute-start(bf16[256,2048]{1,0:T(8,128)(2,1)} %param.35), channel_id=1, source_target_pairs={{0,4},{4,0},{1,5},{5,1},{2,6},{6,2},{3,7},{7,3},{8,12},{12,8},{9,1... | collective-permute-start | bytes 3145736 | tf_op jit(solution)/shard_map/ppermute | solution.py:342
  170.8 24.6 %collective-permute-start.29 = (bf16[256,2048]{1,0:T(8,128)(2,1)}, bf16[256,2048]{1,0:T(8,128)(2,1)}, u32[]{:S(2)}, u32[]{:S(2)}) collective-permute-start(bf16[256,2048]{1,0:T(8,128)(2,1)} %param.35), channel_id=1, source_target_pairs={{0,1},{1,0},{2,3},{3,2},{4,5},{5,4},{6,7},{7,6},{8,9},{9,8},{10,11... | collective-permute-start | bytes 3145736 | tf_op jit(solution)/shard_map/ppermute | solution.py:342
  184.3 275.4 %reduce-scatter.4.cloned.1.call-start = ((), (), s32[]{:S(2)}) async-start(), calls=%async_computation.10 | async-start | bytes 3932160 | tf_op jit(solution)/shard_map/reduce_scatter | solution.py:1002
  195.5 52.8 %collective-permute-start.16 = (bf16[256,2048]{1,0:T(8,128)(2,1)}, bf16[256,2048]{1,0:T(8,128)(2,1)}, u32[]{:S(2)}, u32[]{:S(2)}) collective-permute-start(bf16[256,2048]{1,0:T(8,128)(2,1)} %get-tuple-element.180), channel_id=1, source_target_pairs={{0,1},{1,0},{2,3},{3,2},{4,5},{5,4},{6,7},{7,6},{8,9},{9,8},{10,11... | collective-permute-start | bytes 3145736 | tf_op jit(solution)/shard_map/ppermute | solution.py:342
  197.3 43.6 %collective-permute-start.32 = (bf16[256,2048]{1,0:T(8,128)(2,1)}, bf16[256,2048]{1,0:T(8,128)(2,1)}, u32[]{:S(2)}, u32[]{:S(2)}) collective-permute-start(bf16[256,2048]{1,0:T(8,128)(2,1)} %collective-permute-done.27), channel_id=1, source_target_pairs={{0,1},{1,0},{2,3},{3,2},{4,5},{5,4},{6,7},{7,6},{8,9},{9,8},{10,11... | collective-permute-start | bytes 3145736 | tf_op jit(solution)/shard_map/ppermute | solution.py:342
  199.7 41.2 %collective-permute-start.33 = (bf16[256,2048]{1,0:T(8,128)(2,1)}, bf16[256,2048]{1,0:T(8,128)(2,1)}, u32[]{:S(2)}, u32[]{:S(2)}) collective-permute-start(bf16[256,2048]{1,0:T(8,128)(2,1)} %collective-permute-done.28), channel_id=1, source_target_pairs={{0,1},{1,0},{2,3},{3,2},{4,5},{5,4},{6,7},{7,6},{8,9},{9,8},{10,11... | collective-permute-start | bytes 3145736 | tf_op jit(solution)/shard_map/ppermute | solution.py:342
  234.3 24.0 %collective-permute-start.22 = (bf16[256,2048]{1,0:T(8,128)(2,1)S(1)}, bf16[256,2048]{1,0:T(8,128)(2,1)S(1)}, u32[]{:S(2)}, u32[]{:S(2)}) collective-permute-start(bf16[256,2048]{1,0:T(8,128)(2,1)S(1)} %pad_maximum_fusion), channel_id=1, source_target_pairs={{0,2},{2,0},{1,3},{3,1},{4,6},{6,4},{5,7},{7,5},{8,10},{10,8},{9,1... | collective-permute-start | bytes 3145736 | tf_op jit(solution)/shard_map/ppermute | solution.py:342
  235.2 23.7 %collective-permute-start.23 = (bf16[256,2048]{1,0:T(8,128)(2,1)S(1)}, bf16[256,2048]{1,0:T(8,128)(2,1)S(1)}, u32[]{:S(2)}, u32[]{:S(2)}) collective-permute-start(bf16[256,2048]{1,0:T(8,128)(2,1)S(1)} %pad_maximum_fusion.1), channel_id=1, source_target_pairs={{0,4},{4,0},{1,5},{5,1},{2,6},{6,2},{3,7},{7,3},{8,12},{12,8},{9,1... | collective-permute-start | bytes 3145736 | tf_op jit(solution)/shard_map/ppermute | solution.py:342
  261.3 23.0 %collective-permute-start.24 = (bf16[256,2048]{1,0:T(8,128)(2,1)S(1)}, bf16[256,2048]{1,0:T(8,128)(2,1)S(1)}, u32[]{:S(2)}, u32[]{:S(2)}) collective-permute-start(bf16[256,2048]{1,0:T(8,128)(2,1)S(1)} %multiply_convert_fusion.refs_0_), channel_id=1, source_target_pairs={{0,2},{2,0},{1,3},{3,1},{4,6},{6,4},{5,7},{7,5},{8,10},{10,8},{9,1... | collective-permute-start | bytes 3145736 | tf_op jit(solution)/shard_map/ppermute | solution.py:342
  262.5 22.7 %collective-permute-start.25 = (bf16[256,2048]{1,0:T(8,128)(2,1)S(1)}, bf16[256,2048]{1,0:T(8,128)(2,1)S(1)}, u32[]{:S(2)}, u32[]{:S(2)}) collective-permute-start(bf16[256,2048]{1,0:T(8,128)(2,1)S(1)} %multiply_convert_fusion.refs_0_), channel_id=1, source_target_pairs={{0,4},{4,0},{1,5},{5,1},{2,6},{6,2},{3,7},{7,3},{8,12},{12,8},{9,1... | collective-permute-start | bytes 3145736 | tf_op jit(solution)/shard_map/ppermute | solution.py:342
  263.4 21.7 %collective-permute-start.26 = (bf16[256,2048]{1,0:T(8,128)(2,1)S(1)}, bf16[256,2048]{1,0:T(8,128)(2,1)S(1)}, u32[]{:S(2)}, u32[]{:S(2)}) collective-permute-start(bf16[256,2048]{1,0:T(8,128)(2,1)S(1)} %multiply_convert_fusion.refs_0_), channel_id=1, source_target_pairs={{0,1},{1,0},{2,3},{3,2},{4,5},{5,4},{6,7},{7,6},{8,9},{9,8},{10,11... | collective-permute-start | bytes 3145736 | tf_op jit(solution)/shard_map/ppermute | solution.py:342
  350.1 26.3 %collective-permute-start.40 = (bf16[256,2048]{1,0:T(8,128)(2,1)}, bf16[256,2048]{1,0:T(8,128)(2,1)}, u32[]{:S(2)}, u32[]{:S(2)}) collective-permute-start(bf16[256,2048]{1,0:T(8,128)(2,1)} %get-tuple-element.208), channel_id=1, source_target_pairs={{0,1},{1,0},{2,3},{3,2},{4,5},{5,4},{6,7},{7,6},{8,9},{9,8},{10,11... | collective-permute-start | bytes 3145736 | tf_op jit(solution)/shard_map/ppermute | solution.py:342
  368.8 171.3 %reduce-scatter.6.cloned.1.call-start = ((), (), s32[]{:S(2)}) async-start(), calls=%async_computation.11 | async-start | bytes 3932160 | tf_op jit(solution)/shard_map/reduce_scatter | solution.py:1006
  374.3 24.9 %collective-permute-start.46 = (bf16[256,2048]{1,0:T(8,128)(2,1)S(1)}, bf16[256,2048]{1,0:T(8,128)(2,1)S(1)}, u32[]{:S(2)}, u32[]{:S(2)}) collective-permute-start(bf16[256,2048]{1,0:T(8,128)(2,1)S(1)} %pad_maximum_fusion.3), channel_id=1, source_target_pairs={{0,2},{2,0},{1,3},{3,1},{4,6},{6,4},{5,7},{7,5},{8,10},{10,8},{9,1... | collective-permute-start | bytes 3145736 | tf_op jit(solution)/shard_map/ppermute | solution.py:342
  375.5 24.4 %collective-permute-start.47 = (bf16[256,2048]{1,0:T(8,128)(2,1)S(1)}, bf16[256,2048]{1,0:T(8,128)(2,1)S(1)}, u32[]{:S(2)}, u32[]{:S(2)}) collective-permute-start(bf16[256,2048]{1,0:T(8,128)(2,1)S(1)} %pad_maximum_fusion.4), channel_id=1, source_target_pairs={{0,4},{4,0},{1,5},{5,1},{2,6},{6,2},{3,7},{7,3},{8,12},{12,8},{9,1... | collective-permute-start | bytes 3145736 | tf_op jit(solution)/shard_map/ppermute | solution.py:342
  414.7 161.3 %reduce-scatter.8.cloned.1.call-start = ((), (), s32[]{:S(2)}) async-start(), calls=%async_computation.12 | async-start | bytes 3932160 | tf_op jit(solution)/shard_map/reduce_scatter | solution.py:1007
  414.9 23.9 %collective-permute-start.48 = (bf16[256,2048]{1,0:T(8,128)(2,1)}, bf16[256,2048]{1,0:T(8,128)(2,1)}, u32[]{:S(2)}, u32[]{:S(2)}) collective-permute-start(bf16[256,2048]{1,0:T(8,128)(2,1)} %get-tuple-element.325.refs_0_), channel_id=1, source_target_pairs={{0,2},{2,0},{1,3},{3,1},{4,6},{6,4},{5,7},{7,5},{8,10},{10,8},{9,1... | collective-permute-start | bytes 3145736 | tf_op jit(solution)/shard_map/ppermute | solution.py:342
  416.0 23.7 %collective-permute-start.49 = (bf16[256,2048]{1,0:T(8,128)(2,1)}, bf16[256,2048]{1,0:T(8,128)(2,1)}, u32[]{:S(2)}, u32[]{:S(2)}) collective-permute-start(bf16[256,2048]{1,0:T(8,128)(2,1)} %get-tuple-element.325.refs_0_), channel_id=1, source_target_pairs={{0,4},{4,0},{1,5},{5,1},{2,6},{6,2},{3,7},{7,3},{8,12},{12,8},{9,1... | collective-permute-start | bytes 3145736 | tf_op jit(solution)/shard_map/ppermute | solution.py:342
  416.8 22.9 %collective-permute-start.50 = (bf16[256,2048]{1,0:T(8,128)(2,1)}, bf16[256,2048]{1,0:T(8,128)(2,1)S(1)}, u32[]{:S(2)}, u32[]{:S(2)}) collective-permute-start(bf16[256,2048]{1,0:T(8,128)(2,1)} %get-tuple-element.325.refs_0_), channel_id=1, source_target_pairs={{0,1},{1,0},{2,3},{3,2},{4,5},{5,4},{6,7},{7,6},{8,9},{9,8},{10,11... | collective-permute-start | bytes 3145736 | tf_op jit(solution)/shard_map/ppermute | solution.py:342
  525.8 32.3 %collective-permute-start.56 = (bf16[256,2048]{1,0:T(8,128)(2,1)}, bf16[256,2048]{1,0:T(8,128)(2,1)}, u32[]{:S(2)}, u32[]{:S(2)}) collective-permute-start(bf16[256,2048]{1,0:T(8,128)(2,1)} %get-tuple-element.237), channel_id=1, source_target_pairs={{0,1},{1,0},{2,3},{3,2},{4,5},{5,4},{6,7},{7,6},{8,9},{9,8},{10,11... | collective-permute-start | bytes 3145736 | tf_op jit(solution)/shard_map/ppermute | solution.py:342
  537.2 54.3 %collective-permute-start.67 = (bf16[512,768]{1,0:T(8,128)(2,1)}, bf16[512,768]{1,0:T(8,128)(2,1)}, u32[]{:S(2)}, u32[]{:S(2)}) collective-permute-start(bf16[512,768]{1,0:T(8,128)(2,1)} %get-tuple-element.330), channel_id=1, source_target_pairs={{0,8},{8,0},{1,9},{9,1},{2,10},{10,2},{3,11},{11,3},{4,12},{12,4},... | collective-permute-start | bytes 2359304 | tf_op jit(solution)/shard_map/ppermute | solution.py:342
  537.9 54.2 %collective-permute-start.68 = (bf16[512,768]{1,0:T(8,128)(2,1)}, bf16[512,768]{1,0:T(8,128)(2,1)}, u32[]{:S(2)}, u32[]{:S(2)}) collective-permute-start(bf16[512,768]{1,0:T(8,128)(2,1)} %get-tuple-element.329), channel_id=1, source_target_pairs={{0,8},{8,0},{1,9},{9,1},{2,10},{10,2},{3,11},{11,3},{4,12},{12,4},... | collective-permute-start | bytes 2359304 | tf_op jit(solution)/shard_map/ppermute | solution.py:342
  543.7 59.4 %collective-permute-start.64 = (bf16[256,2048]{1,0:T(8,128)(2,1)}, bf16[256,2048]{1,0:T(8,128)(2,1)}, u32[]{:S(2)}, u32[]{:S(2)}) collective-permute-start(bf16[256,2048]{1,0:T(8,128)(2,1)} %copy-done.46), channel_id=1, source_target_pairs={{0,1},{1,0},{2,3},{3,2},{4,5},{5,4},{6,7},{7,6},{8,9},{9,8},{10,11... | collective-permute-start | bytes 3145736 | tf_op jit(solution)/shard_map/ppermute | solution.py:342
  574.8 26.4 %collective-permute-start.65 = (bf16[256,2048]{1,0:T(8,128)(2,1)}, bf16[256,2048]{1,0:T(8,128)(2,1)}, u32[]{:S(2)}, u32[]{:S(2)}) collective-permute-start(bf16[256,2048]{1,0:T(8,128)(2,1)} %pad_maximum_fusion.5), channel_id=1, source_target_pairs={{0,2},{2,0},{1,3},{3,1},{4,6},{6,4},{5,7},{7,5},{8,10},{10,8},{9,1... | collective-permute-start | bytes 3145736 | tf_op jit(solution)/shard_map/ppermute | solution.py:342
  575.1 27.4 %collective-permute-start.66 = (bf16[256,2048]{1,0:T(8,128)(2,1)}, bf16[256,2048]{1,0:T(8,128)(2,1)}, u32[]{:S(2)}, u32[]{:S(2)}) collective-permute-start(bf16[256,2048]{1,0:T(8,128)(2,1)} %pad_maximum_fusion.6), channel_id=1, source_target_pairs={{0,4},{4,0},{1,5},{5,1},{2,6},{6,2},{3,7},{7,3},{8,12},{12,8},{9,1... | collective-permute-start | bytes 3145736 | tf_op jit(solution)/shard_map/ppermute | solution.py:342
  576.0 74.5 %all-to-all-start.4 = ((bf16[8,64,768]{2,1,0:T(8,128)(2,1)}), bf16[8,64,768]{2,1,0:T(8,128)(2,1)S(1)}, u32[]{:S(2)}, u32[]{:S(2)}) async-start(bf16[8,64,768]{2,1,0:T(8,128)(2,1)} %bitcast.102), calls=%async_computation.7 | async-start | bytes 1572864 | tf_op jit(solution)/shard_map/all_to_all | solution.py:466
  591.5 30.0 %collective-permute-start.70 = (bf16[256,2048]{1,0:T(8,128)(2,1)S(1)}, bf16[256,2048]{1,0:T(8,128)(2,1)S(1)}, u32[]{:S(2)}, u32[]{:S(2)}) collective-permute-start(bf16[256,2048]{1,0:T(8,128)(2,1)S(1)} %get-tuple-element.263), channel_id=1, source_target_pairs={{0,1},{1,0},{2,3},{3,2},{4,5},{5,4},{6,7},{7,6},{8,9},{9,8},{10,11... | collective-permute-start | bytes 3145736 | tf_op jit(solution)/shard_map/ppermute | solution.py:342
  602.5 42.4 %collective-permute-start.74 = (bf16[512,768]{1,0:T(8,128)(2,1)S(1)}, bf16[512,768]{1,0:T(8,128)(2,1)S(1)}, u32[]{:S(2)}, u32[]{:S(2)}) collective-permute-start(bf16[512,768]{1,0:T(8,128)(2,1)S(1)} %fusion.9), channel_id=1, source_target_pairs={{0,16},{16,0},{1,17},{17,1},{2,18},{18,2},{3,19},{19,3},{4,20},{20... | collective-permute-start | bytes 2359304 | tf_op jit(solution)/shard_map/ppermute | solution.py:342
  603.1 93.1 %collective-permute-start.61 = (bf16[256,2048]{1,0:T(8,128)(2,1)}, bf16[256,2048]{1,0:T(8,128)(2,1)}, u32[]{:S(2)}, u32[]{:S(2)}) collective-permute-start(bf16[256,2048]{1,0:T(8,128)(2,1)} %get-tuple-element.250), channel_id=1, source_target_pairs={{0,1},{1,0},{2,3},{3,2},{4,5},{5,4},{6,7},{7,6},{8,9},{9,8},{10,11... | collective-permute-start | bytes 3145736 | tf_op jit(solution)/shard_map/ppermute | solution.py:342
  623.5 21.4 %collective-permute-start.79 = (bf16[2,80,2048]{2,1,0:T(8,128)(2,1)S(1)}, bf16[2,80,2048]{2,1,0:T(8,128)(2,1)S(1)}, u32[]{:S(2)}, u32[]{:S(2)}) collective-permute-start(bf16[2,80,2048]{2,1,0:T(8,128)(2,1)S(1)} %dynamic-slice_bitcast_fusion.2), channel_id=1, source_target_pairs={{0,1},{1,0},{2,3},{3,2},{4,5},{5,4},{6,7},{7,6},{8,9},{9,8},{10,11... | collective-permute-start | bytes 1966088 | tf_op jit(solution)/shard_map/ppermute | solution.py:342
  641.7 50.6 %collective-permute-start.72 = (bf16[256,2048]{1,0:T(8,128)(2,1)}, bf16[256,2048]{1,0:T(8,128)(2,1)}, u32[]{:S(2)}, u32[]{:S(2)}) collective-permute-start(bf16[256,2048]{1,0:T(8,128)(2,1)} %pad_maximum_fusion.7), channel_id=1, source_target_pairs={{0,2},{2,0},{1,3},{3,1},{4,6},{6,4},{5,7},{7,5},{8,10},{10,8},{9,1... | collective-permute-start | bytes 3145736 | tf_op jit(solution)/shard_map/ppermute | solution.py:342
  644.9 22.9 %collective-permute-start.78 = (f32[80,328]{1,0:T(8,128)}, f32[80,328]{1,0:T(8,128)}, u32[]{:S(2)}, u32[]{:S(2)}) collective-permute-start(f32[80,328]{1,0:T(8,128)} %bitcast_add_fusion), channel_id=1, source_target_pairs={{0,16},{16,0},{1,17},{17,1},{2,18},{18,2},{3,19},{19,3},{4,20},{20... | collective-permute-start | bytes 314888 | tf_op jit(solution)/shard_map/ppermute | solution.py:342
  646.0 25.5 %collective-permute-start.80 = (bf16[80,2048]{1,0:T(8,128)(2,1)}, bf16[80,2048]{1,0:T(8,128)(2,1)}, u32[]{:S(2)}, u32[]{:S(2)}) collective-permute-start(bf16[80,2048]{1,0:T(8,128)(2,1)} %get-tuple-element.332), channel_id=1, source_target_pairs={{0,8},{8,0},{1,9},{9,1},{2,10},{10,2},{3,11},{11,3},{4,12},{12,4},... | collective-permute-start | bytes 983048 | tf_op jit(solution)/shard_map/ppermute | solution.py:342
  648.1 23.5 %collective-permute-start.81 = (bf16[80,2048]{1,0:T(8,128)(2,1)}, bf16[80,2048]{1,0:T(8,128)(2,1)}, u32[]{:S(2)}, u32[]{:S(2)}) collective-permute-start(bf16[80,2048]{1,0:T(8,128)(2,1)} %get-tuple-element.331), channel_id=1, source_target_pairs={{0,8},{8,0},{1,9},{9,1},{2,10},{10,2},{3,11},{11,3},{4,12},{12,4},... | collective-permute-start | bytes 983048 | tf_op jit(solution)/shard_map/ppermute | solution.py:342
  650.5 26.5 %all-to-all-start.3 = ((bf16[8,64,768]{2,1,0:T(8,128)(2,1)}), bf16[8,64,768]{2,1,0:T(8,128)(2,1)S(1)}, u32[]{:S(2)}, u32[]{:S(2)}) async-start(bf16[8,64,768]{2,1,0:T(8,128)(2,1)} %bitcast.99), calls=%async_computation.6 | async-start | bytes 1572864 | tf_op jit(solution)/shard_map/all_to_all | solution.py:466
  667.8 28.4 %collective-permute-start.73 = (bf16[256,2048]{1,0:T(8,128)(2,1)}, bf16[256,2048]{1,0:T(8,128)(2,1)}, u32[]{:S(2)}, u32[]{:S(2)}) collective-permute-start(bf16[256,2048]{1,0:T(8,128)(2,1)} %pad_maximum_fusion.8), channel_id=1, source_target_pairs={{0,4},{4,0},{1,5},{5,1},{2,6},{6,2},{3,7},{7,3},{8,12},{12,8},{9,1... | collective-permute-start | bytes 3145736 | tf_op jit(solution)/shard_map/ppermute | solution.py:342
  (137 other events, 1465.4 us)
Sparse Core Ops, SparseCore 0:
  99.4 62.8 all-gather.2
  184.4 113.5 all-gather.4
  368.9 58.7 reduce-scatter.3
  429.9 60.2 reduce-scatter.5
  492.4 70.7 reduce-scatter.7
